TPU v7x, 32 devices: a whole 2x2x4 slice. The times are simulated.
32 devices in a mesh: grp: 2 (over y), gy: 4 (over z), gz: 2 (over x), vert: 2 (over core).
Axes of the slice: x: 2, y: 2, z: 4, core: 2. Of those that a mesh axis runs over, the one named last changes fastest.
Arguments:
- field: float32 [16, 64, 64, 512], P(('grp', 'vert'), 'gy', 'gz'), parts along dimension 0, as said below
- omega_x: float32 [512, 128], replicated, may hold values from -6 to 6
- omega_y: float32 [64, 32], replicated, may hold values from -6 to 6
- rank_x: int32 [2], P('grp'), parts along dimension 0, may hold values from 64 to 128
- rank_y: int32 [2], P('grp'), parts along dimension 0, may hold values from 16 to 32
Outputs:
- core: float32 [16, 32, 64, 128], P(('grp', 'vert'), 'gy', 'gz'), parts along dimension 0
- factor_x: float32 [1024, 128], P('grp'), parts along dimension 0
- factor_y: float32 [128, 32], P('grp'), parts along dimension 0
There are 2 independent parts, one for each index of `grp`. A program takes and returns all parts, laid end to end along the dimension named above; an argument that names none is the same for every part. Nothing has to cross between parts.
Inputs may be any that keep to these rules, and one draw needn't show every extreme that they name: field values are finite and of order one; their spread differs between cells of the first dimension.
All inputs are finite; a program needn't handle non-finite values.
Results may differ from a plain program's by a relative error of at most 0.000086.
Values sent between devices are 32-bit elements; how exact they have to be, the bound alone decides.
No kernel may reach another device: no remote copies, remote signals or barrier semaphores. Data moves between devices by JAX's collectives and lax.ppermute only.
A program may use at most 64 MiB of HBM per device.

v0:
```python
import jax
import jax.numpy as jnp
from jax import lax
from jax.sharding import PartitionSpec as P


def orthonormal(sketch, trunc_rank):
    precise = lax.Precision.HIGHEST
    small_gram = jnp.dot(sketch.T, sketch, precision=precise)
    lower_factor = jnp.linalg.cholesky(small_gram)
    basis = lax.linalg.triangular_solve(
        lower_factor, sketch, left_side=False, lower=True, transpose_a=True
    )
    column_ids = jnp.arange(sketch.shape[1], dtype=jnp.int32)
    kept = (column_ids < trunc_rank[0]).astype(jnp.float32)
    return basis * kept[None, :]


def body(field, omega_x, omega_y, rank_x, rank_y):
    precise = lax.Precision.HIGHEST
    planes, rows_y, rows_z, cells_x = field.shape
    all_planes = planes * lax.axis_size("vert")
    all_rows_y = rows_y * lax.axis_size("gy")
    all_rows_z = rows_z * lax.axis_size("gz")
    flat = field.reshape(-1, cells_x)
    local_gram = jnp.dot(flat.T, flat, precision=precise)
    gram_x = lax.psum(local_gram, ("gy", "gz", "vert")) / float(
        all_planes * all_rows_y * all_rows_z
    )
    sketch_x = jnp.dot(gram_x, omega_x, precision=precise)
    factor_x = orthonormal(sketch_x, rank_x)
    ranks_x = factor_x.shape[1]
    core_x = jnp.dot(flat, factor_x, precision=precise).reshape(planes, rows_y, rows_z, ranks_x)
    spread = lax.all_to_all(core_x, "gy", split_axis=2, concat_axis=1, tiled=True)
    divisor_y = float(all_planes * all_rows_z * ranks_x)
    local_gram_y = jnp.einsum("vazr,vbzr->ab", spread, spread, precision=precise)
    gram_y = lax.psum(local_gram_y, ("gy", "gz", "vert")) / divisor_y
    sketch_y = jnp.dot(gram_y, omega_y, precision=precise)
    factor_y = orthonormal(sketch_y, rank_y)
    own_rows = lax.dynamic_slice_in_dim(factor_y, lax.axis_index("gy") * rows_y, rows_y, 0)
    partial_core = jnp.einsum("vyzr,yk->vkzr", core_x, own_rows, precision=precise)
    core = lax.psum_scatter(partial_core, "gy", scatter_dimension=1, tiled=True)
    return (core, factor_x, factor_y)


def solution(mesh):
    in_specs = (P(("grp", "vert"), "gy", "gz", None), P(), P(), P("grp"), P("grp"))
    out_specs = (P(("grp", "vert"), "gy", "gz", None), P("grp", None), P("grp", None))
    return jax.shard_map(body, mesh=mesh, in_specs=in_specs, out_specs=out_specs, check_vma=False)
```

profile of v0, /device:TPU:0, one launch (start us, length us, event | category | flops | bytes accessed | tf_op | source)
XLA Modules:
  0.0 297.8 jit_solution(9026091987991495649)
XLA Ops:
  7.2 0.0 copy-start
  7.2 0.0 all-reduce.2.cloned.1.call-start
  7.2 10.3 %convolution_bitcast_fusion.2 = f32[512,512]{1,0:T(8,128)} fusion(f32[4,16,32,512]{3,2,1,0:T(8,128)} %param.5), kind=kOutput, calls=%fused_computation.2 | convolution fusion | flops 6442450944 | bytes 5242880 | tf_op jit(solution)/shard_map/dot_general | solution.py:26
  17.5 0.0 all-reduce.2.cloned.1.call-update
  18.2 95.4 %all-reduce.2.cloned.1.call-done = f32[512,512]{1,0:T(8,128)} async-done(((f32[512,512]{1,0:T(8,128)}), f32[512,512]{1,0:T(8,128)}) %all-reduce.2.cloned.1.call-update) | async-done | bytes 1048592 | tf_op jit(solution)/shard_map/psum | solution.py:27
  113.7 0.0 copy-done
  113.7 2.2 fusion.2
  115.9 0.6 fusion.19
  116.5 0.1 copy.20
  116.6 11.7 %cholesky.29 = f32[128,128]{1,0:T(8,128)S(1)} custom-call(f32[128,128]{1,0:T(8,128)S(1)} %fusion.7), custom_call_target="Cholesky" | custom-call | tf_op jit(solution)/shard_map/jit(cholesky)/cholesky | solution.py:10
  128.3 0.6 compare_reduce_fusion.1
  129.0 0.7 fusion.5
  129.6 9.8 %custom-call.12 = f32[1,128,128]{1,2,0:T(8,128)S(1)} custom-call(f32[1,128,128]{2,1,0:T(8,128)S(1)} %fusion.5), custom_call_target="InvertDiagBlocksLowerTriangular" | custom-call | tf_op jit(solution)/shard_map/triangular_solve | solution.py:11
  139.5 0.4 convolution_multiply_fusion
  139.8 0.0 copy-start.1
  139.8 6.7 %convolution_bitcast_fusion = f32[2048,128]{0,1:T(8,128)S(1)} fusion(f32[512,128]{1,0:T(8,128)S(1)} %convolution_multiply_fusion, f32[2048,512]{1,0:T(8,128)} %bitcast.57), kind=kOutput, calls=%fused_computation | convolution fusion | flops 1610612736 | bytes 5505024 | tf_op jit(solution)/shard_map/dot_general | solution.py:33
  146.6 0.3 copy.21
  146.9 0.0 copy-start.3
  146.9 1.8 copy.22
  148.8 0.0 copy-done.1
  148.8 3.8 %all-to-all-start = ((f32[4,16,32,128]{3,1,0,2:T(8,128)}), f32[4,16,32,128]{3,1,0,2:T(8,128)S(1)}, u32[]{:S(2)}, u32[]{:S(2)}) async-start(f32[4,16,32,128]{3,1,0,2:T(8,128)} %copy.22), calls=%async_computation | async-start | bytes 2097152 | tf_op jit(solution)/shard_map/all_to_all | solution.py:34
  152.6 0.0 reduce-scatter.2.cloned.1.call-start
  153.2 24.4 %all-to-all-done = f32[4,16,32,128]{3,1,0,2:T(8,128)S(1)} async-done(((f32[4,16,32,128]{3,1,0,2:T(8,128)}), f32[4,16,32,128]{3,1,0,2:T(8,128)S(1)}, u32[]{:S(2)}, u32[]{:S(2)}) %all-to-all-start) | async-done | bytes 1048608 | tf_op jit(solution)/shard_map/all_to_all | solution.py:34
  177.6 0.6 copy.24
  178.3 1.0 convolution_bitcast_fusion.3
  179.2 57.6 %psum.15 = f32[64,64]{1,0:T(8,128)S(1)} all-reduce(f32[64,64]{1,0:T(8,128)S(1)} %convolution_bitcast_fusion.3), channel_id=1, replica_groups=mesh['grp'=2,'gy'=4,'gz'=2,'vert'=2] {'gy','gz','vert'}, use_global_device_ids=true, to_apply=%region_3.4 | all-reduce | flops 4096 | bytes 32768 | tf_op jit(solution)/shard_map/psum | solution.py:37
  236.9 0.0 copy-done.3
  236.9 0.2 fusion.8
  237.0 0.1 fusion.20
  237.2 0.1 copy.27
  237.3 2.9 cholesky.61
  240.2 0.6 compare_reduce_fusion
  240.9 0.7 fusion.10
  241.5 2.5 custom-call.13
  244.0 0.2 convolution_multiply_fusion.1
  244.2 0.0 copy-start.2
  244.2 3.5 %convolution_bitcast_fusion.1 = f32[4,32,32,128]{3,1,2,0:T(8,128)} fusion(f32[4,16,32,128]{3,2,1,0:T(8,128)S(1)} %bitcast.56, f32[64,32]{0,1:T(8,128)S(1)} %convolution_multiply_fusion.1, s32[]{:T(128)S(6)} %select_n.13), kind=kOutput, calls=%fused_computation.1 | convolution fusion | flops 100663296 | bytes 3153924 | tf_op jit(solution)/shard_map/vyzr,yk->vkzr/dot_general | solution.py:41
  247.8 0.0 reduce-scatter.2.cloned.1.call-update
  247.8 41.3 %reduce-scatter.2.cloned.1.call-done = f32[4,8,32,128]{3,1,2,0:T(8,128)} async-done(((f32[4,32,32,128]{3,1,2,0:T(8,128)}), f32[4,8,32,128]{3,1,2,0:T(8,128)}) %reduce-scatter.2.cloned.1.call-update) | async-done | bytes 524304 | tf_op jit(solution)/shard_map/reduce_scatter | solution.py:42
  289.1 1.9 copy.30
  291.0 0.0 copy-done.2
  (6 shorter events, 0.1 us)
Async XLA Ops:
  7.2 106.5 %copy-start = (f32[512,128]{1,0:T(8,128)S(1)}, f32[512,128]{1,0:T(8,128)}, u32[]{:S(2)}) copy-start(f32[512,128]{1,0:T(8,128)} %param.6) | copy-start | bytes 786436
  7.2 106.5 %all-reduce.2.cloned.1.call-start = ((), (), s32[]{:S(2)}) async-start(), calls=%async_computation.2 | async-start | bytes 2097152 | tf_op jit(solution)/shard_map/psum | solution.py:27
  139.8 8.9 %copy-start.1 = (f32[512,128]{1,0:T(8,128)}, f32[512,128]{1,0:T(8,128)S(1)}, u32[]{:S(2)}) copy-start(f32[512,128]{1,0:T(8,128)S(1)} %convolution_multiply_fusion) | copy-start | bytes 786436
  146.9 89.9 %copy-start.3 = (f32[64,32]{0,1:T(8,128)S(1)}, f32[64,32]{0,1:T(8,128)}, u32[]{:S(2)}) copy-start(f32[64,32]{0,1:T(8,128)} %param.7) | copy-start | bytes 24580
  148.8 28.9 %all-to-all-start = ((f32[4,16,32,128]{3,1,0,2:T(8,128)}), f32[4,16,32,128]{3,1,0,2:T(8,128)S(1)}, u32[]{:S(2)}, u32[]{:S(2)}) async-start(f32[4,16,32,128]{3,1,0,2:T(8,128)} %copy.22), calls=%async_computation | async-start | bytes 2097152 | tf_op jit(solution)/shard_map/all_to_all | solution.py:34
  152.6 136.5 %reduce-scatter.2.cloned.1.call-start = ((), (), s32[]{:S(2)}) async-start(), calls=%async_computation.3 | async-start | bytes 2621440 | tf_op jit(solution)/shard_map/reduce_scatter | solution.py:42
  244.2 46.8 %copy-start.2 = (f32[64,32]{0,1:T(8,128)}, f32[64,32]{0,1:T(8,128)S(1)}, u32[]{:S(2)}) copy-start(f32[64,32]{0,1:T(8,128)S(1)} %convolution_multiply_fusion.1) | copy-start | bytes 24580
Sparse Core Ops, SparseCore 0:
  17.7 95.9 all-reduce.1
  247.9 41.0 reduce-scatter.1
where the time goes:
time: 298 us
  waiting for transfers between devices  161 us (54%)
  blocking collectives  57.6 us (19%)
  other arithmetic  29.6 us (10%)
  matrix products  25.3 us (8%)
  between operations  15.5 us (5%)
  local copies, waits for them, and re-layouts  4.87 us (2%)
  starting transfers between devices  3.84 us (1%)
    psum x1, waiting for transfers between devices, body(): lax.psum(local_gram, ('gy', 'gz', 'vert'))  95.4 us
    psum x1, blocking collectives, body(): gram_y = lax.psum(local_gram_y, ('gy', 'gz', 'vert')) / divisor_y  57.6 us
    reduce_scatter x1, waiting for transfers between devices, body(): core = lax.psum_scatter(partial_core, 'gy', scatter_dimension=1, tiled=True)  41.3 us
    all_to_all x1, waiting for transfers between devices, body(): lax.all_to_all(core_x, 'gy', split_axis=2, concat_axis=1, tiled=True)  24.4 us
    another operation x6, other arithmetic, orthonormal(): lower_factor = jnp.linalg.cholesky(small_gram)  16 us
    another operation x4, other arithmetic, orthonormal(): lax.linalg.triangular_solve(lower_factor, sketch, left_side=False, lower=...  13.6 us
    dot_general x1, matrix products, body(): local_gram = jnp.dot(flat.T, flat, precision=precise)  10.3 us
    dot_general x1, matrix products, body(): jnp.dot(flat, factor_x, precision=precise)  6.75 us
  transfers between devices with their start and end apart: 3, of which 3 were waited for; matrix products, arithmetic and copies ran while one was open for 0% of the time, Pallas kernels for 0%

commit v1 on v0

v1 whole, which is shorter than its diff:
```python
import jax
import jax.numpy as jnp
from jax import lax
from jax.sharding import PartitionSpec as P

HIGH = lax.Precision.HIGH
HIGHEST = lax.Precision.HIGHEST


def swap(value, axes, step):
    count = lax.axis_size(axes)
    assert count & (count - 1) == 0
    return lax.ppermute(value, axes, [(i, i ^ step) for i in range(count)])


def steps(count):
    return sorted(range(1, count), key=lambda s: -(s & 2) * 4 - s)


def by_step(blocks, me, count):
    if count == 4:
        pairs = blocks.reshape((2, 2) + blocks.shape[1:])
        pairs = jnp.where(me & 2 != 0, pairs[::-1], pairs)
        pairs = jnp.where(me & 1 != 0, pairs[:, ::-1], pairs)
        return pairs.reshape(blocks.shape)
    return jnp.take(blocks, me ^ jnp.arange(count), axis=0)


def sum_over_gy(part):
    count = lax.axis_size("gy")
    got = [swap(part, "gy", s) for s in steps(count)]
    for other in got:
        part = part + other
    return part


def sum_sketch(part):
    axes = ("gz", "vert")
    count = lax.axis_size(axes)
    me = lax.axis_index("gz") * lax.axis_size("vert") + lax.axis_index("vert")
    share = part.shape[0] // count
    cut = lambda who: lax.dynamic_slice_in_dim(part, who * share, share, 0)
    got = [swap(cut(me ^ s), axes, s) for s in steps(count)]
    mine = cut(me)
    for other in got:
        mine = mine + other
    mine = sum_over_gy(mine)
    whole = jnp.zeros_like(part)
    whole = lax.dynamic_update_slice_in_dim(whole, mine, me * share, 0)
    got = [(s, swap(mine, axes, s)) for s in steps(count)]
    for s, other in got:
        whole = lax.dynamic_update_slice_in_dim(whole, other, (me ^ s) * share, 0)
    return whole


def inverse_factor(small_gram, rank):
    lower = jnp.linalg.cholesky(small_gram)
    eye = jnp.eye(lower.shape[0], dtype=jnp.float32)
    inverse = lax.linalg.triangular_solve(lower, eye, left_side=False, lower=True, transpose_a=True)
    kept = (jnp.arange(lower.shape[0], dtype=jnp.int32) < rank[0]).astype(jnp.float32)
    return inverse * kept[None, :]


def body(field, omega_x, omega_y, rank_x, rank_y):
    planes, rows_y, rows_z, cells_x = field.shape
    ranks_x = omega_x.shape[1]
    ranks_y = omega_y.shape[1]
    n_gy = lax.axis_size("gy")
    gy = lax.axis_index("gy")
    all_planes = planes * lax.axis_size("vert")
    all_rows_y = rows_y * n_gy
    all_rows_z = rows_z * lax.axis_size("gz")
    flat = field.reshape(-1, cells_x)

    projected = jnp.dot(flat, omega_x, precision=HIGH)
    part = lax.dot_general(projected, flat, (((0,), (0,)), ((), ())), precision=HIGH)
    sketch_t = sum_sketch(part) / float(all_planes * all_rows_y * all_rows_z)

    share_z = rows_z // n_gy
    raw = lax.dot_general(flat, sketch_t, (((1,), (1,)), ((), ())), precision=HIGH)
    raw = raw.reshape(planes * rows_y, rows_z, ranks_x)
    cut = lambda who: lax.dynamic_slice_in_dim(raw, who * share_z, share_z, 1)
    chunks = [None] * n_gy
    for s in steps(n_gy):
        chunks[s] = swap(cut(gy ^ s), "gy", s)
    chunks[0] = cut(gy)

    small_gram = lax.dot_general(sketch_t, sketch_t, (((1,), (1,)), ((), ())), precision=HIGHEST)
    inverse_x = inverse_factor(small_gram, rank_x)
    factor_x = lax.dot_general(sketch_t, inverse_x, (((0,), (0,)), ((), ())), precision=HIGH)

    spread = jnp.stack(chunks).reshape(-1, ranks_x)
    spread = jnp.dot(spread, inverse_x, precision=HIGH)
    spread = spread.reshape(n_gy, planes, rows_y, share_z, ranks_x)
    local_gram_y = jnp.einsum("gvazr,hvbzr->gahb", spread, spread, precision=HIGH)
    local_gram_y = local_gram_y.reshape(all_rows_y, all_rows_y)
    omega_p = by_step(omega_y.reshape(n_gy, rows_y, ranks_y), gy, n_gy).reshape(all_rows_y, ranks_y)
    part_y = jnp.dot(local_gram_y, omega_p, precision=HIGHEST)
    part_y = by_step(part_y.reshape(n_gy, rows_y, ranks_y), gy, n_gy).reshape(all_rows_y, ranks_y)
    for axis in ("vert", "gz"):
        count = lax.axis_size(axis)
        got = [swap(part_y, axis, s) for s in steps(count)]
        for other in got:
            part_y = part_y + other
    sketch_y = sum_over_gy(part_y) / float(all_planes * all_rows_z * ranks_x)

    small_gram_y = lax.dot_general(sketch_y, sketch_y, (((0,), (0,)), ((), ())), precision=HIGHEST)
    inverse_y = inverse_factor(small_gram_y, rank_y)
    factor_y = jnp.dot(sketch_y, inverse_y, precision=HIGHEST)

    share_k = ranks_y // n_gy
    weights = by_step(factor_y.reshape(n_gy, rows_y, ranks_y), gy, n_gy)
    weights = weights.reshape(n_gy, rows_y, n_gy, share_k)
    weights = jnp.moveaxis(by_step(jnp.moveaxis(weights, 2, 0), gy, n_gy), 0, 2)
    mixed = jnp.einsum("gvyzr,gyhk->hvkzr", spread, weights, precision=HIGH)
    pieces = [None] * n_gy
    for s in steps(n_gy):
        pieces[s] = swap(mixed[s], "gy", s)
    pieces[0] = mixed[0]
    core = by_step(jnp.stack(pieces), gy, n_gy)
    core = jnp.moveaxis(core, 0, 2).reshape(planes, share_k, rows_z, ranks_x)
    return (core, factor_x, factor_y)


def solution(mesh):
    in_specs = (P(("grp", "vert"), "gy", "gz", None), P(), P(), P("grp"), P("grp"))
    out_specs = (P(("grp", "vert"), "gy", "gz", None), P("grp", None), P("grp", None))
    return jax.shard_map(body, mesh=mesh, in_specs=in_specs, out_specs=out_specs, check_vma=False)
```

time: 298 us -> 102 us (0.34)
  waiting for transfers between devices: 161 us -> 26.8 us
  blocking collectives: 57.6 us -> 0 us
  starting transfers between devices: 3.84 us -> 23.6 us
  between operations: 15.5 us -> 2.38 us
  matrix products: 25.3 us -> 16.5 us
    psum x1 -> x0, waiting for transfers between devices: 95.4 us -> none  [body(): lax.psum(local_gram, ('gy', 'gz', 'vert'))]
    psum x1 -> x0, blocking collectives: 57.6 us -> none  [body(): gram_y = lax.psum(local_gram_y, ('gy', 'gz', 'vert')) / divisor_y]
    reduce_scatter x1 -> x0, waiting for transfers between devices: 41.3 us -> none  [body(): core = lax.psum_scatter(partial_core, 'gy', scatter_dimension=1, tiled=True)]
    ppermute x0 -> x20, waiting for transfers between devices: none -> 26.8 us  [swap(): return lax.ppermute(value, axes, [(i, i ^ step) for i in range(count)])]
    all_to_all x1 -> x0, waiting for transfers between devices: 24.4 us -> none  [body(): lax.all_to_all(core_x, 'gy', split_axis=2, concat_axis=1, tiled=True)]
    ppermute x0 -> x20, starting transfers between devices: none -> 23.6 us  [swap(): return lax.ppermute(value, axes, [(i, i ^ step) for i in range(count)])]
    dot_general x8 -> x11, matrix products: 24.7 us -> 16.2 us  [the longest x1 4.39 us: body(): projected = jnp.dot(flat, omega_x, precision=HIGH)]
    all_to_all x1 -> x0, starting transfers between devices: 3.8 us -> none  [body(): lax.all_to_all(core_x, 'gy', split_axis=2, concat_axis=1, tiled=True)]
  transfers between devices with their start and end apart: 3 -> 20, of which waited for: 3 -> 12; matrix products, arithmetic and copies ran while one was open for 0% -> 24% of each run, Pallas kernels for 0% -> 0%
where the time goes in v1:
time: 102 us
  other arithmetic  30 us (29%)
  waiting for transfers between devices  26.8 us (26%)
  starting transfers between devices  23.6 us (23%)
  matrix products  16.5 us (16%)
  local copies, waits for them, and re-layouts  2.99 us (3%)
  between operations  2.38 us (2%)
    ppermute x20, waiting for transfers between devices, swap(): return lax.ppermute(value, axes, [(i, i ^ step) for i in range(count)])  26.8 us
    ppermute x20, starting transfers between devices, swap(): return lax.ppermute(value, axes, [(i, i ^ step) for i in range(count)])  23.6 us
    another operation x6, other arithmetic, inverse_factor(): lower = jnp.linalg.cholesky(small_gram)  16 us
    another operation x4, other arithmetic, inverse_factor(): lax.linalg.triangular_solve(lower, eye, left_side=False, lower=True, tran...  13.7 us
    dot_general x1, matrix products, body(): projected = jnp.dot(flat, omega_x, precision=HIGH)  4.39 us
    dot_general x1, matrix products, body(): lax.dot_general(flat, sketch_t, (((1,), (1,)), ((), ())), precision=HIGH)  4.38 us
    dot_general x1, matrix products, body(): jnp.einsum('gvazr,hvbzr->gahb', spread, spread, precision=HIGH)  2.49 us
  transfers between devices with their start and end apart: 20, of which 12 were waited for; matrix products, arithmetic and copies ran while one was open for 24% of the time, Pallas kernels for 0%

profile of v1, /device:TPU:0, one launch (start us, length us, event | category | flops | bytes accessed | tf_op | source)
XLA Modules:
  0.0 102.3 jit_solution(12786505969372234134)
XLA Ops:
  0.7 0.9 copy-done
  1.6 4.4 %fusion.33 = f32[2048,128]{1,0:T(8,128)S(1)} fusion(f32[2048,512]{1,0:T(8,128)} %bitcast.99, f32[512,128]{1,0:T(8,128)S(1)} %copy-done), kind=kOutput, calls=%fused_computation.82 | convolution fusion | flops 805306368 | bytes 5505024 | tf_op jit(solution)/shard_map/dot_general | solution.py:75
  6.0 1.5 %fusion.34 = f32[128,512]{1,0:T(8,128)S(1)} fusion(f32[2048,128]{1,0:T(8,128)S(1)} %fusion.33, f32[2048,512]{1,0:T(8,128)S(1)} %bitcast.101), kind=kOutput, calls=%fused_computation.83 | convolution fusion | flops 805306368 | bytes 5505024 | tf_op jit(solution)/shard_map/dot_general | solution.py:76
  7.6 0.5 collective-permute-start.2
  8.1 2.6 %collective-permute-start.1 = (f32[32,512]{1,0:T(8,128)S(1)}, f32[32,512]{1,0:T(8,128)S(1)}, u32[]{:S(2)}, u32[]{:S(2)}) collective-permute-start(f32[32,512]{1,0:T(8,128)S(1)} %get-tuple-element.15), channel_id=1, source_target_pairs={{0,2},{1,3},{2,0},{3,1},{4,6},{5,7},{6,4},{7,5},{8,10},{9,11},{10,... | collective-permute-start | bytes 196616 | tf_op jit(solution)/shard_map/ppermute | solution.py:13
  10.7 0.1 collective-permute-start
  10.8 0.1 copy.28
  10.9 2.5 %collective-permute-done.1 = f32[32,512]{1,0:T(8,128)S(1)} collective-permute-done((f32[32,512]{1,0:T(8,128)S(1)}, f32[32,512]{1,0:T(8,128)S(1)}, u32[]{:S(2)}, u32[]{:S(2)}) %collective-permute-start.1) | collective-permute-done | bytes 65568 | tf_op jit(solution)/shard_map/ppermute | solution.py:13
  13.4 1.4 %collective-permute-done = f32[32,512]{1,0:T(8,128)S(1)} collective-permute-done((f32[32,512]{1,0:T(8,128)S(1)}, f32[32,512]{1,0:T(8,128)S(1)}, u32[]{:S(2)}, u32[]{:S(2)}) %collective-permute-start) | collective-permute-done | bytes 65568 | tf_op jit(solution)/shard_map/ppermute | solution.py:13
  14.7 1.6 %collective-permute-start.5 = (f32[32,512]{1,0:T(8,128)S(1)}, f32[32,512]{1,0:T(8,128)S(1)}, u32[]{:S(2)}, u32[]{:S(2)}) collective-permute-start(f32[32,512]{1,0:T(8,128)S(1)} %add_add_fusion.1), channel_id=1, source_target_pairs={{0,4},{4,0},{8,12},{12,8},{1,5},{5,1},{9,13},{13,9},{2,6},{6,2},{1... | collective-permute-start | bytes 196616 | tf_op jit(solution)/shard_map/ppermute | solution.py:13
  16.4 2.6 %collective-permute-start.4 = (f32[32,512]{1,0:T(8,128)S(1)}, f32[32,512]{1,0:T(8,128)S(1)}, u32[]{:S(2)}, u32[]{:S(2)}) collective-permute-start(f32[32,512]{1,0:T(8,128)S(1)} %add_add_fusion.1), channel_id=1, source_target_pairs={{0,8},{4,12},{8,0},{12,4},{1,9},{5,13},{9,1},{13,5},{2,10},{6,14},... | collective-permute-start | bytes 196616 | tf_op jit(solution)/shard_map/ppermute | solution.py:13
  19.0 0.2 collective-permute-start.3
  19.9 4.1 %collective-permute-done.4 = f32[32,512]{1,0:T(8,128)S(1)} collective-permute-done((f32[32,512]{1,0:T(8,128)S(1)}, f32[32,512]{1,0:T(8,128)S(1)}, u32[]{:S(2)}, u32[]{:S(2)}) %collective-permute-start.4) | collective-permute-done | bytes 65568 | tf_op jit(solution)/shard_map/ppermute | solution.py:13
  23.9 1.2 %collective-permute-done.3 = f32[32,512]{1,0:T(8,128)S(1)} collective-permute-done((f32[32,512]{1,0:T(8,128)S(1)}, f32[32,512]{1,0:T(8,128)S(1)}, u32[]{:S(2)}, u32[]{:S(2)}) %collective-permute-start.3) | collective-permute-done | bytes 65568 | tf_op jit(solution)/shard_map/ppermute | solution.py:13
  25.2 0.1 collective-permute-start.6
  25.3 1.4 %collective-permute-start.7 = (f32[32,512]{1,0:T(8,128)S(1)}, f32[32,512]{1,0:T(8,128)S(1)}, u32[]{:S(2)}, u32[]{:S(2)}) collective-permute-start(f32[32,512]{1,0:T(8,128)S(1)} %get-tuple-element.4), channel_id=1, source_target_pairs={{0,2},{1,3},{2,0},{3,1},{4,6},{5,7},{6,4},{7,5},{8,10},{9,11},{10,... | collective-permute-start | bytes 196616 | tf_op jit(solution)/shard_map/ppermute | solution.py:13
  26.7 0.4 collective-permute-start.8
  27.1 2.5 %collective-permute-done.6 = f32[32,512]{1,0:T(8,128)S(1)} collective-permute-done((f32[32,512]{1,0:T(8,128)S(1)}, f32[32,512]{1,0:T(8,128)S(1)}, u32[]{:S(2)}, u32[]{:S(2)}) %collective-permute-start.6) | collective-permute-done | bytes 65568 | tf_op jit(solution)/shard_map/ppermute | solution.py:13
  29.7 1.2 %collective-permute-done.7 = f32[32,512]{1,0:T(8,128)S(1)} collective-permute-done((f32[32,512]{1,0:T(8,128)S(1)}, f32[32,512]{1,0:T(8,128)S(1)}, u32[]{:S(2)}, u32[]{:S(2)}) %collective-permute-start.7) | collective-permute-done | bytes 65568 | tf_op jit(solution)/shard_map/ppermute | solution.py:13
  30.9 4.4 %convolution_bitcast_fusion = f32[2048,128]{0,1:T(8,128)S(1)} fusion(f32[2048,512]{1,0:T(8,128)} %bitcast.100, f32[128,512]{1,0:T(8,128)S(1)} %constant_dynamic-update-slice_fusion), kind=kOutput, calls=%fused_computation | convolution fusion | flops 805371904 | bytes 5505024 | tf_op jit(solution)/shard_map/dot_general | solution.py:80
  35.3 0.4 fusion.15
  35.7 0.3 copy.23
  36.0 0.1 constant_dynamic-slice_fusion.3
  36.2 2.3 %collective-permute-start.11 = (f32[64,8,128]{2,1,0:T(8,128)S(1)}, f32[64,8,128]{2,1,0:T(8,128)S(1)}, u32[]{:S(2)}, u32[]{:S(2)}) collective-permute-start(f32[64,8,128]{2,1,0:T(8,128)S(1)} %get-tuple-element.6), channel_id=1, source_target_pairs={{0,12},{4,8},{8,4},{12,0},{1,13},{5,9},{9,5},{13,1},{2,14},{6,10},... | collective-permute-start | bytes 786440 | tf_op jit(solution)/shard_map/ppermute | solution.py:13
  38.5 0.3 collective-permute-start.10
  38.8 1.9 %collective-permute-start.9 = (f32[64,8,128]{2,1,0:T(8,128)S(1)}, f32[64,8,128]{2,1,0:T(8,128)S(1)}, u32[]{:S(2)}, u32[]{:S(2)}) collective-permute-start(f32[64,8,128]{2,1,0:T(8,128)S(1)} %get-tuple-element.8), channel_id=1, source_target_pairs={{0,4},{4,0},{8,12},{12,8},{1,5},{5,1},{9,13},{13,9},{2,6},{6,2},{1... | collective-permute-start | bytes 786440 | tf_op jit(solution)/shard_map/ppermute | solution.py:13
  40.6 0.1 copy.24
  40.7 11.7 %cholesky.26 = f32[128,128]{1,0:T(8,128)S(1)} custom-call(f32[128,128]{1,0:T(8,128)S(1)} %fusion.24), custom_call_target="Cholesky" | custom-call | tf_op jit(solution)/shard_map/jit(cholesky)/cholesky | solution.py:57
  52.5 0.6 compare_reduce_fusion.1
  53.1 0.7 fusion.21
  53.8 10.0 %custom-call.12 = f32[1,128,128]{1,2,0:T(8,128)S(1)} custom-call(f32[1,128,128]{2,1,0:T(8,128)S(1)} %fusion.21), custom_call_target="InvertDiagBlocksLowerTriangular" | custom-call | tf_op jit(solution)/shard_map/triangular_solve | solution.py:59
  63.8 0.2 convolution_multiply_fusion
  64.0 0.6 fusion
  64.6 2.5 %convolution_bitcast_fusion.2 = f32[4,16,4,16]{3,1,2,0:T(8,128)S(1)} fusion(f32[4,4,16,8,128,1]{4,3,2,1,0,5:T(8,128)S(1)} %bitcast.102, f32[4,4,16,8,128]{4,3,2,1,0:T(8,128)S(1)} %fusion), kind=kOutput, calls=%fused_computation.2 | convolution fusion | flops 100663296 | bytes 2113536 | tf_op jit(solution)/shard_map/gvazr,hvbzr->gahb/dot_general | solution.py:95
  67.1 0.1 copy.27
  67.1 0.1 dot_general.44
  67.2 0.2 fusion.35
  67.4 0.1 collective-permute-start.12
  67.5 1.2 %collective-permute-done.12 = f32[64,32]{1,0:T(8,128)S(1)} collective-permute-done((f32[64,32]{1,0:T(8,128)S(1)}, f32[64,32]{1,0:T(8,128)S(1)}, u32[]{:S(2)}, u32[]{:S(2)}) %collective-permute-start.12) | collective-permute-done | bytes 8224 | tf_op jit(solution)/shard_map/ppermute | solution.py:13
  68.7 0.8 collective-permute-start.13
  70.1 2.5 %collective-permute-done.13 = f32[64,32]{1,0:T(8,128)S(1)} collective-permute-done((f32[64,32]{1,0:T(8,128)S(1)}, f32[64,32]{1,0:T(8,128)S(1)}, u32[]{:S(2)}, u32[]{:S(2)}) %collective-permute-start.13) | collective-permute-done | bytes 8224 | tf_op jit(solution)/shard_map/ppermute | solution.py:13
  72.6 0.2 collective-permute-start.16
  72.8 2.6 %collective-permute-start.15 = (f32[64,32]{1,0:T(8,128)S(1)}, f32[64,32]{1,0:T(8,128)S(1)}, u32[]{:S(2)}, u32[]{:S(2)}) collective-permute-start(f32[64,32]{1,0:T(8,128)S(1)} %add.103), channel_id=1, source_target_pairs={{0,8},{4,12},{8,0},{12,4},{1,9},{5,13},{9,1},{13,5},{2,10},{6,14},... | collective-permute-start | bytes 24584 | tf_op jit(solution)/shard_map/ppermute | solution.py:13
  75.4 1.6 %collective-permute-start.14 = (f32[64,32]{1,0:T(8,128)S(1)}, f32[64,32]{1,0:T(8,128)S(1)}, u32[]{:S(2)}, u32[]{:S(2)}) collective-permute-start(f32[64,32]{1,0:T(8,128)S(1)} %add.103), channel_id=1, source_target_pairs={{0,12},{4,8},{8,4},{12,0},{1,13},{5,9},{9,5},{13,1},{2,14},{6,10},... | collective-permute-start | bytes 24584 | tf_op jit(solution)/shard_map/ppermute | solution.py:13
  77.0 0.6 collective-permute-done.15
  77.6 3.5 %collective-permute-done.14 = f32[64,32]{1,0:T(8,128)S(1)} collective-permute-done((f32[64,32]{1,0:T(8,128)S(1)}, f32[64,32]{1,0:T(8,128)S(1)}, u32[]{:S(2)}, u32[]{:S(2)}) %collective-permute-start.14) | collective-permute-done | bytes 8224 | tf_op jit(solution)/shard_map/ppermute | solution.py:13
  81.1 0.2 fusion.36
  81.4 0.1 copy.30
  81.5 2.9 %cholesky.55 = f32[32,32]{1,0:T(8,128)S(1)} custom-call(f32[32,32]{1,0:T(8,128)S(1)} %fusion.27), custom_call_target="Cholesky" | custom-call | tf_op jit(solution)/shard_map/jit(cholesky)/cholesky | solution.py:57
  84.4 0.6 compare_reduce_fusion
  85.1 0.7 fusion.25
  85.7 2.4 %custom-call.13 = f32[1,32,32]{1,2,0:T(8,128)S(1)} custom-call(f32[1,32,32]{2,1,0:T(8,128)S(1)} %fusion.25), custom_call_target="InvertDiagBlocksLowerTriangular" | custom-call | tf_op jit(solution)/shard_map/triangular_solve | solution.py:59
  88.2 0.1 convolution_multiply_fusion.1
  88.3 0.2 fusion.37
  88.5 0.0 copy-start.2
  88.6 0.1 copy.31
  88.7 0.1 copy.32
  88.8 0.8 convolution_bitcast_fusion.1
  89.6 1.7 %collective-permute-start.19 = (f32[4,8,8,128]{3,1,2,0:T(8,128)S(1)}, f32[4,8,8,128]{3,1,2,0:T(8,128)S(1)}, u32[]{:S(2)}, u32[]{:S(2)}) collective-permute-start(f32[4,8,8,128]{3,1,2,0:T(8,128)S(1)} %get-tuple-element.10), channel_id=1, source_target_pairs={{0,12},{4,8},{8,4},{12,0},{1,13},{5,9},{9,5},{13,1},{2,14},{6,10},... | collective-permute-start | bytes 393224 | tf_op jit(solution)/shard_map/ppermute | solution.py:13
  91.3 2.8 %collective-permute-start.17 = (f32[4,8,8,128]{3,1,2,0:T(8,128)S(1)}, f32[4,8,8,128]{3,1,2,0:T(8,128)S(1)}, u32[]{:S(2)}, u32[]{:S(2)}) collective-permute-start(f32[4,8,8,128]{3,1,2,0:T(8,128)S(1)} %get-tuple-element.12), channel_id=1, source_target_pairs={{0,4},{4,0},{8,12},{12,8},{1,5},{5,1},{9,13},{13,9},{2,6},{6,2},{1... | collective-permute-start | bytes 393224 | tf_op jit(solution)/shard_map/ppermute | solution.py:13
  94.0 1.1 %fusion.13 = f32[512,128]{1,0:T(8,128)} fusion(f32[128,128]{1,0:T(8,128)S(1)} %convolution_multiply_fusion, f32[128,512]{1,0:T(8,128)S(1)} %constant_dynamic-update-slice_fusion), kind=kOutput, calls=%fused_computation.22 | convolution fusion | flops 50397184 | bytes 589824 | tf_op jit(solution)/shard_map/dot_general | solution.py:90
  95.1 2.1 %collective-permute-done.19 = f32[4,8,8,128]{3,1,2,0:T(8,128)S(1)} collective-permute-done((f32[4,8,8,128]{3,1,2,0:T(8,128)S(1)}, f32[4,8,8,128]{3,1,2,0:T(8,128)S(1)}, u32[]{:S(2)}, u32[]{:S(2)}) %collective-permute-start.19) | collective-permute-done | bytes 131104 | tf_op jit(solution)/shard_map/ppermute | solution.py:13
  97.2 4.0 %collective-permute-done.18 = f32[4,8,8,128]{3,1,2,0:T(8,128)S(1)} collective-permute-done((f32[4,8,8,128]{3,1,2,0:T(8,128)S(1)}, f32[4,8,8,128]{3,1,2,0:T(8,128)S(1)}, u32[]{:S(2)}, u32[]{:S(2)}) %collective-permute-start.18) | collective-permute-done | bytes 131104 | tf_op jit(solution)/shard_map/ppermute | solution.py:13
  101.4 0.9 copy.56
  (44 shorter events, 0.5 us)
Async XLA Ops:
  0.6 1.0 copy-start
  0.7 5.3 %copy-start.1 = (f32[4,16,32,512]{3,2,1,0:T(8,128)S(1)}, f32[4,16,32,512]{3,2,1,0:T(8,128)}, u32[]{:S(2)}) copy-start(f32[4,16,32,512]{3,2,1,0:T(8,128)} %param.5) | copy-start | bytes 12582916
  6.0 4.8 %copy-start.3 = (f32[64,32]{0,1:T(8,128)S(1)}, f32[64,32]{0,1:T(8,128)}, u32[]{:S(2)}) copy-start(f32[64,32]{0,1:T(8,128)} %param.7) | copy-start | bytes 24580
  7.6 3.3 %collective-permute-start.2 = (f32[32,512]{1,0:T(8,128)S(1)}, f32[32,512]{1,0:T(8,128)S(1)}, u32[]{:S(2)}, u32[]{:S(2)}) collective-permute-start(f32[32,512]{1,0:T(8,128)S(1)} %get-tuple-element.14), channel_id=1, source_target_pairs={{0,1},{1,0},{2,3},{3,2},{4,5},{5,4},{6,7},{7,6},{8,9},{9,8},{10,11... | collective-permute-start | bytes 196616 | tf_op jit(solution)/shard_map/ppermute | solution.py:13
  8.1 5.3 %collective-permute-start.1 = (f32[32,512]{1,0:T(8,128)S(1)}, f32[32,512]{1,0:T(8,128)S(1)}, u32[]{:S(2)}, u32[]{:S(2)}) collective-permute-start(f32[32,512]{1,0:T(8,128)S(1)} %get-tuple-element.15), channel_id=1, source_target_pairs={{0,2},{1,3},{2,0},{3,1},{4,6},{5,7},{6,4},{7,5},{8,10},{9,11},{10,... | collective-permute-start | bytes 196616 | tf_op jit(solution)/shard_map/ppermute | solution.py:13
  10.7 4.0 %collective-permute-start = (f32[32,512]{1,0:T(8,128)S(1)}, f32[32,512]{1,0:T(8,128)S(1)}, u32[]{:S(2)}, u32[]{:S(2)}) collective-permute-start(f32[32,512]{1,0:T(8,128)S(1)} %get-tuple-element.13), channel_id=1, source_target_pairs={{0,3},{1,2},{2,1},{3,0},{4,7},{5,6},{6,5},{7,4},{8,11},{9,10},{10,... | collective-permute-start | bytes 196616 | tf_op jit(solution)/shard_map/ppermute | solution.py:13
  14.7 5.1 %collective-permute-start.5 = (f32[32,512]{1,0:T(8,128)S(1)}, f32[32,512]{1,0:T(8,128)S(1)}, u32[]{:S(2)}, u32[]{:S(2)}) collective-permute-start(f32[32,512]{1,0:T(8,128)S(1)} %add_add_fusion.1), channel_id=1, source_target_pairs={{0,4},{4,0},{8,12},{12,8},{1,5},{5,1},{9,13},{13,9},{2,6},{6,2},{1... | collective-permute-start | bytes 196616 | tf_op jit(solution)/shard_map/ppermute | solution.py:13
  16.4 7.6 %collective-permute-start.4 = (f32[32,512]{1,0:T(8,128)S(1)}, f32[32,512]{1,0:T(8,128)S(1)}, u32[]{:S(2)}, u32[]{:S(2)}) collective-permute-start(f32[32,512]{1,0:T(8,128)S(1)} %add_add_fusion.1), channel_id=1, source_target_pairs={{0,8},{4,12},{8,0},{12,4},{1,9},{5,13},{9,1},{13,5},{2,10},{6,14},... | collective-permute-start | bytes 196616 | tf_op jit(solution)/shard_map/ppermute | solution.py:13
  19.0 6.2 %collective-permute-start.3 = (f32[32,512]{1,0:T(8,128)S(1)}, f32[32,512]{1,0:T(8,128)S(1)}, u32[]{:S(2)}, u32[]{:S(2)}) collective-permute-start(f32[32,512]{1,0:T(8,128)S(1)} %add_add_fusion.1), channel_id=1, source_target_pairs={{0,12},{4,8},{8,4},{12,0},{1,13},{5,9},{9,5},{13,1},{2,14},{6,10},... | collective-permute-start | bytes 196616 | tf_op jit(solution)/shard_map/ppermute | solution.py:13
  25.2 4.5 %collective-permute-start.6 = (f32[32,512]{1,0:T(8,128)S(1)}, f32[32,512]{1,0:T(8,128)S(1)}, u32[]{:S(2)}, u32[]{:S(2)}) collective-permute-start(f32[32,512]{1,0:T(8,128)S(1)} %get-tuple-element.4), channel_id=1, source_target_pairs={{0,3},{1,2},{2,1},{3,0},{4,7},{5,6},{6,5},{7,4},{8,11},{9,10},{10,... | collective-permute-start | bytes 196616 | tf_op jit(solution)/shard_map/ppermute | solution.py:13
  25.3 5.6 %collective-permute-start.7 = (f32[32,512]{1,0:T(8,128)S(1)}, f32[32,512]{1,0:T(8,128)S(1)}, u32[]{:S(2)}, u32[]{:S(2)}) collective-permute-start(f32[32,512]{1,0:T(8,128)S(1)} %get-tuple-element.4), channel_id=1, source_target_pairs={{0,2},{1,3},{2,0},{3,1},{4,6},{5,7},{6,4},{7,5},{8,10},{9,11},{10,... | collective-permute-start | bytes 196616 | tf_op jit(solution)/shard_map/ppermute | solution.py:13
  26.7 4.2 %collective-permute-start.8 = (f32[32,512]{1,0:T(8,128)S(1)}, f32[32,512]{1,0:T(8,128)S(1)}, u32[]{:S(2)}, u32[]{:S(2)}) collective-permute-start(f32[32,512]{1,0:T(8,128)S(1)} %get-tuple-element.4), channel_id=1, source_target_pairs={{0,1},{1,0},{2,3},{3,2},{4,5},{5,4},{6,7},{7,6},{8,9},{9,8},{10,11... | collective-permute-start | bytes 196616 | tf_op jit(solution)/shard_map/ppermute | solution.py:13
  36.2 27.8 %collective-permute-start.11 = (f32[64,8,128]{2,1,0:T(8,128)S(1)}, f32[64,8,128]{2,1,0:T(8,128)S(1)}, u32[]{:S(2)}, u32[]{:S(2)}) collective-permute-start(f32[64,8,128]{2,1,0:T(8,128)S(1)} %get-tuple-element.6), channel_id=1, source_target_pairs={{0,12},{4,8},{8,4},{12,0},{1,13},{5,9},{9,5},{13,1},{2,14},{6,10},... | collective-permute-start | bytes 786440 | tf_op jit(solution)/shard_map/ppermute | solution.py:13
  38.5 25.5 %collective-permute-start.10 = (f32[64,8,128]{2,1,0:T(8,128)S(1)}, f32[64,8,128]{2,1,0:T(8,128)S(1)}, u32[]{:S(2)}, u32[]{:S(2)}) collective-permute-start(f32[64,8,128]{2,1,0:T(8,128)S(1)} %get-tuple-element.7), channel_id=1, source_target_pairs={{0,8},{4,12},{8,0},{12,4},{1,9},{5,13},{9,1},{13,5},{2,10},{6,14},... | collective-permute-start | bytes 786440 | tf_op jit(solution)/shard_map/ppermute | solution.py:13
  38.8 25.2 %collective-permute-start.9 = (f32[64,8,128]{2,1,0:T(8,128)S(1)}, f32[64,8,128]{2,1,0:T(8,128)S(1)}, u32[]{:S(2)}, u32[]{:S(2)}) collective-permute-start(f32[64,8,128]{2,1,0:T(8,128)S(1)} %get-tuple-element.8), channel_id=1, source_target_pairs={{0,4},{4,0},{8,12},{12,8},{1,5},{5,1},{9,13},{13,9},{2,6},{6,2},{1... | collective-permute-start | bytes 786440 | tf_op jit(solution)/shard_map/ppermute | solution.py:13
  67.4 1.3 %collective-permute-start.12 = (f32[64,32]{1,0:T(8,128)S(1)}, f32[64,32]{1,0:T(8,128)S(1)}, u32[]{:S(2)}, u32[]{:S(2)}) collective-permute-start(f32[64,32]{1,0:T(8,128)S(1)} %bitcast.114), channel_id=1, source_target_pairs={{0,1},{1,0},{2,3},{3,2},{4,5},{5,4},{6,7},{7,6},{8,9},{9,8},{10,11... | collective-permute-start | bytes 24584 | tf_op jit(solution)/shard_map/ppermute | solution.py:13
  68.7 3.9 %collective-permute-start.13 = (f32[64,32]{1,0:T(8,128)S(1)}, f32[64,32]{1,0:T(8,128)S(1)}, u32[]{:S(2)}, u32[]{:S(2)}) collective-permute-start(f32[64,32]{1,0:T(8,128)S(1)} %bitcast_add_fusion.2), channel_id=1, source_target_pairs={{0,2},{2,0},{1,3},{3,1},{4,6},{6,4},{5,7},{7,5},{8,10},{10,8},{9,1... | collective-permute-start | bytes 24584 | tf_op jit(solution)/shard_map/ppermute | solution.py:13
  72.6 4.4 %collective-permute-start.16 = (f32[64,32]{1,0:T(8,128)S(1)}, f32[64,32]{1,0:T(8,128)S(1)}, u32[]{:S(2)}, u32[]{:S(2)}) collective-permute-start(f32[64,32]{1,0:T(8,128)S(1)} %add.103), channel_id=1, source_target_pairs={{0,4},{4,0},{8,12},{12,8},{1,5},{5,1},{9,13},{13,9},{2,6},{6,2},{1... | collective-permute-start | bytes 24584 | tf_op jit(solution)/shard_map/ppermute | solution.py:13
  72.8 4.8 %collective-permute-start.15 = (f32[64,32]{1,0:T(8,128)S(1)}, f32[64,32]{1,0:T(8,128)S(1)}, u32[]{:S(2)}, u32[]{:S(2)}) collective-permute-start(f32[64,32]{1,0:T(8,128)S(1)} %add.103), channel_id=1, source_target_pairs={{0,8},{4,12},{8,0},{12,4},{1,9},{5,13},{9,1},{13,5},{2,10},{6,14},... | collective-permute-start | bytes 24584 | tf_op jit(solution)/shard_map/ppermute | solution.py:13
  75.4 5.7 %collective-permute-start.14 = (f32[64,32]{1,0:T(8,128)S(1)}, f32[64,32]{1,0:T(8,128)S(1)}, u32[]{:S(2)}, u32[]{:S(2)}) collective-permute-start(f32[64,32]{1,0:T(8,128)S(1)} %add.103), channel_id=1, source_target_pairs={{0,12},{4,8},{8,4},{12,0},{1,13},{5,9},{9,5},{13,1},{2,14},{6,10},... | collective-permute-start | bytes 24584 | tf_op jit(solution)/shard_map/ppermute | solution.py:13
  88.5 13.8 %copy-start.2 = (f32[64,32]{0,1:T(8,128)}, f32[64,32]{0,1:T(8,128)S(1)}, u32[]{:S(2)}) copy-start(f32[64,32]{0,1:T(8,128)S(1)} %fusion.37) | copy-start | bytes 24580
  89.6 7.6 %collective-permute-start.19 = (f32[4,8,8,128]{3,1,2,0:T(8,128)S(1)}, f32[4,8,8,128]{3,1,2,0:T(8,128)S(1)}, u32[]{:S(2)}, u32[]{:S(2)}) collective-permute-start(f32[4,8,8,128]{3,1,2,0:T(8,128)S(1)} %get-tuple-element.10), channel_id=1, source_target_pairs={{0,12},{4,8},{8,4},{12,0},{1,13},{5,9},{9,5},{13,1},{2,14},{6,10},... | collective-permute-start | bytes 393224 | tf_op jit(solution)/shard_map/ppermute | solution.py:13
  91.3 10.0 %collective-permute-start.18 = (f32[4,8,8,128]{3,1,2,0:T(8,128)S(1)}, f32[4,8,8,128]{3,1,2,0:T(8,128)S(1)}, u32[]{:S(2)}, u32[]{:S(2)}) collective-permute-start(f32[4,8,8,128]{3,1,2,0:T(8,128)S(1)} %get-tuple-element.11), channel_id=1, source_target_pairs={{0,8},{4,12},{8,0},{12,4},{1,9},{5,13},{9,1},{13,5},{2,10},{6,14},... | collective-permute-start | bytes 393224 | tf_op jit(solution)/shard_map/ppermute | solution.py:13
  91.3 10.0 %collective-permute-start.17 = (f32[4,8,8,128]{3,1,2,0:T(8,128)S(1)}, f32[4,8,8,128]{3,1,2,0:T(8,128)S(1)}, u32[]{:S(2)}, u32[]{:S(2)}) collective-permute-start(f32[4,8,8,128]{3,1,2,0:T(8,128)S(1)} %get-tuple-element.12), channel_id=1, source_target_pairs={{0,4},{4,0},{8,12},{12,8},{1,5},{5,1},{9,13},{13,9},{2,6},{6,2},{1... | collective-permute-start | bytes 393224 | tf_op jit(solution)/shard_map/ppermute | solution.py:13

commit v2 on v1

--- a/solution.py
+++ b/solution.py
@@ -1,6 +1,10 @@
+import functools
+
 import jax
 import jax.numpy as jnp
 from jax import lax
+from jax.experimental import pallas as pl
+from jax.experimental.pallas import tpu as pltpu
 from jax.sharding import PartitionSpec as P
 
 HIGH = lax.Precision.HIGH
@@ -53,12 +57,171 @@
     return whole
 
 
-def inverse_factor(small_gram, rank):
-    lower = jnp.linalg.cholesky(small_gram)
-    eye = jnp.eye(lower.shape[0], dtype=jnp.float32)
-    inverse = lax.linalg.triangular_solve(lower, eye, left_side=False, lower=True, transpose_a=True)
-    kept = (jnp.arange(lower.shape[0], dtype=jnp.int32) < rank[0]).astype(jnp.float32)
-    return inverse * kept[None, :]
+def dims(left, right):
+    return (((left,), (right,)), ((), ()))
+
+
+def mxu(a, b, numbers):
+    return lax.dot_general(a, b, numbers, preferred_element_type=jnp.float32)
+
+
+def exact(a, b, numbers):
+    return lax.dot_general(a, b, numbers, precision=HIGHEST, preferred_element_type=jnp.float32)
+
+
+def halves(value):
+    high = value.astype(jnp.bfloat16)
+    return high, (value - high.astype(jnp.float32)).astype(jnp.bfloat16)
+
+
+def vmem(count):
+    return [pl.BlockSpec(memory_space=pltpu.VMEM)] * count
+
+
+def sketch_kernel(field_ref, omega_ref, out_ref, wide, narrow):
+    width = omega_ref.shape[1]
+    high, low = halves(field_ref[...])
+    omega_high, omega_low = halves(omega_ref[...])
+    both = mxu(high, jnp.concatenate([omega_high, omega_low], axis=1), dims(1, 0))
+    projected = both[:, :width] + (both[:, width:] + mxu(low, omega_high, dims(1, 0)))
+    proj_high, proj_low = halves(projected)
+    first = mxu(jnp.concatenate([proj_high, proj_low], axis=1), high, dims(0, 0))
+    second = mxu(proj_high, low, dims(0, 0))
+
+    @pl.when(pl.program_id(0) == 0)
+    def _():
+        wide[...] = first
+        narrow[...] = second
+
+    @pl.when(pl.program_id(0) > 0)
+    def _():
+        wide[...] += first
+        narrow[...] += second
+
+    @pl.when(pl.program_id(0) == pl.num_programs(0) - 1)
+    def _():
+        out_ref[...] = wide[:width, :] + (wide[width:, :] + narrow[...])
+
+
+def sketch_part(flat, omega):
+    rows, cells = flat.shape
+    width = omega.shape[1]
+    block = 512
+    return pl.pallas_call(
+        sketch_kernel,
+        grid=(rows // block,),
+        in_specs=[
+            pl.BlockSpec((block, cells), lambda i: (i, 0)),
+            pl.BlockSpec((cells, width), lambda i: (0, 0)),
+        ],
+        out_specs=pl.BlockSpec((width, cells), lambda i: (0, 0)),
+        out_shape=jax.ShapeDtypeStruct((width, cells), jnp.float32),
+        scratch_shapes=[pltpu.VMEM((2 * width, cells), jnp.float32), pltpu.VMEM((width, cells), jnp.float32)],
+        name="sketch",
+    )(flat, omega)
+
+
+def chunk_kernel(where_ref, field_ref, sketch_ref, out_ref):
+    width = sketch_ref.shape[0]
+    rows, share, cells = field_ref.shape
+    high, low = halves(field_ref[...].reshape(rows * share, cells))
+    sketch_high, sketch_low = halves(sketch_ref[...])
+    both = mxu(high, jnp.concatenate([sketch_high, sketch_low], axis=0), dims(1, 1))
+    raw = both[:, :width] + (both[:, width:] + mxu(low, sketch_high, dims(1, 1)))
+    out_ref[...] = raw.reshape(rows, share, width)
+
+
+def field_chunk(where, field, sketch_t, share):
+    rows, _, cells = field.shape
+    width = sketch_t.shape[0]
+    block = rows // 2
+    return pl.pallas_call(
+        chunk_kernel,
+        grid_spec=pltpu.PrefetchScalarGridSpec(
+            num_scalar_prefetch=1,
+            grid=(rows // block,),
+            in_specs=[
+                pl.BlockSpec((block, share, cells), lambda i, w: (i, w[0], 0)),
+                pl.BlockSpec((width, cells), lambda i, w: (0, 0)),
+            ],
+            out_specs=pl.BlockSpec((block, share, width), lambda i, w: (i, 0, 0)),
+        ),
+        out_shape=jax.ShapeDtypeStruct((rows, share, width), jnp.float32),
+        name="chunk",
+    )(where, field, sketch_t)
+
+
+def eliminate(gram, count, rank, out_ref):
+    lanes = lax.broadcasted_iota(jnp.int32, (8, count), 1)
+    subs = lax.broadcasted_iota(jnp.int32, (8, count), 0)
+    blocks = count // 8
+    full = lambda x: jnp.broadcast_to(x, (8, count))
+    left = [gram[8 * b:8 * b + 8, :] for b in range(blocks)]
+    right = [(lanes == subs + 8 * b).astype(jnp.float32) for b in range(blocks)]
+    for j in range(0, count, 2):
+        b, s = divmod(j, 8)
+        l0, l1 = full(left[b][s:s + 1, :]), full(left[b][s + 1:s + 2, :])
+        r0, r1 = full(right[b][s:s + 1, :]), full(right[b][s + 1:s + 2, :])
+        p, q, t = full(l0[:, j:j + 1]), full(l0[:, j + 1:j + 2]), full(l1[:, j + 1:j + 2])
+        inv = 1.0 / (p * t - q * q)
+        ratio = q / p
+        first = r0 * lax.rsqrt(p)
+        second = (r1 - ratio * r0) * lax.rsqrt(t - q * ratio)
+        out_ref[j:j + 1, :] = jnp.where(j < rank, first[0:1], 0.0)
+        out_ref[j + 1:j + 2, :] = jnp.where(j + 1 < rank, second[0:1], 0.0)
+        if j + 2 >= count:
+            break
+        u0 = (l0 * t - l1 * q) * inv
+        u1 = (l1 * p - l0 * q) * inv
+        v0 = (r0 * t - r1 * q) * inv
+        v1 = (r1 * p - r0 * q) * inv
+        for i in range(b, blocks):
+            if i == b and s == 6:
+                continue
+            c0, c1 = full(left[i][:, j:j + 1]), full(left[i][:, j + 1:j + 2])
+            if i == b:
+                c0 = jnp.where(subs > s + 1, c0, 0.0)
+                c1 = jnp.where(subs > s + 1, c1, 0.0)
+            left[i] = left[i] - c0 * u0 - c1 * u1
+            right[i] = right[i] - c0 * v0 - c1 * v1
+
+
+def factor_x_kernel(rank_ref, sketch_ref, out_ref):
+    sketch_t = sketch_ref[...]
+    eliminate(exact(sketch_t, sketch_t, dims(1, 1)), sketch_t.shape[0], rank_ref[0], out_ref)
+
+
+def inverse_factor_x(rank, sketch_t):
+    width = sketch_t.shape[0]
+    return pl.pallas_call(
+        factor_x_kernel,
+        in_specs=[pl.BlockSpec(memory_space=pltpu.SMEM)] + vmem(1),
+        out_specs=pl.BlockSpec(memory_space=pltpu.VMEM),
+        out_shape=jax.ShapeDtypeStruct((width, width), jnp.float32),
+        name="factor_x",
+    )(rank, sketch_t)
+
+
+def factor_y_kernel(divisor, rank_ref, *refs):
+    *part_refs, out_ref, inverse = refs
+    sketch = part_refs[0][...]
+    for ref in part_refs[1:]:
+        sketch = sketch + ref[...]
+    sketch = sketch / divisor
+    eliminate(exact(sketch, sketch, dims(0, 0)), sketch.shape[1], rank_ref[0], inverse)
+    out_ref[...] = exact(sketch, inverse[...], dims(1, 1))
+
+
+def make_factor_y(rank, parts, divisor):
+    rows, width = parts[0].shape
+    return pl.pallas_call(
+        functools.partial(factor_y_kernel, divisor),
+        in_specs=[pl.BlockSpec(memory_space=pltpu.SMEM)] + vmem(len(parts)),
+        out_specs=pl.BlockSpec(memory_space=pltpu.VMEM),
+        out_shape=jax.ShapeDtypeStruct((rows, width), jnp.float32),
+        scratch_shapes=[pltpu.VMEM((width, width), jnp.float32)],
+        name="factor_y",
+    )(rank, *parts)
 
 
 def body(field, omega_x, omega_y, rank_x, rank_y):
@@ -72,25 +235,26 @@
     all_rows_z = rows_z * lax.axis_size("gz")
     flat = field.reshape(-1, cells_x)
 
-    projected = jnp.dot(flat, omega_x, precision=HIGH)
-    part = lax.dot_general(projected, flat, (((0,), (0,)), ((), ())), precision=HIGH)
-    sketch_t = sum_sketch(part) / float(all_planes * all_rows_y * all_rows_z)
+    sketch_t = sum_sketch(sketch_part(flat, omega_x)) / float(all_planes * all_rows_y * all_rows_z)
 
     share_z = rows_z // n_gy
-    raw = lax.dot_general(flat, sketch_t, (((1,), (1,)), ((), ())), precision=HIGH)
-    raw = raw.reshape(planes * rows_y, rows_z, ranks_x)
-    cut = lambda who: lax.dynamic_slice_in_dim(raw, who * share_z, share_z, 1)
+    field_z = field.reshape(planes * rows_y, rows_z, cells_x)
+    if share_z % 8 == 0:
+        cut = lambda who: field_chunk(who[None].astype(jnp.int32), field_z, sketch_t, share_z)
+    else:
+        raw = lax.dot_general(flat, sketch_t, dims(1, 1), precision=HIGH)
+        raw = raw.reshape(planes * rows_y, rows_z, ranks_x)
+        cut = lambda who: lax.dynamic_slice_in_dim(raw, who * share_z, share_z, 1)
     chunks = [None] * n_gy
     for s in steps(n_gy):
         chunks[s] = swap(cut(gy ^ s), "gy", s)
     chunks[0] = cut(gy)
 
-    small_gram = lax.dot_general(sketch_t, sketch_t, (((1,), (1,)), ((), ())), precision=HIGHEST)
-    inverse_x = inverse_factor(small_gram, rank_x)
-    factor_x = lax.dot_general(sketch_t, inverse_x, (((0,), (0,)), ((), ())), precision=HIGH)
+    inverse_x = inverse_factor_x(rank_x, sketch_t)
+    factor_x = lax.dot_general(sketch_t, inverse_x, dims(0, 1), precision=HIGH)
 
     spread = jnp.stack(chunks).reshape(-1, ranks_x)
-    spread = jnp.dot(spread, inverse_x, precision=HIGH)
+    spread = lax.dot_general(spread, inverse_x, dims(1, 1), precision=HIGH)
     spread = spread.reshape(n_gy, planes, rows_y, share_z, ranks_x)
     local_gram_y = jnp.einsum("gvazr,hvbzr->gahb", spread, spread, precision=HIGH)
     local_gram_y = local_gram_y.reshape(all_rows_y, all_rows_y)
@@ -102,11 +266,8 @@
         got = [swap(part_y, axis, s) for s in steps(count)]
         for other in got:
             part_y = part_y + other
-    sketch_y = sum_over_gy(part_y) / float(all_planes * all_rows_z * ranks_x)
-
-    small_gram_y = lax.dot_general(sketch_y, sketch_y, (((0,), (0,)), ((), ())), precision=HIGHEST)
-    inverse_y = inverse_factor(small_gram_y, rank_y)
-    factor_y = jnp.dot(sketch_y, inverse_y, precision=HIGHEST)
+    parts = [part_y] + [swap(part_y, "gy", s) for s in steps(n_gy)]
+    factor_y = make_factor_y(rank_y, parts, float(all_planes * all_rows_z * ranks_x))
 
     share_k = ranks_y // n_gy
     weights = by_step(factor_y.reshape(n_gy, rows_y, ranks_y), gy, n_gy)

time: 102 us -> 98.8 us (0.969)
  Pallas kernels: 0 us -> 30.2 us
  other arithmetic: 30 us -> 2.65 us
  matrix products: 16.5 us -> 6.08 us
  starting transfers between devices: 23.6 us -> 26.1 us
  local copies, waits for them, and re-layouts: 2.99 us -> 4.29 us
    pallas_call x0 -> x7, Pallas kernels: none -> 30.2 us  [the longest x1 10.7 us: inverse_factor_x(): pl.pallas_call(factor_x_kernel, in_specs=[pl.BlockSpec(memory_space=pltpu...]
    another operation x10 -> x0, other arithmetic: 29.7 us -> none  [the longest x6 16 us: inverse_factor(): lower = jnp.linalg.cholesky(small_gram)]
    dot_general x8 -> x2, matrix products: 12.8 us -> 2.66 us  [the longest x1 1.57 us: body(): spread = lax.dot_general(spread, inverse_x, dims(1, 1), precision=HIGH)]
    ppermute x20, starting transfers between devices: 23.6 us -> 26.1 us  [swap(): return lax.ppermute(value, axes, [(i, i ^ step) for i in range(count)])]
    unnamed x9 -> x14, local copies, waits for them, and re-layouts: 1.02 us -> 2.14 us
  transfers between devices with their start and end apart: 20 -> 20, of which waited for: 12 -> 13; matrix products, arithmetic and copies ran while one was open for 24% -> 3% of each run, Pallas kernels for 0% -> 18%
where the time goes in v2:
time: 98.8 us; the launch traced here: 98.1 us
  Pallas kernels  30.2 us (31%)
  waiting for transfers between devices  26.6 us (27%)
  starting transfers between devices  26.1 us (26%)
  matrix products  6.08 us (6%)
  local copies, waits for them, and re-layouts  4.29 us (4%)
  other arithmetic  2.65 us (3%)
  between operations  2.18 us (2%)
    ppermute x20, waiting for transfers between devices, swap(): return lax.ppermute(value, axes, [(i, i ^ step) for i in range(count)])  26.6 us
    ppermute x20, starting transfers between devices, swap(): return lax.ppermute(value, axes, [(i, i ^ step) for i in range(count)])  26.1 us
    pallas_call x1, Pallas kernels, inverse_factor_x(): pl.pallas_call(factor_x_kernel, in_specs=[pl.BlockSpec(memory_space=pltpu...  10.7 us
    pallas_call x4, Pallas kernels, field_chunk(): pl.pallas_call(chunk_kernel, grid_spec=pltpu.PrefetchScalarGridSpec(num_s...  9.89 us
    pallas_call x1, Pallas kernels, sketch_part(): pl.pallas_call(sketch_kernel, grid=(rows // block,), in_specs=[pl.BlockSp...  5.8 us
    pallas_call x1, Pallas kernels, make_factor_y(): pl.pallas_call(functools.partial(factor_y_kernel, divisor), in_specs=[pl....  3.8 us
    dot_general x1, matrix products, body(): jnp.einsum('gvazr,hvbzr->gahb', spread, spread, precision=HIGH)  2.49 us
    unnamed x14, local copies, waits for them, and re-layouts  2.14 us
  transfers between devices with their start and end apart: 20, of which 13 were waited for; matrix products, arithmetic and copies ran while one was open for 3% of the time, Pallas kernels for 18%

profile of v2, /device:TPU:0, one launch (start us, length us, event | category | flops | bytes accessed | tf_op | source)
XLA Modules:
  0.0 98.1 jit_solution(12647787184510828568)
XLA Ops:
  0.7 5.8 %sketch.1 = f32[128,512]{1,0:T(8,128)} custom-call(f32[2048,512]{1,0:T(8,128)} %bitcast.70, f32[512,128]{1,0:T(8,128)} %omega_ref.1), custom_call_target="tpu_custom_call" | custom-call | tf_op jit(solution)/shard_map/sketch/pallas_call | solution.py:110
  6.5 0.9 constant_dynamic-slice_fusion.2
  7.4 2.4 %collective-permute-start = (f32[32,512]{1,0:T(8,128)S(1)}, f32[32,512]{1,0:T(8,128)S(1)}, u32[]{:S(2)}, u32[]{:S(2)}) collective-permute-start(f32[32,512]{1,0:T(8,128)S(1)} %get-tuple-element.15), channel_id=1, source_target_pairs={{0,3},{1,2},{2,1},{3,0},{4,7},{5,6},{6,5},{7,4},{8,11},{9,10},{10,... | collective-permute-start | bytes 196616 | tf_op jit(solution)/shard_map/ppermute | solution.py:17
  9.8 0.6 collective-permute-start.1
  10.5 0.0 collective-permute-start.2
  10.5 1.8 %collective-permute-done = f32[32,512]{1,0:T(8,128)S(1)} collective-permute-done((f32[32,512]{1,0:T(8,128)S(1)}, f32[32,512]{1,0:T(8,128)S(1)}, u32[]{:S(2)}, u32[]{:S(2)}) %collective-permute-start) | collective-permute-done | bytes 65568 | tf_op jit(solution)/shard_map/ppermute | solution.py:17
  12.3 2.2 %collective-permute-done.1 = f32[32,512]{1,0:T(8,128)S(1)} collective-permute-done((f32[32,512]{1,0:T(8,128)S(1)}, f32[32,512]{1,0:T(8,128)S(1)}, u32[]{:S(2)}, u32[]{:S(2)}) %collective-permute-start.1) | collective-permute-done | bytes 65568 | tf_op jit(solution)/shard_map/ppermute | solution.py:17
  14.5 0.0 collective-permute-done.2
  14.5 0.9 add_add_fusion.1
  15.4 3.9 %collective-permute-start.3 = (f32[32,512]{1,0:T(8,128)S(1)}, f32[32,512]{1,0:T(8,128)S(1)}, u32[]{:S(2)}, u32[]{:S(2)}) collective-permute-start(f32[32,512]{1,0:T(8,128)S(1)} %add_add_fusion.1), channel_id=1, source_target_pairs={{0,12},{4,8},{8,4},{12,0},{1,13},{5,9},{9,5},{13,1},{2,14},{6,10},... | collective-permute-start | bytes 196616 | tf_op jit(solution)/shard_map/ppermute | solution.py:17
  19.2 0.0 collective-permute-start.4
  19.2 0.6 collective-permute-start.5
  19.9 1.9 %collective-permute-done.3 = f32[32,512]{1,0:T(8,128)S(1)} collective-permute-done((f32[32,512]{1,0:T(8,128)S(1)}, f32[32,512]{1,0:T(8,128)S(1)}, u32[]{:S(2)}, u32[]{:S(2)}) %collective-permute-start.3) | collective-permute-done | bytes 65568 | tf_op jit(solution)/shard_map/ppermute | solution.py:17
  21.7 3.2 %collective-permute-done.4 = f32[32,512]{1,0:T(8,128)S(1)} collective-permute-done((f32[32,512]{1,0:T(8,128)S(1)}, f32[32,512]{1,0:T(8,128)S(1)}, u32[]{:S(2)}, u32[]{:S(2)}) %collective-permute-start.4) | collective-permute-done | bytes 65568 | tf_op jit(solution)/shard_map/ppermute | solution.py:17
  24.9 0.0 collective-permute-done.5
  25.0 1.0 collective-permute-start.6
  26.0 0.1 copy.20
  26.1 0.8 collective-permute-start.7
  26.9 0.2 collective-permute-start.8
  27.1 2.2 %collective-permute-done.6 = f32[32,512]{1,0:T(8,128)S(1)} collective-permute-done((f32[32,512]{1,0:T(8,128)S(1)}, f32[32,512]{1,0:T(8,128)S(1)}, u32[]{:S(2)}, u32[]{:S(2)}) %collective-permute-start.6) | collective-permute-done | bytes 65568 | tf_op jit(solution)/shard_map/ppermute | solution.py:17
  29.3 1.6 %collective-permute-done.7 = f32[32,512]{1,0:T(8,128)S(1)} collective-permute-done((f32[32,512]{1,0:T(8,128)S(1)}, f32[32,512]{1,0:T(8,128)S(1)}, u32[]{:S(2)}, u32[]{:S(2)}) %collective-permute-start.7) | collective-permute-done | bytes 65568 | tf_op jit(solution)/shard_map/ppermute | solution.py:17
  30.9 0.0 collective-permute-done.8
  31.0 0.7 broadcast_multiply_fusion.sketch_ref
  31.7 2.5 %chunk.5 = f32[64,8,128]{2,1,0:T(8,128)} custom-call(s32[1]{0:T(128)} %bitcast.4.where_ref, f32[64,32,512]{2,1,0:T(8,128)} %bitcast.71, f32[128,512]{1,0:T(8,128)} %broadcast_multiply_fusion.sketch_ref), custom_call_target="tpu_custom_call" | custom-call | tf_op jit(solution)/shard_map/chunk/pallas_call | solution.py:138
  34.2 0.9 collective-permute-start.9
  35.1 2.5 %chunk.6 = f32[64,8,128]{2,1,0:T(8,128)} custom-call(s32[1]{0:T(128)} %bitcast.6.where_ref, f32[64,32,512]{2,1,0:T(8,128)} %bitcast.72, f32[128,512]{1,0:T(8,128)} %broadcast_multiply_fusion.sketch_ref), custom_call_target="tpu_custom_call" | custom-call | tf_op jit(solution)/shard_map/chunk/pallas_call | solution.py:138
  37.5 2.3 %collective-permute-start.10 = (f32[64,8,128]{2,1,0:T(8,128)}, f32[64,8,128]{2,1,0:T(8,128)S(1)}, u32[]{:S(2)}, u32[]{:S(2)}) collective-permute-start(f32[64,8,128]{2,1,0:T(8,128)} %chunk.6), channel_id=1, source_target_pairs={{0,8},{4,12},{8,0},{12,4},{1,9},{5,13},{9,1},{13,5},{2,10},{6,14},... | collective-permute-start | bytes 786440 | tf_op jit(solution)/shard_map/ppermute | solution.py:17
  39.8 2.5 %chunk.7 = f32[64,8,128]{2,1,0:T(8,128)} custom-call(s32[1]{0:T(128)} %bitcast.8.where_ref, f32[64,32,512]{2,1,0:T(8,128)} %bitcast.73, f32[128,512]{1,0:T(8,128)} %broadcast_multiply_fusion.sketch_ref), custom_call_target="tpu_custom_call" | custom-call | tf_op jit(solution)/shard_map/chunk/pallas_call | solution.py:138
  42.3 1.2 %collective-permute-start.11 = (f32[64,8,128]{2,1,0:T(8,128)}, f32[64,8,128]{2,1,0:T(8,128)S(1)}, u32[]{:S(2)}, u32[]{:S(2)}) collective-permute-start(f32[64,8,128]{2,1,0:T(8,128)} %chunk.7), channel_id=1, source_target_pairs={{0,12},{4,8},{8,4},{12,0},{1,13},{5,9},{9,5},{13,1},{2,14},{6,10},... | collective-permute-start | bytes 786440 | tf_op jit(solution)/shard_map/ppermute | solution.py:17
  44.2 2.5 %chunk.4 = f32[64,8,128]{2,1,0:T(8,128)} custom-call(s32[1]{0:T(128)} %bitcast.where_ref, f32[64,32,512]{2,1,0:T(8,128)} %bitcast.74, f32[128,512]{1,0:T(8,128)} %broadcast_multiply_fusion.sketch_ref), custom_call_target="tpu_custom_call" | custom-call | tf_op jit(solution)/shard_map/chunk/pallas_call | solution.py:138
  46.7 10.7 %factor_x.1 = f32[128,128]{1,0:T(8,128)} custom-call(s32[1]{0:T(128)S(6)} %copy.52.rank_ref, f32[128,512]{1,0:T(8,128)} %broadcast_multiply_fusion.sketch_ref), custom_call_target="tpu_custom_call" | custom-call | tf_op jit(solution)/shard_map/factor_x/pallas_call | solution.py:196
  57.3 0.0 collective-permute-done.9
  57.3 1.7 %collective-permute-done.10 = f32[64,8,128]{2,1,0:T(8,128)S(1)} collective-permute-done((f32[64,8,128]{2,1,0:T(8,128)}, f32[64,8,128]{2,1,0:T(8,128)S(1)}, u32[]{:S(2)}, u32[]{:S(2)}) %collective-permute-start.10) | collective-permute-done | bytes 262176 | tf_op jit(solution)/shard_map/ppermute | solution.py:17
  59.1 0.0 collective-permute-done.11
  59.1 1.6 %fusion = f32[4,4,16,8,128]{4,3,2,1,0:T(8,128)S(1)} fusion(f32[1,4,16,8,128]{4,3,2,1,0:T(8,128)S(1)} %bitcast.83, f32[1,4,16,8,128]{4,3,2,1,0:T(8,128)S(1)} %bitcast.82, f32[1,4,16,8,128]{4,3,2,1,0:T(8,128)S(1)} %bitcast.81, f32[1,4,16,8,128]{4,3,2,1,0:T(8,128)} %bitcast.78, f32[128,128]{1,0:T(8,128)} %factor_x.1), kind=kOutput, calls=%fused_computation.2 | convolution fusion | flops 202113024 | bytes 2162688 | tf_op jit(solution)/shard_map/dot_general | solution.py:257
  60.7 2.5 %convolution_bitcast_fusion.1 = f32[4,16,4,16]{3,1,2,0:T(8,128)S(1)} fusion(f32[4,4,16,8,128,1]{4,3,2,1,0,5:T(8,128)S(1)} %bitcast.75, f32[4,4,16,8,128]{4,3,2,1,0:T(8,128)S(1)} %fusion), kind=kOutput, calls=%fused_computation.1 | convolution fusion | flops 100663296 | bytes 2113536 | tf_op jit(solution)/shard_map/gvazr,hvbzr->gahb/dot_general | solution.py:259
  63.2 0.1 copy.19
  63.2 0.1 dot_general.19
  63.3 0.2 fusion.17
  63.5 0.1 collective-permute-start.12
  63.6 1.2 %collective-permute-done.12 = f32[64,32]{1,0:T(8,128)S(1)} collective-permute-done((f32[64,32]{1,0:T(8,128)S(1)}, f32[64,32]{1,0:T(8,128)S(1)}, u32[]{:S(2)}, u32[]{:S(2)}) %collective-permute-start.12) | collective-permute-done | bytes 8224 | tf_op jit(solution)/shard_map/ppermute | solution.py:17
  64.8 1.0 %collective-permute-start.13 = (f32[64,32]{1,0:T(8,128)S(1)}, f32[64,32]{1,0:T(8,128)S(1)}, u32[]{:S(2)}, u32[]{:S(2)}) collective-permute-start(f32[64,32]{1,0:T(8,128)S(1)} %bitcast_add_fusion), channel_id=1, source_target_pairs={{0,2},{2,0},{1,3},{3,1},{4,6},{6,4},{5,7},{7,5},{8,10},{10,8},{9,1... | collective-permute-start | bytes 24584 | tf_op jit(solution)/shard_map/ppermute | solution.py:17
  65.8 2.9 %collective-permute-done.13 = f32[64,32]{1,0:T(8,128)S(1)} collective-permute-done((f32[64,32]{1,0:T(8,128)S(1)}, f32[64,32]{1,0:T(8,128)S(1)}, u32[]{:S(2)}, u32[]{:S(2)}) %collective-permute-start.13) | collective-permute-done | bytes 8224 | tf_op jit(solution)/shard_map/ppermute | solution.py:17
  68.7 2.0 %collective-permute-start.14 = (f32[64,32]{1,0:T(8,128)S(1)}, f32[64,32]{1,0:T(8,128)S(1)}, u32[]{:S(2)}, u32[]{:S(2)}) collective-permute-start(f32[64,32]{1,0:T(8,128)S(1)} %add.55.refs_0_), channel_id=1, source_target_pairs={{0,12},{4,8},{8,4},{12,0},{1,13},{5,9},{9,5},{13,1},{2,14},{6,10},... | collective-permute-start | bytes 24584 | tf_op jit(solution)/shard_map/ppermute | solution.py:17
  70.8 4.6 %collective-permute-start.15 = (f32[64,32]{1,0:T(8,128)S(1)}, f32[64,32]{1,0:T(8,128)S(1)}, u32[]{:S(2)}, u32[]{:S(2)}) collective-permute-start(f32[64,32]{1,0:T(8,128)S(1)} %add.55.refs_0_), channel_id=1, source_target_pairs={{0,8},{4,12},{8,0},{12,4},{1,9},{5,13},{9,1},{13,5},{2,10},{6,14},... | collective-permute-start | bytes 24584 | tf_op jit(solution)/shard_map/ppermute | solution.py:17
  75.3 0.0 collective-permute-start.16
  76.0 0.0 collective-permute-done.14.refs_1_
  76.0 0.0 copy-start.2
  76.0 1.6 %collective-permute-done.15.refs_2_ = f32[64,32]{1,0:T(8,128)S(1)} collective-permute-done((f32[64,32]{1,0:T(8,128)S(1)}, f32[64,32]{1,0:T(8,128)S(1)}, u32[]{:S(2)}, u32[]{:S(2)}) %collective-permute-start.15) | collective-permute-done | bytes 8224 | tf_op jit(solution)/shard_map/ppermute | solution.py:17
  77.6 1.6 %collective-permute-done.16.refs_3_ = f32[64,32]{1,0:T(8,128)S(1)} collective-permute-done((f32[64,32]{1,0:T(8,128)S(1)}, f32[64,32]{1,0:T(8,128)S(1)}, u32[]{:S(2)}, u32[]{:S(2)}) %collective-permute-start.16) | collective-permute-done | bytes 8224 | tf_op jit(solution)/shard_map/ppermute | solution.py:17
  79.3 0.6 copy-done.4
  79.9 3.8 %factor_y.1 = f32[64,32]{1,0:T(8,128)} custom-call(s32[1]{0:T(128)S(6)} %copy.53.rank_ref, f32[64,32]{1,0:T(8,128)} %copy-done.1, f32[64,32]{1,0:T(8,128)} %copy-done.2, f32[64,32]{1,0:T(8,128)} %copy-done.3, f32[64,32]{1,0:T(8,128)} %copy-done.4), custom_call_target="tpu_custom_call" | custom-call | tf_op jit(solution)/shard_map/factor_y/pallas_call | solution.py:217
  83.7 0.8 reverse_select_fusion.5
  84.5 0.1 copy.22
  84.6 0.8 convolution_bitcast_fusion
  85.5 1.1 %collective-permute-start.17 = (f32[4,8,8,128]{3,1,2,0:T(8,128)S(1)}, f32[4,8,8,128]{3,1,2,0:T(8,128)S(1)}, u32[]{:S(2)}, u32[]{:S(2)}) collective-permute-start(f32[4,8,8,128]{3,1,2,0:T(8,128)S(1)} %get-tuple-element.14), channel_id=1, source_target_pairs={{0,4},{4,0},{8,12},{12,8},{1,5},{5,1},{9,13},{13,9},{2,6},{6,2},{1... | collective-permute-start | bytes 393224 | tf_op jit(solution)/shard_map/ppermute | solution.py:17
  86.6 1.4 %collective-permute-start.18 = (f32[4,8,8,128]{3,1,2,0:T(8,128)S(1)}, f32[4,8,8,128]{3,1,2,0:T(8,128)S(1)}, u32[]{:S(2)}, u32[]{:S(2)}) collective-permute-start(f32[4,8,8,128]{3,1,2,0:T(8,128)S(1)} %get-tuple-element.13), channel_id=1, source_target_pairs={{0,8},{4,12},{8,0},{12,4},{1,9},{5,13},{9,1},{13,5},{2,10},{6,14},... | collective-permute-start | bytes 393224 | tf_op jit(solution)/shard_map/ppermute | solution.py:17
  88.0 1.9 %collective-permute-start.19 = (f32[4,8,8,128]{3,1,2,0:T(8,128)S(1)}, f32[4,8,8,128]{3,1,2,0:T(8,128)S(1)}, u32[]{:S(2)}, u32[]{:S(2)}) collective-permute-start(f32[4,8,8,128]{3,1,2,0:T(8,128)S(1)} %get-tuple-element.12), channel_id=1, source_target_pairs={{0,12},{4,8},{8,4},{12,0},{1,13},{5,9},{9,5},{13,1},{2,14},{6,10},... | collective-permute-start | bytes 393224 | tf_op jit(solution)/shard_map/ppermute | solution.py:17
  89.9 1.1 %fusion.15 = f32[512,128]{1,0:T(8,128)} fusion(f32[128,128]{1,0:T(8,128)S(1)} %copy-done, f32[128,512]{1,0:T(8,128)S(1)} %constant_dynamic-update-slice_fusion), kind=kOutput, calls=%fused_computation.43 | convolution fusion | flops 50397184 | bytes 589824 | tf_op jit(solution)/shard_map/dot_general | solution.py:254
  91.0 1.4 %copy.26 = f32[64,32]{0,1:T(8,128)} copy(f32[64,32]{1,0:T(8,128)} %factor_y.1) | data formatting | bytes 16384
  92.4 0.6 collective-permute-done.17
  93.0 4.0 %collective-permute-done.18 = f32[4,8,8,128]{3,1,2,0:T(8,128)S(1)} collective-permute-done((f32[4,8,8,128]{3,1,2,0:T(8,128)S(1)}, f32[4,8,8,128]{3,1,2,0:T(8,128)S(1)}, u32[]{:S(2)}, u32[]{:S(2)}) %collective-permute-start.18) | collective-permute-done | bytes 131104 | tf_op jit(solution)/shard_map/ppermute | solution.py:17
  97.0 0.0 collective-permute-done.19
  97.2 0.9 copy.47
  (29 shorter events, 0.3 us)
Async XLA Ops:
  0.6 25.4 %copy-start.5 = (f32[64,32]{0,1:T(8,128)S(1)}, f32[64,32]{0,1:T(8,128)}, u32[]{:S(2)}) copy-start(f32[64,32]{0,1:T(8,128)} %param.7) | copy-start | bytes 24580
  7.4 4.9 %collective-permute-start = (f32[32,512]{1,0:T(8,128)S(1)}, f32[32,512]{1,0:T(8,128)S(1)}, u32[]{:S(2)}, u32[]{:S(2)}) collective-permute-start(f32[32,512]{1,0:T(8,128)S(1)} %get-tuple-element.15), channel_id=1, source_target_pairs={{0,3},{1,2},{2,1},{3,0},{4,7},{5,6},{6,5},{7,4},{8,11},{9,10},{10,... | collective-permute-start | bytes 196616 | tf_op jit(solution)/shard_map/ppermute | solution.py:17
  9.8 4.7 %collective-permute-start.1 = (f32[32,512]{1,0:T(8,128)S(1)}, f32[32,512]{1,0:T(8,128)S(1)}, u32[]{:S(2)}, u32[]{:S(2)}) collective-permute-start(f32[32,512]{1,0:T(8,128)S(1)} %get-tuple-element.17), channel_id=1, source_target_pairs={{0,2},{1,3},{2,0},{3,1},{4,6},{5,7},{6,4},{7,5},{8,10},{9,11},{10,... | collective-permute-start | bytes 196616 | tf_op jit(solution)/shard_map/ppermute | solution.py:17
  10.5 4.0 %collective-permute-start.2 = (f32[32,512]{1,0:T(8,128)S(1)}, f32[32,512]{1,0:T(8,128)S(1)}, u32[]{:S(2)}, u32[]{:S(2)}) collective-permute-start(f32[32,512]{1,0:T(8,128)S(1)} %get-tuple-element.16), channel_id=1, source_target_pairs={{0,1},{1,0},{2,3},{3,2},{4,5},{5,4},{6,7},{7,6},{8,9},{9,8},{10,11... | collective-permute-start | bytes 196616 | tf_op jit(solution)/shard_map/ppermute | solution.py:17
  15.4 6.4 %collective-permute-start.3 = (f32[32,512]{1,0:T(8,128)S(1)}, f32[32,512]{1,0:T(8,128)S(1)}, u32[]{:S(2)}, u32[]{:S(2)}) collective-permute-start(f32[32,512]{1,0:T(8,128)S(1)} %add_add_fusion.1), channel_id=1, source_target_pairs={{0,12},{4,8},{8,4},{12,0},{1,13},{5,9},{9,5},{13,1},{2,14},{6,10},... | collective-permute-start | bytes 196616 | tf_op jit(solution)/shard_map/ppermute | solution.py:17
  19.2 5.7 %collective-permute-start.4 = (f32[32,512]{1,0:T(8,128)S(1)}, f32[32,512]{1,0:T(8,128)S(1)}, u32[]{:S(2)}, u32[]{:S(2)}) collective-permute-start(f32[32,512]{1,0:T(8,128)S(1)} %add_add_fusion.1), channel_id=1, source_target_pairs={{0,8},{4,12},{8,0},{12,4},{1,9},{5,13},{9,1},{13,5},{2,10},{6,14},... | collective-permute-start | bytes 196616 | tf_op jit(solution)/shard_map/ppermute | solution.py:17
  19.2 5.7 %collective-permute-start.5 = (f32[32,512]{1,0:T(8,128)S(1)}, f32[32,512]{1,0:T(8,128)S(1)}, u32[]{:S(2)}, u32[]{:S(2)}) collective-permute-start(f32[32,512]{1,0:T(8,128)S(1)} %add_add_fusion.1), channel_id=1, source_target_pairs={{0,4},{4,0},{8,12},{12,8},{1,5},{5,1},{9,13},{13,9},{2,6},{6,2},{1... | collective-permute-start | bytes 196616 | tf_op jit(solution)/shard_map/ppermute | solution.py:17
  25.0 4.3 %collective-permute-start.6 = (f32[32,512]{1,0:T(8,128)S(1)}, f32[32,512]{1,0:T(8,128)S(1)}, u32[]{:S(2)}, u32[]{:S(2)}) collective-permute-start(f32[32,512]{1,0:T(8,128)S(1)} %get-tuple-element.10), channel_id=1, source_target_pairs={{0,3},{1,2},{2,1},{3,0},{4,7},{5,6},{6,5},{7,4},{8,11},{9,10},{10,... | collective-permute-start | bytes 196616 | tf_op jit(solution)/shard_map/ppermute | solution.py:17
  26.1 4.9 %collective-permute-start.7 = (f32[32,512]{1,0:T(8,128)S(1)}, f32[32,512]{1,0:T(8,128)S(1)}, u32[]{:S(2)}, u32[]{:S(2)}) collective-permute-start(f32[32,512]{1,0:T(8,128)S(1)} %get-tuple-element.10), channel_id=1, source_target_pairs={{0,2},{1,3},{2,0},{3,1},{4,6},{5,7},{6,4},{7,5},{8,10},{9,11},{10,... | collective-permute-start | bytes 196616 | tf_op jit(solution)/shard_map/ppermute | solution.py:17
  26.9 4.1 %collective-permute-start.8 = (f32[32,512]{1,0:T(8,128)S(1)}, f32[32,512]{1,0:T(8,128)S(1)}, u32[]{:S(2)}, u32[]{:S(2)}) collective-permute-start(f32[32,512]{1,0:T(8,128)S(1)} %get-tuple-element.10), channel_id=1, source_target_pairs={{0,1},{1,0},{2,3},{3,2},{4,5},{5,4},{6,7},{7,6},{8,9},{9,8},{10,11... | collective-permute-start | bytes 196616 | tf_op jit(solution)/shard_map/ppermute | solution.py:17
  34.2 23.2 %collective-permute-start.9 = (f32[64,8,128]{2,1,0:T(8,128)}, f32[64,8,128]{2,1,0:T(8,128)S(1)}, u32[]{:S(2)}, u32[]{:S(2)}) collective-permute-start(f32[64,8,128]{2,1,0:T(8,128)} %chunk.5), channel_id=1, source_target_pairs={{0,4},{4,0},{8,12},{12,8},{1,5},{5,1},{9,13},{13,9},{2,6},{6,2},{1... | collective-permute-start | bytes 786440 | tf_op jit(solution)/shard_map/ppermute | solution.py:17
  37.5 21.5 %collective-permute-start.10 = (f32[64,8,128]{2,1,0:T(8,128)}, f32[64,8,128]{2,1,0:T(8,128)S(1)}, u32[]{:S(2)}, u32[]{:S(2)}) collective-permute-start(f32[64,8,128]{2,1,0:T(8,128)} %chunk.6), channel_id=1, source_target_pairs={{0,8},{4,12},{8,0},{12,4},{1,9},{5,13},{9,1},{13,5},{2,10},{6,14},... | collective-permute-start | bytes 786440 | tf_op jit(solution)/shard_map/ppermute | solution.py:17
  42.3 16.8 %collective-permute-start.11 = (f32[64,8,128]{2,1,0:T(8,128)}, f32[64,8,128]{2,1,0:T(8,128)S(1)}, u32[]{:S(2)}, u32[]{:S(2)}) collective-permute-start(f32[64,8,128]{2,1,0:T(8,128)} %chunk.7), channel_id=1, source_target_pairs={{0,12},{4,8},{8,4},{12,0},{1,13},{5,9},{9,5},{13,1},{2,14},{6,10},... | collective-permute-start | bytes 786440 | tf_op jit(solution)/shard_map/ppermute | solution.py:17
  59.1 30.8 %copy-start = (f32[128,128]{1,0:T(8,128)S(1)}, f32[128,128]{1,0:T(8,128)}, u32[]{:S(2)}) copy-start(f32[128,128]{1,0:T(8,128)} %factor_x.1) | copy-start | bytes 196612
  63.5 1.3 %collective-permute-start.12 = (f32[64,32]{1,0:T(8,128)S(1)}, f32[64,32]{1,0:T(8,128)S(1)}, u32[]{:S(2)}, u32[]{:S(2)}) collective-permute-start(f32[64,32]{1,0:T(8,128)S(1)} %bitcast.87), channel_id=1, source_target_pairs={{0,1},{1,0},{2,3},{3,2},{4,5},{5,4},{6,7},{7,6},{8,9},{9,8},{10,11... | collective-permute-start | bytes 24584 | tf_op jit(solution)/shard_map/ppermute | solution.py:17
  64.8 3.9 %collective-permute-start.13 = (f32[64,32]{1,0:T(8,128)S(1)}, f32[64,32]{1,0:T(8,128)S(1)}, u32[]{:S(2)}, u32[]{:S(2)}) collective-permute-start(f32[64,32]{1,0:T(8,128)S(1)} %bitcast_add_fusion), channel_id=1, source_target_pairs={{0,2},{2,0},{1,3},{3,1},{4,6},{6,4},{5,7},{7,5},{8,10},{10,8},{9,1... | collective-permute-start | bytes 24584 | tf_op jit(solution)/shard_map/ppermute | solution.py:17
  68.7 10.5 %copy-start.1 = (f32[64,32]{1,0:T(8,128)}, f32[64,32]{1,0:T(8,128)S(1)}, u32[]{:S(2)}) copy-start(f32[64,32]{1,0:T(8,128)S(1)} %add.55.refs_0_) | copy-start | bytes 24580
  68.7 7.3 %collective-permute-start.14 = (f32[64,32]{1,0:T(8,128)S(1)}, f32[64,32]{1,0:T(8,128)S(1)}, u32[]{:S(2)}, u32[]{:S(2)}) collective-permute-start(f32[64,32]{1,0:T(8,128)S(1)} %add.55.refs_0_), channel_id=1, source_target_pairs={{0,12},{4,8},{8,4},{12,0},{1,13},{5,9},{9,5},{13,1},{2,14},{6,10},... | collective-permute-start | bytes 24584 | tf_op jit(solution)/shard_map/ppermute | solution.py:17
  70.8 6.8 %collective-permute-start.15 = (f32[64,32]{1,0:T(8,128)S(1)}, f32[64,32]{1,0:T(8,128)S(1)}, u32[]{:S(2)}, u32[]{:S(2)}) collective-permute-start(f32[64,32]{1,0:T(8,128)S(1)} %add.55.refs_0_), channel_id=1, source_target_pairs={{0,8},{4,12},{8,0},{12,4},{1,9},{5,13},{9,1},{13,5},{2,10},{6,14},... | collective-permute-start | bytes 24584 | tf_op jit(solution)/shard_map/ppermute | solution.py:17
  75.3 3.9 %collective-permute-start.16 = (f32[64,32]{1,0:T(8,128)S(1)}, f32[64,32]{1,0:T(8,128)S(1)}, u32[]{:S(2)}, u32[]{:S(2)}) collective-permute-start(f32[64,32]{1,0:T(8,128)S(1)} %add.55.refs_0_), channel_id=1, source_target_pairs={{0,4},{4,0},{8,12},{12,8},{1,5},{5,1},{9,13},{13,9},{2,6},{6,2},{1... | collective-permute-start | bytes 24584 | tf_op jit(solution)/shard_map/ppermute | solution.py:17
  76.0 3.3 %copy-start.2 = (f32[64,32]{1,0:T(8,128)}, f32[64,32]{1,0:T(8,128)S(1)}, u32[]{:S(2)}) copy-start(f32[64,32]{1,0:T(8,128)S(1)} %collective-permute-done.14.refs_1_) | copy-start | bytes 24580
  77.6 1.6 %copy-start.3 = (f32[64,32]{1,0:T(8,128)}, f32[64,32]{1,0:T(8,128)S(1)}, u32[]{:S(2)}) copy-start(f32[64,32]{1,0:T(8,128)S(1)} %collective-permute-done.15.refs_2_) | copy-start | bytes 24580
  79.3 0.6 copy-start.4
  85.5 7.6 %collective-permute-start.17 = (f32[4,8,8,128]{3,1,2,0:T(8,128)S(1)}, f32[4,8,8,128]{3,1,2,0:T(8,128)S(1)}, u32[]{:S(2)}, u32[]{:S(2)}) collective-permute-start(f32[4,8,8,128]{3,1,2,0:T(8,128)S(1)} %get-tuple-element.14), channel_id=1, source_target_pairs={{0,4},{4,0},{8,12},{12,8},{1,5},{5,1},{9,13},{13,9},{2,6},{6,2},{1... | collective-permute-start | bytes 393224 | tf_op jit(solution)/shard_map/ppermute | solution.py:17
  86.6 10.5 %collective-permute-start.18 = (f32[4,8,8,128]{3,1,2,0:T(8,128)S(1)}, f32[4,8,8,128]{3,1,2,0:T(8,128)S(1)}, u32[]{:S(2)}, u32[]{:S(2)}) collective-permute-start(f32[4,8,8,128]{3,1,2,0:T(8,128)S(1)} %get-tuple-element.13), channel_id=1, source_target_pairs={{0,8},{4,12},{8,0},{12,4},{1,9},{5,13},{9,1},{13,5},{2,10},{6,14},... | collective-permute-start | bytes 393224 | tf_op jit(solution)/shard_map/ppermute | solution.py:17
  88.0 9.0 %collective-permute-start.19 = (f32[4,8,8,128]{3,1,2,0:T(8,128)S(1)}, f32[4,8,8,128]{3,1,2,0:T(8,128)S(1)}, u32[]{:S(2)}, u32[]{:S(2)}) collective-permute-start(f32[4,8,8,128]{3,1,2,0:T(8,128)S(1)} %get-tuple-element.12), channel_id=1, source_target_pairs={{0,12},{4,8},{8,4},{12,0},{1,13},{5,9},{9,5},{13,1},{2,14},{6,10},... | collective-permute-start | bytes 393224 | tf_op jit(solution)/shard_map/ppermute | solution.py:17

commit v3 on v2

--- a/solution.py
+++ b/solution.py
@@ -38,18 +38,16 @@
     return part
 
 
-def sum_sketch(part):
+def sum_sketch(parts, me):
     axes = ("gz", "vert")
-    count = lax.axis_size(axes)
-    me = lax.axis_index("gz") * lax.axis_size("vert") + lax.axis_index("vert")
-    share = part.shape[0] // count
-    cut = lambda who: lax.dynamic_slice_in_dim(part, who * share, share, 0)
-    got = [swap(cut(me ^ s), axes, s) for s in steps(count)]
-    mine = cut(me)
+    count = len(parts)
+    got = [swap(parts[s], axes, s) for s in steps(count)]
+    mine = parts[0]
     for other in got:
         mine = mine + other
     mine = sum_over_gy(mine)
-    whole = jnp.zeros_like(part)
+    share, cells = mine.shape
+    whole = jnp.zeros((share * count, cells), jnp.float32)
     whole = lax.dynamic_update_slice_in_dim(whole, mine, me * share, 0)
     got = [(s, swap(mine, axes, s)) for s in steps(count)]
     for s, other in got:
@@ -74,57 +72,85 @@
     return high, (value - high.astype(jnp.float32)).astype(jnp.bfloat16)
 
 
-def vmem(count):
-    return [pl.BlockSpec(memory_space=pltpu.VMEM)] * count
-
-
-def sketch_kernel(field_ref, omega_ref, out_ref, wide, narrow):
+VMEM = pl.BlockSpec(memory_space=pltpu.VMEM)
+SMEM = pl.BlockSpec(memory_space=pltpu.SMEM)
+
+
+def held(value):
+    return pltpu.with_memory_space_constraint(value, pltpu.VMEM)
+
+
+def kernel_call(body, name, out_shape, scalars, values, scratch=(), limit=16, whole_out=False):
+    many = isinstance(out_shape, list)
+    shapes = out_shape if many else [out_shape]
+    if whole_out:
+        outs = [jax.ShapeDtypeStruct(shape, jnp.float32) for shape in shapes]
+    else:
+        outs = [pltpu.VMEM(shape, jnp.float32) for shape in shapes]
+    return pl.pallas_call(
+        body,
+        in_specs=[SMEM] * len(scalars) + [VMEM] * len(values),
+        out_specs=[VMEM] * len(outs) if many else VMEM,
+        out_shape=outs if many else outs[0],
+        scratch_shapes=list(scratch),
+        compiler_params=pltpu.CompilerParams(vmem_limit_bytes=limit << 20),
+        name=name,
+    )(*scalars, *[held(value) for value in values])
+
+
+PIECES = 4
+
+
+def sketch_kernel(me_ref, field_hbm, omega_ref, field_ref, *refs):
+    *part_refs, total, arrived = refs
     width = omega_ref.shape[1]
-    high, low = halves(field_ref[...])
+    block = field_ref.shape[0] // PIECES
+    copies = []
+    for i in range(PIECES):
+        rows = pl.ds(i * block, block)
+        copies.append(pltpu.make_async_copy(field_hbm.at[rows], field_ref.at[rows], arrived.at[i]))
+        copies[i].start()
     omega_high, omega_low = halves(omega_ref[...])
-    both = mxu(high, jnp.concatenate([omega_high, omega_low], axis=1), dims(1, 0))
-    projected = both[:, :width] + (both[:, width:] + mxu(low, omega_high, dims(1, 0)))
-    proj_high, proj_low = halves(projected)
-    first = mxu(jnp.concatenate([proj_high, proj_low], axis=1), high, dims(0, 0))
-    second = mxu(proj_high, low, dims(0, 0))
-
-    @pl.when(pl.program_id(0) == 0)
-    def _():
-        wide[...] = first
-        narrow[...] = second
-
-    @pl.when(pl.program_id(0) > 0)
-    def _():
-        wide[...] += first
-        narrow[...] += second
-
-    @pl.when(pl.program_id(0) == pl.num_programs(0) - 1)
-    def _():
-        out_ref[...] = wide[:width, :] + (wide[width:, :] + narrow[...])
-
-
-def sketch_part(flat, omega):
+    omega_both = jnp.concatenate([omega_high, omega_low], axis=1)
+    wide = narrow = None
+    for i in range(PIECES):
+        copies[i].wait()
+        high, low = halves(field_ref[i * block:(i + 1) * block, :])
+        both = mxu(high, omega_both, dims(1, 0))
+        projected = both[:, :width] + (both[:, width:] + mxu(low, omega_high, dims(1, 0)))
+        proj_high, proj_low = halves(projected)
+        first = mxu(jnp.concatenate([proj_high, proj_low], axis=1), high, dims(0, 0))
+        second = mxu(proj_high, low, dims(0, 0))
+        wide = first if wide is None else wide + first
+        narrow = second if narrow is None else narrow + second
+    total[...] = wide[:width, :] + (wide[width:, :] + narrow)
+    share = width // len(part_refs)
+    for k, ref in enumerate(part_refs):
+        start = pl.multiple_of((me_ref[0] ^ k) * share, share)
+        ref[...] = total[pl.ds(start, share), :]
+
+
+def sketch_parts(me, count, flat, omega):
     rows, cells = flat.shape
     width = omega.shape[1]
-    block = 512
-    return pl.pallas_call(
+    out = pl.pallas_call(
         sketch_kernel,
-        grid=(rows // block,),
-        in_specs=[
-            pl.BlockSpec((block, cells), lambda i: (i, 0)),
-            pl.BlockSpec((cells, width), lambda i: (0, 0)),
-        ],
-        out_specs=pl.BlockSpec((width, cells), lambda i: (0, 0)),
-        out_shape=jax.ShapeDtypeStruct((width, cells), jnp.float32),
-        scratch_shapes=[pltpu.VMEM((2 * width, cells), jnp.float32), pltpu.VMEM((width, cells), jnp.float32)],
+        in_specs=[SMEM, pl.BlockSpec(memory_space=pltpu.HBM), VMEM],
+        out_specs=[VMEM] * (1 + count),
+        out_shape=[pltpu.VMEM((rows, cells), jnp.float32)]
+        + [pltpu.VMEM((width // count, cells), jnp.float32)] * count,
+        scratch_shapes=[pltpu.VMEM((width, cells), jnp.float32), pltpu.SemaphoreType.DMA((PIECES,))],
+        compiler_params=pltpu.CompilerParams(vmem_limit_bytes=24 << 20),
         name="sketch",
-    )(flat, omega)
+    )(me, flat, held(omega))
+    return out[0], out[1:]
 
 
 def chunk_kernel(where_ref, field_ref, sketch_ref, out_ref):
-    width = sketch_ref.shape[0]
-    rows, share, cells = field_ref.shape
-    high, low = halves(field_ref[...].reshape(rows * share, cells))
+    width, cells = sketch_ref.shape
+    rows, share, _ = out_ref.shape
+    start = pl.multiple_of(where_ref[0] * share, share)
+    high, low = halves(field_ref[:, pl.ds(start, share), :].reshape(rows * share, cells))
     sketch_high, sketch_low = halves(sketch_ref[...])
     both = mxu(high, jnp.concatenate([sketch_high, sketch_low], axis=0), dims(1, 1))
     raw = both[:, :width] + (both[:, width:] + mxu(low, sketch_high, dims(1, 1)))
@@ -132,23 +158,59 @@
 
 
 def field_chunk(where, field, sketch_t, share):
-    rows, _, cells = field.shape
-    width = sketch_t.shape[0]
-    block = rows // 2
-    return pl.pallas_call(
-        chunk_kernel,
-        grid_spec=pltpu.PrefetchScalarGridSpec(
-            num_scalar_prefetch=1,
-            grid=(rows // block,),
-            in_specs=[
-                pl.BlockSpec((block, share, cells), lambda i, w: (i, w[0], 0)),
-                pl.BlockSpec((width, cells), lambda i, w: (0, 0)),
-            ],
-            out_specs=pl.BlockSpec((block, share, width), lambda i, w: (i, 0, 0)),
-        ),
-        out_shape=jax.ShapeDtypeStruct((rows, share, width), jnp.float32),
-        name="chunk",
-    )(where, field, sketch_t)
+    shape = (field.shape[0], share, sketch_t.shape[0])
+    return kernel_call(chunk_kernel, "chunk", shape, [where], [field, sketch_t])
+
+
+def gram_kernel(planes, me_ref, inverse_ref, omega_ref, *refs):
+    *chunk_refs, spread_ref, part_ref = refs
+    rows, share, width = chunk_refs[0].shape
+    rows_y = rows // planes
+    inv_high, inv_low = halves(inverse_ref[...])
+    inv_both = jnp.concatenate([inv_high, inv_low], axis=0)
+    slabs, weights = [], []
+    for k, ref in enumerate(chunk_refs):
+        high, low = halves(ref[...].reshape(rows * share, width))
+        both = mxu(high, inv_both, dims(1, 1))
+        value = both[:, :width] + (both[:, width:] + mxu(low, inv_high, dims(1, 1)))
+        value = jnp.swapaxes(value.reshape(planes, rows_y, share, width), 1, 2)
+        slabs.append(jnp.concatenate([value[v, z] for v in range(planes) for z in range(share)], axis=1))
+        start = pl.multiple_of((me_ref[0] ^ k) * rows_y, rows_y)
+        weights.append(omega_ref[pl.ds(start, rows_y), :])
+    spread = jnp.concatenate(slabs, axis=0)
+    spread_ref[...] = spread
+    high, low = halves(spread)
+    gram = mxu(high, high, dims(1, 1)) + (mxu(high, low, dims(1, 1)) + mxu(low, high, dims(1, 1)))
+    part = exact(gram, jnp.concatenate(weights, axis=0), dims(1, 0))
+    for k in range(len(chunk_refs)):
+        start = pl.multiple_of((me_ref[0] ^ k) * rows_y, rows_y)
+        part_ref[pl.ds(start, rows_y), :] = part[k * rows_y:(k + 1) * rows_y, :]
+
+
+def mix_kernel(me_ref, factor_ref, spread_ref, *refs):
+    *out_refs, mixed = refs
+    planes, share_k, share_z, width = out_refs[0].shape
+    count = len(out_refs)
+    rows_y = factor_ref.shape[0] // count
+    own = [factor_ref[pl.ds(pl.multiple_of((me_ref[0] ^ k) * rows_y, rows_y), rows_y), :] for k in range(count)]
+    fac_high, fac_low = halves(jnp.concatenate(own, axis=0))
+    high, low = halves(spread_ref[...])
+    mixed[...] = mxu(fac_high, high, dims(0, 0)) + (mxu(fac_high, low, dims(0, 0)) + mxu(fac_low, high, dims(0, 0)))
+    for k, ref in enumerate(out_refs):
+        start = pl.multiple_of((me_ref[0] ^ k) * share_k, share_k)
+        block = mixed[pl.ds(start, share_k), :]
+        for v in range(planes):
+            at = lambda z: (v * share_z + z) * width
+            rows = jnp.stack([block[:, at(z):at(z) + width] for z in range(share_z)], axis=0)
+            ref[v] = jnp.swapaxes(rows, 0, 1)
+
+
+def place_kernel(me_ref, *refs):
+    *piece_refs, out_ref = refs
+    share = piece_refs[0].shape[2]
+    for k, ref in enumerate(piece_refs):
+        start = pl.multiple_of((me_ref[0] ^ k) * share, share)
+        out_ref[:, :, pl.ds(start, share), :] = ref[...]
 
 
 def eliminate(gram, count, rank, out_ref):
@@ -193,13 +255,7 @@
 
 def inverse_factor_x(rank, sketch_t):
     width = sketch_t.shape[0]
-    return pl.pallas_call(
-        factor_x_kernel,
-        in_specs=[pl.BlockSpec(memory_space=pltpu.SMEM)] + vmem(1),
-        out_specs=pl.BlockSpec(memory_space=pltpu.VMEM),
-        out_shape=jax.ShapeDtypeStruct((width, width), jnp.float32),
-        name="factor_x",
-    )(rank, sketch_t)
+    return kernel_call(factor_x_kernel, "factor_x", (width, width), [rank], [sketch_t])
 
 
 def factor_y_kernel(divisor, rank_ref, *refs):
@@ -213,15 +269,10 @@
 
 
 def make_factor_y(rank, parts, divisor):
-    rows, width = parts[0].shape
-    return pl.pallas_call(
-        functools.partial(factor_y_kernel, divisor),
-        in_specs=[pl.BlockSpec(memory_space=pltpu.SMEM)] + vmem(len(parts)),
-        out_specs=pl.BlockSpec(memory_space=pltpu.VMEM),
-        out_shape=jax.ShapeDtypeStruct((rows, width), jnp.float32),
-        scratch_shapes=[pltpu.VMEM((width, width), jnp.float32)],
-        name="factor_y",
-    )(rank, *parts)
+    width = parts[0].shape[1]
+    scratch = [pltpu.VMEM((width, width), jnp.float32)]
+    kernel = functools.partial(factor_y_kernel, divisor)
+    return kernel_call(kernel, "factor_y", parts[0].shape, [rank], parts, scratch)
 
 
 def body(field, omega_x, omega_y, rank_x, rank_y):
@@ -235,11 +286,17 @@
     all_rows_z = rows_z * lax.axis_size("gz")
     flat = field.reshape(-1, cells_x)
 
-    sketch_t = sum_sketch(sketch_part(flat, omega_x)) / float(all_planes * all_rows_y * all_rows_z)
+    here = gy[None].astype(jnp.int32)
+    quarter = lax.axis_index("gz") * lax.axis_size("vert") + lax.axis_index("vert")
+    n_quarter = lax.axis_size(("gz", "vert"))
+    field_v, parts = sketch_parts(quarter[None].astype(jnp.int32), n_quarter, flat, omega_x)
+    sketch_t = sum_sketch(parts, quarter) / float(all_planes * all_rows_y * all_rows_z)
 
     share_z = rows_z // n_gy
-    field_z = field.reshape(planes * rows_y, rows_z, cells_x)
-    if share_z % 8 == 0:
+    share_k = ranks_y // n_gy
+    field_z = field_v.reshape(planes * rows_y, rows_z, cells_x)
+    tiled = share_z % 8 == 0 and share_k % 8 == 0
+    if tiled:
         cut = lambda who: field_chunk(who[None].astype(jnp.int32), field_z, sketch_t, share_z)
     else:
         raw = lax.dot_general(flat, sketch_t, dims(1, 1), precision=HIGH)
@@ -253,14 +310,24 @@
     inverse_x = inverse_factor_x(rank_x, sketch_t)
     factor_x = lax.dot_general(sketch_t, inverse_x, dims(0, 1), precision=HIGH)
 
-    spread = jnp.stack(chunks).reshape(-1, ranks_x)
-    spread = lax.dot_general(spread, inverse_x, dims(1, 1), precision=HIGH)
-    spread = spread.reshape(n_gy, planes, rows_y, share_z, ranks_x)
-    local_gram_y = jnp.einsum("gvazr,hvbzr->gahb", spread, spread, precision=HIGH)
-    local_gram_y = local_gram_y.reshape(all_rows_y, all_rows_y)
-    omega_p = by_step(omega_y.reshape(n_gy, rows_y, ranks_y), gy, n_gy).reshape(all_rows_y, ranks_y)
-    part_y = jnp.dot(local_gram_y, omega_p, precision=HIGHEST)
-    part_y = by_step(part_y.reshape(n_gy, rows_y, ranks_y), gy, n_gy).reshape(all_rows_y, ranks_y)
+    if tiled:
+        samples = planes * share_z * ranks_x
+        spread, part_y = kernel_call(
+            functools.partial(gram_kernel, planes),
+            "gram",
+            [(all_rows_y, samples), (all_rows_y, ranks_y)],
+            [here],
+            [inverse_x, omega_y] + chunks,
+        )
+    else:
+        spread = jnp.stack(chunks).reshape(-1, ranks_x)
+        spread = lax.dot_general(spread, inverse_x, dims(1, 1), precision=HIGH)
+        spread = spread.reshape(n_gy, planes, rows_y, share_z, ranks_x)
+        local_gram_y = jnp.einsum("gvazr,hvbzr->gahb", spread, spread, precision=HIGH)
+        local_gram_y = local_gram_y.reshape(all_rows_y, all_rows_y)
+        omega_p = by_step(omega_y.reshape(n_gy, rows_y, ranks_y), gy, n_gy).reshape(all_rows_y, ranks_y)
+        part_y = jnp.dot(local_gram_y, omega_p, precision=HIGHEST)
+        part_y = by_step(part_y.reshape(n_gy, rows_y, ranks_y), gy, n_gy).reshape(all_rows_y, ranks_y)
     for axis in ("vert", "gz"):
         count = lax.axis_size(axis)
         got = [swap(part_y, axis, s) for s in steps(count)]
@@ -269,7 +336,16 @@
     parts = [part_y] + [swap(part_y, "gy", s) for s in steps(n_gy)]
     factor_y = make_factor_y(rank_y, parts, float(all_planes * all_rows_z * ranks_x))
 
-    share_k = ranks_y // n_gy
+    if tiled:
+        shape = (planes, share_k, share_z, ranks_x)
+        scratch = [pltpu.VMEM((ranks_y, spread.shape[1]), jnp.float32)]
+        mixed = kernel_call(mix_kernel, "mix", [shape] * n_gy, [here], [factor_y, spread], scratch)
+        pieces = [mixed[0]] + [None] * (n_gy - 1)
+        for s in steps(n_gy):
+            pieces[s] = swap(mixed[s], "gy", s)
+        shape = (planes, share_k, rows_z, ranks_x)
+        core = kernel_call(place_kernel, "place", shape, [here], pieces, whole_out=True)
+        return (core, factor_x, factor_y)
     weights = by_step(factor_y.reshape(n_gy, rows_y, ranks_y), gy, n_gy)
     weights = weights.reshape(n_gy, rows_y, n_gy, share_k)
     weights = jnp.moveaxis(by_step(jnp.moveaxis(weights, 2, 0), gy, n_gy), 0, 2)

time: 98.8 us -> 89.8 us (0.909)
  Pallas kernels: 30.2 us -> 19.8 us
  local copies, waits for them, and re-layouts: 4.29 us -> 10.3 us
  waiting for transfers between devices: 26.6 us -> 32.4 us
  matrix products: 6.08 us -> 1.1 us
  other arithmetic: 2.65 us -> 0.08 us
  starting transfers between devices: 26.1 us -> 23.8 us
    pallas_call x7 -> x10, Pallas kernels: 30.2 us -> 19.8 us  [the longest x9 16.7 us: kernel_call(): pl.pallas_call(body, in_specs=[SMEM] * len(scalars) + [VMEM] * len(values...]
    unnamed x14, local copies, waits for them, and re-layouts: 2.14 us -> 10.2 us
    ppermute x20, waiting for transfers between devices: 26.6 us -> 32.4 us  [swap(): return lax.ppermute(value, axes, [(i, i ^ step) for i in range(count)])]
    dot_general x4 -> x0, matrix products: 4.99 us -> none  [the longest x1 2.49 us: body(): jnp.einsum('gvazr,hvbzr->gahb', spread, spread, precision=HIGH)]
    ppermute x20, starting transfers between devices: 26.1 us -> 23.8 us  [swap(): return lax.ppermute(value, axes, [(i, i ^ step) for i in range(count)])]
  transfers between devices with their start and end apart: 20 -> 20, of which waited for: 13 -> 13; matrix products, arithmetic and copies ran while one was open for 3% -> 2% of each run, Pallas kernels for 18% -> 12%
where the time goes in v3:
time: 89.8 us; the launch traced here: 89.6 us
  waiting for transfers between devices  32.4 us (36%)
  starting transfers between devices  23.8 us (27%)
  Pallas kernels  19.8 us (22%)
  local copies, waits for them, and re-layouts  10.3 us (11%)
  between operations  2.12 us (2%)
  matrix products  1.1 us (1%)
    ppermute x20, waiting for transfers between devices, swap(): return lax.ppermute(value, axes, [(i, i ^ step) for i in range(count)])  32.4 us
    ppermute x20, starting transfers between devices, swap(): return lax.ppermute(value, axes, [(i, i ^ step) for i in range(count)])  23.8 us
    pallas_call x9, Pallas kernels, kernel_call(): pl.pallas_call(body, in_specs=[SMEM] * len(scalars) + [VMEM] * len(values...  16.7 us
    unnamed x14, local copies, waits for them, and re-layouts  10.2 us
    pallas_call x1, Pallas kernels, sketch_parts(): pl.pallas_call(sketch_kernel, in_specs=[SMEM, pl.BlockSpec(memory_space=p...  3.14 us
  transfers between devices with their start and end apart: 20, of which 13 were waited for; matrix products, arithmetic and copies ran while one was open for 2% of the time, Pallas kernels for 12%

profile of v3, /device:TPU:0, one launch (start us, length us, event | category | flops | bytes accessed | tf_op | source)
XLA Modules:
  0.0 89.6 jit_solution(3161657872652911963)
XLA Ops:
  0.6 0.0 copy-start.3
  0.6 2.2 %copy-done.3 = f32[4,16,32,512]{3,2,1,0:T(8,128)S(1)} copy-done((f32[4,16,32,512]{3,2,1,0:T(8,128)S(1)}, f32[4,16,32,512]{3,2,1,0:T(8,128)}, u32[]{:S(2)}) %copy-start.3) | copy-done | bytes 4194328
  2.8 0.0 copy-start.4
  2.8 0.9 %copy-done.4 = f32[512,128]{1,0:T(8,128)S(1)} copy-done((f32[512,128]{1,0:T(8,128)S(1)}, f32[512,128]{1,0:T(8,128)}, u32[]{:S(2)}) %copy-start.4) | copy-done | bytes 262168
  3.8 3.1 %sketch.1 = (f32[2048,512]{1,0:T(8,128)S(1)}, f32[32,512]{1,0:T(8,128)S(1)}, f32[32,512]{1,0:T(8,128)S(1)}, f32[32,512]{1,0:T(8,128)S(1)}, f32[32,512]{1,0:T(8,128)S(1)}) custom-call(s32[1]{0:T(128)} %bitcast.1.me_ref, f32[2048,512]{1,0:T(8,128)S(1)} %bitcast.12, f32[512,128]{1,0:T(8,128)S(1)} %copy-done.4), custom_call_target="tpu_custom_call" | custom-call | tf_op jit(solution)/shard_map/sketch/pallas_call | solution.py:136
  6.9 0.0 copy-start
  6.9 1.9 %copy-done = f32[2048,512]{1,0:T(8,128)} copy-done((f32[2048,512]{1,0:T(8,128)}, f32[2048,512]{1,0:T(8,128)S(1)}, u32[]{:S(2)}) %copy-start) | copy-done | bytes 4194328
  8.9 2.4 %collective-permute-start = (f32[32,512]{1,0:T(8,128)S(1)}, f32[32,512]{1,0:T(8,128)S(1)}, u32[]{:S(2)}, u32[]{:S(2)}) collective-permute-start(f32[32,512]{1,0:T(8,128)S(1)} %get-tuple-element.15), channel_id=1, source_target_pairs={{0,3},{1,2},{2,1},{3,0},{4,7},{5,6},{6,5},{7,4},{8,11},{9,10},{10,... | collective-permute-start | bytes 196616 | tf_op jit(solution)/shard_map/ppermute | solution.py:17
  11.3 0.6 collective-permute-start.1
  11.9 0.1 collective-permute-start.2
  11.9 1.8 %collective-permute-done = f32[32,512]{1,0:T(8,128)S(1)} collective-permute-done((f32[32,512]{1,0:T(8,128)S(1)}, f32[32,512]{1,0:T(8,128)S(1)}, u32[]{:S(2)}, u32[]{:S(2)}) %collective-permute-start) | collective-permute-done | bytes 65568 | tf_op jit(solution)/shard_map/ppermute | solution.py:17
  13.8 2.2 %collective-permute-done.1 = f32[32,512]{1,0:T(8,128)S(1)} collective-permute-done((f32[32,512]{1,0:T(8,128)S(1)}, f32[32,512]{1,0:T(8,128)S(1)}, u32[]{:S(2)}, u32[]{:S(2)}) %collective-permute-start.1) | collective-permute-done | bytes 65568 | tf_op jit(solution)/shard_map/ppermute | solution.py:17
  15.9 0.0 collective-permute-done.2
  16.0 3.9 %collective-permute-start.3 = (f32[32,512]{1,0:T(8,128)S(1)}, f32[32,512]{1,0:T(8,128)S(1)}, u32[]{:S(2)}, u32[]{:S(2)}) collective-permute-start(f32[32,512]{1,0:T(8,128)S(1)} %add_add_fusion.1), channel_id=1, source_target_pairs={{0,12},{4,8},{8,4},{12,0},{1,13},{5,9},{9,5},{13,1},{2,14},{6,10},... | collective-permute-start | bytes 196616 | tf_op jit(solution)/shard_map/ppermute | solution.py:17
  19.8 0.0 collective-permute-start.4
  19.8 0.6 collective-permute-start.5
  20.5 1.9 %collective-permute-done.3 = f32[32,512]{1,0:T(8,128)S(1)} collective-permute-done((f32[32,512]{1,0:T(8,128)S(1)}, f32[32,512]{1,0:T(8,128)S(1)}, u32[]{:S(2)}, u32[]{:S(2)}) %collective-permute-start.3) | collective-permute-done | bytes 65568 | tf_op jit(solution)/shard_map/ppermute | solution.py:17
  22.3 3.2 %collective-permute-done.4 = f32[32,512]{1,0:T(8,128)S(1)} collective-permute-done((f32[32,512]{1,0:T(8,128)S(1)}, f32[32,512]{1,0:T(8,128)S(1)}, u32[]{:S(2)}, u32[]{:S(2)}) %collective-permute-start.4) | collective-permute-done | bytes 65568 | tf_op jit(solution)/shard_map/ppermute | solution.py:17
  25.5 0.0 collective-permute-done.5
  25.6 1.0 %collective-permute-start.6 = (f32[32,512]{1,0:T(8,128)S(1)}, f32[32,512]{1,0:T(8,128)S(1)}, u32[]{:S(2)}, u32[]{:S(2)}) collective-permute-start(f32[32,512]{1,0:T(8,128)S(1)} %get-tuple-element.29), channel_id=1, source_target_pairs={{0,3},{1,2},{2,1},{3,0},{4,7},{5,6},{6,5},{7,4},{8,11},{9,10},{10,... | collective-permute-start | bytes 196616 | tf_op jit(solution)/shard_map/ppermute | solution.py:17
  26.6 0.9 collective-permute-start.7
  27.4 0.1 collective-permute-start.8
  27.5 2.3 %collective-permute-done.6 = f32[32,512]{1,0:T(8,128)S(1)} collective-permute-done((f32[32,512]{1,0:T(8,128)S(1)}, f32[32,512]{1,0:T(8,128)S(1)}, u32[]{:S(2)}, u32[]{:S(2)}) %collective-permute-start.6) | collective-permute-done | bytes 65568 | tf_op jit(solution)/shard_map/ppermute | solution.py:17
  29.8 1.6 %collective-permute-done.7 = f32[32,512]{1,0:T(8,128)S(1)} collective-permute-done((f32[32,512]{1,0:T(8,128)S(1)}, f32[32,512]{1,0:T(8,128)S(1)}, u32[]{:S(2)}, u32[]{:S(2)}) %collective-permute-start.7) | collective-permute-done | bytes 65568 | tf_op jit(solution)/shard_map/ppermute | solution.py:17
  31.5 0.0 collective-permute-done.8
  31.5 0.0 copy-start.1
  31.5 2.2 %copy-done.1 = f32[2048,512]{1,0:T(8,128)S(1)} copy-done((f32[2048,512]{1,0:T(8,128)S(1)}, f32[2048,512]{1,0:T(8,128)}, u32[]{:S(2)}) %copy-start.1) | copy-done | bytes 4194328
  33.7 0.5 chunk.7
  34.2 2.7 %collective-permute-start.11 = (f32[64,8,128]{2,1,0:T(8,128)S(1)}, f32[64,8,128]{2,1,0:T(8,128)S(1)}, u32[]{:S(2)}, u32[]{:S(2)}) collective-permute-start(f32[64,8,128]{2,1,0:T(8,128)S(1)} %chunk.7), channel_id=1, source_target_pairs={{0,12},{4,8},{8,4},{12,0},{1,13},{5,9},{9,5},{13,1},{2,14},{6,10},... | collective-permute-start | bytes 786440 | tf_op jit(solution)/shard_map/ppermute | solution.py:17
  36.9 0.5 chunk.6
  37.4 0.1 collective-permute-start.10
  37.5 0.5 chunk.5
  37.9 1.8 %collective-permute-start.9 = (f32[64,8,128]{2,1,0:T(8,128)S(1)}, f32[64,8,128]{2,1,0:T(8,128)S(1)}, u32[]{:S(2)}, u32[]{:S(2)}) collective-permute-start(f32[64,8,128]{2,1,0:T(8,128)S(1)} %chunk.5), channel_id=1, source_target_pairs={{0,4},{4,0},{8,12},{12,8},{1,5},{5,1},{9,13},{13,9},{2,6},{6,2},{1... | collective-permute-start | bytes 786440 | tf_op jit(solution)/shard_map/ppermute | solution.py:17
  40.4 0.0 copy-done.5
  40.4 0.1 copy.8.omega_ref
  40.5 9.1 %factor_x.1.inverse_ref = f32[128,128]{1,0:T(8,128)S(1)} custom-call(s32[1]{0:T(128)S(6)} %copy.14.rank_ref, f32[128,512]{1,0:T(8,128)S(1)} %broadcast_multiply_fusion.sketch_ref), custom_call_target="tpu_custom_call" | custom-call | tf_op jit(solution)/shard_map/factor_x/pallas_call | solution.py:90
  49.6 0.0 copy-start.2
  49.6 2.2 %copy-done.2 = f32[2048,512]{1,0:T(8,128)S(1)} copy-done((f32[2048,512]{1,0:T(8,128)S(1)}, f32[2048,512]{1,0:T(8,128)}, u32[]{:S(2)}) %copy-start.2) | copy-done | bytes 4194328
  51.8 0.5 chunk.4.refs_0_
  52.2 0.0 collective-permute-done.11.refs_3_
  52.2 7.7 %collective-permute-done.10.refs_2_ = f32[64,8,128]{2,1,0:T(8,128)S(1)} collective-permute-done((f32[64,8,128]{2,1,0:T(8,128)S(1)}, f32[64,8,128]{2,1,0:T(8,128)S(1)}, u32[]{:S(2)}, u32[]{:S(2)}) %collective-permute-start.10) | collective-permute-done | bytes 262176 | tf_op jit(solution)/shard_map/ppermute | solution.py:17
  59.9 0.0 collective-permute-done.9.refs_1_
  59.9 1.9 %gram.1 = (f32[64,4096]{1,0:T(8,128)S(1)}, f32[64,32]{1,0:T(8,128)S(1)}) custom-call(s32[1]{0:T(128)} %bitcast.where_ref.me_ref, f32[128,128]{1,0:T(8,128)S(1)} %factor_x.1.inverse_ref, f32[64,32]{1,0:T(8,128)S(1)} %copy.8.omega_ref, f32[64,8,128]{2,1,0:T(8,128)S(1)} %chunk.4.refs_0_, f32[64,8,128]{2,1,0:T(8,128)S(1)} %collective-permute-done.9.refs_1_, ...), custom_call_target="tpu_custom_call" | custom-call | tf_op jit(solution)/shard_map/gram/pallas_call | solution.py:90
  61.9 0.0 collective-permute-start.12
  61.9 1.2 %collective-permute-done.12 = f32[64,32]{1,0:T(8,128)S(1)} collective-permute-done((f32[64,32]{1,0:T(8,128)S(1)}, f32[64,32]{1,0:T(8,128)S(1)}, u32[]{:S(2)}, u32[]{:S(2)}) %collective-permute-start.12) | collective-permute-done | bytes 8224 | tf_op jit(solution)/shard_map/ppermute | solution.py:17
  63.1 0.9 %collective-permute-start.13 = (f32[64,32]{1,0:T(8,128)S(1)}, f32[64,32]{1,0:T(8,128)S(1)}, u32[]{:S(2)}, u32[]{:S(2)}) collective-permute-start(f32[64,32]{1,0:T(8,128)S(1)} %add.50), channel_id=1, source_target_pairs={{0,2},{2,0},{1,3},{3,1},{4,6},{6,4},{5,7},{7,5},{8,10},{10,8},{9,1... | collective-permute-start | bytes 24584 | tf_op jit(solution)/shard_map/ppermute | solution.py:17
  64.0 3.0 %collective-permute-done.13 = f32[64,32]{1,0:T(8,128)S(1)} collective-permute-done((f32[64,32]{1,0:T(8,128)S(1)}, f32[64,32]{1,0:T(8,128)S(1)}, u32[]{:S(2)}, u32[]{:S(2)}) %collective-permute-start.13) | collective-permute-done | bytes 8224 | tf_op jit(solution)/shard_map/ppermute | solution.py:17
  67.0 1.8 %collective-permute-start.14 = (f32[64,32]{1,0:T(8,128)S(1)}, f32[64,32]{1,0:T(8,128)S(1)}, u32[]{:S(2)}, u32[]{:S(2)}) collective-permute-start(f32[64,32]{1,0:T(8,128)S(1)} %add.51.refs_0_), channel_id=1, source_target_pairs={{0,12},{4,8},{8,4},{12,0},{1,13},{5,9},{9,5},{13,1},{2,14},{6,10},... | collective-permute-start | bytes 24584 | tf_op jit(solution)/shard_map/ppermute | solution.py:17
  68.9 0.0 collective-permute-start.15
  68.9 2.6 %collective-permute-start.16 = (f32[64,32]{1,0:T(8,128)S(1)}, f32[64,32]{1,0:T(8,128)S(1)}, u32[]{:S(2)}, u32[]{:S(2)}) collective-permute-start(f32[64,32]{1,0:T(8,128)S(1)} %add.51.refs_0_), channel_id=1, source_target_pairs={{0,4},{4,0},{8,12},{12,8},{1,5},{5,1},{9,13},{13,9},{2,6},{6,2},{1... | collective-permute-start | bytes 24584 | tf_op jit(solution)/shard_map/ppermute | solution.py:17
  72.1 0.9 collective-permute-done.14.refs_1_
  73.0 0.7 collective-permute-done.15.refs_2_
  73.7 0.0 collective-permute-done.16.refs_3_
  73.7 2.4 %factor_y.1.factor_ref = f32[64,32]{1,0:T(8,128)S(1)} custom-call(s32[1]{0:T(128)S(6)} %copy.15.rank_ref, f32[64,32]{1,0:T(8,128)S(1)} %add.51.refs_0_, f32[64,32]{1,0:T(8,128)S(1)} %collective-permute-done.14.refs_1_, f32[64,32]{1,0:T(8,128)S(1)} %collective-permute-done.15.refs_2_, f32[64,32]{1,0:T(8,128)S(1)} %collective-permute-done.16.refs_3_), custom_call_target="tpu_custom_call" | custom-call | tf_op jit(solution)/shard_map/factor_y/pallas_call | solution.py:90
  76.0 0.5 mix.1
  76.6 1.7 %collective-permute-start.17 = (f32[4,8,8,128]{3,2,1,0:T(8,128)S(1)}, f32[4,8,8,128]{3,2,1,0:T(8,128)S(1)}, u32[]{:S(2)}, u32[]{:S(2)}) collective-permute-start(f32[4,8,8,128]{3,2,1,0:T(8,128)S(1)} %get-tuple-element.22), channel_id=1, source_target_pairs={{0,4},{4,0},{8,12},{12,8},{1,5},{5,1},{9,13},{13,9},{2,6},{6,2},{1... | collective-permute-start | bytes 393224 | tf_op jit(solution)/shard_map/ppermute | solution.py:17
  78.3 0.9 %collective-permute-start.18 = (f32[4,8,8,128]{3,2,1,0:T(8,128)S(1)}, f32[4,8,8,128]{3,2,1,0:T(8,128)S(1)}, u32[]{:S(2)}, u32[]{:S(2)}) collective-permute-start(f32[4,8,8,128]{3,2,1,0:T(8,128)S(1)} %get-tuple-element.23), channel_id=1, source_target_pairs={{0,8},{4,12},{8,0},{12,4},{1,9},{5,13},{9,1},{13,5},{2,10},{6,14},... | collective-permute-start | bytes 393224 | tf_op jit(solution)/shard_map/ppermute | solution.py:17
  79.2 1.8 %collective-permute-start.19 = (f32[4,8,8,128]{3,2,1,0:T(8,128)S(1)}, f32[4,8,8,128]{3,2,1,0:T(8,128)S(1)}, u32[]{:S(2)}, u32[]{:S(2)}) collective-permute-start(f32[4,8,8,128]{3,2,1,0:T(8,128)S(1)} %get-tuple-element.24), channel_id=1, source_target_pairs={{0,12},{4,8},{8,4},{12,0},{1,13},{5,9},{9,5},{13,1},{2,14},{6,10},... | collective-permute-start | bytes 393224 | tf_op jit(solution)/shard_map/ppermute | solution.py:17
  81.0 1.1 %fusion = f32[512,128]{1,0:T(8,128)} fusion(f32[128,128]{1,0:T(8,128)S(1)} %factor_x.1.inverse_ref, f32[128,512]{1,0:T(8,128)S(1)} %constant_dynamic-update-slice_fusion), kind=kOutput, calls=%fused_computation.7 | convolution fusion | flops 50397184 | bytes 589824 | tf_op jit(solution)/shard_map/dot_general | solution.py:311
  82.1 0.7 copy.9
  82.8 1.5 %collective-permute-done.17.refs_1_ = f32[4,8,8,128]{3,2,1,0:T(8,128)S(1)} collective-permute-done((f32[4,8,8,128]{3,2,1,0:T(8,128)S(1)}, f32[4,8,8,128]{3,2,1,0:T(8,128)S(1)}, u32[]{:S(2)}, u32[]{:S(2)}) %collective-permute-start.17) | collective-permute-done | bytes 131104 | tf_op jit(solution)/shard_map/ppermute | solution.py:17
  84.3 4.3 %collective-permute-done.18.refs_2_ = f32[4,8,8,128]{3,2,1,0:T(8,128)S(1)} collective-permute-done((f32[4,8,8,128]{3,2,1,0:T(8,128)S(1)}, f32[4,8,8,128]{3,2,1,0:T(8,128)S(1)}, u32[]{:S(2)}, u32[]{:S(2)}) %collective-permute-start.18) | collective-permute-done | bytes 131104 | tf_op jit(solution)/shard_map/ppermute | solution.py:17
  88.7 0.0 collective-permute-done.19.refs_3_
  88.7 0.9 place.1
  (10 shorter events, 0.1 us)
Async XLA Ops:
  0.6 2.2 %copy-start.3 = (f32[4,16,32,512]{3,2,1,0:T(8,128)S(1)}, f32[4,16,32,512]{3,2,1,0:T(8,128)}, u32[]{:S(2)}) copy-start(f32[4,16,32,512]{3,2,1,0:T(8,128)} %param.5) | copy-start | bytes 12582916
  2.8 0.9 %copy-start.4 = (f32[512,128]{1,0:T(8,128)S(1)}, f32[512,128]{1,0:T(8,128)}, u32[]{:S(2)}) copy-start(f32[512,128]{1,0:T(8,128)} %omega_ref.2) | copy-start | bytes 786436
  6.9 2.0 %copy-start = (f32[2048,512]{1,0:T(8,128)}, f32[2048,512]{1,0:T(8,128)S(1)}, u32[]{:S(2)}) copy-start(f32[2048,512]{1,0:T(8,128)S(1)} %get-tuple-element.18) | copy-start | bytes 12582916
  8.9 4.9 %collective-permute-start = (f32[32,512]{1,0:T(8,128)S(1)}, f32[32,512]{1,0:T(8,128)S(1)}, u32[]{:S(2)}, u32[]{:S(2)}) collective-permute-start(f32[32,512]{1,0:T(8,128)S(1)} %get-tuple-element.15), channel_id=1, source_target_pairs={{0,3},{1,2},{2,1},{3,0},{4,7},{5,6},{6,5},{7,4},{8,11},{9,10},{10,... | collective-permute-start | bytes 196616 | tf_op jit(solution)/shard_map/ppermute | solution.py:17
  11.3 4.7 %collective-permute-start.1 = (f32[32,512]{1,0:T(8,128)S(1)}, f32[32,512]{1,0:T(8,128)S(1)}, u32[]{:S(2)}, u32[]{:S(2)}) collective-permute-start(f32[32,512]{1,0:T(8,128)S(1)} %get-tuple-element.16), channel_id=1, source_target_pairs={{0,2},{1,3},{2,0},{3,1},{4,6},{5,7},{6,4},{7,5},{8,10},{9,11},{10,... | collective-permute-start | bytes 196616 | tf_op jit(solution)/shard_map/ppermute | solution.py:17
  11.9 4.1 %collective-permute-start.2 = (f32[32,512]{1,0:T(8,128)S(1)}, f32[32,512]{1,0:T(8,128)S(1)}, u32[]{:S(2)}, u32[]{:S(2)}) collective-permute-start(f32[32,512]{1,0:T(8,128)S(1)} %get-tuple-element.17), channel_id=1, source_target_pairs={{0,1},{1,0},{2,3},{3,2},{4,5},{5,4},{6,7},{7,6},{8,9},{9,8},{10,11... | collective-permute-start | bytes 196616 | tf_op jit(solution)/shard_map/ppermute | solution.py:17
  16.0 6.4 %collective-permute-start.3 = (f32[32,512]{1,0:T(8,128)S(1)}, f32[32,512]{1,0:T(8,128)S(1)}, u32[]{:S(2)}, u32[]{:S(2)}) collective-permute-start(f32[32,512]{1,0:T(8,128)S(1)} %add_add_fusion.1), channel_id=1, source_target_pairs={{0,12},{4,8},{8,4},{12,0},{1,13},{5,9},{9,5},{13,1},{2,14},{6,10},... | collective-permute-start | bytes 196616 | tf_op jit(solution)/shard_map/ppermute | solution.py:17
  19.8 5.7 %collective-permute-start.4 = (f32[32,512]{1,0:T(8,128)S(1)}, f32[32,512]{1,0:T(8,128)S(1)}, u32[]{:S(2)}, u32[]{:S(2)}) collective-permute-start(f32[32,512]{1,0:T(8,128)S(1)} %add_add_fusion.1), channel_id=1, source_target_pairs={{0,8},{4,12},{8,0},{12,4},{1,9},{5,13},{9,1},{13,5},{2,10},{6,14},... | collective-permute-start | bytes 196616 | tf_op jit(solution)/shard_map/ppermute | solution.py:17
  19.8 5.7 %collective-permute-start.5 = (f32[32,512]{1,0:T(8,128)S(1)}, f32[32,512]{1,0:T(8,128)S(1)}, u32[]{:S(2)}, u32[]{:S(2)}) collective-permute-start(f32[32,512]{1,0:T(8,128)S(1)} %add_add_fusion.1), channel_id=1, source_target_pairs={{0,4},{4,0},{8,12},{12,8},{1,5},{5,1},{9,13},{13,9},{2,6},{6,2},{1... | collective-permute-start | bytes 196616 | tf_op jit(solution)/shard_map/ppermute | solution.py:17
  25.6 4.2 %collective-permute-start.6 = (f32[32,512]{1,0:T(8,128)S(1)}, f32[32,512]{1,0:T(8,128)S(1)}, u32[]{:S(2)}, u32[]{:S(2)}) collective-permute-start(f32[32,512]{1,0:T(8,128)S(1)} %get-tuple-element.29), channel_id=1, source_target_pairs={{0,3},{1,2},{2,1},{3,0},{4,7},{5,6},{6,5},{7,4},{8,11},{9,10},{10,... | collective-permute-start | bytes 196616 | tf_op jit(solution)/shard_map/ppermute | solution.py:17
  26.6 4.9 %collective-permute-start.7 = (f32[32,512]{1,0:T(8,128)S(1)}, f32[32,512]{1,0:T(8,128)S(1)}, u32[]{:S(2)}, u32[]{:S(2)}) collective-permute-start(f32[32,512]{1,0:T(8,128)S(1)} %get-tuple-element.29), channel_id=1, source_target_pairs={{0,2},{1,3},{2,0},{3,1},{4,6},{5,7},{6,4},{7,5},{8,10},{9,11},{10,... | collective-permute-start | bytes 196616 | tf_op jit(solution)/shard_map/ppermute | solution.py:17
  27.4 4.0 %collective-permute-start.8 = (f32[32,512]{1,0:T(8,128)S(1)}, f32[32,512]{1,0:T(8,128)S(1)}, u32[]{:S(2)}, u32[]{:S(2)}) collective-permute-start(f32[32,512]{1,0:T(8,128)S(1)} %get-tuple-element.29), channel_id=1, source_target_pairs={{0,1},{1,0},{2,3},{3,2},{4,5},{5,4},{6,7},{7,6},{8,9},{9,8},{10,11... | collective-permute-start | bytes 196616 | tf_op jit(solution)/shard_map/ppermute | solution.py:17
  31.5 2.2 %copy-start.1 = (f32[2048,512]{1,0:T(8,128)S(1)}, f32[2048,512]{1,0:T(8,128)}, u32[]{:S(2)}) copy-start(f32[2048,512]{1,0:T(8,128)} %copy-done) | copy-start | bytes 12582916
  34.2 18.1 %collective-permute-start.11 = (f32[64,8,128]{2,1,0:T(8,128)S(1)}, f32[64,8,128]{2,1,0:T(8,128)S(1)}, u32[]{:S(2)}, u32[]{:S(2)}) collective-permute-start(f32[64,8,128]{2,1,0:T(8,128)S(1)} %chunk.7), channel_id=1, source_target_pairs={{0,12},{4,8},{8,4},{12,0},{1,13},{5,9},{9,5},{13,1},{2,14},{6,10},... | collective-permute-start | bytes 786440 | tf_op jit(solution)/shard_map/ppermute | solution.py:17
  36.9 3.5 %copy-start.5 = (f32[64,32]{0,1:T(8,128)S(1)}, f32[64,32]{0,1:T(8,128)}, u32[]{:S(2)}) copy-start(f32[64,32]{0,1:T(8,128)} %param.7) | copy-start | bytes 24580
  37.4 22.5 %collective-permute-start.10 = (f32[64,8,128]{2,1,0:T(8,128)S(1)}, f32[64,8,128]{2,1,0:T(8,128)S(1)}, u32[]{:S(2)}, u32[]{:S(2)}) collective-permute-start(f32[64,8,128]{2,1,0:T(8,128)S(1)} %chunk.6), channel_id=1, source_target_pairs={{0,8},{4,12},{8,0},{12,4},{1,9},{5,13},{9,1},{13,5},{2,10},{6,14},... | collective-permute-start | bytes 786440 | tf_op jit(solution)/shard_map/ppermute | solution.py:17
  37.9 22.0 %collective-permute-start.9 = (f32[64,8,128]{2,1,0:T(8,128)S(1)}, f32[64,8,128]{2,1,0:T(8,128)S(1)}, u32[]{:S(2)}, u32[]{:S(2)}) collective-permute-start(f32[64,8,128]{2,1,0:T(8,128)S(1)} %chunk.5), channel_id=1, source_target_pairs={{0,4},{4,0},{8,12},{12,8},{1,5},{5,1},{9,13},{13,9},{2,6},{6,2},{1... | collective-permute-start | bytes 786440 | tf_op jit(solution)/shard_map/ppermute | solution.py:17
  49.6 2.2 %copy-start.2 = (f32[2048,512]{1,0:T(8,128)S(1)}, f32[2048,512]{1,0:T(8,128)}, u32[]{:S(2)}) copy-start(f32[2048,512]{1,0:T(8,128)} %copy-done) | copy-start | bytes 12582916
  61.9 1.2 %collective-permute-start.12 = (f32[64,32]{1,0:T(8,128)S(1)}, f32[64,32]{1,0:T(8,128)S(1)}, u32[]{:S(2)}, u32[]{:S(2)}) collective-permute-start(f32[64,32]{1,0:T(8,128)S(1)} %get-tuple-element.19), channel_id=1, source_target_pairs={{0,1},{1,0},{2,3},{3,2},{4,5},{5,4},{6,7},{7,6},{8,9},{9,8},{10,11... | collective-permute-start | bytes 24584 | tf_op jit(solution)/shard_map/ppermute | solution.py:17
  63.1 3.9 %collective-permute-start.13 = (f32[64,32]{1,0:T(8,128)S(1)}, f32[64,32]{1,0:T(8,128)S(1)}, u32[]{:S(2)}, u32[]{:S(2)}) collective-permute-start(f32[64,32]{1,0:T(8,128)S(1)} %add.50), channel_id=1, source_target_pairs={{0,2},{2,0},{1,3},{3,1},{4,6},{6,4},{5,7},{7,5},{8,10},{10,8},{9,1... | collective-permute-start | bytes 24584 | tf_op jit(solution)/shard_map/ppermute | solution.py:17
  67.0 5.9 %collective-permute-start.14 = (f32[64,32]{1,0:T(8,128)S(1)}, f32[64,32]{1,0:T(8,128)S(1)}, u32[]{:S(2)}, u32[]{:S(2)}) collective-permute-start(f32[64,32]{1,0:T(8,128)S(1)} %add.51.refs_0_), channel_id=1, source_target_pairs={{0,12},{4,8},{8,4},{12,0},{1,13},{5,9},{9,5},{13,1},{2,14},{6,10},... | collective-permute-start | bytes 24584 | tf_op jit(solution)/shard_map/ppermute | solution.py:17
  68.9 4.8 %collective-permute-start.15 = (f32[64,32]{1,0:T(8,128)S(1)}, f32[64,32]{1,0:T(8,128)S(1)}, u32[]{:S(2)}, u32[]{:S(2)}) collective-permute-start(f32[64,32]{1,0:T(8,128)S(1)} %add.51.refs_0_), channel_id=1, source_target_pairs={{0,8},{4,12},{8,0},{12,4},{1,9},{5,13},{9,1},{13,5},{2,10},{6,14},... | collective-permute-start | bytes 24584 | tf_op jit(solution)/shard_map/ppermute | solution.py:17
  68.9 4.8 %collective-permute-start.16 = (f32[64,32]{1,0:T(8,128)S(1)}, f32[64,32]{1,0:T(8,128)S(1)}, u32[]{:S(2)}, u32[]{:S(2)}) collective-permute-start(f32[64,32]{1,0:T(8,128)S(1)} %add.51.refs_0_), channel_id=1, source_target_pairs={{0,4},{4,0},{8,12},{12,8},{1,5},{5,1},{9,13},{13,9},{2,6},{6,2},{1... | collective-permute-start | bytes 24584 | tf_op jit(solution)/shard_map/ppermute | solution.py:17
  76.6 7.8 %collective-permute-start.17 = (f32[4,8,8,128]{3,2,1,0:T(8,128)S(1)}, f32[4,8,8,128]{3,2,1,0:T(8,128)S(1)}, u32[]{:S(2)}, u32[]{:S(2)}) collective-permute-start(f32[4,8,8,128]{3,2,1,0:T(8,128)S(1)} %get-tuple-element.22), channel_id=1, source_target_pairs={{0,4},{4,0},{8,12},{12,8},{1,5},{5,1},{9,13},{13,9},{2,6},{6,2},{1... | collective-permute-start | bytes 393224 | tf_op jit(solution)/shard_map/ppermute | solution.py:17
  78.3 10.4 %collective-permute-start.18 = (f32[4,8,8,128]{3,2,1,0:T(8,128)S(1)}, f32[4,8,8,128]{3,2,1,0:T(8,128)S(1)}, u32[]{:S(2)}, u32[]{:S(2)}) collective-permute-start(f32[4,8,8,128]{3,2,1,0:T(8,128)S(1)} %get-tuple-element.23), channel_id=1, source_target_pairs={{0,8},{4,12},{8,0},{12,4},{1,9},{5,13},{9,1},{13,5},{2,10},{6,14},... | collective-permute-start | bytes 393224 | tf_op jit(solution)/shard_map/ppermute | solution.py:17
  79.2 9.5 %collective-permute-start.19 = (f32[4,8,8,128]{3,2,1,0:T(8,128)S(1)}, f32[4,8,8,128]{3,2,1,0:T(8,128)S(1)}, u32[]{:S(2)}, u32[]{:S(2)}) collective-permute-start(f32[4,8,8,128]{3,2,1,0:T(8,128)S(1)} %get-tuple-element.24), channel_id=1, source_target_pairs={{0,12},{4,8},{8,4},{12,0},{1,13},{5,9},{9,5},{13,1},{2,14},{6,10},... | collective-permute-start | bytes 393224 | tf_op jit(solution)/shard_map/ppermute | solution.py:17

commit v4 on v3

--- a/solution.py
+++ b/solution.py
@@ -38,7 +38,7 @@
     return part
 
 
-def sum_sketch(parts, me):
+def sum_sketch(parts):
     axes = ("gz", "vert")
     count = len(parts)
     got = [swap(parts[s], axes, s) for s in steps(count)]
@@ -46,13 +46,10 @@
     for other in got:
         mine = mine + other
     mine = sum_over_gy(mine)
-    share, cells = mine.shape
-    whole = jnp.zeros((share * count, cells), jnp.float32)
-    whole = lax.dynamic_update_slice_in_dim(whole, mine, me * share, 0)
-    got = [(s, swap(mine, axes, s)) for s in steps(count)]
-    for s, other in got:
-        whole = lax.dynamic_update_slice_in_dim(whole, other, (me ^ s) * share, 0)
-    return whole
+    pieces = [mine] + [None] * (count - 1)
+    for s in steps(count):
+        pieces[s] = swap(mine, axes, s)
+    return pieces
 
 
 def dims(left, right):
@@ -101,8 +98,10 @@
 PIECES = 4
 
 
-def sketch_kernel(me_ref, field_hbm, omega_ref, field_ref, *refs):
-    *part_refs, total, arrived = refs
+def sketch_kernel(me_ref, here_ref, field_hbm, omega_hbm, field_ref, *refs):
+    *part_refs, omega_ref, total, arrived = refs
+    omega_copy = pltpu.make_async_copy(omega_hbm, omega_ref, arrived.at[PIECES])
+    omega_copy.start()
     width = omega_ref.shape[1]
     block = field_ref.shape[0] // PIECES
     copies = []
@@ -110,6 +109,7 @@
         rows = pl.ds(i * block, block)
         copies.append(pltpu.make_async_copy(field_hbm.at[rows], field_ref.at[rows], arrived.at[i]))
         copies[i].start()
+    omega_copy.wait()
     omega_high, omega_low = halves(omega_ref[...])
     omega_both = jnp.concatenate([omega_high, omega_low], axis=1)
     wide = narrow = None
@@ -130,36 +130,53 @@
         ref[...] = total[pl.ds(start, share), :]
 
 
-def sketch_parts(me, count, flat, omega):
+def sketch_parts(me, here, count, flat, omega):
     rows, cells = flat.shape
     width = omega.shape[1]
+    far = pl.BlockSpec(memory_space=pltpu.HBM)
     out = pl.pallas_call(
         sketch_kernel,
-        in_specs=[SMEM, pl.BlockSpec(memory_space=pltpu.HBM), VMEM],
+        in_specs=[SMEM, SMEM, far, far],
         out_specs=[VMEM] * (1 + count),
         out_shape=[pltpu.VMEM((rows, cells), jnp.float32)]
         + [pltpu.VMEM((width // count, cells), jnp.float32)] * count,
-        scratch_shapes=[pltpu.VMEM((width, cells), jnp.float32), pltpu.SemaphoreType.DMA((PIECES,))],
+        scratch_shapes=[
+            pltpu.VMEM((cells, width), jnp.float32),
+            pltpu.VMEM((width, cells), jnp.float32),
+            pltpu.SemaphoreType.DMA((PIECES + 1,)),
+        ],
         compiler_params=pltpu.CompilerParams(vmem_limit_bytes=24 << 20),
         name="sketch",
-    )(me, flat, held(omega))
+    )(me, here, *[pltpu.with_memory_space_constraint(x, pltpu.HBM) for x in (flat, omega)])
     return out[0], out[1:]
 
 
-def chunk_kernel(where_ref, field_ref, sketch_ref, out_ref):
-    width, cells = sketch_ref.shape
+def gather_sketch(scale, me_ref, piece_refs, whole):
+    share = piece_refs[0].shape[0]
+    for k, ref in enumerate(piece_refs):
+        start = pl.multiple_of((me_ref[0] ^ k) * share, share)
+        whole[pl.ds(start, share), :] = ref[...] * scale
+    return whole[...]
+
+
+def chunk_kernel(scale, step, me_ref, here_ref, field_ref, *refs):
+    *piece_refs, out_ref, whole = refs
+    sketch = gather_sketch(scale, me_ref, piece_refs, whole)
+    width, cells = sketch.shape
     rows, share, _ = out_ref.shape
-    start = pl.multiple_of(where_ref[0] * share, share)
+    start = pl.multiple_of((here_ref[0] ^ step) * share, share)
     high, low = halves(field_ref[:, pl.ds(start, share), :].reshape(rows * share, cells))
-    sketch_high, sketch_low = halves(sketch_ref[...])
+    sketch_high, sketch_low = halves(sketch)
     both = mxu(high, jnp.concatenate([sketch_high, sketch_low], axis=0), dims(1, 1))
     raw = both[:, :width] + (both[:, width:] + mxu(low, sketch_high, dims(1, 1)))
     out_ref[...] = raw.reshape(rows, share, width)
 
 
-def field_chunk(where, field, sketch_t, share):
-    shape = (field.shape[0], share, sketch_t.shape[0])
-    return kernel_call(chunk_kernel, "chunk", shape, [where], [field, sketch_t])
+def field_chunk(scale, step, places, field, pieces, share):
+    width, cells = pieces[0].shape[0] * len(pieces), field.shape[2]
+    scratch = [pltpu.VMEM((width, cells), jnp.float32)]
+    kernel = functools.partial(chunk_kernel, scale, step)
+    return kernel_call(kernel, "chunk", (field.shape[0], share, width), places, [field] + pieces, scratch)
 
 
 def gram_kernel(planes, me_ref, inverse_ref, omega_ref, *refs):
@@ -168,32 +185,23 @@
     rows_y = rows // planes
     inv_high, inv_low = halves(inverse_ref[...])
     inv_both = jnp.concatenate([inv_high, inv_low], axis=0)
-    slabs, weights = [], []
     for k, ref in enumerate(chunk_refs):
         high, low = halves(ref[...].reshape(rows * share, width))
         both = mxu(high, inv_both, dims(1, 1))
         value = both[:, :width] + (both[:, width:] + mxu(low, inv_high, dims(1, 1)))
         value = jnp.swapaxes(value.reshape(planes, rows_y, share, width), 1, 2)
-        slabs.append(jnp.concatenate([value[v, z] for v in range(planes) for z in range(share)], axis=1))
         start = pl.multiple_of((me_ref[0] ^ k) * rows_y, rows_y)
-        weights.append(omega_ref[pl.ds(start, rows_y), :])
-    spread = jnp.concatenate(slabs, axis=0)
-    spread_ref[...] = spread
-    high, low = halves(spread)
+        slab = jnp.concatenate([value[v, z] for v in range(planes) for z in range(share)], axis=1)
+        spread_ref[pl.ds(start, rows_y), :] = slab
+    high, low = halves(spread_ref[...])
     gram = mxu(high, high, dims(1, 1)) + (mxu(high, low, dims(1, 1)) + mxu(low, high, dims(1, 1)))
-    part = exact(gram, jnp.concatenate(weights, axis=0), dims(1, 0))
-    for k in range(len(chunk_refs)):
-        start = pl.multiple_of((me_ref[0] ^ k) * rows_y, rows_y)
-        part_ref[pl.ds(start, rows_y), :] = part[k * rows_y:(k + 1) * rows_y, :]
+    part_ref[...] = exact(gram, omega_ref[...], dims(1, 1))
 
 
 def mix_kernel(me_ref, factor_ref, spread_ref, *refs):
     *out_refs, mixed = refs
     planes, share_k, share_z, width = out_refs[0].shape
-    count = len(out_refs)
-    rows_y = factor_ref.shape[0] // count
-    own = [factor_ref[pl.ds(pl.multiple_of((me_ref[0] ^ k) * rows_y, rows_y), rows_y), :] for k in range(count)]
-    fac_high, fac_low = halves(jnp.concatenate(own, axis=0))
+    fac_high, fac_low = halves(factor_ref[...])
     high, low = halves(spread_ref[...])
     mixed[...] = mxu(fac_high, high, dims(0, 0)) + (mxu(fac_high, low, dims(0, 0)) + mxu(fac_low, high, dims(0, 0)))
     for k, ref in enumerate(out_refs):
@@ -248,14 +256,30 @@
             right[i] = right[i] - c0 * v0 - c1 * v1
 
 
-def factor_x_kernel(rank_ref, sketch_ref, out_ref):
-    sketch_t = sketch_ref[...]
+def factor_x_kernel(scale, rank_ref, me_ref, *refs):
+    *piece_refs, out_ref, sketch_ref = refs
+    sketch_t = gather_sketch(scale, me_ref, piece_refs, sketch_ref)
     eliminate(exact(sketch_t, sketch_t, dims(1, 1)), sketch_t.shape[0], rank_ref[0], out_ref)
 
 
-def inverse_factor_x(rank, sketch_t):
-    width = sketch_t.shape[0]
-    return kernel_call(factor_x_kernel, "factor_x", (width, width), [rank], [sketch_t])
+def inverse_factor_x(scale, rank, me, pieces):
+    width = pieces[0].shape[0] * len(pieces)
+    scratch = [pltpu.VMEM((width, pieces[0].shape[1]), jnp.float32)]
+    kernel = functools.partial(factor_x_kernel, scale)
+    return kernel_call(kernel, "factor_x", (width, width), [rank, me], pieces, scratch)
+
+
+def apply_kernel(scale, me_ref, inverse_ref, *refs):
+    *piece_refs, out_ref, whole = refs
+    sketch_t = gather_sketch(scale, me_ref, piece_refs, whole)
+    out_ref[...] = exact(sketch_t, inverse_ref[...], dims(0, 1))
+
+
+def make_factor_x(scale, me, inverse, pieces):
+    width, cells = inverse.shape[0], pieces[0].shape[1]
+    scratch = [pltpu.VMEM((width, cells), jnp.float32)]
+    kernel = functools.partial(apply_kernel, scale)
+    return kernel_call(kernel, "apply", (cells, width), [me], [inverse] + pieces, scratch, whole_out=True)
 
 
 def factor_y_kernel(divisor, rank_ref, *refs):
@@ -289,26 +313,30 @@
     here = gy[None].astype(jnp.int32)
     quarter = lax.axis_index("gz") * lax.axis_size("vert") + lax.axis_index("vert")
     n_quarter = lax.axis_size(("gz", "vert"))
-    field_v, parts = sketch_parts(quarter[None].astype(jnp.int32), n_quarter, flat, omega_x)
-    sketch_t = sum_sketch(parts, quarter) / float(all_planes * all_rows_y * all_rows_z)
+    quarter = quarter[None].astype(jnp.int32)
+    field_v, parts = sketch_parts(quarter, here, n_quarter, flat, omega_x)
+    pieces = sum_sketch(parts)
+    scale = 1.0 / float(all_planes * all_rows_y * all_rows_z)
 
     share_z = rows_z // n_gy
     share_k = ranks_y // n_gy
     field_z = field_v.reshape(planes * rows_y, rows_z, cells_x)
     tiled = share_z % 8 == 0 and share_k % 8 == 0
     if tiled:
-        cut = lambda who: field_chunk(who[None].astype(jnp.int32), field_z, sketch_t, share_z)
+        cut = lambda s: field_chunk(scale, s, [quarter, here], field_z, pieces, share_z)
     else:
+        sketch_t = jnp.take(jnp.stack(pieces), quarter ^ jnp.arange(n_quarter), axis=0)
+        sketch_t = sketch_t.reshape(ranks_x, cells_x) * scale
         raw = lax.dot_general(flat, sketch_t, dims(1, 1), precision=HIGH)
         raw = raw.reshape(planes * rows_y, rows_z, ranks_x)
-        cut = lambda who: lax.dynamic_slice_in_dim(raw, who * share_z, share_z, 1)
+        cut = lambda s: lax.dynamic_slice_in_dim(raw, (gy ^ s) * share_z, share_z, 1)
     chunks = [None] * n_gy
     for s in steps(n_gy):
-        chunks[s] = swap(cut(gy ^ s), "gy", s)
-    chunks[0] = cut(gy)
-
-    inverse_x = inverse_factor_x(rank_x, sketch_t)
-    factor_x = lax.dot_general(sketch_t, inverse_x, dims(0, 1), precision=HIGH)
+        chunks[s] = swap(cut(s), "gy", s)
+    chunks[0] = cut(0)
+
+    inverse_x = inverse_factor_x(scale, rank_x, quarter, pieces)
+    factor_x = make_factor_x(scale, quarter, inverse_x, pieces)
 
     if tiled:
         samples = planes * share_z * ranks_x
@@ -317,7 +345,7 @@
             "gram",
             [(all_rows_y, samples), (all_rows_y, ranks_y)],
             [here],
-            [inverse_x, omega_y] + chunks,
+            [inverse_x, omega_y.T] + chunks,
         )
     else:
         spread = jnp.stack(chunks).reshape(-1, ranks_x)

time: 89.8 us -> 84.8 us (0.944)
  local copies, waits for them, and re-layouts: 10.3 us -> 0.69 us
  starting transfers between devices: 23.8 us -> 26.6 us
  Pallas kernels: 19.8 us -> 22.2 us
  matrix products: 1.1 us -> 0 us
    unnamed x14 -> x3, local copies, waits for them, and re-layouts: 10.2 us -> 0.69 us
    ppermute x20, starting transfers between devices: 23.8 us -> 26.6 us  [swap(): return lax.ppermute(value, axes, [(i, i ^ step) for i in range(count)])]
    pallas_call x9 -> x10, Pallas kernels: 16.7 us -> 18.1 us  [kernel_call(): pl.pallas_call(body, in_specs=[SMEM] * len(scalars) + [VMEM] * len(values...]
    dot_general x1 -> x0, matrix products: 1.1 us -> none  [body(): factor_x = lax.dot_general(sketch_t, inverse_x, dims(0, 1), precision=HIGH)]
    pallas_call x1, Pallas kernels: 3.14 us -> 4.13 us  [sketch_parts(): pl.pallas_call(sketch_kernel, in_specs=[SMEM, SMEM, far, far], out_specs=...]
  transfers between devices with their start and end apart: 20 -> 20, of which waited for: 13 -> 13; matrix products, arithmetic and copies ran while one was open for 2% -> 1% of each run, Pallas kernels for 12% -> 14%
where the time goes in v4:
time: 84.8 us; the launch traced here: 84.6 us
  waiting for transfers between devices  33.1 us (39%)
  starting transfers between devices  26.6 us (31%)
  Pallas kernels  22.2 us (26%)
  between operations  2.05 us (2%)
    ppermute x20, waiting for transfers between devices, swap(): return lax.ppermute(value, axes, [(i, i ^ step) for i in range(count)])  33.1 us
    ppermute x20, starting transfers between devices, swap(): return lax.ppermute(value, axes, [(i, i ^ step) for i in range(count)])  26.6 us
    pallas_call x10, Pallas kernels, kernel_call(): pl.pallas_call(body, in_specs=[SMEM] * len(scalars) + [VMEM] * len(values...  18.1 us
    pallas_call x1, Pallas kernels, sketch_parts(): pl.pallas_call(sketch_kernel, in_specs=[SMEM, SMEM, far, far], out_specs=...  4.13 us
  transfers between devices with their start and end apart: 20, of which 13 were waited for; matrix products, arithmetic and copies ran while one was open for 1% of the time, Pallas kernels for 14%

profile of v4, /device:TPU:0, one launch (start us, length us, event | category | flops | bytes accessed | tf_op | source)
XLA Modules:
  0.0 84.6 jit_solution(4936687892461546950)
XLA Ops:
  0.6 4.1 %sketch.1 = (f32[2048,512]{1,0:T(8,128)S(1)}, f32[32,512]{1,0:T(8,128)S(1)}, f32[32,512]{1,0:T(8,128)S(1)}, f32[32,512]{1,0:T(8,128)S(1)}, f32[32,512]{1,0:T(8,128)S(1)}) custom-call(s32[1]{0:T(128)} %bitcast.1.me_ref, s32[1]{0:T(128)} %bitcast.here_ref.me_ref, f32[2048,512]{1,0:T(8,128)} %bitcast.10, f32[512,128]{1,0:T(8,128)} %omega_hbm.1), custom_call_target="tpu_custom_call" | custom-call | tf_op jit(solution)/shard_map/sketch/pallas_call | solution.py:137
  4.8 0.5 collective-permute-start.2
  5.3 2.6 %collective-permute-start.1 = (f32[32,512]{1,0:T(8,128)S(1)}, f32[32,512]{1,0:T(8,128)S(1)}, u32[]{:S(2)}, u32[]{:S(2)}) collective-permute-start(f32[32,512]{1,0:T(8,128)S(1)} %get-tuple-element.16), channel_id=1, source_target_pairs={{0,2},{1,3},{2,0},{3,1},{4,6},{5,7},{6,4},{7,5},{8,10},{9,11},{10,... | collective-permute-start | bytes 196616 | tf_op jit(solution)/shard_map/ppermute | solution.py:17
  7.9 0.1 collective-permute-start
  7.9 0.0 collective-permute-done.2
  7.9 2.6 %collective-permute-done.1 = f32[32,512]{1,0:T(8,128)S(1)} collective-permute-done((f32[32,512]{1,0:T(8,128)S(1)}, f32[32,512]{1,0:T(8,128)S(1)}, u32[]{:S(2)}, u32[]{:S(2)}) %collective-permute-start.1) | collective-permute-done | bytes 65568 | tf_op jit(solution)/shard_map/ppermute | solution.py:17
  10.5 1.4 %collective-permute-done = f32[32,512]{1,0:T(8,128)S(1)} collective-permute-done((f32[32,512]{1,0:T(8,128)S(1)}, f32[32,512]{1,0:T(8,128)S(1)}, u32[]{:S(2)}, u32[]{:S(2)}) %collective-permute-start) | collective-permute-done | bytes 65568 | tf_op jit(solution)/shard_map/ppermute | solution.py:17
  11.9 1.6 %collective-permute-start.5 = (f32[32,512]{1,0:T(8,128)S(1)}, f32[32,512]{1,0:T(8,128)S(1)}, u32[]{:S(2)}, u32[]{:S(2)}) collective-permute-start(f32[32,512]{1,0:T(8,128)S(1)} %add_add_fusion.1), channel_id=1, source_target_pairs={{0,4},{4,0},{8,12},{12,8},{1,5},{5,1},{9,13},{13,9},{2,6},{6,2},{1... | collective-permute-start | bytes 196616 | tf_op jit(solution)/shard_map/ppermute | solution.py:17
  13.6 2.6 %collective-permute-start.4 = (f32[32,512]{1,0:T(8,128)S(1)}, f32[32,512]{1,0:T(8,128)S(1)}, u32[]{:S(2)}, u32[]{:S(2)}) collective-permute-start(f32[32,512]{1,0:T(8,128)S(1)} %add_add_fusion.1), channel_id=1, source_target_pairs={{0,8},{4,12},{8,0},{12,4},{1,9},{5,13},{9,1},{13,5},{2,10},{6,14},... | collective-permute-start | bytes 196616 | tf_op jit(solution)/shard_map/ppermute | solution.py:17
  16.1 0.2 collective-permute-start.3
  16.4 0.0 collective-permute-done.5
  16.4 4.7 %collective-permute-done.4 = f32[32,512]{1,0:T(8,128)S(1)} collective-permute-done((f32[32,512]{1,0:T(8,128)S(1)}, f32[32,512]{1,0:T(8,128)S(1)}, u32[]{:S(2)}, u32[]{:S(2)}) %collective-permute-start.4) | collective-permute-done | bytes 65568 | tf_op jit(solution)/shard_map/ppermute | solution.py:17
  21.1 1.2 %collective-permute-done.3 = f32[32,512]{1,0:T(8,128)S(1)} collective-permute-done((f32[32,512]{1,0:T(8,128)S(1)}, f32[32,512]{1,0:T(8,128)S(1)}, u32[]{:S(2)}, u32[]{:S(2)}) %collective-permute-start.3) | collective-permute-done | bytes 65568 | tf_op jit(solution)/shard_map/ppermute | solution.py:17
  22.3 0.1 collective-permute-start.6
  22.4 1.4 %collective-permute-start.7 = (f32[32,512]{1,0:T(8,128)S(1)}, f32[32,512]{1,0:T(8,128)S(1)}, u32[]{:S(2)}, u32[]{:S(2)}) collective-permute-start(f32[32,512]{1,0:T(8,128)S(1)} %add_add_fusion.refs_0_), channel_id=1, source_target_pairs={{0,2},{1,3},{2,0},{3,1},{4,6},{5,7},{6,4},{7,5},{8,10},{9,11},{10,... | collective-permute-start | bytes 196616 | tf_op jit(solution)/shard_map/ppermute | solution.py:17
  23.8 0.5 collective-permute-start.8
  24.3 0.0 collective-permute-done.6.refs_1_
  24.3 2.8 %collective-permute-done.7.refs_2_ = f32[32,512]{1,0:T(8,128)S(1)} collective-permute-done((f32[32,512]{1,0:T(8,128)S(1)}, f32[32,512]{1,0:T(8,128)S(1)}, u32[]{:S(2)}, u32[]{:S(2)}) %collective-permute-start.7) | collective-permute-done | bytes 65568 | tf_op jit(solution)/shard_map/ppermute | solution.py:17
  27.1 1.0 %collective-permute-done.8.refs_3_ = f32[32,512]{1,0:T(8,128)S(1)} collective-permute-done((f32[32,512]{1,0:T(8,128)S(1)}, f32[32,512]{1,0:T(8,128)S(1)}, u32[]{:S(2)}, u32[]{:S(2)}) %collective-permute-start.8) | collective-permute-done | bytes 65568 | tf_op jit(solution)/shard_map/ppermute | solution.py:17
  28.1 0.5 chunk.5
  28.6 0.8 collective-permute-start.9
  29.4 0.5 chunk.6
  29.9 0.0 copy-start
  29.9 1.8 %collective-permute-start.10 = (f32[64,8,128]{2,1,0:T(8,128)S(1)}, f32[64,8,128]{2,1,0:T(8,128)S(1)}, u32[]{:S(2)}, u32[]{:S(2)}) collective-permute-start(f32[64,8,128]{2,1,0:T(8,128)S(1)} %chunk.6), channel_id=1, source_target_pairs={{0,8},{4,12},{8,0},{12,4},{1,9},{5,13},{9,1},{13,5},{2,10},{6,14},... | collective-permute-start | bytes 786440 | tf_op jit(solution)/shard_map/ppermute | solution.py:17
  31.7 0.5 chunk.7
  32.2 2.0 %collective-permute-start.11 = (f32[64,8,128]{2,1,0:T(8,128)S(1)}, f32[64,8,128]{2,1,0:T(8,128)S(1)}, u32[]{:S(2)}, u32[]{:S(2)}) collective-permute-start(f32[64,8,128]{2,1,0:T(8,128)S(1)} %chunk.7), channel_id=1, source_target_pairs={{0,12},{4,8},{8,4},{12,0},{1,13},{5,9},{9,5},{13,1},{2,14},{6,10},... | collective-permute-start | bytes 786440 | tf_op jit(solution)/shard_map/ppermute | solution.py:17
  34.8 0.5 chunk.4.refs_0_
  35.3 9.1 %factor_x.1.inverse_ref = f32[128,128]{1,0:T(8,128)S(1)} custom-call(s32[1]{0:T(128)S(6)} %copy.9.rank_ref, s32[1]{0:T(128)} %bitcast.1.me_ref, f32[32,512]{1,0:T(8,128)S(1)} %add_add_fusion.refs_0_, f32[32,512]{1,0:T(8,128)S(1)} %collective-permute-done.6.refs_1_, f32[32,512]{1,0:T(8,128)S(1)} %collective-permute-done.7.refs_2_, ...), custom_call_target="tpu_custom_call" | custom-call | tf_op jit(solution)/shard_map/factor_x/pallas_call | solution.py:87
  44.5 0.0 collective-permute-done.9.refs_1_
  44.5 6.9 %collective-permute-done.10.refs_2_ = f32[64,8,128]{2,1,0:T(8,128)S(1)} collective-permute-done((f32[64,8,128]{2,1,0:T(8,128)S(1)}, f32[64,8,128]{2,1,0:T(8,128)S(1)}, u32[]{:S(2)}, u32[]{:S(2)}) %collective-permute-start.10) | collective-permute-done | bytes 262176 | tf_op jit(solution)/shard_map/ppermute | solution.py:17
  51.3 0.0 collective-permute-done.11.refs_3_
  51.3 0.0 copy-done
  51.3 2.0 %gram.1 = (f32[64,4096]{1,0:T(8,128)S(1)}, f32[64,32]{1,0:T(8,128)S(1)}) custom-call(s32[1]{0:T(128)} %bitcast.here_ref.me_ref, f32[128,128]{1,0:T(8,128)S(1)} %factor_x.1.inverse_ref, f32[32,64]{1,0:T(8,128)S(1)} %bitcast.9, f32[64,8,128]{2,1,0:T(8,128)S(1)} %chunk.4.refs_0_, f32[64,8,128]{2,1,0:T(8,128)S(1)} %collective-permute-done.9.refs_1_, ...), custom_call_target="tpu_custom_call" | custom-call | tf_op jit(solution)/shard_map/gram/pallas_call | solution.py:87
  53.4 0.0 collective-permute-start.12
  53.4 1.2 %collective-permute-done.12 = f32[64,32]{1,0:T(8,128)S(1)} collective-permute-done((f32[64,32]{1,0:T(8,128)S(1)}, f32[64,32]{1,0:T(8,128)S(1)}, u32[]{:S(2)}, u32[]{:S(2)}) %collective-permute-start.12) | collective-permute-done | bytes 8224 | tf_op jit(solution)/shard_map/ppermute | solution.py:17
  54.6 1.4 %collective-permute-start.13 = (f32[64,32]{1,0:T(8,128)S(1)}, f32[64,32]{1,0:T(8,128)S(1)}, u32[]{:S(2)}, u32[]{:S(2)}) collective-permute-start(f32[64,32]{1,0:T(8,128)S(1)} %add.34), channel_id=1, source_target_pairs={{0,2},{2,0},{1,3},{3,1},{4,6},{6,4},{5,7},{7,5},{8,10},{10,8},{9,1... | collective-permute-start | bytes 24584 | tf_op jit(solution)/shard_map/ppermute | solution.py:17
  56.0 2.5 %collective-permute-done.13 = f32[64,32]{1,0:T(8,128)S(1)} collective-permute-done((f32[64,32]{1,0:T(8,128)S(1)}, f32[64,32]{1,0:T(8,128)S(1)}, u32[]{:S(2)}, u32[]{:S(2)}) %collective-permute-start.13) | collective-permute-done | bytes 8224 | tf_op jit(solution)/shard_map/ppermute | solution.py:17
  58.5 2.4 %collective-permute-start.14 = (f32[64,32]{1,0:T(8,128)S(1)}, f32[64,32]{1,0:T(8,128)S(1)}, u32[]{:S(2)}, u32[]{:S(2)}) collective-permute-start(f32[64,32]{1,0:T(8,128)S(1)} %add.35.refs_0_), channel_id=1, source_target_pairs={{0,12},{4,8},{8,4},{12,0},{1,13},{5,9},{9,5},{13,1},{2,14},{6,10},... | collective-permute-start | bytes 24584 | tf_op jit(solution)/shard_map/ppermute | solution.py:17
  60.9 4.2 %collective-permute-start.15 = (f32[64,32]{1,0:T(8,128)S(1)}, f32[64,32]{1,0:T(8,128)S(1)}, u32[]{:S(2)}, u32[]{:S(2)}) collective-permute-start(f32[64,32]{1,0:T(8,128)S(1)} %add.35.refs_0_), channel_id=1, source_target_pairs={{0,8},{4,12},{8,0},{12,4},{1,9},{5,13},{9,1},{13,5},{2,10},{6,14},... | collective-permute-start | bytes 24584 | tf_op jit(solution)/shard_map/ppermute | solution.py:17
  65.1 0.0 collective-permute-start.16
  65.8 0.0 collective-permute-done.14.refs_1_
  65.8 1.9 %collective-permute-done.15.refs_2_ = f32[64,32]{1,0:T(8,128)S(1)} collective-permute-done((f32[64,32]{1,0:T(8,128)S(1)}, f32[64,32]{1,0:T(8,128)S(1)}, u32[]{:S(2)}, u32[]{:S(2)}) %collective-permute-start.15) | collective-permute-done | bytes 8224 | tf_op jit(solution)/shard_map/ppermute | solution.py:17
  67.7 1.3 %collective-permute-done.16.refs_3_ = f32[64,32]{1,0:T(8,128)S(1)} collective-permute-done((f32[64,32]{1,0:T(8,128)S(1)}, f32[64,32]{1,0:T(8,128)S(1)}, u32[]{:S(2)}, u32[]{:S(2)}) %collective-permute-start.16) | collective-permute-done | bytes 8224 | tf_op jit(solution)/shard_map/ppermute | solution.py:17
  69.0 2.4 %factor_y.1.factor_ref = f32[64,32]{1,0:T(8,128)S(1)} custom-call(s32[1]{0:T(128)S(6)} %copy.10.rank_ref, f32[64,32]{1,0:T(8,128)S(1)} %add.35.refs_0_, f32[64,32]{1,0:T(8,128)S(1)} %collective-permute-done.14.refs_1_, f32[64,32]{1,0:T(8,128)S(1)} %collective-permute-done.15.refs_2_, f32[64,32]{1,0:T(8,128)S(1)} %collective-permute-done.16.refs_3_), custom_call_target="tpu_custom_call" | custom-call | tf_op jit(solution)/shard_map/factor_y/pallas_call | solution.py:87
  71.4 0.5 mix.1
  72.0 1.0 %collective-permute-start.17 = (f32[4,8,8,128]{3,2,1,0:T(8,128)S(1)}, f32[4,8,8,128]{3,2,1,0:T(8,128)S(1)}, u32[]{:S(2)}, u32[]{:S(2)}) collective-permute-start(f32[4,8,8,128]{3,2,1,0:T(8,128)S(1)} %get-tuple-element.22), channel_id=1, source_target_pairs={{0,4},{4,0},{8,12},{12,8},{1,5},{5,1},{9,13},{13,9},{2,6},{6,2},{1... | collective-permute-start | bytes 393224 | tf_op jit(solution)/shard_map/ppermute | solution.py:17
  72.9 2.0 %collective-permute-start.18 = (f32[4,8,8,128]{3,2,1,0:T(8,128)S(1)}, f32[4,8,8,128]{3,2,1,0:T(8,128)S(1)}, u32[]{:S(2)}, u32[]{:S(2)}) collective-permute-start(f32[4,8,8,128]{3,2,1,0:T(8,128)S(1)} %get-tuple-element.23), channel_id=1, source_target_pairs={{0,8},{4,12},{8,0},{12,4},{1,9},{5,13},{9,1},{13,5},{2,10},{6,14},... | collective-permute-start | bytes 393224 | tf_op jit(solution)/shard_map/ppermute | solution.py:17
  75.0 1.4 %collective-permute-start.19 = (f32[4,8,8,128]{3,2,1,0:T(8,128)S(1)}, f32[4,8,8,128]{3,2,1,0:T(8,128)S(1)}, u32[]{:S(2)}, u32[]{:S(2)}) collective-permute-start(f32[4,8,8,128]{3,2,1,0:T(8,128)S(1)} %get-tuple-element.24), channel_id=1, source_target_pairs={{0,12},{4,8},{8,4},{12,0},{1,13},{5,9},{9,5},{13,1},{2,14},{6,10},... | collective-permute-start | bytes 393224 | tf_op jit(solution)/shard_map/ppermute | solution.py:17
  76.4 1.1 %apply.1 = f32[512,128]{1,0:T(8,128)} custom-call(s32[1]{0:T(128)} %bitcast.1.me_ref, f32[128,128]{1,0:T(8,128)S(1)} %factor_x.1.inverse_ref, f32[32,512]{1,0:T(8,128)S(1)} %add_add_fusion.refs_0_, f32[32,512]{1,0:T(8,128)S(1)} %collective-permute-done.6.refs_1_, f32[32,512]{1,0:T(8,128)S(1)} %collective-permute-done.7.refs_2_, ...), custom_call_target="tpu_custom_call" | custom-call | tf_op jit(solution)/shard_map/apply/pallas_call | solution.py:87
  77.6 0.7 copy.8
  78.2 1.4 %collective-permute-done.17.refs_1_ = f32[4,8,8,128]{3,2,1,0:T(8,128)S(1)} collective-permute-done((f32[4,8,8,128]{3,2,1,0:T(8,128)S(1)}, f32[4,8,8,128]{3,2,1,0:T(8,128)S(1)}, u32[]{:S(2)}, u32[]{:S(2)}) %collective-permute-start.17) | collective-permute-done | bytes 131104 | tf_op jit(solution)/shard_map/ppermute | solution.py:17
  79.6 4.1 %collective-permute-done.18.refs_2_ = f32[4,8,8,128]{3,2,1,0:T(8,128)S(1)} collective-permute-done((f32[4,8,8,128]{3,2,1,0:T(8,128)S(1)}, f32[4,8,8,128]{3,2,1,0:T(8,128)S(1)}, u32[]{:S(2)}, u32[]{:S(2)}) %collective-permute-start.18) | collective-permute-done | bytes 131104 | tf_op jit(solution)/shard_map/ppermute | solution.py:17
  83.7 0.0 collective-permute-done.19.refs_3_
  83.7 0.9 %place.1 = f32[4,8,32,128]{3,2,1,0:T(8,128)} custom-call(s32[1]{0:T(128)} %bitcast.here_ref.me_ref, f32[4,8,8,128]{3,2,1,0:T(8,128)S(1)} %get-tuple-element.21.refs_0_, f32[4,8,8,128]{3,2,1,0:T(8,128)S(1)} %collective-permute-done.17.refs_1_, f32[4,8,8,128]{3,2,1,0:T(8,128)S(1)} %collective-permute-done.18.refs_2_, ...), custom_call_target="tpu_custom_call" | custom-call | tf_op jit(solution)/shard_map/place/pallas_call | solution.py:87
  (4 shorter events, 0.1 us)
Async XLA Ops:
  4.8 3.2 %collective-permute-start.2 = (f32[32,512]{1,0:T(8,128)S(1)}, f32[32,512]{1,0:T(8,128)S(1)}, u32[]{:S(2)}, u32[]{:S(2)}) collective-permute-start(f32[32,512]{1,0:T(8,128)S(1)} %get-tuple-element.17), channel_id=1, source_target_pairs={{0,1},{1,0},{2,3},{3,2},{4,5},{5,4},{6,7},{7,6},{8,9},{9,8},{10,11... | collective-permute-start | bytes 196616 | tf_op jit(solution)/shard_map/ppermute | solution.py:17
  5.3 5.3 %collective-permute-start.1 = (f32[32,512]{1,0:T(8,128)S(1)}, f32[32,512]{1,0:T(8,128)S(1)}, u32[]{:S(2)}, u32[]{:S(2)}) collective-permute-start(f32[32,512]{1,0:T(8,128)S(1)} %get-tuple-element.16), channel_id=1, source_target_pairs={{0,2},{1,3},{2,0},{3,1},{4,6},{5,7},{6,4},{7,5},{8,10},{9,11},{10,... | collective-permute-start | bytes 196616 | tf_op jit(solution)/shard_map/ppermute | solution.py:17
  7.9 4.0 %collective-permute-start = (f32[32,512]{1,0:T(8,128)S(1)}, f32[32,512]{1,0:T(8,128)S(1)}, u32[]{:S(2)}, u32[]{:S(2)}) collective-permute-start(f32[32,512]{1,0:T(8,128)S(1)} %get-tuple-element.15), channel_id=1, source_target_pairs={{0,3},{1,2},{2,1},{3,0},{4,7},{5,6},{6,5},{7,4},{8,11},{9,10},{10,... | collective-permute-start | bytes 196616 | tf_op jit(solution)/shard_map/ppermute | solution.py:17
  11.9 4.5 %collective-permute-start.5 = (f32[32,512]{1,0:T(8,128)S(1)}, f32[32,512]{1,0:T(8,128)S(1)}, u32[]{:S(2)}, u32[]{:S(2)}) collective-permute-start(f32[32,512]{1,0:T(8,128)S(1)} %add_add_fusion.1), channel_id=1, source_target_pairs={{0,4},{4,0},{8,12},{12,8},{1,5},{5,1},{9,13},{13,9},{2,6},{6,2},{1... | collective-permute-start | bytes 196616 | tf_op jit(solution)/shard_map/ppermute | solution.py:17
  13.6 7.6 %collective-permute-start.4 = (f32[32,512]{1,0:T(8,128)S(1)}, f32[32,512]{1,0:T(8,128)S(1)}, u32[]{:S(2)}, u32[]{:S(2)}) collective-permute-start(f32[32,512]{1,0:T(8,128)S(1)} %add_add_fusion.1), channel_id=1, source_target_pairs={{0,8},{4,12},{8,0},{12,4},{1,9},{5,13},{9,1},{13,5},{2,10},{6,14},... | collective-permute-start | bytes 196616 | tf_op jit(solution)/shard_map/ppermute | solution.py:17
  16.1 6.2 %collective-permute-start.3 = (f32[32,512]{1,0:T(8,128)S(1)}, f32[32,512]{1,0:T(8,128)S(1)}, u32[]{:S(2)}, u32[]{:S(2)}) collective-permute-start(f32[32,512]{1,0:T(8,128)S(1)} %add_add_fusion.1), channel_id=1, source_target_pairs={{0,12},{4,8},{8,4},{12,0},{1,13},{5,9},{9,5},{13,1},{2,14},{6,10},... | collective-permute-start | bytes 196616 | tf_op jit(solution)/shard_map/ppermute | solution.py:17
  22.3 1.9 %collective-permute-start.6 = (f32[32,512]{1,0:T(8,128)S(1)}, f32[32,512]{1,0:T(8,128)S(1)}, u32[]{:S(2)}, u32[]{:S(2)}) collective-permute-start(f32[32,512]{1,0:T(8,128)S(1)} %add_add_fusion.refs_0_), channel_id=1, source_target_pairs={{0,1},{1,0},{2,3},{3,2},{4,5},{5,4},{6,7},{7,6},{8,9},{9,8},{10,11... | collective-permute-start | bytes 196616 | tf_op jit(solution)/shard_map/ppermute | solution.py:17
  22.4 4.6 %collective-permute-start.7 = (f32[32,512]{1,0:T(8,128)S(1)}, f32[32,512]{1,0:T(8,128)S(1)}, u32[]{:S(2)}, u32[]{:S(2)}) collective-permute-start(f32[32,512]{1,0:T(8,128)S(1)} %add_add_fusion.refs_0_), channel_id=1, source_target_pairs={{0,2},{1,3},{2,0},{3,1},{4,6},{5,7},{6,4},{7,5},{8,10},{9,11},{10,... | collective-permute-start | bytes 196616 | tf_op jit(solution)/shard_map/ppermute | solution.py:17
  23.8 4.3 %collective-permute-start.8 = (f32[32,512]{1,0:T(8,128)S(1)}, f32[32,512]{1,0:T(8,128)S(1)}, u32[]{:S(2)}, u32[]{:S(2)}) collective-permute-start(f32[32,512]{1,0:T(8,128)S(1)} %add_add_fusion.refs_0_), channel_id=1, source_target_pairs={{0,3},{1,2},{2,1},{3,0},{4,7},{5,6},{6,5},{7,4},{8,11},{9,10},{10,... | collective-permute-start | bytes 196616 | tf_op jit(solution)/shard_map/ppermute | solution.py:17
  28.6 15.9 %collective-permute-start.9 = (f32[64,8,128]{2,1,0:T(8,128)S(1)}, f32[64,8,128]{2,1,0:T(8,128)S(1)}, u32[]{:S(2)}, u32[]{:S(2)}) collective-permute-start(f32[64,8,128]{2,1,0:T(8,128)S(1)} %chunk.5), channel_id=1, source_target_pairs={{0,4},{4,0},{8,12},{12,8},{1,5},{5,1},{9,13},{13,9},{2,6},{6,2},{1... | collective-permute-start | bytes 786440 | tf_op jit(solution)/shard_map/ppermute | solution.py:17
  29.9 21.4 %copy-start = (f32[64,32]{0,1:T(8,128)S(1)}, f32[64,32]{0,1:T(8,128)}, u32[]{:S(2)}) copy-start(f32[64,32]{0,1:T(8,128)} %param.7) | copy-start | bytes 24580
  29.9 21.4 %collective-permute-start.10 = (f32[64,8,128]{2,1,0:T(8,128)S(1)}, f32[64,8,128]{2,1,0:T(8,128)S(1)}, u32[]{:S(2)}, u32[]{:S(2)}) collective-permute-start(f32[64,8,128]{2,1,0:T(8,128)S(1)} %chunk.6), channel_id=1, source_target_pairs={{0,8},{4,12},{8,0},{12,4},{1,9},{5,13},{9,1},{13,5},{2,10},{6,14},... | collective-permute-start | bytes 786440 | tf_op jit(solution)/shard_map/ppermute | solution.py:17
  32.2 19.1 %collective-permute-start.11 = (f32[64,8,128]{2,1,0:T(8,128)S(1)}, f32[64,8,128]{2,1,0:T(8,128)S(1)}, u32[]{:S(2)}, u32[]{:S(2)}) collective-permute-start(f32[64,8,128]{2,1,0:T(8,128)S(1)} %chunk.7), channel_id=1, source_target_pairs={{0,12},{4,8},{8,4},{12,0},{1,13},{5,9},{9,5},{13,1},{2,14},{6,10},... | collective-permute-start | bytes 786440 | tf_op jit(solution)/shard_map/ppermute | solution.py:17
  53.4 1.2 %collective-permute-start.12 = (f32[64,32]{1,0:T(8,128)S(1)}, f32[64,32]{1,0:T(8,128)S(1)}, u32[]{:S(2)}, u32[]{:S(2)}) collective-permute-start(f32[64,32]{1,0:T(8,128)S(1)} %get-tuple-element.19), channel_id=1, source_target_pairs={{0,1},{1,0},{2,3},{3,2},{4,5},{5,4},{6,7},{7,6},{8,9},{9,8},{10,11... | collective-permute-start | bytes 24584 | tf_op jit(solution)/shard_map/ppermute | solution.py:17
  54.6 3.9 %collective-permute-start.13 = (f32[64,32]{1,0:T(8,128)S(1)}, f32[64,32]{1,0:T(8,128)S(1)}, u32[]{:S(2)}, u32[]{:S(2)}) collective-permute-start(f32[64,32]{1,0:T(8,128)S(1)} %add.34), channel_id=1, source_target_pairs={{0,2},{2,0},{1,3},{3,1},{4,6},{6,4},{5,7},{7,5},{8,10},{10,8},{9,1... | collective-permute-start | bytes 24584 | tf_op jit(solution)/shard_map/ppermute | solution.py:17
  58.5 7.3 %collective-permute-start.14 = (f32[64,32]{1,0:T(8,128)S(1)}, f32[64,32]{1,0:T(8,128)S(1)}, u32[]{:S(2)}, u32[]{:S(2)}) collective-permute-start(f32[64,32]{1,0:T(8,128)S(1)} %add.35.refs_0_), channel_id=1, source_target_pairs={{0,12},{4,8},{8,4},{12,0},{1,13},{5,9},{9,5},{13,1},{2,14},{6,10},... | collective-permute-start | bytes 24584 | tf_op jit(solution)/shard_map/ppermute | solution.py:17
  60.9 6.8 %collective-permute-start.15 = (f32[64,32]{1,0:T(8,128)S(1)}, f32[64,32]{1,0:T(8,128)S(1)}, u32[]{:S(2)}, u32[]{:S(2)}) collective-permute-start(f32[64,32]{1,0:T(8,128)S(1)} %add.35.refs_0_), channel_id=1, source_target_pairs={{0,8},{4,12},{8,0},{12,4},{1,9},{5,13},{9,1},{13,5},{2,10},{6,14},... | collective-permute-start | bytes 24584 | tf_op jit(solution)/shard_map/ppermute | solution.py:17
  65.1 3.9 %collective-permute-start.16 = (f32[64,32]{1,0:T(8,128)S(1)}, f32[64,32]{1,0:T(8,128)S(1)}, u32[]{:S(2)}, u32[]{:S(2)}) collective-permute-start(f32[64,32]{1,0:T(8,128)S(1)} %add.35.refs_0_), channel_id=1, source_target_pairs={{0,4},{4,0},{8,12},{12,8},{1,5},{5,1},{9,13},{13,9},{2,6},{6,2},{1... | collective-permute-start | bytes 24584 | tf_op jit(solution)/shard_map/ppermute | solution.py:17
  72.0 7.7 %collective-permute-start.17 = (f32[4,8,8,128]{3,2,1,0:T(8,128)S(1)}, f32[4,8,8,128]{3,2,1,0:T(8,128)S(1)}, u32[]{:S(2)}, u32[]{:S(2)}) collective-permute-start(f32[4,8,8,128]{3,2,1,0:T(8,128)S(1)} %get-tuple-element.22), channel_id=1, source_target_pairs={{0,4},{4,0},{8,12},{12,8},{1,5},{5,1},{9,13},{13,9},{2,6},{6,2},{1... | collective-permute-start | bytes 393224 | tf_op jit(solution)/shard_map/ppermute | solution.py:17
  72.9 10.8 %collective-permute-start.18 = (f32[4,8,8,128]{3,2,1,0:T(8,128)S(1)}, f32[4,8,8,128]{3,2,1,0:T(8,128)S(1)}, u32[]{:S(2)}, u32[]{:S(2)}) collective-permute-start(f32[4,8,8,128]{3,2,1,0:T(8,128)S(1)} %get-tuple-element.23), channel_id=1, source_target_pairs={{0,8},{4,12},{8,0},{12,4},{1,9},{5,13},{9,1},{13,5},{2,10},{6,14},... | collective-permute-start | bytes 393224 | tf_op jit(solution)/shard_map/ppermute | solution.py:17
  75.0 8.8 %collective-permute-start.19 = (f32[4,8,8,128]{3,2,1,0:T(8,128)S(1)}, f32[4,8,8,128]{3,2,1,0:T(8,128)S(1)}, u32[]{:S(2)}, u32[]{:S(2)}) collective-permute-start(f32[4,8,8,128]{3,2,1,0:T(8,128)S(1)} %get-tuple-element.24), channel_id=1, source_target_pairs={{0,12},{4,8},{8,4},{12,0},{1,13},{5,9},{9,5},{13,1},{2,14},{6,10},... | collective-permute-start | bytes 393224 | tf_op jit(solution)/shard_map/ppermute | solution.py:17

commit v5 on v4

--- a/solution.py
+++ b/solution.py
@@ -160,7 +160,7 @@
 
 
 def chunk_kernel(scale, step, me_ref, here_ref, field_ref, *refs):
-    *piece_refs, out_ref, whole = refs
+    *piece_refs, _, out_ref, whole = refs
     sketch = gather_sketch(scale, me_ref, piece_refs, whole)
     width, cells = sketch.shape
     rows, share, _ = out_ref.shape
@@ -172,39 +172,57 @@
     out_ref[...] = raw.reshape(rows, share, width)
 
 
-def field_chunk(scale, step, places, field, pieces, share):
+def field_chunk(scale, step, places, field, pieces, share, after):
     width, cells = pieces[0].shape[0] * len(pieces), field.shape[2]
     scratch = [pltpu.VMEM((width, cells), jnp.float32)]
     kernel = functools.partial(chunk_kernel, scale, step)
-    return kernel_call(kernel, "chunk", (field.shape[0], share, width), places, [field] + pieces, scratch)
-
-
-def gram_kernel(planes, me_ref, inverse_ref, omega_ref, *refs):
-    *chunk_refs, spread_ref, part_ref = refs
-    rows, share, width = chunk_refs[0].shape
-    rows_y = rows // planes
+    shape = (field.shape[0], share, width)
+    return kernel_call(kernel, "chunk", shape, places, [field] + pieces + [after], scratch)
+
+
+def lift_kernel(planes, inverse_ref, chunk_ref, *refs):
+    out_ref = refs[-1]
+    rows, share, width = chunk_ref.shape
     inv_high, inv_low = halves(inverse_ref[...])
-    inv_both = jnp.concatenate([inv_high, inv_low], axis=0)
-    for k, ref in enumerate(chunk_refs):
-        high, low = halves(ref[...].reshape(rows * share, width))
-        both = mxu(high, inv_both, dims(1, 1))
-        value = both[:, :width] + (both[:, width:] + mxu(low, inv_high, dims(1, 1)))
-        value = jnp.swapaxes(value.reshape(planes, rows_y, share, width), 1, 2)
-        start = pl.multiple_of((me_ref[0] ^ k) * rows_y, rows_y)
-        slab = jnp.concatenate([value[v, z] for v in range(planes) for z in range(share)], axis=1)
-        spread_ref[pl.ds(start, rows_y), :] = slab
-    high, low = halves(spread_ref[...])
-    gram = mxu(high, high, dims(1, 1)) + (mxu(high, low, dims(1, 1)) + mxu(low, high, dims(1, 1)))
-    part_ref[...] = exact(gram, omega_ref[...], dims(1, 1))
-
-
-def mix_kernel(me_ref, factor_ref, spread_ref, *refs):
-    *out_refs, mixed = refs
+    high, low = halves(chunk_ref[...].reshape(rows * share, width))
+    both = mxu(high, jnp.concatenate([inv_high, inv_low], axis=0), dims(1, 1))
+    value = both[:, :width] + (both[:, width:] + mxu(low, inv_high, dims(1, 1)))
+    value = jnp.swapaxes(value.reshape(planes, rows // planes, share, width), 1, 2)
+    for v in range(planes):
+        for z in range(share):
+            at = (v * share + z) * width
+            out_ref[:, at:at + width] = value[v, z]
+
+
+def lift(planes, inverse, chunk, after):
+    rows, share, width = chunk.shape
+    shape = (rows // planes, planes * share * width)
+    return kernel_call(functools.partial(lift_kernel, planes), "lift", shape, [], [inverse, chunk] + after)
+
+
+def gram_kernel(me_ref, omega_ref, *refs):
+    *slab_refs, part_ref, rows_ref, cols_ref = refs
+    share = slab_refs[0].shape[0]
+    high, low = halves(jnp.concatenate([ref[...] for ref in slab_refs], axis=0))
+    rows_ref[...] = mxu(high, high, dims(1, 1)) + (mxu(high, low, dims(1, 1)) + mxu(low, high, dims(1, 1)))
+    for ref, out in ((rows_ref, cols_ref), (cols_ref, rows_ref)):
+        value = ref[...].T
+        for k in range(len(slab_refs)):
+            start = pl.multiple_of((me_ref[0] ^ k) * share, share)
+            out[pl.ds(start, share), :] = value[k * share:(k + 1) * share, :]
+    part_ref[...] = exact(rows_ref[...], omega_ref[...], dims(1, 1))
+
+
+def mix_kernel(which, me_ref, factor_ref, *refs):
+    count = factor_ref.shape[0] // refs[0].shape[0]
+    slab_refs, out_refs, mixed = refs[:count], refs[-1 - len(which):-1], refs[-1]
     planes, share_k, share_z, width = out_refs[0].shape
-    fac_high, fac_low = halves(factor_ref[...])
-    high, low = halves(spread_ref[...])
+    rows_y = slab_refs[0].shape[0]
+    own = [factor_ref[pl.ds(pl.multiple_of((me_ref[0] ^ k) * rows_y, rows_y), rows_y), :] for k in range(count)]
+    fac_high, fac_low = halves(jnp.concatenate(own, axis=0))
+    high, low = halves(jnp.concatenate([ref[...] for ref in slab_refs], axis=0))
     mixed[...] = mxu(fac_high, high, dims(0, 0)) + (mxu(fac_high, low, dims(0, 0)) + mxu(fac_low, high, dims(0, 0)))
-    for k, ref in enumerate(out_refs):
+    for k, ref in zip(which, out_refs):
         start = pl.multiple_of((me_ref[0] ^ k) * share_k, share_k)
         block = mixed[pl.ds(start, share_k), :]
         for v in range(planes):
@@ -213,12 +231,30 @@
             ref[v] = jnp.swapaxes(rows, 0, 1)
 
 
-def place_kernel(me_ref, *refs):
-    *piece_refs, out_ref = refs
+def place_kernel(order, me_ref, *refs):
+    *piece_refs, out_hbm, placed = refs
     share = piece_refs[0].shape[2]
-    for k, ref in enumerate(piece_refs):
+    copies = []
+    for k, ref in zip(order, piece_refs):
         start = pl.multiple_of((me_ref[0] ^ k) * share, share)
-        out_ref[:, :, pl.ds(start, share), :] = ref[...]
+        copy = pltpu.make_async_copy(ref, out_hbm.at[:, :, pl.ds(start, share), :], placed.at[k])
+        copy.start()
+        copies.append(copy)
+    for copy in copies:
+        copy.wait()
+
+
+def place(me, pieces, shape):
+    order = steps(len(pieces)) + [0]
+    return pl.pallas_call(
+        functools.partial(place_kernel, order),
+        in_specs=[SMEM] + [VMEM] * len(pieces),
+        out_specs=pl.BlockSpec(memory_space=pltpu.HBM),
+        out_shape=jax.ShapeDtypeStruct(shape, jnp.float32),
+        scratch_shapes=[pltpu.SemaphoreType.DMA((len(pieces),))],
+        compiler_params=pltpu.CompilerParams(vmem_limit_bytes=16 << 20),
+        name="place",
+    )(me, *[held(pieces[k]) for k in order])
 
 
 def eliminate(gram, count, rank, out_ref):
@@ -323,30 +359,32 @@
     field_z = field_v.reshape(planes * rows_y, rows_z, cells_x)
     tiled = share_z % 8 == 0 and share_k % 8 == 0
     if tiled:
-        cut = lambda s: field_chunk(scale, s, [quarter, here], field_z, pieces, share_z)
+        cut = lambda s, after: field_chunk(scale, s, [quarter, here], field_z, pieces, share_z, after)
     else:
         sketch_t = jnp.take(jnp.stack(pieces), quarter ^ jnp.arange(n_quarter), axis=0)
         sketch_t = sketch_t.reshape(ranks_x, cells_x) * scale
         raw = lax.dot_general(flat, sketch_t, dims(1, 1), precision=HIGH)
         raw = raw.reshape(planes * rows_y, rows_z, ranks_x)
-        cut = lambda s: lax.dynamic_slice_in_dim(raw, (gy ^ s) * share_z, share_z, 1)
+        cut = lambda s, after: lax.dynamic_slice_in_dim(raw, (gy ^ s) * share_z, share_z, 1)
     chunks = [None] * n_gy
+    after = pieces[0]
     for s in steps(n_gy):
-        chunks[s] = swap(cut(s), "gy", s)
-    chunks[0] = cut(0)
+        after = cut(s, after)
+        chunks[s] = swap(after, "gy", s)
+    chunks[0] = cut(0, after)
 
     inverse_x = inverse_factor_x(scale, rank_x, quarter, pieces)
     factor_x = make_factor_x(scale, quarter, inverse_x, pieces)
 
     if tiled:
-        samples = planes * share_z * ranks_x
-        spread, part_y = kernel_call(
-            functools.partial(gram_kernel, planes),
-            "gram",
-            [(all_rows_y, samples), (all_rows_y, ranks_y)],
-            [here],
-            [inverse_x, omega_y.T] + chunks,
-        )
+        slabs = [None] * n_gy
+        after = []
+        for s in [0] + steps(n_gy):
+            slabs[s] = lift(planes, inverse_x, chunks[s], after)
+            after = [slabs[s]]
+        scratch = [pltpu.VMEM((all_rows_y, all_rows_y), jnp.float32)] * 2
+        shape = (all_rows_y, ranks_y)
+        part_y = kernel_call(gram_kernel, "gram", shape, [here], [omega_y.T] + slabs, scratch)
     else:
         spread = jnp.stack(chunks).reshape(-1, ranks_x)
         spread = lax.dot_general(spread, inverse_x, dims(1, 1), precision=HIGH)
@@ -366,13 +404,15 @@
 
     if tiled:
         shape = (planes, share_k, share_z, ranks_x)
-        scratch = [pltpu.VMEM((ranks_y, spread.shape[1]), jnp.float32)]
-        mixed = kernel_call(mix_kernel, "mix", [shape] * n_gy, [here], [factor_y, spread], scratch)
-        pieces = [mixed[0]] + [None] * (n_gy - 1)
-        for s in steps(n_gy):
-            pieces[s] = swap(mixed[s], "gy", s)
-        shape = (planes, share_k, rows_z, ranks_x)
-        core = kernel_call(place_kernel, "place", shape, [here], pieces, whole_out=True)
+        scratch = [pltpu.VMEM((ranks_y, planes * share_z * ranks_x), jnp.float32)]
+
+        which = steps(n_gy) + [0]
+        kernel = functools.partial(mix_kernel, which)
+        blocks = kernel_call(kernel, "mix", [shape] * n_gy, [here], [factor_y] + slabs, scratch)
+        pieces = [None] * n_gy
+        for s, block in zip(which, blocks):
+            pieces[s] = swap(block, "gy", s) if s else block
+        core = place(here, pieces, (planes, share_k, rows_z, ranks_x))
         return (core, factor_x, factor_y)
     weights = by_step(factor_y.reshape(n_gy, rows_y, ranks_y), gy, n_gy)
     weights = weights.reshape(n_gy, rows_y, n_gy, share_k)

time: 84.8 us -> 85.1 us (level)
  waiting for transfers between devices: 33.1 us -> 36.1 us
  starting transfers between devices: 26.6 us -> 23.8 us
    ppermute x20, waiting for transfers between devices: 33.1 us -> 36.1 us  [swap(): return lax.ppermute(value, axes, [(i, i ^ step) for i in range(count)])]
    ppermute x20, starting transfers between devices: 26.6 us -> 23.8 us  [swap(): return lax.ppermute(value, axes, [(i, i ^ step) for i in range(count)])]
    pallas_call x10 -> x13, Pallas kernels: 18.1 us -> 17.3 us  [kernel_call(): pl.pallas_call(body, in_specs=[SMEM] * len(scalars) + [VMEM] * len(values...]
  transfers between devices with their start and end apart: 20 -> 20, of which waited for: 13 -> 12; matrix products, arithmetic and copies ran while one was open for 1% -> 1% of each run, Pallas kernels for 14% -> 15%
where the time goes in v5:
time: 85.1 us; the launch traced here: 84.9 us
  waiting for transfers between devices  36.1 us (42%)
  starting transfers between devices  23.8 us (28%)
  Pallas kernels  22.2 us (26%)
  between operations  2.12 us (2%)
    ppermute x20, waiting for transfers between devices, swap(): return lax.ppermute(value, axes, [(i, i ^ step) for i in range(count)])  36.1 us
    ppermute x20, starting transfers between devices, swap(): return lax.ppermute(value, axes, [(i, i ^ step) for i in range(count)])  23.8 us
    pallas_call x13, Pallas kernels, kernel_call(): pl.pallas_call(body, in_specs=[SMEM] * len(scalars) + [VMEM] * len(values...  17.3 us
    pallas_call x1, Pallas kernels, sketch_parts(): pl.pallas_call(sketch_kernel, in_specs=[SMEM, SMEM, far, far], out_specs=...  4.13 us
  transfers between devices with their start and end apart: 20, of which 12 were waited for; matrix products, arithmetic and copies ran while one was open for 1% of the time, Pallas kernels for 15%

profile of v5, /device:TPU:0, one launch (start us, length us, event | category | flops | bytes accessed | tf_op | source)
XLA Modules:
  0.0 84.9 jit_solution(4365810364172213503)
XLA Ops:
  0.6 4.1 %sketch.1 = (f32[2048,512]{1,0:T(8,128)S(1)}, f32[32,512]{1,0:T(8,128)S(1)}, f32[32,512]{1,0:T(8,128)S(1)}, f32[32,512]{1,0:T(8,128)S(1)}, f32[32,512]{1,0:T(8,128)S(1)}) custom-call(s32[1]{0:T(128)} %bitcast.2.me_ref, s32[1]{0:T(128)} %bitcast.here_ref.me_ref, f32[2048,512]{1,0:T(8,128)} %bitcast.10, f32[512,128]{1,0:T(8,128)} %omega_hbm.1), custom_call_target="tpu_custom_call" | custom-call | tf_op jit(solution)/shard_map/sketch/pallas_call | solution.py:137
  4.8 2.4 %collective-permute-start = (f32[32,512]{1,0:T(8,128)S(1)}, f32[32,512]{1,0:T(8,128)S(1)}, u32[]{:S(2)}, u32[]{:S(2)}) collective-permute-start(f32[32,512]{1,0:T(8,128)S(1)} %get-tuple-element.13), channel_id=1, source_target_pairs={{0,3},{1,2},{2,1},{3,0},{4,7},{5,6},{6,5},{7,4},{8,11},{9,10},{10,... | collective-permute-start | bytes 196616 | tf_op jit(solution)/shard_map/ppermute | solution.py:17
  7.2 0.7 collective-permute-start.1
  7.9 0.0 collective-permute-start.2
  7.9 1.8 %collective-permute-done = f32[32,512]{1,0:T(8,128)S(1)} collective-permute-done((f32[32,512]{1,0:T(8,128)S(1)}, f32[32,512]{1,0:T(8,128)S(1)}, u32[]{:S(2)}, u32[]{:S(2)}) %collective-permute-start) | collective-permute-done | bytes 65568 | tf_op jit(solution)/shard_map/ppermute | solution.py:17
  9.7 2.2 %collective-permute-done.1 = f32[32,512]{1,0:T(8,128)S(1)} collective-permute-done((f32[32,512]{1,0:T(8,128)S(1)}, f32[32,512]{1,0:T(8,128)S(1)}, u32[]{:S(2)}, u32[]{:S(2)}) %collective-permute-start.1) | collective-permute-done | bytes 65568 | tf_op jit(solution)/shard_map/ppermute | solution.py:17
  11.9 0.0 collective-permute-done.2
  11.9 1.8 %collective-permute-start.5 = (f32[32,512]{1,0:T(8,128)S(1)}, f32[32,512]{1,0:T(8,128)S(1)}, u32[]{:S(2)}, u32[]{:S(2)}) collective-permute-start(f32[32,512]{1,0:T(8,128)S(1)} %add_add_fusion.1), channel_id=1, source_target_pairs={{0,4},{4,0},{8,12},{12,8},{1,5},{5,1},{9,13},{13,9},{2,6},{6,2},{1... | collective-permute-start | bytes 196616 | tf_op jit(solution)/shard_map/ppermute | solution.py:17
  13.7 2.6 %collective-permute-start.4 = (f32[32,512]{1,0:T(8,128)S(1)}, f32[32,512]{1,0:T(8,128)S(1)}, u32[]{:S(2)}, u32[]{:S(2)}) collective-permute-start(f32[32,512]{1,0:T(8,128)S(1)} %add_add_fusion.1), channel_id=1, source_target_pairs={{0,8},{4,12},{8,0},{12,4},{1,9},{5,13},{9,1},{13,5},{2,10},{6,14},... | collective-permute-start | bytes 196616 | tf_op jit(solution)/shard_map/ppermute | solution.py:17
  16.3 0.0 collective-permute-start.3
  16.4 0.0 collective-permute-done.5
  16.4 4.8 %collective-permute-done.4 = f32[32,512]{1,0:T(8,128)S(1)} collective-permute-done((f32[32,512]{1,0:T(8,128)S(1)}, f32[32,512]{1,0:T(8,128)S(1)}, u32[]{:S(2)}, u32[]{:S(2)}) %collective-permute-start.4) | collective-permute-done | bytes 65568 | tf_op jit(solution)/shard_map/ppermute | solution.py:17
  21.2 1.3 %collective-permute-done.3 = f32[32,512]{1,0:T(8,128)S(1)} collective-permute-done((f32[32,512]{1,0:T(8,128)S(1)}, f32[32,512]{1,0:T(8,128)S(1)}, u32[]{:S(2)}, u32[]{:S(2)}) %collective-permute-start.3) | collective-permute-done | bytes 65568 | tf_op jit(solution)/shard_map/ppermute | solution.py:17
  22.5 0.1 collective-permute-start.8
  22.6 1.5 %collective-permute-start.7 = (f32[32,512]{1,0:T(8,128)S(1)}, f32[32,512]{1,0:T(8,128)S(1)}, u32[]{:S(2)}, u32[]{:S(2)}) collective-permute-start(f32[32,512]{1,0:T(8,128)S(1)} %add_add_fusion.refs_0_.refs_4_), channel_id=1, source_target_pairs={{0,2},{1,3},{2,0},{3,1},{4,6},{5,7},{6,4},{7,5},{8,10},{9,11},{10,... | collective-permute-start | bytes 196616 | tf_op jit(solution)/shard_map/ppermute | solution.py:17
  24.1 0.3 collective-permute-start.6
  24.5 2.5 %collective-permute-done.8.refs_3_ = f32[32,512]{1,0:T(8,128)S(1)} collective-permute-done((f32[32,512]{1,0:T(8,128)S(1)}, f32[32,512]{1,0:T(8,128)S(1)}, u32[]{:S(2)}, u32[]{:S(2)}) %collective-permute-start.8) | collective-permute-done | bytes 65568 | tf_op jit(solution)/shard_map/ppermute | solution.py:17
  26.9 1.4 %collective-permute-done.7.refs_2_ = f32[32,512]{1,0:T(8,128)S(1)} collective-permute-done((f32[32,512]{1,0:T(8,128)S(1)}, f32[32,512]{1,0:T(8,128)S(1)}, u32[]{:S(2)}, u32[]{:S(2)}) %collective-permute-start.7) | collective-permute-done | bytes 65568 | tf_op jit(solution)/shard_map/ppermute | solution.py:17
  28.4 0.0 collective-permute-done.6.refs_1_
  28.4 0.5 chunk.4.refs_4_
  28.9 1.9 %collective-permute-start.11 = (f32[64,8,128]{2,1,0:T(8,128)S(1)}, f32[64,8,128]{2,1,0:T(8,128)S(1)}, u32[]{:S(2)}, u32[]{:S(2)}) collective-permute-start(f32[64,8,128]{2,1,0:T(8,128)S(1)} %chunk.4.refs_4_), channel_id=1, source_target_pairs={{0,12},{4,8},{8,4},{12,0},{1,13},{5,9},{9,5},{13,1},{2,14},{6,10},... | collective-permute-start | bytes 786440 | tf_op jit(solution)/shard_map/ppermute | solution.py:17
  30.8 0.5 chunk.5.refs_4_
  31.3 0.4 collective-permute-start.10
  31.6 0.5 chunk.6.refs_4_
  32.1 2.4 %collective-permute-start.9 = (f32[64,8,128]{2,1,0:T(8,128)S(1)}, f32[64,8,128]{2,1,0:T(8,128)S(1)}, u32[]{:S(2)}, u32[]{:S(2)}) collective-permute-start(f32[64,8,128]{2,1,0:T(8,128)S(1)} %chunk.6.refs_4_), channel_id=1, source_target_pairs={{0,4},{4,0},{8,12},{12,8},{1,5},{5,1},{9,13},{13,9},{2,6},{6,2},{1... | collective-permute-start | bytes 786440 | tf_op jit(solution)/shard_map/ppermute | solution.py:17
  35.2 0.0 copy-start
  35.2 0.5 chunk.7.chunk_ref
  35.7 9.1 %factor_x.1.inverse_ref = f32[128,128]{1,0:T(8,128)S(1)} custom-call(s32[1]{0:T(128)S(6)} %copy.9.rank_ref, s32[1]{0:T(128)} %bitcast.2.me_ref, f32[32,512]{1,0:T(8,128)S(1)} %add_add_fusion.refs_0_.refs_4_, f32[32,512]{1,0:T(8,128)S(1)} %collective-permute-done.6.refs_1_, f32[32,512]{1,0:T(8,128)S(1)} %collective-permute-done.7.refs_2_, ...), custom_call_target="tpu_custom_call" | custom-call | tf_op jit(solution)/shard_map/factor_x/pallas_call | solution.py:87
  44.8 0.3 lift.4.refs_0_
  45.1 0.0 collective-permute-done.11.chunk_ref
  45.1 0.3 lift.5.refs_0_.refs_3_
  45.4 8.8 %collective-permute-done.10.chunk_ref = f32[64,8,128]{2,1,0:T(8,128)S(1)} collective-permute-done((f32[64,8,128]{2,1,0:T(8,128)S(1)}, f32[64,8,128]{2,1,0:T(8,128)S(1)}, u32[]{:S(2)}, u32[]{:S(2)}) %collective-permute-start.10) | collective-permute-done | bytes 262176 | tf_op jit(solution)/shard_map/ppermute | solution.py:17
  54.2 0.3 lift.6.refs_0_.refs_2_
  54.5 0.0 collective-permute-done.9.chunk_ref
  54.5 0.3 lift.7.refs_1_
  54.8 0.0 copy-done
  54.8 1.0 %gram.1 = f32[64,32]{1,0:T(8,128)S(1)} custom-call(s32[1]{0:T(128)} %bitcast.here_ref.me_ref, f32[32,64]{1,0:T(8,128)S(1)} %bitcast.9, f32[16,4096]{1,0:T(8,128)S(1)} %lift.4.refs_0_, f32[16,4096]{1,0:T(8,128)S(1)} %lift.7.refs_1_, f32[16,4096]{1,0:T(8,128)S(1)} %lift.6.refs_0_.refs_2_, f32[16,4096]{1,0:T(8,128)S(1)} %lift.5.refs_0_.refs_3_), custom_call_target="tpu_custom_call" | custom-call | tf_op jit(solution)/shard_map/gram/pallas_call | solution.py:87
  55.8 0.0 collective-permute-start.12
  55.8 1.2 %collective-permute-done.12 = f32[64,32]{1,0:T(8,128)S(1)} collective-permute-done((f32[64,32]{1,0:T(8,128)S(1)}, f32[64,32]{1,0:T(8,128)S(1)}, u32[]{:S(2)}, u32[]{:S(2)}) %collective-permute-start.12) | collective-permute-done | bytes 8224 | tf_op jit(solution)/shard_map/ppermute | solution.py:17
  57.0 0.9 %collective-permute-start.13 = (f32[64,32]{1,0:T(8,128)S(1)}, f32[64,32]{1,0:T(8,128)S(1)}, u32[]{:S(2)}, u32[]{:S(2)}) collective-permute-start(f32[64,32]{1,0:T(8,128)S(1)} %add.34), channel_id=1, source_target_pairs={{0,2},{2,0},{1,3},{3,1},{4,6},{6,4},{5,7},{7,5},{8,10},{10,8},{9,1... | collective-permute-start | bytes 24584 | tf_op jit(solution)/shard_map/ppermute | solution.py:17
  57.8 3.0 %collective-permute-done.13 = f32[64,32]{1,0:T(8,128)S(1)} collective-permute-done((f32[64,32]{1,0:T(8,128)S(1)}, f32[64,32]{1,0:T(8,128)S(1)}, u32[]{:S(2)}, u32[]{:S(2)}) %collective-permute-start.13) | collective-permute-done | bytes 8224 | tf_op jit(solution)/shard_map/ppermute | solution.py:17
  60.9 0.0 collective-permute-start.16
  60.9 2.9 %collective-permute-start.15 = (f32[64,32]{1,0:T(8,128)S(1)}, f32[64,32]{1,0:T(8,128)S(1)}, u32[]{:S(2)}, u32[]{:S(2)}) collective-permute-start(f32[64,32]{1,0:T(8,128)S(1)} %add.35.refs_0_), channel_id=1, source_target_pairs={{0,8},{4,12},{8,0},{12,4},{1,9},{5,13},{9,1},{13,5},{2,10},{6,14},... | collective-permute-start | bytes 24584 | tf_op jit(solution)/shard_map/ppermute | solution.py:17
  63.8 1.4 %collective-permute-start.14 = (f32[64,32]{1,0:T(8,128)S(1)}, f32[64,32]{1,0:T(8,128)S(1)}, u32[]{:S(2)}, u32[]{:S(2)}) collective-permute-start(f32[64,32]{1,0:T(8,128)S(1)} %add.35.refs_0_), channel_id=1, source_target_pairs={{0,12},{4,8},{8,4},{12,0},{1,13},{5,9},{9,5},{13,1},{2,14},{6,10},... | collective-permute-start | bytes 24584 | tf_op jit(solution)/shard_map/ppermute | solution.py:17
  65.9 0.0 collective-permute-done.16.refs_3_
  66.0 0.0 collective-permute-done.15.refs_2_
  66.0 3.6 %collective-permute-done.14.refs_1_ = f32[64,32]{1,0:T(8,128)S(1)} collective-permute-done((f32[64,32]{1,0:T(8,128)S(1)}, f32[64,32]{1,0:T(8,128)S(1)}, u32[]{:S(2)}, u32[]{:S(2)}) %collective-permute-start.14) | collective-permute-done | bytes 8224 | tf_op jit(solution)/shard_map/ppermute | solution.py:17
  69.6 2.4 %factor_y.1.factor_ref = f32[64,32]{1,0:T(8,128)S(1)} custom-call(s32[1]{0:T(128)S(6)} %copy.10.rank_ref, f32[64,32]{1,0:T(8,128)S(1)} %add.35.refs_0_, f32[64,32]{1,0:T(8,128)S(1)} %collective-permute-done.14.refs_1_, f32[64,32]{1,0:T(8,128)S(1)} %collective-permute-done.15.refs_2_, f32[64,32]{1,0:T(8,128)S(1)} %collective-permute-done.16.refs_3_), custom_call_target="tpu_custom_call" | custom-call | tf_op jit(solution)/shard_map/factor_y/pallas_call | solution.py:87
  71.9 0.5 mix.1
  72.5 1.5 %collective-permute-start.17 = (f32[4,8,8,128]{3,2,1,0:T(8,128)S(1)}, f32[4,8,8,128]{3,2,1,0:T(8,128)S(1)}, u32[]{:S(2)}, u32[]{:S(2)}) collective-permute-start(f32[4,8,8,128]{3,2,1,0:T(8,128)S(1)} %get-tuple-element.17), channel_id=1, source_target_pairs={{0,12},{4,8},{8,4},{12,0},{1,13},{5,9},{9,5},{13,1},{2,14},{6,10},... | collective-permute-start | bytes 393224 | tf_op jit(solution)/shard_map/ppermute | solution.py:17
  74.0 0.0 collective-permute-start.18
  74.0 2.9 %collective-permute-start.19 = (f32[4,8,8,128]{3,2,1,0:T(8,128)S(1)}, f32[4,8,8,128]{3,2,1,0:T(8,128)S(1)}, u32[]{:S(2)}, u32[]{:S(2)}) collective-permute-start(f32[4,8,8,128]{3,2,1,0:T(8,128)S(1)} %get-tuple-element.19), channel_id=1, source_target_pairs={{0,4},{4,0},{8,12},{12,8},{1,5},{5,1},{9,13},{13,9},{2,6},{6,2},{1... | collective-permute-start | bytes 393224 | tf_op jit(solution)/shard_map/ppermute | solution.py:17
  76.9 1.1 %apply.1 = f32[512,128]{1,0:T(8,128)} custom-call(s32[1]{0:T(128)} %bitcast.2.me_ref, f32[128,128]{1,0:T(8,128)S(1)} %factor_x.1.inverse_ref, f32[32,512]{1,0:T(8,128)S(1)} %add_add_fusion.refs_0_.refs_4_, f32[32,512]{1,0:T(8,128)S(1)} %collective-permute-done.6.refs_1_, f32[32,512]{1,0:T(8,128)S(1)} %collective-permute-done.7.refs_2_, ...), custom_call_target="tpu_custom_call" | custom-call | tf_op jit(solution)/shard_map/apply/pallas_call | solution.py:87
  78.1 0.7 copy.8
  78.8 1.5 %collective-permute-done.17.refs_0_ = f32[4,8,8,128]{3,2,1,0:T(8,128)S(1)} collective-permute-done((f32[4,8,8,128]{3,2,1,0:T(8,128)S(1)}, f32[4,8,8,128]{3,2,1,0:T(8,128)S(1)}, u32[]{:S(2)}, u32[]{:S(2)}) %collective-permute-start.17) | collective-permute-done | bytes 131104 | tf_op jit(solution)/shard_map/ppermute | solution.py:17
  80.3 3.8 %collective-permute-done.18.refs_1_ = f32[4,8,8,128]{3,2,1,0:T(8,128)S(1)} collective-permute-done((f32[4,8,8,128]{3,2,1,0:T(8,128)S(1)}, f32[4,8,8,128]{3,2,1,0:T(8,128)S(1)}, u32[]{:S(2)}, u32[]{:S(2)}) %collective-permute-start.18) | collective-permute-done | bytes 131104 | tf_op jit(solution)/shard_map/ppermute | solution.py:17
  84.1 0.0 collective-permute-done.19.refs_2_
  84.1 0.8 place.1
  (4 shorter events, 0.1 us)
Async XLA Ops:
  4.8 4.9 %collective-permute-start = (f32[32,512]{1,0:T(8,128)S(1)}, f32[32,512]{1,0:T(8,128)S(1)}, u32[]{:S(2)}, u32[]{:S(2)}) collective-permute-start(f32[32,512]{1,0:T(8,128)S(1)} %get-tuple-element.13), channel_id=1, source_target_pairs={{0,3},{1,2},{2,1},{3,0},{4,7},{5,6},{6,5},{7,4},{8,11},{9,10},{10,... | collective-permute-start | bytes 196616 | tf_op jit(solution)/shard_map/ppermute | solution.py:17
  7.2 4.7 %collective-permute-start.1 = (f32[32,512]{1,0:T(8,128)S(1)}, f32[32,512]{1,0:T(8,128)S(1)}, u32[]{:S(2)}, u32[]{:S(2)}) collective-permute-start(f32[32,512]{1,0:T(8,128)S(1)} %get-tuple-element.14), channel_id=1, source_target_pairs={{0,2},{1,3},{2,0},{3,1},{4,6},{5,7},{6,4},{7,5},{8,10},{9,11},{10,... | collective-permute-start | bytes 196616 | tf_op jit(solution)/shard_map/ppermute | solution.py:17
  7.9 4.0 %collective-permute-start.2 = (f32[32,512]{1,0:T(8,128)S(1)}, f32[32,512]{1,0:T(8,128)S(1)}, u32[]{:S(2)}, u32[]{:S(2)}) collective-permute-start(f32[32,512]{1,0:T(8,128)S(1)} %get-tuple-element.15), channel_id=1, source_target_pairs={{0,1},{1,0},{2,3},{3,2},{4,5},{5,4},{6,7},{7,6},{8,9},{9,8},{10,11... | collective-permute-start | bytes 196616 | tf_op jit(solution)/shard_map/ppermute | solution.py:17
  11.9 4.5 %collective-permute-start.5 = (f32[32,512]{1,0:T(8,128)S(1)}, f32[32,512]{1,0:T(8,128)S(1)}, u32[]{:S(2)}, u32[]{:S(2)}) collective-permute-start(f32[32,512]{1,0:T(8,128)S(1)} %add_add_fusion.1), channel_id=1, source_target_pairs={{0,4},{4,0},{8,12},{12,8},{1,5},{5,1},{9,13},{13,9},{2,6},{6,2},{1... | collective-permute-start | bytes 196616 | tf_op jit(solution)/shard_map/ppermute | solution.py:17
  13.7 7.4 %collective-permute-start.4 = (f32[32,512]{1,0:T(8,128)S(1)}, f32[32,512]{1,0:T(8,128)S(1)}, u32[]{:S(2)}, u32[]{:S(2)}) collective-permute-start(f32[32,512]{1,0:T(8,128)S(1)} %add_add_fusion.1), channel_id=1, source_target_pairs={{0,8},{4,12},{8,0},{12,4},{1,9},{5,13},{9,1},{13,5},{2,10},{6,14},... | collective-permute-start | bytes 196616 | tf_op jit(solution)/shard_map/ppermute | solution.py:17
  16.3 6.2 %collective-permute-start.3 = (f32[32,512]{1,0:T(8,128)S(1)}, f32[32,512]{1,0:T(8,128)S(1)}, u32[]{:S(2)}, u32[]{:S(2)}) collective-permute-start(f32[32,512]{1,0:T(8,128)S(1)} %add_add_fusion.1), channel_id=1, source_target_pairs={{0,12},{4,8},{8,4},{12,0},{1,13},{5,9},{9,5},{13,1},{2,14},{6,10},... | collective-permute-start | bytes 196616 | tf_op jit(solution)/shard_map/ppermute | solution.py:17
  22.5 4.4 %collective-permute-start.8 = (f32[32,512]{1,0:T(8,128)S(1)}, f32[32,512]{1,0:T(8,128)S(1)}, u32[]{:S(2)}, u32[]{:S(2)}) collective-permute-start(f32[32,512]{1,0:T(8,128)S(1)} %add_add_fusion.refs_0_.refs_4_), channel_id=1, source_target_pairs={{0,3},{1,2},{2,1},{3,0},{4,7},{5,6},{6,5},{7,4},{8,11},{9,10},{10,... | collective-permute-start | bytes 196616 | tf_op jit(solution)/shard_map/ppermute | solution.py:17
  22.6 5.8 %collective-permute-start.7 = (f32[32,512]{1,0:T(8,128)S(1)}, f32[32,512]{1,0:T(8,128)S(1)}, u32[]{:S(2)}, u32[]{:S(2)}) collective-permute-start(f32[32,512]{1,0:T(8,128)S(1)} %add_add_fusion.refs_0_.refs_4_), channel_id=1, source_target_pairs={{0,2},{1,3},{2,0},{3,1},{4,6},{5,7},{6,4},{7,5},{8,10},{9,11},{10,... | collective-permute-start | bytes 196616 | tf_op jit(solution)/shard_map/ppermute | solution.py:17
  24.1 4.2 %collective-permute-start.6 = (f32[32,512]{1,0:T(8,128)S(1)}, f32[32,512]{1,0:T(8,128)S(1)}, u32[]{:S(2)}, u32[]{:S(2)}) collective-permute-start(f32[32,512]{1,0:T(8,128)S(1)} %add_add_fusion.refs_0_.refs_4_), channel_id=1, source_target_pairs={{0,1},{1,0},{2,3},{3,2},{4,5},{5,4},{6,7},{7,6},{8,9},{9,8},{10,11... | collective-permute-start | bytes 196616 | tf_op jit(solution)/shard_map/ppermute | solution.py:17
  28.9 16.2 %collective-permute-start.11 = (f32[64,8,128]{2,1,0:T(8,128)S(1)}, f32[64,8,128]{2,1,0:T(8,128)S(1)}, u32[]{:S(2)}, u32[]{:S(2)}) collective-permute-start(f32[64,8,128]{2,1,0:T(8,128)S(1)} %chunk.4.refs_4_), channel_id=1, source_target_pairs={{0,12},{4,8},{8,4},{12,0},{1,13},{5,9},{9,5},{13,1},{2,14},{6,10},... | collective-permute-start | bytes 786440 | tf_op jit(solution)/shard_map/ppermute | solution.py:17
  31.3 22.9 %collective-permute-start.10 = (f32[64,8,128]{2,1,0:T(8,128)S(1)}, f32[64,8,128]{2,1,0:T(8,128)S(1)}, u32[]{:S(2)}, u32[]{:S(2)}) collective-permute-start(f32[64,8,128]{2,1,0:T(8,128)S(1)} %chunk.5.refs_4_), channel_id=1, source_target_pairs={{0,8},{4,12},{8,0},{12,4},{1,9},{5,13},{9,1},{13,5},{2,10},{6,14},... | collective-permute-start | bytes 786440 | tf_op jit(solution)/shard_map/ppermute | solution.py:17
  32.1 22.3 %collective-permute-start.9 = (f32[64,8,128]{2,1,0:T(8,128)S(1)}, f32[64,8,128]{2,1,0:T(8,128)S(1)}, u32[]{:S(2)}, u32[]{:S(2)}) collective-permute-start(f32[64,8,128]{2,1,0:T(8,128)S(1)} %chunk.6.refs_4_), channel_id=1, source_target_pairs={{0,4},{4,0},{8,12},{12,8},{1,5},{5,1},{9,13},{13,9},{2,6},{6,2},{1... | collective-permute-start | bytes 786440 | tf_op jit(solution)/shard_map/ppermute | solution.py:17
  35.2 19.6 %copy-start = (f32[64,32]{0,1:T(8,128)S(1)}, f32[64,32]{0,1:T(8,128)}, u32[]{:S(2)}) copy-start(f32[64,32]{0,1:T(8,128)} %param.7) | copy-start | bytes 24580
  55.8 1.2 %collective-permute-start.12 = (f32[64,32]{1,0:T(8,128)S(1)}, f32[64,32]{1,0:T(8,128)S(1)}, u32[]{:S(2)}, u32[]{:S(2)}) collective-permute-start(f32[64,32]{1,0:T(8,128)S(1)} %gram.1), channel_id=1, source_target_pairs={{0,1},{1,0},{2,3},{3,2},{4,5},{5,4},{6,7},{7,6},{8,9},{9,8},{10,11... | collective-permute-start | bytes 24584 | tf_op jit(solution)/shard_map/ppermute | solution.py:17
  57.0 3.9 %collective-permute-start.13 = (f32[64,32]{1,0:T(8,128)S(1)}, f32[64,32]{1,0:T(8,128)S(1)}, u32[]{:S(2)}, u32[]{:S(2)}) collective-permute-start(f32[64,32]{1,0:T(8,128)S(1)} %add.34), channel_id=1, source_target_pairs={{0,2},{2,0},{1,3},{3,1},{4,6},{6,4},{5,7},{7,5},{8,10},{10,8},{9,1... | collective-permute-start | bytes 24584 | tf_op jit(solution)/shard_map/ppermute | solution.py:17
  60.9 5.0 %collective-permute-start.16 = (f32[64,32]{1,0:T(8,128)S(1)}, f32[64,32]{1,0:T(8,128)S(1)}, u32[]{:S(2)}, u32[]{:S(2)}) collective-permute-start(f32[64,32]{1,0:T(8,128)S(1)} %add.35.refs_0_), channel_id=1, source_target_pairs={{0,4},{4,0},{8,12},{12,8},{1,5},{5,1},{9,13},{13,9},{2,6},{6,2},{1... | collective-permute-start | bytes 24584 | tf_op jit(solution)/shard_map/ppermute | solution.py:17
  60.9 5.0 %collective-permute-start.15 = (f32[64,32]{1,0:T(8,128)S(1)}, f32[64,32]{1,0:T(8,128)S(1)}, u32[]{:S(2)}, u32[]{:S(2)}) collective-permute-start(f32[64,32]{1,0:T(8,128)S(1)} %add.35.refs_0_), channel_id=1, source_target_pairs={{0,8},{4,12},{8,0},{12,4},{1,9},{5,13},{9,1},{13,5},{2,10},{6,14},... | collective-permute-start | bytes 24584 | tf_op jit(solution)/shard_map/ppermute | solution.py:17
  63.8 5.7 %collective-permute-start.14 = (f32[64,32]{1,0:T(8,128)S(1)}, f32[64,32]{1,0:T(8,128)S(1)}, u32[]{:S(2)}, u32[]{:S(2)}) collective-permute-start(f32[64,32]{1,0:T(8,128)S(1)} %add.35.refs_0_), channel_id=1, source_target_pairs={{0,12},{4,8},{8,4},{12,0},{1,13},{5,9},{9,5},{13,1},{2,14},{6,10},... | collective-permute-start | bytes 24584 | tf_op jit(solution)/shard_map/ppermute | solution.py:17
  72.5 7.8 %collective-permute-start.17 = (f32[4,8,8,128]{3,2,1,0:T(8,128)S(1)}, f32[4,8,8,128]{3,2,1,0:T(8,128)S(1)}, u32[]{:S(2)}, u32[]{:S(2)}) collective-permute-start(f32[4,8,8,128]{3,2,1,0:T(8,128)S(1)} %get-tuple-element.17), channel_id=1, source_target_pairs={{0,12},{4,8},{8,4},{12,0},{1,13},{5,9},{9,5},{13,1},{2,14},{6,10},... | collective-permute-start | bytes 393224 | tf_op jit(solution)/shard_map/ppermute | solution.py:17
  74.0 10.1 %collective-permute-start.18 = (f32[4,8,8,128]{3,2,1,0:T(8,128)S(1)}, f32[4,8,8,128]{3,2,1,0:T(8,128)S(1)}, u32[]{:S(2)}, u32[]{:S(2)}) collective-permute-start(f32[4,8,8,128]{3,2,1,0:T(8,128)S(1)} %get-tuple-element.18), channel_id=1, source_target_pairs={{0,8},{4,12},{8,0},{12,4},{1,9},{5,13},{9,1},{13,5},{2,10},{6,14},... | collective-permute-start | bytes 393224 | tf_op jit(solution)/shard_map/ppermute | solution.py:17
  74.0 10.1 %collective-permute-start.19 = (f32[4,8,8,128]{3,2,1,0:T(8,128)S(1)}, f32[4,8,8,128]{3,2,1,0:T(8,128)S(1)}, u32[]{:S(2)}, u32[]{:S(2)}) collective-permute-start(f32[4,8,8,128]{3,2,1,0:T(8,128)S(1)} %get-tuple-element.19), channel_id=1, source_target_pairs={{0,4},{4,0},{8,12},{12,8},{1,5},{5,1},{9,13},{13,9},{2,6},{6,2},{1... | collective-permute-start | bytes 393224 | tf_op jit(solution)/shard_map/ppermute | solution.py:17

commit v6 on v5

--- a/solution.py
+++ b/solution.py
@@ -18,7 +18,7 @@
 
 
 def steps(count):
-    return sorted(range(1, count), key=lambda s: -(s & 2) * 4 - s)
+    return sorted(range(1, count), key=lambda s: (s % 4 != 2, s))
 
 
 def by_step(blocks, me, count):
@@ -39,16 +39,23 @@
 
 
 def sum_sketch(parts):
-    axes = ("gz", "vert")
-    count = len(parts)
-    got = [swap(parts[s], axes, s) for s in steps(count)]
-    mine = parts[0]
-    for other in got:
+    cores = lax.axis_size("vert")
+    count = lax.axis_size("gz")
+    sums = []
+    for z in [*steps(count), 0]:
+        total = parts[z * cores]
+        for v in steps(cores):
+            total = total + swap(parts[z * cores + v], "vert", v)
+        sums.append(swap(total, "gz", z) if z else total)
+    mine = sums[-1]
+    for other in sums[:-1]:
         mine = mine + other
     mine = sum_over_gy(mine)
-    pieces = [mine] + [None] * (count - 1)
-    for s in steps(count):
-        pieces[s] = swap(mine, axes, s)
+    pieces = [None] * (count * cores)
+    for z in [*steps(count), 0]:
+        pieces[z * cores] = swap(mine, "gz", z) if z else mine
+        for v in steps(cores):
+            pieces[z * cores + v] = swap(pieces[z * cores], "vert", v)
     return pieces
 
 
@@ -95,7 +102,7 @@
     )(*scalars, *[held(value) for value in values])
 
 
-PIECES = 4
+PIECES = 3
 
 
 def sketch_kernel(me_ref, here_ref, field_hbm, omega_hbm, field_ref, *refs):
@@ -103,10 +110,11 @@
     omega_copy = pltpu.make_async_copy(omega_hbm, omega_ref, arrived.at[PIECES])
     omega_copy.start()
     width = omega_ref.shape[1]
-    block = field_ref.shape[0] // PIECES
+    eighth = field_ref.shape[0] // 8
+    ends = [0, 2 * eighth, 5 * eighth, 8 * eighth]
     copies = []
     for i in range(PIECES):
-        rows = pl.ds(i * block, block)
+        rows = pl.ds(ends[i], ends[i + 1] - ends[i])
         copies.append(pltpu.make_async_copy(field_hbm.at[rows], field_ref.at[rows], arrived.at[i]))
         copies[i].start()
     omega_copy.wait()
@@ -115,7 +123,7 @@
     wide = narrow = None
     for i in range(PIECES):
         copies[i].wait()
-        high, low = halves(field_ref[i * block:(i + 1) * block, :])
+        high, low = halves(field_ref[ends[i]:ends[i + 1], :])
         both = mxu(high, omega_both, dims(1, 0))
         projected = both[:, :width] + (both[:, width:] + mxu(low, omega_high, dims(1, 0)))
         proj_high, proj_low = halves(projected)
@@ -264,32 +272,35 @@
     full = lambda x: jnp.broadcast_to(x, (8, count))
     left = [gram[8 * b:8 * b + 8, :] for b in range(blocks)]
     right = [(lanes == subs + 8 * b).astype(jnp.float32) for b in range(blocks)]
-    for j in range(0, count, 2):
-        b, s = divmod(j, 8)
-        l0, l1 = full(left[b][s:s + 1, :]), full(left[b][s + 1:s + 2, :])
-        r0, r1 = full(right[b][s:s + 1, :]), full(right[b][s + 1:s + 2, :])
-        p, q, t = full(l0[:, j:j + 1]), full(l0[:, j + 1:j + 2]), full(l1[:, j + 1:j + 2])
-        inv = 1.0 / (p * t - q * q)
-        ratio = q / p
-        first = r0 * lax.rsqrt(p)
-        second = (r1 - ratio * r0) * lax.rsqrt(t - q * ratio)
-        out_ref[j:j + 1, :] = jnp.where(j < rank, first[0:1], 0.0)
-        out_ref[j + 1:j + 2, :] = jnp.where(j + 1 < rank, second[0:1], 0.0)
-        if j + 2 >= count:
+    for b in range(blocks):
+        at = 8 * b
+        l = [full(left[b][k:k + 1, :]) for k in range(8)]
+        r = [full(right[b][k:k + 1, :]) for k in range(8)]
+        a = {(k, m): full(l[k][:, at + m:at + m + 1]) for k in range(8) for m in range(k, 8)}
+        inv, f = {}, {}
+        for k in range(8):
+            inv[k] = 1.0 / a[k, k]
+            for m in range(k + 1, 8):
+                f[k, m] = a[k, m] * inv[k]
+                for q in range(m, 8):
+                    a[m, q] = a[m, q] - f[k, m] * a[k, q]
+                l[m] = l[m] - f[k, m] * l[k]
+                r[m] = r[m] - f[k, m] * r[k]
+            row = (r[k] * lax.rsqrt(a[k, k]))[0:1]
+            out_ref[at + k:at + k + 1, :] = jnp.where(at + k < rank, row, 0.0)
+        if b + 1 == blocks:
             break
-        u0 = (l0 * t - l1 * q) * inv
-        u1 = (l1 * p - l0 * q) * inv
-        v0 = (r0 * t - r1 * q) * inv
-        v1 = (r1 * p - r0 * q) * inv
-        for i in range(b, blocks):
-            if i == b and s == 6:
-                continue
-            c0, c1 = full(left[i][:, j:j + 1]), full(left[i][:, j + 1:j + 2])
-            if i == b:
-                c0 = jnp.where(subs > s + 1, c0, 0.0)
-                c1 = jnp.where(subs > s + 1, c1, 0.0)
-            left[i] = left[i] - c0 * u0 - c1 * u1
-            right[i] = right[i] - c0 * v0 - c1 * v1
+        w, v = {}, {}
+        for k in reversed(range(8)):
+            w[k], v[k] = l[k] * inv[k], r[k] * inv[k]
+            for m in range(k + 1, 8):
+                w[k] = w[k] - f[k, m] * w[m]
+                v[k] = v[k] - f[k, m] * v[m]
+        for i in range(b + 1, blocks):
+            column = [full(left[i][:, at + k:at + k + 1]) for k in range(8)]
+            for k in range(8):
+                left[i] = left[i] - column[k] * w[k]
+                right[i] = right[i] - column[k] * v[k]
 
 
 def factor_x_kernel(scale, rank_ref, me_ref, *refs):

time: 85.1 us -> 79.6 us (0.935)
  Pallas kernels: 22.2 us -> 17.8 us
  waiting for transfers between devices: 36.1 us -> 32.1 us
  starting transfers between devices: 23.8 us -> 26.6 us
    pallas_call x13, Pallas kernels: 17.3 us -> 13.1 us  [kernel_call(): pl.pallas_call(body, in_specs=[SMEM] * len(scalars) + [VMEM] * len(values...]
    ppermute x20, waiting for transfers between devices: 36.1 us -> 32.1 us  [swap(): return lax.ppermute(value, axes, [(i, i ^ step) for i in range(count)])]
    ppermute x20, starting transfers between devices: 23.8 us -> 26.6 us  [swap(): return lax.ppermute(value, axes, [(i, i ^ step) for i in range(count)])]
  transfers between devices with their start and end apart: 20 -> 20, of which waited for: 12 -> 14; matrix products, arithmetic and copies ran while one was open for 1% -> 1% of each run, Pallas kernels for 15% -> 12%
where the time goes in v6:
time: 79.6 us; the launch traced here: 79.4 us
  waiting for transfers between devices  32.1 us (40%)
  starting transfers between devices  26.6 us (33%)
  Pallas kernels  17.8 us (22%)
  between operations  2.09 us (3%)
    ppermute x20, waiting for transfers between devices, swap(): return lax.ppermute(value, axes, [(i, i ^ step) for i in range(count)])  32.1 us
    ppermute x20, starting transfers between devices, swap(): return lax.ppermute(value, axes, [(i, i ^ step) for i in range(count)])  26.6 us
    pallas_call x13, Pallas kernels, kernel_call(): pl.pallas_call(body, in_specs=[SMEM] * len(scalars) + [VMEM] * len(values...  13.1 us
    pallas_call x1, Pallas kernels, sketch_parts(): pl.pallas_call(sketch_kernel, in_specs=[SMEM, SMEM, far, far], out_specs=...  3.85 us
  transfers between devices with their start and end apart: 20, of which 14 were waited for; matrix products, arithmetic and copies ran while one was open for 1% of the time, Pallas kernels for 12%

profile of v6, /device:TPU:0, one launch (start us, length us, event | category | flops | bytes accessed | tf_op | source)
XLA Modules:
  0.0 79.4 jit_solution(15398795556250076378)
XLA Ops:
  0.6 3.9 %sketch.1 = (f32[2048,512]{1,0:T(8,128)S(1)}, f32[32,512]{1,0:T(8,128)S(1)}, f32[32,512]{1,0:T(8,128)S(1)}, f32[32,512]{1,0:T(8,128)S(1)}, f32[32,512]{1,0:T(8,128)S(1)}) custom-call(s32[1]{0:T(128)} %bitcast.2.me_ref, s32[1]{0:T(128)} %bitcast.here_ref.me_ref, f32[2048,512]{1,0:T(8,128)} %bitcast.10, f32[512,128]{1,0:T(8,128)} %omega_hbm.1), custom_call_target="tpu_custom_call" | custom-call | tf_op jit(solution)/shard_map/sketch/pallas_call | solution.py:145
  4.5 0.5 collective-permute-start.1
  5.0 0.1 collective-permute-start
  5.1 0.8 %collective-permute-done.1 = f32[32,512]{1,0:T(8,128)S(1)} collective-permute-done((f32[32,512]{1,0:T(8,128)S(1)}, f32[32,512]{1,0:T(8,128)S(1)}, u32[]{:S(2)}, u32[]{:S(2)}) %collective-permute-start.1) | collective-permute-done | bytes 65568 | tf_op jit(solution)/shard_map/ppermute | solution.py:17
  5.9 2.9 %collective-permute-start.2 = (f32[32,512]{1,0:T(8,128)S(1)}, f32[32,512]{1,0:T(8,128)S(1)}, u32[]{:S(2)}, u32[]{:S(2)}) collective-permute-start(f32[32,512]{1,0:T(8,128)S(1)} %add.29), channel_id=1, source_target_pairs={{0,2},{2,0},{1,3},{3,1},{4,6},{6,4},{5,7},{7,5},{8,10},{10,8},{9,1... | collective-permute-start | bytes 196616 | tf_op jit(solution)/shard_map/ppermute | solution.py:17
  8.8 0.0 collective-permute-done
  8.8 2.4 %collective-permute-done.2 = f32[32,512]{1,0:T(8,128)S(1)} collective-permute-done((f32[32,512]{1,0:T(8,128)S(1)}, f32[32,512]{1,0:T(8,128)S(1)}, u32[]{:S(2)}, u32[]{:S(2)}) %collective-permute-start.2) | collective-permute-done | bytes 65568 | tf_op jit(solution)/shard_map/ppermute | solution.py:17
  11.3 4.0 %collective-permute-start.5 = (f32[32,512]{1,0:T(8,128)S(1)}, f32[32,512]{1,0:T(8,128)S(1)}, u32[]{:S(2)}, u32[]{:S(2)}) collective-permute-start(f32[32,512]{1,0:T(8,128)S(1)} %add_add_fusion.1), channel_id=1, source_target_pairs={{0,12},{4,8},{8,4},{12,0},{1,13},{5,9},{9,5},{13,1},{2,14},{6,10},... | collective-permute-start | bytes 196616 | tf_op jit(solution)/shard_map/ppermute | solution.py:17
  15.3 0.0 collective-permute-start.4
  15.3 0.6 collective-permute-start.3
  15.9 1.8 %collective-permute-done.5 = f32[32,512]{1,0:T(8,128)S(1)} collective-permute-done((f32[32,512]{1,0:T(8,128)S(1)}, f32[32,512]{1,0:T(8,128)S(1)}, u32[]{:S(2)}, u32[]{:S(2)}) %collective-permute-start.5) | collective-permute-done | bytes 65568 | tf_op jit(solution)/shard_map/ppermute | solution.py:17
  17.7 1.9 %collective-permute-done.4 = f32[32,512]{1,0:T(8,128)S(1)} collective-permute-done((f32[32,512]{1,0:T(8,128)S(1)}, f32[32,512]{1,0:T(8,128)S(1)}, u32[]{:S(2)}, u32[]{:S(2)}) %collective-permute-start.4) | collective-permute-done | bytes 65568 | tf_op jit(solution)/shard_map/ppermute | solution.py:17
  19.6 0.9 %collective-permute-done.3 = f32[32,512]{1,0:T(8,128)S(1)} collective-permute-done((f32[32,512]{1,0:T(8,128)S(1)}, f32[32,512]{1,0:T(8,128)S(1)}, u32[]{:S(2)}, u32[]{:S(2)}) %collective-permute-start.3) | collective-permute-done | bytes 65568 | tf_op jit(solution)/shard_map/ppermute | solution.py:17
  20.5 1.6 %collective-permute-start.7 = (f32[32,512]{1,0:T(8,128)S(1)}, f32[32,512]{1,0:T(8,128)S(1)}, u32[]{:S(2)}, u32[]{:S(2)}) collective-permute-start(f32[32,512]{1,0:T(8,128)S(1)} %add_add_fusion.refs_0_.refs_4_), channel_id=1, source_target_pairs={{0,2},{2,0},{1,3},{3,1},{4,6},{6,4},{5,7},{7,5},{8,10},{10,8},{9,1... | collective-permute-start | bytes 196616 | tf_op jit(solution)/shard_map/ppermute | solution.py:17
  22.1 0.0 collective-permute-start.6
  22.1 2.8 %collective-permute-done.7.refs_2_ = f32[32,512]{1,0:T(8,128)S(1)} collective-permute-done((f32[32,512]{1,0:T(8,128)S(1)}, f32[32,512]{1,0:T(8,128)S(1)}, u32[]{:S(2)}, u32[]{:S(2)}) %collective-permute-start.7) | collective-permute-done | bytes 65568 | tf_op jit(solution)/shard_map/ppermute | solution.py:17
  24.8 0.0 collective-permute-start.8
  24.8 0.0 collective-permute-done.6.refs_1_
  24.8 1.2 %collective-permute-done.8.refs_3_ = f32[32,512]{1,0:T(8,128)S(1)} collective-permute-done((f32[32,512]{1,0:T(8,128)S(1)}, f32[32,512]{1,0:T(8,128)S(1)}, u32[]{:S(2)}, u32[]{:S(2)}) %collective-permute-start.8) | collective-permute-done | bytes 65568 | tf_op jit(solution)/shard_map/ppermute | solution.py:17
  26.1 0.5 chunk.4.refs_4_
  26.6 1.8 %collective-permute-start.10 = (f32[64,8,128]{2,1,0:T(8,128)S(1)}, f32[64,8,128]{2,1,0:T(8,128)S(1)}, u32[]{:S(2)}, u32[]{:S(2)}) collective-permute-start(f32[64,8,128]{2,1,0:T(8,128)S(1)} %chunk.4.refs_4_), channel_id=1, source_target_pairs={{0,8},{4,12},{8,0},{12,4},{1,9},{5,13},{9,1},{13,5},{2,10},{6,14},... | collective-permute-start | bytes 786440 | tf_op jit(solution)/shard_map/ppermute | solution.py:17
  28.3 0.5 chunk.5.refs_4_
  28.8 2.1 %collective-permute-start.9 = (f32[64,8,128]{2,1,0:T(8,128)S(1)}, f32[64,8,128]{2,1,0:T(8,128)S(1)}, u32[]{:S(2)}, u32[]{:S(2)}) collective-permute-start(f32[64,8,128]{2,1,0:T(8,128)S(1)} %chunk.5.refs_4_), channel_id=1, source_target_pairs={{0,4},{4,0},{8,12},{12,8},{1,5},{5,1},{9,13},{13,9},{2,6},{6,2},{1... | collective-permute-start | bytes 786440 | tf_op jit(solution)/shard_map/ppermute | solution.py:17
  30.9 0.5 chunk.6.refs_4_
  31.4 0.7 collective-permute-start.11
  32.8 0.0 copy-start
  32.8 0.5 chunk.7.chunk_ref
  33.4 6.0 %factor_x.1.inverse_ref = f32[128,128]{1,0:T(8,128)S(1)} custom-call(s32[1]{0:T(128)S(6)} %copy.9.rank_ref, s32[1]{0:T(128)} %bitcast.2.me_ref, f32[32,512]{1,0:T(8,128)S(1)} %add_add_fusion.refs_0_.refs_4_, f32[32,512]{1,0:T(8,128)S(1)} %collective-permute-done.6.refs_1_, f32[32,512]{1,0:T(8,128)S(1)} %collective-permute-done.7.refs_2_, ...), custom_call_target="tpu_custom_call" | custom-call | tf_op jit(solution)/shard_map/factor_x/pallas_call | solution.py:94
  39.4 0.3 lift.4.refs_0_
  39.7 2.7 %collective-permute-done.10.chunk_ref = f32[64,8,128]{2,1,0:T(8,128)S(1)} collective-permute-done((f32[64,8,128]{2,1,0:T(8,128)S(1)}, f32[64,8,128]{2,1,0:T(8,128)S(1)}, u32[]{:S(2)}, u32[]{:S(2)}) %collective-permute-start.10) | collective-permute-done | bytes 262176 | tf_op jit(solution)/shard_map/ppermute | solution.py:17
  42.4 0.3 lift.5.refs_0_.refs_2_
  42.6 0.0 collective-permute-done.9.chunk_ref
  42.7 0.3 lift.6.refs_0_.refs_1_
  43.0 5.8 %collective-permute-done.11.chunk_ref = f32[64,8,128]{2,1,0:T(8,128)S(1)} collective-permute-done((f32[64,8,128]{2,1,0:T(8,128)S(1)}, f32[64,8,128]{2,1,0:T(8,128)S(1)}, u32[]{:S(2)}, u32[]{:S(2)}) %collective-permute-start.11) | collective-permute-done | bytes 262176 | tf_op jit(solution)/shard_map/ppermute | solution.py:17
  48.8 0.3 lift.7.refs_3_
  49.0 0.0 copy-done
  49.1 1.0 %gram.1 = f32[64,32]{1,0:T(8,128)S(1)} custom-call(s32[1]{0:T(128)} %bitcast.here_ref.me_ref, f32[32,64]{1,0:T(8,128)S(1)} %bitcast.9, f32[16,4096]{1,0:T(8,128)S(1)} %lift.4.refs_0_, f32[16,4096]{1,0:T(8,128)S(1)} %lift.6.refs_0_.refs_1_, f32[16,4096]{1,0:T(8,128)S(1)} %lift.5.refs_0_.refs_2_, f32[16,4096]{1,0:T(8,128)S(1)} %lift.7.refs_3_), custom_call_target="tpu_custom_call" | custom-call | tf_op jit(solution)/shard_map/gram/pallas_call | solution.py:94
  50.0 0.0 collective-permute-start.12
  50.0 1.2 %collective-permute-done.12 = f32[64,32]{1,0:T(8,128)S(1)} collective-permute-done((f32[64,32]{1,0:T(8,128)S(1)}, f32[64,32]{1,0:T(8,128)S(1)}, u32[]{:S(2)}, u32[]{:S(2)}) %collective-permute-start.12) | collective-permute-done | bytes 8224 | tf_op jit(solution)/shard_map/ppermute | solution.py:17
  51.2 1.5 %collective-permute-start.13 = (f32[64,32]{1,0:T(8,128)S(1)}, f32[64,32]{1,0:T(8,128)S(1)}, u32[]{:S(2)}, u32[]{:S(2)}) collective-permute-start(f32[64,32]{1,0:T(8,128)S(1)} %add.34), channel_id=1, source_target_pairs={{0,2},{2,0},{1,3},{3,1},{4,6},{6,4},{5,7},{7,5},{8,10},{10,8},{9,1... | collective-permute-start | bytes 24584 | tf_op jit(solution)/shard_map/ppermute | solution.py:17
  52.8 2.4 %collective-permute-done.13 = f32[64,32]{1,0:T(8,128)S(1)} collective-permute-done((f32[64,32]{1,0:T(8,128)S(1)}, f32[64,32]{1,0:T(8,128)S(1)}, u32[]{:S(2)}, u32[]{:S(2)}) %collective-permute-start.13) | collective-permute-done | bytes 8224 | tf_op jit(solution)/shard_map/ppermute | solution.py:17
  55.2 2.4 %collective-permute-start.16 = (f32[64,32]{1,0:T(8,128)S(1)}, f32[64,32]{1,0:T(8,128)S(1)}, u32[]{:S(2)}, u32[]{:S(2)}) collective-permute-start(f32[64,32]{1,0:T(8,128)S(1)} %add.35.refs_0_), channel_id=1, source_target_pairs={{0,12},{4,8},{8,4},{12,0},{1,13},{5,9},{9,5},{13,1},{2,14},{6,10},... | collective-permute-start | bytes 24584 | tf_op jit(solution)/shard_map/ppermute | solution.py:17
  57.6 3.9 %collective-permute-start.15 = (f32[64,32]{1,0:T(8,128)S(1)}, f32[64,32]{1,0:T(8,128)S(1)}, u32[]{:S(2)}, u32[]{:S(2)}) collective-permute-start(f32[64,32]{1,0:T(8,128)S(1)} %add.35.refs_0_), channel_id=1, source_target_pairs={{0,4},{4,0},{8,12},{12,8},{1,5},{5,1},{9,13},{13,9},{2,6},{6,2},{1... | collective-permute-start | bytes 24584 | tf_op jit(solution)/shard_map/ppermute | solution.py:17
  61.5 0.0 collective-permute-start.14
  62.1 0.0 collective-permute-done.16.refs_3_
  62.1 1.2 %collective-permute-done.15.refs_2_ = f32[64,32]{1,0:T(8,128)S(1)} collective-permute-done((f32[64,32]{1,0:T(8,128)S(1)}, f32[64,32]{1,0:T(8,128)S(1)}, u32[]{:S(2)}, u32[]{:S(2)}) %collective-permute-start.15) | collective-permute-done | bytes 8224 | tf_op jit(solution)/shard_map/ppermute | solution.py:17
  63.4 2.9 %collective-permute-done.14.refs_1_ = f32[64,32]{1,0:T(8,128)S(1)} collective-permute-done((f32[64,32]{1,0:T(8,128)S(1)}, f32[64,32]{1,0:T(8,128)S(1)}, u32[]{:S(2)}, u32[]{:S(2)}) %collective-permute-start.14) | collective-permute-done | bytes 8224 | tf_op jit(solution)/shard_map/ppermute | solution.py:17
  66.3 1.4 %factor_y.1.factor_ref = f32[64,32]{1,0:T(8,128)S(1)} custom-call(s32[1]{0:T(128)S(6)} %copy.10.rank_ref, f32[64,32]{1,0:T(8,128)S(1)} %add.35.refs_0_, f32[64,32]{1,0:T(8,128)S(1)} %collective-permute-done.14.refs_1_, f32[64,32]{1,0:T(8,128)S(1)} %collective-permute-done.15.refs_2_, f32[64,32]{1,0:T(8,128)S(1)} %collective-permute-done.16.refs_3_), custom_call_target="tpu_custom_call" | custom-call | tf_op jit(solution)/shard_map/factor_y/pallas_call | solution.py:94
  67.6 0.5 mix.1
  68.2 0.5 collective-permute-start.17
  68.7 1.7 %collective-permute-start.18 = (f32[4,8,8,128]{3,2,1,0:T(8,128)S(1)}, f32[4,8,8,128]{3,2,1,0:T(8,128)S(1)}, u32[]{:S(2)}, u32[]{:S(2)}) collective-permute-start(f32[4,8,8,128]{3,2,1,0:T(8,128)S(1)} %get-tuple-element.18), channel_id=1, source_target_pairs={{0,4},{4,0},{8,12},{12,8},{1,5},{5,1},{9,13},{13,9},{2,6},{6,2},{1... | collective-permute-start | bytes 393224 | tf_op jit(solution)/shard_map/ppermute | solution.py:17
  70.4 2.3 %collective-permute-start.19 = (f32[4,8,8,128]{3,2,1,0:T(8,128)S(1)}, f32[4,8,8,128]{3,2,1,0:T(8,128)S(1)}, u32[]{:S(2)}, u32[]{:S(2)}) collective-permute-start(f32[4,8,8,128]{3,2,1,0:T(8,128)S(1)} %get-tuple-element.19), channel_id=1, source_target_pairs={{0,12},{4,8},{8,4},{12,0},{1,13},{5,9},{9,5},{13,1},{2,14},{6,10},... | collective-permute-start | bytes 393224 | tf_op jit(solution)/shard_map/ppermute | solution.py:17
  72.6 1.1 %apply.1 = f32[512,128]{1,0:T(8,128)} custom-call(s32[1]{0:T(128)} %bitcast.2.me_ref, f32[128,128]{1,0:T(8,128)S(1)} %factor_x.1.inverse_ref, f32[32,512]{1,0:T(8,128)S(1)} %add_add_fusion.refs_0_.refs_4_, f32[32,512]{1,0:T(8,128)S(1)} %collective-permute-done.6.refs_1_, f32[32,512]{1,0:T(8,128)S(1)} %collective-permute-done.7.refs_2_, ...), custom_call_target="tpu_custom_call" | custom-call | tf_op jit(solution)/shard_map/apply/pallas_call | solution.py:94
  73.8 0.7 copy.8
  74.5 4.1 %collective-permute-done.17.refs_0_ = f32[4,8,8,128]{3,2,1,0:T(8,128)S(1)} collective-permute-done((f32[4,8,8,128]{3,2,1,0:T(8,128)S(1)}, f32[4,8,8,128]{3,2,1,0:T(8,128)S(1)}, u32[]{:S(2)}, u32[]{:S(2)}) %collective-permute-start.17) | collective-permute-done | bytes 131104 | tf_op jit(solution)/shard_map/ppermute | solution.py:17
  78.6 0.0 collective-permute-done.18.refs_1_
  78.6 0.0 collective-permute-done.19.refs_2_
  78.6 0.8 %place.1 = f32[4,8,32,128]{3,2,1,0:T(8,128)} custom-call(s32[1]{0:T(128)} %bitcast.here_ref.me_ref, f32[4,8,8,128]{3,2,1,0:T(8,128)S(1)} %collective-permute-done.17.refs_0_, f32[4,8,8,128]{3,2,1,0:T(8,128)S(1)} %collective-permute-done.18.refs_1_, f32[4,8,8,128]{3,2,1,0:T(8,128)S(1)} %collective-permute-done.19.refs_2_, ...), custom_call_target="tpu_custom_call" | custom-call | tf_op jit(solution)/shard_map/place/pallas_call | solution.py:257
  (5 shorter events, 0.1 us)
Async XLA Ops:
  4.5 1.4 %collective-permute-start.1 = (f32[32,512]{1,0:T(8,128)S(1)}, f32[32,512]{1,0:T(8,128)S(1)}, u32[]{:S(2)}, u32[]{:S(2)}) collective-permute-start(f32[32,512]{1,0:T(8,128)S(1)} %get-tuple-element.15), channel_id=1, source_target_pairs={{0,1},{1,0},{2,3},{3,2},{4,5},{5,4},{6,7},{7,6},{8,9},{9,8},{10,11... | collective-permute-start | bytes 196616 | tf_op jit(solution)/shard_map/ppermute | solution.py:17
  5.0 3.8 %collective-permute-start = (f32[32,512]{1,0:T(8,128)S(1)}, f32[32,512]{1,0:T(8,128)S(1)}, u32[]{:S(2)}, u32[]{:S(2)}) collective-permute-start(f32[32,512]{1,0:T(8,128)S(1)} %get-tuple-element.13), channel_id=1, source_target_pairs={{0,1},{1,0},{2,3},{3,2},{4,5},{5,4},{6,7},{7,6},{8,9},{9,8},{10,11... | collective-permute-start | bytes 196616 | tf_op jit(solution)/shard_map/ppermute | solution.py:17
  5.9 5.3 %collective-permute-start.2 = (f32[32,512]{1,0:T(8,128)S(1)}, f32[32,512]{1,0:T(8,128)S(1)}, u32[]{:S(2)}, u32[]{:S(2)}) collective-permute-start(f32[32,512]{1,0:T(8,128)S(1)} %add.29), channel_id=1, source_target_pairs={{0,2},{2,0},{1,3},{3,1},{4,6},{6,4},{5,7},{7,5},{8,10},{10,8},{9,1... | collective-permute-start | bytes 196616 | tf_op jit(solution)/shard_map/ppermute | solution.py:17
  11.3 6.4 %collective-permute-start.5 = (f32[32,512]{1,0:T(8,128)S(1)}, f32[32,512]{1,0:T(8,128)S(1)}, u32[]{:S(2)}, u32[]{:S(2)}) collective-permute-start(f32[32,512]{1,0:T(8,128)S(1)} %add_add_fusion.1), channel_id=1, source_target_pairs={{0,12},{4,8},{8,4},{12,0},{1,13},{5,9},{9,5},{13,1},{2,14},{6,10},... | collective-permute-start | bytes 196616 | tf_op jit(solution)/shard_map/ppermute | solution.py:17
  15.3 4.3 %collective-permute-start.4 = (f32[32,512]{1,0:T(8,128)S(1)}, f32[32,512]{1,0:T(8,128)S(1)}, u32[]{:S(2)}, u32[]{:S(2)}) collective-permute-start(f32[32,512]{1,0:T(8,128)S(1)} %add_add_fusion.1), channel_id=1, source_target_pairs={{0,4},{4,0},{8,12},{12,8},{1,5},{5,1},{9,13},{13,9},{2,6},{6,2},{1... | collective-permute-start | bytes 196616 | tf_op jit(solution)/shard_map/ppermute | solution.py:17
  15.3 5.2 %collective-permute-start.3 = (f32[32,512]{1,0:T(8,128)S(1)}, f32[32,512]{1,0:T(8,128)S(1)}, u32[]{:S(2)}, u32[]{:S(2)}) collective-permute-start(f32[32,512]{1,0:T(8,128)S(1)} %add_add_fusion.1), channel_id=1, source_target_pairs={{0,8},{4,12},{8,0},{12,4},{1,9},{5,13},{9,1},{13,5},{2,10},{6,14},... | collective-permute-start | bytes 196616 | tf_op jit(solution)/shard_map/ppermute | solution.py:17
  20.5 4.3 %collective-permute-start.7 = (f32[32,512]{1,0:T(8,128)S(1)}, f32[32,512]{1,0:T(8,128)S(1)}, u32[]{:S(2)}, u32[]{:S(2)}) collective-permute-start(f32[32,512]{1,0:T(8,128)S(1)} %add_add_fusion.refs_0_.refs_4_), channel_id=1, source_target_pairs={{0,2},{2,0},{1,3},{3,1},{4,6},{6,4},{5,7},{7,5},{8,10},{10,8},{9,1... | collective-permute-start | bytes 196616 | tf_op jit(solution)/shard_map/ppermute | solution.py:17
  22.1 2.8 %collective-permute-start.6 = (f32[32,512]{1,0:T(8,128)S(1)}, f32[32,512]{1,0:T(8,128)S(1)}, u32[]{:S(2)}, u32[]{:S(2)}) collective-permute-start(f32[32,512]{1,0:T(8,128)S(1)} %add_add_fusion.refs_0_.refs_4_), channel_id=1, source_target_pairs={{0,1},{1,0},{2,3},{3,2},{4,5},{5,4},{6,7},{7,6},{8,9},{9,8},{10,11... | collective-permute-start | bytes 196616 | tf_op jit(solution)/shard_map/ppermute | solution.py:17
  24.8 1.3 %collective-permute-start.8 = (f32[32,512]{1,0:T(8,128)S(1)}, f32[32,512]{1,0:T(8,128)S(1)}, u32[]{:S(2)}, u32[]{:S(2)}) collective-permute-start(f32[32,512]{1,0:T(8,128)S(1)} %collective-permute-done.7.refs_2_), channel_id=1, source_target_pairs={{0,1},{1,0},{2,3},{3,2},{4,5},{5,4},{6,7},{7,6},{8,9},{9,8},{10,11... | collective-permute-start | bytes 196616 | tf_op jit(solution)/shard_map/ppermute | solution.py:17
  26.6 15.8 %collective-permute-start.10 = (f32[64,8,128]{2,1,0:T(8,128)S(1)}, f32[64,8,128]{2,1,0:T(8,128)S(1)}, u32[]{:S(2)}, u32[]{:S(2)}) collective-permute-start(f32[64,8,128]{2,1,0:T(8,128)S(1)} %chunk.4.refs_4_), channel_id=1, source_target_pairs={{0,8},{4,12},{8,0},{12,4},{1,9},{5,13},{9,1},{13,5},{2,10},{6,14},... | collective-permute-start | bytes 786440 | tf_op jit(solution)/shard_map/ppermute | solution.py:17
  28.8 13.8 %collective-permute-start.9 = (f32[64,8,128]{2,1,0:T(8,128)S(1)}, f32[64,8,128]{2,1,0:T(8,128)S(1)}, u32[]{:S(2)}, u32[]{:S(2)}) collective-permute-start(f32[64,8,128]{2,1,0:T(8,128)S(1)} %chunk.5.refs_4_), channel_id=1, source_target_pairs={{0,4},{4,0},{8,12},{12,8},{1,5},{5,1},{9,13},{13,9},{2,6},{6,2},{1... | collective-permute-start | bytes 786440 | tf_op jit(solution)/shard_map/ppermute | solution.py:17
  31.4 17.3 %collective-permute-start.11 = (f32[64,8,128]{2,1,0:T(8,128)S(1)}, f32[64,8,128]{2,1,0:T(8,128)S(1)}, u32[]{:S(2)}, u32[]{:S(2)}) collective-permute-start(f32[64,8,128]{2,1,0:T(8,128)S(1)} %chunk.6.refs_4_), channel_id=1, source_target_pairs={{0,12},{4,8},{8,4},{12,0},{1,13},{5,9},{9,5},{13,1},{2,14},{6,10},... | collective-permute-start | bytes 786440 | tf_op jit(solution)/shard_map/ppermute | solution.py:17
  32.8 16.2 %copy-start = (f32[64,32]{0,1:T(8,128)S(1)}, f32[64,32]{0,1:T(8,128)}, u32[]{:S(2)}) copy-start(f32[64,32]{0,1:T(8,128)} %param.7) | copy-start | bytes 24580
  50.0 1.2 %collective-permute-start.12 = (f32[64,32]{1,0:T(8,128)S(1)}, f32[64,32]{1,0:T(8,128)S(1)}, u32[]{:S(2)}, u32[]{:S(2)}) collective-permute-start(f32[64,32]{1,0:T(8,128)S(1)} %gram.1), channel_id=1, source_target_pairs={{0,1},{1,0},{2,3},{3,2},{4,5},{5,4},{6,7},{7,6},{8,9},{9,8},{10,11... | collective-permute-start | bytes 24584 | tf_op jit(solution)/shard_map/ppermute | solution.py:17
  51.2 3.9 %collective-permute-start.13 = (f32[64,32]{1,0:T(8,128)S(1)}, f32[64,32]{1,0:T(8,128)S(1)}, u32[]{:S(2)}, u32[]{:S(2)}) collective-permute-start(f32[64,32]{1,0:T(8,128)S(1)} %add.34), channel_id=1, source_target_pairs={{0,2},{2,0},{1,3},{3,1},{4,6},{6,4},{5,7},{7,5},{8,10},{10,8},{9,1... | collective-permute-start | bytes 24584 | tf_op jit(solution)/shard_map/ppermute | solution.py:17
  55.2 7.0 %collective-permute-start.16 = (f32[64,32]{1,0:T(8,128)S(1)}, f32[64,32]{1,0:T(8,128)S(1)}, u32[]{:S(2)}, u32[]{:S(2)}) collective-permute-start(f32[64,32]{1,0:T(8,128)S(1)} %add.35.refs_0_), channel_id=1, source_target_pairs={{0,12},{4,8},{8,4},{12,0},{1,13},{5,9},{9,5},{13,1},{2,14},{6,10},... | collective-permute-start | bytes 24584 | tf_op jit(solution)/shard_map/ppermute | solution.py:17
  57.6 5.8 %collective-permute-start.15 = (f32[64,32]{1,0:T(8,128)S(1)}, f32[64,32]{1,0:T(8,128)S(1)}, u32[]{:S(2)}, u32[]{:S(2)}) collective-permute-start(f32[64,32]{1,0:T(8,128)S(1)} %add.35.refs_0_), channel_id=1, source_target_pairs={{0,4},{4,0},{8,12},{12,8},{1,5},{5,1},{9,13},{13,9},{2,6},{6,2},{1... | collective-permute-start | bytes 24584 | tf_op jit(solution)/shard_map/ppermute | solution.py:17
  61.5 4.8 %collective-permute-start.14 = (f32[64,32]{1,0:T(8,128)S(1)}, f32[64,32]{1,0:T(8,128)S(1)}, u32[]{:S(2)}, u32[]{:S(2)}) collective-permute-start(f32[64,32]{1,0:T(8,128)S(1)} %add.35.refs_0_), channel_id=1, source_target_pairs={{0,8},{4,12},{8,0},{12,4},{1,9},{5,13},{9,1},{13,5},{2,10},{6,14},... | collective-permute-start | bytes 24584 | tf_op jit(solution)/shard_map/ppermute | solution.py:17
  68.2 10.4 %collective-permute-start.17 = (f32[4,8,8,128]{3,2,1,0:T(8,128)S(1)}, f32[4,8,8,128]{3,2,1,0:T(8,128)S(1)}, u32[]{:S(2)}, u32[]{:S(2)}) collective-permute-start(f32[4,8,8,128]{3,2,1,0:T(8,128)S(1)} %get-tuple-element.17), channel_id=1, source_target_pairs={{0,8},{4,12},{8,0},{12,4},{1,9},{5,13},{9,1},{13,5},{2,10},{6,14},... | collective-permute-start | bytes 393224 | tf_op jit(solution)/shard_map/ppermute | solution.py:17
  68.7 9.9 %collective-permute-start.18 = (f32[4,8,8,128]{3,2,1,0:T(8,128)S(1)}, f32[4,8,8,128]{3,2,1,0:T(8,128)S(1)}, u32[]{:S(2)}, u32[]{:S(2)}) collective-permute-start(f32[4,8,8,128]{3,2,1,0:T(8,128)S(1)} %get-tuple-element.18), channel_id=1, source_target_pairs={{0,4},{4,0},{8,12},{12,8},{1,5},{5,1},{9,13},{13,9},{2,6},{6,2},{1... | collective-permute-start | bytes 393224 | tf_op jit(solution)/shard_map/ppermute | solution.py:17
  70.4 8.2 %collective-permute-start.19 = (f32[4,8,8,128]{3,2,1,0:T(8,128)S(1)}, f32[4,8,8,128]{3,2,1,0:T(8,128)S(1)}, u32[]{:S(2)}, u32[]{:S(2)}) collective-permute-start(f32[4,8,8,128]{3,2,1,0:T(8,128)S(1)} %get-tuple-element.19), channel_id=1, source_target_pairs={{0,12},{4,8},{8,4},{12,0},{1,13},{5,9},{9,5},{13,1},{2,14},{6,10},... | collective-permute-start | bytes 393224 | tf_op jit(solution)/shard_map/ppermute | solution.py:17

commit v7 on v6

--- a/solution.py
+++ b/solution.py
@@ -51,12 +51,7 @@
     for other in sums[:-1]:
         mine = mine + other
     mine = sum_over_gy(mine)
-    pieces = [None] * (count * cores)
-    for z in [*steps(count), 0]:
-        pieces[z * cores] = swap(mine, "gz", z) if z else mine
-        for v in steps(cores):
-            pieces[z * cores + v] = swap(pieces[z * cores], "vert", v)
-    return pieces
+    return [mine] + [swap(mine, ("gz", "vert"), k) for k in range(1, count * cores)]
 
 
 def dims(left, right):
@@ -167,45 +162,44 @@
     return whole[...]
 
 
-def chunk_kernel(scale, step, me_ref, here_ref, field_ref, *refs):
-    *piece_refs, _, out_ref, whole = refs
-    sketch = gather_sketch(scale, me_ref, piece_refs, whole)
-    width, cells = sketch.shape
-    rows, share, _ = out_ref.shape
+def chunk_kernel(scale, step, many, here_ref, field_ref, *refs):
+    piece_refs, out_ref = refs[:many], refs[-1]
+    sketch = jnp.concatenate([ref[...] for ref in piece_refs], axis=0) * scale
+    count = sketch.shape[0]
+    rows, _, cells = field_ref.shape
+    share = out_ref.shape[1] // rows
     start = pl.multiple_of((here_ref[0] ^ step) * share, share)
     high, low = halves(field_ref[:, pl.ds(start, share), :].reshape(rows * share, cells))
     sketch_high, sketch_low = halves(sketch)
-    both = mxu(high, jnp.concatenate([sketch_high, sketch_low], axis=0), dims(1, 1))
-    raw = both[:, :width] + (both[:, width:] + mxu(low, sketch_high, dims(1, 1)))
-    out_ref[...] = raw.reshape(rows, share, width)
-
-
-def field_chunk(scale, step, places, field, pieces, share, after):
-    width, cells = pieces[0].shape[0] * len(pieces), field.shape[2]
-    scratch = [pltpu.VMEM((width, cells), jnp.float32)]
-    kernel = functools.partial(chunk_kernel, scale, step)
-    shape = (field.shape[0], share, width)
-    return kernel_call(kernel, "chunk", shape, places, [field] + pieces + [after], scratch)
-
-
-def lift_kernel(planes, inverse_ref, chunk_ref, *refs):
+    both = mxu(jnp.concatenate([sketch_high, sketch_low], axis=0), high, dims(1, 1))
+    out_ref[...] = both[:count] + (both[count:] + mxu(sketch_high, low, dims(1, 1)))
+
+
+def field_chunk(scale, step, here, field, pieces, share, after):
+    kernel = functools.partial(chunk_kernel, scale, step, len(pieces))
+    shape = (sum(piece.shape[0] for piece in pieces), field.shape[0] * share)
+    return kernel_call(kernel, "chunk", shape, [here], [field] + pieces + after)
+
+
+def lift_kernel(planes, share, count, inverse_ref, *refs):
     out_ref = refs[-1]
-    rows, share, width = chunk_ref.shape
     inv_high, inv_low = halves(inverse_ref[...])
-    high, low = halves(chunk_ref[...].reshape(rows * share, width))
-    both = mxu(high, jnp.concatenate([inv_high, inv_low], axis=0), dims(1, 1))
-    value = both[:, :width] + (both[:, width:] + mxu(low, inv_high, dims(1, 1)))
-    value = jnp.swapaxes(value.reshape(planes, rows // planes, share, width), 1, 2)
+    width = inv_high.shape[1]
+    high, low = halves(jnp.concatenate([ref[...] for ref in refs[:count]], axis=0))
+    both = mxu(high, jnp.concatenate([inv_high, inv_low], axis=1), dims(0, 0))
+    value = both[:, :width] + (both[:, width:] + mxu(low, inv_high, dims(0, 0)))
+    value = jnp.swapaxes(value.reshape(planes, out_ref.shape[0], share, width), 1, 2)
     for v in range(planes):
         for z in range(share):
             at = (v * share + z) * width
             out_ref[:, at:at + width] = value[v, z]
 
 
-def lift(planes, inverse, chunk, after):
-    rows, share, width = chunk.shape
-    shape = (rows // planes, planes * share * width)
-    return kernel_call(functools.partial(lift_kernel, planes), "lift", shape, [], [inverse, chunk] + after)
+def lift(planes, share, inverse, chunk, after):
+    samples, width = chunk[0].shape[1], inverse.shape[1]
+    shape = (samples // (planes * share), planes * share * width)
+    kernel = functools.partial(lift_kernel, planes, share, len(chunk))
+    return kernel_call(kernel, "lift", shape, [], [inverse] + chunk + after)
 
 
 def gram_kernel(me_ref, omega_ref, *refs):
@@ -304,29 +298,33 @@
 
 
 def factor_x_kernel(scale, rank_ref, me_ref, *refs):
-    *piece_refs, out_ref, sketch_ref = refs
+    *piece_refs, out_ref, sketch_ref, inverse_ref = refs
     sketch_t = gather_sketch(scale, me_ref, piece_refs, sketch_ref)
-    eliminate(exact(sketch_t, sketch_t, dims(1, 1)), sketch_t.shape[0], rank_ref[0], out_ref)
+    eliminate(exact(sketch_t, sketch_t, dims(1, 1)), sketch_t.shape[0], rank_ref[0], inverse_ref)
+    inverse_ref[...] = inverse_ref[...].T
+    share = piece_refs[0].shape[0]
+    for k in range(len(piece_refs)):
+        start = pl.multiple_of((me_ref[0] ^ k) * share, share)
+        out_ref[k * share:(k + 1) * share, :] = inverse_ref[pl.ds(start, share), :]
 
 
 def inverse_factor_x(scale, rank, me, pieces):
     width = pieces[0].shape[0] * len(pieces)
-    scratch = [pltpu.VMEM((width, pieces[0].shape[1]), jnp.float32)]
+    scratch = [pltpu.VMEM((width, pieces[0].shape[1]), jnp.float32), pltpu.VMEM((width, width), jnp.float32)]
     kernel = functools.partial(factor_x_kernel, scale)
     return kernel_call(kernel, "factor_x", (width, width), [rank, me], pieces, scratch)
 
 
-def apply_kernel(scale, me_ref, inverse_ref, *refs):
-    *piece_refs, out_ref, whole = refs
-    sketch_t = gather_sketch(scale, me_ref, piece_refs, whole)
-    out_ref[...] = exact(sketch_t, inverse_ref[...], dims(0, 1))
-
-
-def make_factor_x(scale, me, inverse, pieces):
-    width, cells = inverse.shape[0], pieces[0].shape[1]
-    scratch = [pltpu.VMEM((width, cells), jnp.float32)]
+def apply_kernel(scale, inverse_ref, *refs):
+    *piece_refs, out_ref = refs
+    sketch = jnp.concatenate([ref[...] for ref in piece_refs], axis=0) * scale
+    out_ref[...] = exact(sketch, inverse_ref[...], dims(0, 0))
+
+
+def make_factor_x(scale, inverse, pieces):
+    shape = (pieces[0].shape[1], inverse.shape[1])
     kernel = functools.partial(apply_kernel, scale)
-    return kernel_call(kernel, "apply", (cells, width), [me], [inverse] + pieces, scratch, whole_out=True)
+    return kernel_call(kernel, "apply", shape, [], [inverse] + pieces, whole_out=True)
 
 
 def factor_y_kernel(divisor, rank_ref, *refs):
@@ -369,36 +367,44 @@
     share_k = ranks_y // n_gy
     field_z = field_v.reshape(planes * rows_y, rows_z, cells_x)
     tiled = share_z % 8 == 0 and share_k % 8 == 0
+    order = steps(n_gy)
+    chunks = [[] for _ in range(n_gy)]
     if tiled:
-        cut = lambda s, after: field_chunk(scale, s, [quarter, here], field_z, pieces, share_z, after)
+        after, ahead = [], []
+        for s in order:
+            if s & 2:
+                part = field_chunk(scale, s, here, field_z, pieces[:1], share_z, after)
+                after = [part]
+                chunks[s].append(swap(part, "gy", s))
+                ahead.append(chunks[s][0])
+        for s in [2, 1, 3] + [0]:
+            wait = ahead if s == 3 else []
+            part = field_chunk(scale, s, here, field_z, pieces[len(chunks[s]):], share_z, after + wait)
+            after = [part]
+            chunks[s].append(swap(part, "gy", s) if s else part)
     else:
-        sketch_t = jnp.take(jnp.stack(pieces), quarter ^ jnp.arange(n_quarter), axis=0)
-        sketch_t = sketch_t.reshape(ranks_x, cells_x) * scale
-        raw = lax.dot_general(flat, sketch_t, dims(1, 1), precision=HIGH)
+        sketch = jnp.concatenate(pieces, axis=0) * scale
+        raw = lax.dot_general(flat, sketch, dims(1, 1), precision=HIGH)
         raw = raw.reshape(planes * rows_y, rows_z, ranks_x)
-        cut = lambda s, after: lax.dynamic_slice_in_dim(raw, (gy ^ s) * share_z, share_z, 1)
-    chunks = [None] * n_gy
-    after = pieces[0]
-    for s in steps(n_gy):
-        after = cut(s, after)
-        chunks[s] = swap(after, "gy", s)
-    chunks[0] = cut(0, after)
+        for s in order + [0]:
+            chunk = lax.dynamic_slice_in_dim(raw, (gy ^ s) * share_z, share_z, 1)
+            chunks[s] = swap(chunk, "gy", s) if s else chunk
 
     inverse_x = inverse_factor_x(scale, rank_x, quarter, pieces)
-    factor_x = make_factor_x(scale, quarter, inverse_x, pieces)
+    factor_x = make_factor_x(scale, inverse_x, pieces)
 
     if tiled:
         slabs = [None] * n_gy
         after = []
-        for s in [0] + steps(n_gy):
-            slabs[s] = lift(planes, inverse_x, chunks[s], after)
+        for s in [0] + order:
+            slabs[s] = lift(planes, share_z, inverse_x, chunks[s], after)
             after = [slabs[s]]
         scratch = [pltpu.VMEM((all_rows_y, all_rows_y), jnp.float32)] * 2
         shape = (all_rows_y, ranks_y)
         part_y = kernel_call(gram_kernel, "gram", shape, [here], [omega_y.T] + slabs, scratch)
     else:
         spread = jnp.stack(chunks).reshape(-1, ranks_x)
-        spread = lax.dot_general(spread, inverse_x, dims(1, 1), precision=HIGH)
+        spread = lax.dot_general(spread, inverse_x, dims(1, 0), precision=HIGH)
         spread = spread.reshape(n_gy, planes, rows_y, share_z, ranks_x)
         local_gram_y = jnp.einsum("gvazr,hvbzr->gahb", spread, spread, precision=HIGH)
         local_gram_y = local_gram_y.reshape(all_rows_y, all_rows_y)

time: 79.6 us -> 76.4 us (0.960)
  waiting for transfers between devices: 32.1 us -> 24.8 us
  starting transfers between devices: 26.6 us -> 29.7 us
  Pallas kernels: 17.8 us -> 18.8 us
    ppermute x20 -> x22, waiting for transfers between devices: 32.1 us -> 24.8 us  [swap(): return lax.ppermute(value, axes, [(i, i ^ step) for i in range(count)])]
    ppermute x20 -> x22, starting transfers between devices: 26.6 us -> 29.7 us  [swap(): return lax.ppermute(value, axes, [(i, i ^ step) for i in range(count)])]
    pallas_call x13 -> x15, Pallas kernels: 13.1 us -> 14.1 us  [kernel_call(): pl.pallas_call(body, in_specs=[SMEM] * len(scalars) + [VMEM] * len(values...]
  transfers between devices with their start and end apart: 20 -> 22, of which waited for: 14 -> 13; matrix products, arithmetic and copies ran while one was open for 1% -> 1% of each run, Pallas kernels for 12% -> 14%
where the time goes in v7:
time: 76.4 us; the launch traced here: 76.2 us
  starting transfers between devices  29.7 us (39%)
  waiting for transfers between devices  24.8 us (32%)
  Pallas kernels  18.8 us (25%)
  between operations  2.11 us (3%)
    ppermute x22, starting transfers between devices, swap(): return lax.ppermute(value, axes, [(i, i ^ step) for i in range(count)])  29.7 us
    ppermute x22, waiting for transfers between devices, swap(): return lax.ppermute(value, axes, [(i, i ^ step) for i in range(count)])  24.8 us
    pallas_call x15, Pallas kernels, kernel_call(): pl.pallas_call(body, in_specs=[SMEM] * len(scalars) + [VMEM] * len(values...  14.1 us
    pallas_call x1, Pallas kernels, sketch_parts(): pl.pallas_call(sketch_kernel, in_specs=[SMEM, SMEM, far, far], out_specs=...  3.85 us
  transfers between devices with their start and end apart: 22, of which 13 were waited for; matrix products, arithmetic and copies ran while one was open for 1% of the time, Pallas kernels for 14%

profile of v7, /device:TPU:0, one launch (start us, length us, event | category | flops | bytes accessed | tf_op | source)
XLA Modules:
  0.0 76.2 jit_solution(2475423881305926294)
XLA Ops:
  0.6 3.9 %sketch.1 = (f32[2048,512]{1,0:T(8,128)S(1)}, f32[32,512]{1,0:T(8,128)S(1)}, f32[32,512]{1,0:T(8,128)S(1)}, f32[32,512]{1,0:T(8,128)S(1)}, f32[32,512]{1,0:T(8,128)S(1)}) custom-call(s32[1]{0:T(128)} %bitcast.2.me_ref, s32[1]{0:T(128)} %bitcast.here_ref.me_ref, f32[2048,512]{1,0:T(8,128)} %bitcast.12, f32[512,128]{1,0:T(8,128)} %omega_hbm.1), custom_call_target="tpu_custom_call" | custom-call | tf_op jit(solution)/shard_map/sketch/pallas_call | solution.py:140
  4.5 0.5 collective-permute-start.1
  5.0 0.1 collective-permute-start
  5.1 0.8 %collective-permute-done.1 = f32[32,512]{1,0:T(8,128)S(1)} collective-permute-done((f32[32,512]{1,0:T(8,128)S(1)}, f32[32,512]{1,0:T(8,128)S(1)}, u32[]{:S(2)}, u32[]{:S(2)}) %collective-permute-start.1) | collective-permute-done | bytes 65568 | tf_op jit(solution)/shard_map/ppermute | solution.py:17
  5.9 2.9 %collective-permute-start.2 = (f32[32,512]{1,0:T(8,128)S(1)}, f32[32,512]{1,0:T(8,128)S(1)}, u32[]{:S(2)}, u32[]{:S(2)}) collective-permute-start(f32[32,512]{1,0:T(8,128)S(1)} %add.29), channel_id=1, source_target_pairs={{0,2},{2,0},{1,3},{3,1},{4,6},{6,4},{5,7},{7,5},{8,10},{10,8},{9,1... | collective-permute-start | bytes 196616 | tf_op jit(solution)/shard_map/ppermute | solution.py:17
  8.8 0.0 collective-permute-done
  8.8 2.4 %collective-permute-done.2 = f32[32,512]{1,0:T(8,128)S(1)} collective-permute-done((f32[32,512]{1,0:T(8,128)S(1)}, f32[32,512]{1,0:T(8,128)S(1)}, u32[]{:S(2)}, u32[]{:S(2)}) %collective-permute-start.2) | collective-permute-done | bytes 65568 | tf_op jit(solution)/shard_map/ppermute | solution.py:17
  11.3 4.0 %collective-permute-start.5 = (f32[32,512]{1,0:T(8,128)S(1)}, f32[32,512]{1,0:T(8,128)S(1)}, u32[]{:S(2)}, u32[]{:S(2)}) collective-permute-start(f32[32,512]{1,0:T(8,128)S(1)} %add_add_fusion.1), channel_id=1, source_target_pairs={{0,12},{4,8},{8,4},{12,0},{1,13},{5,9},{9,5},{13,1},{2,14},{6,10},... | collective-permute-start | bytes 196616 | tf_op jit(solution)/shard_map/ppermute | solution.py:17
  15.3 0.0 collective-permute-start.4
  15.3 0.6 collective-permute-start.3
  15.9 1.8 %collective-permute-done.5 = f32[32,512]{1,0:T(8,128)S(1)} collective-permute-done((f32[32,512]{1,0:T(8,128)S(1)}, f32[32,512]{1,0:T(8,128)S(1)}, u32[]{:S(2)}, u32[]{:S(2)}) %collective-permute-start.5) | collective-permute-done | bytes 65568 | tf_op jit(solution)/shard_map/ppermute | solution.py:17
  17.7 1.9 %collective-permute-done.4 = f32[32,512]{1,0:T(8,128)S(1)} collective-permute-done((f32[32,512]{1,0:T(8,128)S(1)}, f32[32,512]{1,0:T(8,128)S(1)}, u32[]{:S(2)}, u32[]{:S(2)}) %collective-permute-start.4) | collective-permute-done | bytes 65568 | tf_op jit(solution)/shard_map/ppermute | solution.py:17
  19.6 0.9 %collective-permute-done.3 = f32[32,512]{1,0:T(8,128)S(1)} collective-permute-done((f32[32,512]{1,0:T(8,128)S(1)}, f32[32,512]{1,0:T(8,128)S(1)}, u32[]{:S(2)}, u32[]{:S(2)}) %collective-permute-start.3) | collective-permute-done | bytes 65568 | tf_op jit(solution)/shard_map/ppermute | solution.py:17
  20.5 0.1 collective-permute-start.8
  20.6 1.6 %collective-permute-start.7 = (f32[32,512]{1,0:T(8,128)S(1)}, f32[32,512]{1,0:T(8,128)S(1)}, u32[]{:S(2)}, u32[]{:S(2)}) collective-permute-start(f32[32,512]{1,0:T(8,128)S(1)} %add_add_fusion.refs_0_), channel_id=1, source_target_pairs={{0,2},{1,3},{2,0},{3,1},{4,6},{5,7},{6,4},{7,5},{8,10},{9,11},{10,... | collective-permute-start | bytes 196616 | tf_op jit(solution)/shard_map/ppermute | solution.py:17
  22.1 0.3 collective-permute-start.6
  22.4 0.4 chunk.6.refs_1_
  22.8 0.4 chunk.7.refs_3_
  23.3 1.7 %collective-permute-start.9 = (f32[32,512]{1,0:T(8,128)S(1)}, f32[32,512]{1,0:T(8,128)S(1)}, u32[]{:S(2)}, u32[]{:S(2)}) collective-permute-start(f32[32,512]{1,0:T(8,128)S(1)} %chunk.6.refs_1_), channel_id=1, source_target_pairs={{0,8},{4,12},{8,0},{12,4},{1,9},{5,13},{9,1},{13,5},{2,10},{6,14},... | collective-permute-start | bytes 196616 | tf_op jit(solution)/shard_map/ppermute | solution.py:17
  25.0 2.7 %collective-permute-start.10 = (f32[32,512]{1,0:T(8,128)S(1)}, f32[32,512]{1,0:T(8,128)S(1)}, u32[]{:S(2)}, u32[]{:S(2)}) collective-permute-start(f32[32,512]{1,0:T(8,128)S(1)} %chunk.7.refs_3_), channel_id=1, source_target_pairs={{0,12},{4,8},{8,4},{12,0},{1,13},{5,9},{9,5},{13,1},{2,14},{6,10},... | collective-permute-start | bytes 196616 | tf_op jit(solution)/shard_map/ppermute | solution.py:17
  27.7 0.0 collective-permute-done.8.refs_3_.refs_2_
  27.7 0.0 collective-permute-done.7.refs_2_.refs_1_
  27.7 0.0 collective-permute-done.6.refs_1_.refs_0_
  27.7 0.5 chunk.8.refs_4_
  28.2 0.5 chunk.9.refs_3_
  28.7 0.7 collective-permute-start.11
  29.4 1.7 %collective-permute-start.12 = (f32[96,512]{1,0:T(8,128)S(1)}, f32[96,512]{1,0:T(8,128)S(1)}, u32[]{:S(2)}, u32[]{:S(2)}) collective-permute-start(f32[96,512]{1,0:T(8,128)S(1)} %chunk.8.refs_4_), channel_id=1, source_target_pairs={{0,8},{4,12},{8,0},{12,4},{1,9},{5,13},{9,1},{13,5},{2,10},{6,14},... | collective-permute-start | bytes 589832 | tf_op jit(solution)/shard_map/ppermute | solution.py:17
  31.1 0.3 collective-permute-done.10.refs_5_.refs_0_
  31.4 0.0 collective-permute-done.9.refs_4_.refs_0_
  31.4 0.5 chunk.10.refs_4_
  31.9 2.5 %collective-permute-start.13 = (f32[96,512]{1,0:T(8,128)S(1)}, f32[96,512]{1,0:T(8,128)S(1)}, u32[]{:S(2)}, u32[]{:S(2)}) collective-permute-start(f32[96,512]{1,0:T(8,128)S(1)} %chunk.10.refs_4_), channel_id=1, source_target_pairs={{0,12},{4,8},{8,4},{12,0},{1,13},{5,9},{9,5},{13,1},{2,14},{6,10},... | collective-permute-start | bytes 589832 | tf_op jit(solution)/shard_map/ppermute | solution.py:17
  35.1 0.0 copy-start
  35.1 0.5 chunk.11.refs_0_
  35.6 6.1 %factor_x.1.inverse_ref = f32[128,128]{1,0:T(8,128)S(1)} custom-call(s32[1]{0:T(128)S(6)} %copy.9.rank_ref, s32[1]{0:T(128)} %bitcast.2.me_ref, f32[32,512]{1,0:T(8,128)S(1)} %add_add_fusion.refs_0_, f32[32,512]{1,0:T(8,128)S(1)} %collective-permute-done.6.refs_1_.refs_0_, f32[32,512]{1,0:T(8,128)S(1)} %collective-permute-done.7.refs_2_.refs_1_, ...), custom_call_target="tpu_custom_call" | custom-call | tf_op jit(solution)/shard_map/factor_x/pallas_call | solution.py:89
  41.8 0.3 lift.4.refs_2_.refs_0_
  42.1 4.4 %collective-permute-done.12.refs_1_ = f32[96,512]{1,0:T(8,128)S(1)} collective-permute-done((f32[96,512]{1,0:T(8,128)S(1)}, f32[96,512]{1,0:T(8,128)S(1)}, u32[]{:S(2)}, u32[]{:S(2)}) %collective-permute-start.12) | collective-permute-done | bytes 196640 | tf_op jit(solution)/shard_map/ppermute | solution.py:17
  46.4 0.3 lift.5.refs_1_.refs_2_
  46.7 0.0 collective-permute-done.11.refs_0_
  46.8 0.3 lift.6.refs_2_.refs_1_
  47.1 0.0 collective-permute-done.13.refs_1_
  47.1 0.3 lift.7.refs_3_
  47.4 0.0 copy-done
  47.4 1.0 %gram.1 = f32[64,32]{1,0:T(8,128)S(1)} custom-call(s32[1]{0:T(128)} %bitcast.here_ref.me_ref, f32[32,64]{1,0:T(8,128)S(1)} %bitcast.11, f32[16,4096]{1,0:T(8,128)S(1)} %lift.4.refs_2_.refs_0_, f32[16,4096]{1,0:T(8,128)S(1)} %lift.6.refs_2_.refs_1_, f32[16,4096]{1,0:T(8,128)S(1)} %lift.5.refs_1_.refs_2_, f32[16,4096]{1,0:T(8,128)S(1)} %lift.7.refs_3_), custom_call_target="tpu_custom_call" | custom-call | tf_op jit(solution)/shard_map/gram/pallas_call | solution.py:89
  48.4 0.0 collective-permute-start.14
  48.4 1.2 %collective-permute-done.14 = f32[64,32]{1,0:T(8,128)S(1)} collective-permute-done((f32[64,32]{1,0:T(8,128)S(1)}, f32[64,32]{1,0:T(8,128)S(1)}, u32[]{:S(2)}, u32[]{:S(2)}) %collective-permute-start.14) | collective-permute-done | bytes 8224 | tf_op jit(solution)/shard_map/ppermute | solution.py:17
  49.6 1.1 %collective-permute-start.15 = (f32[64,32]{1,0:T(8,128)S(1)}, f32[64,32]{1,0:T(8,128)S(1)}, u32[]{:S(2)}, u32[]{:S(2)}) collective-permute-start(f32[64,32]{1,0:T(8,128)S(1)} %add.34), channel_id=1, source_target_pairs={{0,2},{2,0},{1,3},{3,1},{4,6},{6,4},{5,7},{7,5},{8,10},{10,8},{9,1... | collective-permute-start | bytes 24584 | tf_op jit(solution)/shard_map/ppermute | solution.py:17
  50.7 2.8 %collective-permute-done.15 = f32[64,32]{1,0:T(8,128)S(1)} collective-permute-done((f32[64,32]{1,0:T(8,128)S(1)}, f32[64,32]{1,0:T(8,128)S(1)}, u32[]{:S(2)}, u32[]{:S(2)}) %collective-permute-start.15) | collective-permute-done | bytes 8224 | tf_op jit(solution)/shard_map/ppermute | solution.py:17
  53.5 1.8 %collective-permute-start.18 = (f32[64,32]{1,0:T(8,128)S(1)}, f32[64,32]{1,0:T(8,128)S(1)}, u32[]{:S(2)}, u32[]{:S(2)}) collective-permute-start(f32[64,32]{1,0:T(8,128)S(1)} %add.35.refs_0_), channel_id=1, source_target_pairs={{0,12},{4,8},{8,4},{12,0},{1,13},{5,9},{9,5},{13,1},{2,14},{6,10},... | collective-permute-start | bytes 24584 | tf_op jit(solution)/shard_map/ppermute | solution.py:17
  55.3 2.9 %collective-permute-start.17 = (f32[64,32]{1,0:T(8,128)S(1)}, f32[64,32]{1,0:T(8,128)S(1)}, u32[]{:S(2)}, u32[]{:S(2)}) collective-permute-start(f32[64,32]{1,0:T(8,128)S(1)} %add.35.refs_0_), channel_id=1, source_target_pairs={{0,4},{4,0},{8,12},{12,8},{1,5},{5,1},{9,13},{13,9},{2,6},{6,2},{1... | collective-permute-start | bytes 24584 | tf_op jit(solution)/shard_map/ppermute | solution.py:17
  58.2 0.0 collective-permute-start.16
  58.9 0.7 collective-permute-done.18.refs_3_
  59.5 0.6 collective-permute-done.17.refs_2_
  60.1 2.9 %collective-permute-done.16.refs_1_ = f32[64,32]{1,0:T(8,128)S(1)} collective-permute-done((f32[64,32]{1,0:T(8,128)S(1)}, f32[64,32]{1,0:T(8,128)S(1)}, u32[]{:S(2)}, u32[]{:S(2)}) %collective-permute-start.16) | collective-permute-done | bytes 8224 | tf_op jit(solution)/shard_map/ppermute | solution.py:17
  63.0 1.4 %factor_y.1.factor_ref = f32[64,32]{1,0:T(8,128)S(1)} custom-call(s32[1]{0:T(128)S(6)} %copy.10.rank_ref, f32[64,32]{1,0:T(8,128)S(1)} %add.35.refs_0_, f32[64,32]{1,0:T(8,128)S(1)} %collective-permute-done.16.refs_1_, f32[64,32]{1,0:T(8,128)S(1)} %collective-permute-done.17.refs_2_, f32[64,32]{1,0:T(8,128)S(1)} %collective-permute-done.18.refs_3_), custom_call_target="tpu_custom_call" | custom-call | tf_op jit(solution)/shard_map/factor_y/pallas_call | solution.py:89
  64.4 0.5 mix.1
  64.9 0.4 collective-permute-start.19
  65.4 1.8 %collective-permute-start.20 = (f32[4,8,8,128]{3,2,1,0:T(8,128)S(1)}, f32[4,8,8,128]{3,2,1,0:T(8,128)S(1)}, u32[]{:S(2)}, u32[]{:S(2)}) collective-permute-start(f32[4,8,8,128]{3,2,1,0:T(8,128)S(1)} %get-tuple-element.18), channel_id=1, source_target_pairs={{0,4},{4,0},{8,12},{12,8},{1,5},{5,1},{9,13},{13,9},{2,6},{6,2},{1... | collective-permute-start | bytes 393224 | tf_op jit(solution)/shard_map/ppermute | solution.py:17
  67.2 2.2 %collective-permute-start.21 = (f32[4,8,8,128]{3,2,1,0:T(8,128)S(1)}, f32[4,8,8,128]{3,2,1,0:T(8,128)S(1)}, u32[]{:S(2)}, u32[]{:S(2)}) collective-permute-start(f32[4,8,8,128]{3,2,1,0:T(8,128)S(1)} %get-tuple-element.19), channel_id=1, source_target_pairs={{0,12},{4,8},{8,4},{12,0},{1,13},{5,9},{9,5},{13,1},{2,14},{6,10},... | collective-permute-start | bytes 393224 | tf_op jit(solution)/shard_map/ppermute | solution.py:17
  69.4 1.1 %apply.1 = f32[512,128]{1,0:T(8,128)} custom-call(f32[128,128]{1,0:T(8,128)S(1)} %factor_x.1.inverse_ref, f32[32,512]{1,0:T(8,128)S(1)} %add_add_fusion.refs_0_, f32[32,512]{1,0:T(8,128)S(1)} %collective-permute-done.6.refs_1_.refs_0_, f32[32,512]{1,0:T(8,128)S(1)} %collective-permute-done.7.refs_2_.refs_1_, f32[32,512]{1,0:T(8,128)S(1)} %collective-permute-done.8.refs_3_.refs_2_), custom_call_target="tpu_custom_call" | custom-call | tf_op jit(solution)/shard_map/apply/pallas_call | solution.py:89
  70.5 0.7 copy.8
  71.2 4.2 %collective-permute-done.19.refs_0_ = f32[4,8,8,128]{3,2,1,0:T(8,128)S(1)} collective-permute-done((f32[4,8,8,128]{3,2,1,0:T(8,128)S(1)}, f32[4,8,8,128]{3,2,1,0:T(8,128)S(1)}, u32[]{:S(2)}, u32[]{:S(2)}) %collective-permute-start.19) | collective-permute-done | bytes 131104 | tf_op jit(solution)/shard_map/ppermute | solution.py:17
  75.4 0.0 collective-permute-done.20.refs_1_
  75.4 0.0 collective-permute-done.21.refs_2_
  75.4 0.8 %place.1 = f32[4,8,32,128]{3,2,1,0:T(8,128)} custom-call(s32[1]{0:T(128)} %bitcast.here_ref.me_ref, f32[4,8,8,128]{3,2,1,0:T(8,128)S(1)} %collective-permute-done.19.refs_0_, f32[4,8,8,128]{3,2,1,0:T(8,128)S(1)} %collective-permute-done.20.refs_1_, f32[4,8,8,128]{3,2,1,0:T(8,128)S(1)} %collective-permute-done.21.refs_2_, ...), custom_call_target="tpu_custom_call" | custom-call | tf_op jit(solution)/shard_map/place/pallas_call | solution.py:251
  (5 shorter events, 0.1 us)
Async XLA Ops:
  4.5 1.4 %collective-permute-start.1 = (f32[32,512]{1,0:T(8,128)S(1)}, f32[32,512]{1,0:T(8,128)S(1)}, u32[]{:S(2)}, u32[]{:S(2)}) collective-permute-start(f32[32,512]{1,0:T(8,128)S(1)} %get-tuple-element.15), channel_id=1, source_target_pairs={{0,1},{1,0},{2,3},{3,2},{4,5},{5,4},{6,7},{7,6},{8,9},{9,8},{10,11... | collective-permute-start | bytes 196616 | tf_op jit(solution)/shard_map/ppermute | solution.py:17
  5.0 3.8 %collective-permute-start = (f32[32,512]{1,0:T(8,128)S(1)}, f32[32,512]{1,0:T(8,128)S(1)}, u32[]{:S(2)}, u32[]{:S(2)}) collective-permute-start(f32[32,512]{1,0:T(8,128)S(1)} %get-tuple-element.13), channel_id=1, source_target_pairs={{0,1},{1,0},{2,3},{3,2},{4,5},{5,4},{6,7},{7,6},{8,9},{9,8},{10,11... | collective-permute-start | bytes 196616 | tf_op jit(solution)/shard_map/ppermute | solution.py:17
  5.9 5.3 %collective-permute-start.2 = (f32[32,512]{1,0:T(8,128)S(1)}, f32[32,512]{1,0:T(8,128)S(1)}, u32[]{:S(2)}, u32[]{:S(2)}) collective-permute-start(f32[32,512]{1,0:T(8,128)S(1)} %add.29), channel_id=1, source_target_pairs={{0,2},{2,0},{1,3},{3,1},{4,6},{6,4},{5,7},{7,5},{8,10},{10,8},{9,1... | collective-permute-start | bytes 196616 | tf_op jit(solution)/shard_map/ppermute | solution.py:17
  11.3 6.4 %collective-permute-start.5 = (f32[32,512]{1,0:T(8,128)S(1)}, f32[32,512]{1,0:T(8,128)S(1)}, u32[]{:S(2)}, u32[]{:S(2)}) collective-permute-start(f32[32,512]{1,0:T(8,128)S(1)} %add_add_fusion.1), channel_id=1, source_target_pairs={{0,12},{4,8},{8,4},{12,0},{1,13},{5,9},{9,5},{13,1},{2,14},{6,10},... | collective-permute-start | bytes 196616 | tf_op jit(solution)/shard_map/ppermute | solution.py:17
  15.3 4.3 %collective-permute-start.4 = (f32[32,512]{1,0:T(8,128)S(1)}, f32[32,512]{1,0:T(8,128)S(1)}, u32[]{:S(2)}, u32[]{:S(2)}) collective-permute-start(f32[32,512]{1,0:T(8,128)S(1)} %add_add_fusion.1), channel_id=1, source_target_pairs={{0,4},{4,0},{8,12},{12,8},{1,5},{5,1},{9,13},{13,9},{2,6},{6,2},{1... | collective-permute-start | bytes 196616 | tf_op jit(solution)/shard_map/ppermute | solution.py:17
  15.3 5.2 %collective-permute-start.3 = (f32[32,512]{1,0:T(8,128)S(1)}, f32[32,512]{1,0:T(8,128)S(1)}, u32[]{:S(2)}, u32[]{:S(2)}) collective-permute-start(f32[32,512]{1,0:T(8,128)S(1)} %add_add_fusion.1), channel_id=1, source_target_pairs={{0,8},{4,12},{8,0},{12,4},{1,9},{5,13},{9,1},{13,5},{2,10},{6,14},... | collective-permute-start | bytes 196616 | tf_op jit(solution)/shard_map/ppermute | solution.py:17
  20.5 7.2 %collective-permute-start.8 = (f32[32,512]{1,0:T(8,128)S(1)}, f32[32,512]{1,0:T(8,128)S(1)}, u32[]{:S(2)}, u32[]{:S(2)}) collective-permute-start(f32[32,512]{1,0:T(8,128)S(1)} %add_add_fusion.refs_0_), channel_id=1, source_target_pairs={{0,3},{1,2},{2,1},{3,0},{4,7},{5,6},{6,5},{7,4},{8,11},{9,10},{10,... | collective-permute-start | bytes 196616 | tf_op jit(solution)/shard_map/ppermute | solution.py:17
  20.6 7.1 %collective-permute-start.7 = (f32[32,512]{1,0:T(8,128)S(1)}, f32[32,512]{1,0:T(8,128)S(1)}, u32[]{:S(2)}, u32[]{:S(2)}) collective-permute-start(f32[32,512]{1,0:T(8,128)S(1)} %add_add_fusion.refs_0_), channel_id=1, source_target_pairs={{0,2},{1,3},{2,0},{3,1},{4,6},{5,7},{6,4},{7,5},{8,10},{9,11},{10,... | collective-permute-start | bytes 196616 | tf_op jit(solution)/shard_map/ppermute | solution.py:17
  22.1 5.6 %collective-permute-start.6 = (f32[32,512]{1,0:T(8,128)S(1)}, f32[32,512]{1,0:T(8,128)S(1)}, u32[]{:S(2)}, u32[]{:S(2)}) collective-permute-start(f32[32,512]{1,0:T(8,128)S(1)} %add_add_fusion.refs_0_), channel_id=1, source_target_pairs={{0,1},{1,0},{2,3},{3,2},{4,5},{5,4},{6,7},{7,6},{8,9},{9,8},{10,11... | collective-permute-start | bytes 196616 | tf_op jit(solution)/shard_map/ppermute | solution.py:17
  23.3 8.1 %collective-permute-start.9 = (f32[32,512]{1,0:T(8,128)S(1)}, f32[32,512]{1,0:T(8,128)S(1)}, u32[]{:S(2)}, u32[]{:S(2)}) collective-permute-start(f32[32,512]{1,0:T(8,128)S(1)} %chunk.6.refs_1_), channel_id=1, source_target_pairs={{0,8},{4,12},{8,0},{12,4},{1,9},{5,13},{9,1},{13,5},{2,10},{6,14},... | collective-permute-start | bytes 196616 | tf_op jit(solution)/shard_map/ppermute | solution.py:17
  25.0 6.4 %collective-permute-start.10 = (f32[32,512]{1,0:T(8,128)S(1)}, f32[32,512]{1,0:T(8,128)S(1)}, u32[]{:S(2)}, u32[]{:S(2)}) collective-permute-start(f32[32,512]{1,0:T(8,128)S(1)} %chunk.7.refs_3_), channel_id=1, source_target_pairs={{0,12},{4,8},{8,4},{12,0},{1,13},{5,9},{9,5},{13,1},{2,14},{6,10},... | collective-permute-start | bytes 196616 | tf_op jit(solution)/shard_map/ppermute | solution.py:17
  28.7 18.0 %collective-permute-start.11 = (f32[128,512]{1,0:T(8,128)S(1)}, f32[128,512]{1,0:T(8,128)S(1)}, u32[]{:S(2)}, u32[]{:S(2)}) collective-permute-start(f32[128,512]{1,0:T(8,128)S(1)} %chunk.9.refs_3_), channel_id=1, source_target_pairs={{0,4},{4,0},{8,12},{12,8},{1,5},{5,1},{9,13},{13,9},{2,6},{6,2},{1... | collective-permute-start | bytes 786440 | tf_op jit(solution)/shard_map/ppermute | solution.py:17
  29.4 17.0 %collective-permute-start.12 = (f32[96,512]{1,0:T(8,128)S(1)}, f32[96,512]{1,0:T(8,128)S(1)}, u32[]{:S(2)}, u32[]{:S(2)}) collective-permute-start(f32[96,512]{1,0:T(8,128)S(1)} %chunk.8.refs_4_), channel_id=1, source_target_pairs={{0,8},{4,12},{8,0},{12,4},{1,9},{5,13},{9,1},{13,5},{2,10},{6,14},... | collective-permute-start | bytes 589832 | tf_op jit(solution)/shard_map/ppermute | solution.py:17
  31.9 15.1 %collective-permute-start.13 = (f32[96,512]{1,0:T(8,128)S(1)}, f32[96,512]{1,0:T(8,128)S(1)}, u32[]{:S(2)}, u32[]{:S(2)}) collective-permute-start(f32[96,512]{1,0:T(8,128)S(1)} %chunk.10.refs_4_), channel_id=1, source_target_pairs={{0,12},{4,8},{8,4},{12,0},{1,13},{5,9},{9,5},{13,1},{2,14},{6,10},... | collective-permute-start | bytes 589832 | tf_op jit(solution)/shard_map/ppermute | solution.py:17
  35.1 12.3 %copy-start = (f32[64,32]{0,1:T(8,128)S(1)}, f32[64,32]{0,1:T(8,128)}, u32[]{:S(2)}) copy-start(f32[64,32]{0,1:T(8,128)} %param.7) | copy-start | bytes 24580
  48.4 1.2 %collective-permute-start.14 = (f32[64,32]{1,0:T(8,128)S(1)}, f32[64,32]{1,0:T(8,128)S(1)}, u32[]{:S(2)}, u32[]{:S(2)}) collective-permute-start(f32[64,32]{1,0:T(8,128)S(1)} %gram.1), channel_id=1, source_target_pairs={{0,1},{1,0},{2,3},{3,2},{4,5},{5,4},{6,7},{7,6},{8,9},{9,8},{10,11... | collective-permute-start | bytes 24584 | tf_op jit(solution)/shard_map/ppermute | solution.py:17
  49.6 3.9 %collective-permute-start.15 = (f32[64,32]{1,0:T(8,128)S(1)}, f32[64,32]{1,0:T(8,128)S(1)}, u32[]{:S(2)}, u32[]{:S(2)}) collective-permute-start(f32[64,32]{1,0:T(8,128)S(1)} %add.34), channel_id=1, source_target_pairs={{0,2},{2,0},{1,3},{3,1},{4,6},{6,4},{5,7},{7,5},{8,10},{10,8},{9,1... | collective-permute-start | bytes 24584 | tf_op jit(solution)/shard_map/ppermute | solution.py:17
  53.5 6.0 %collective-permute-start.18 = (f32[64,32]{1,0:T(8,128)S(1)}, f32[64,32]{1,0:T(8,128)S(1)}, u32[]{:S(2)}, u32[]{:S(2)}) collective-permute-start(f32[64,32]{1,0:T(8,128)S(1)} %add.35.refs_0_), channel_id=1, source_target_pairs={{0,12},{4,8},{8,4},{12,0},{1,13},{5,9},{9,5},{13,1},{2,14},{6,10},... | collective-permute-start | bytes 24584 | tf_op jit(solution)/shard_map/ppermute | solution.py:17
  55.3 4.8 %collective-permute-start.17 = (f32[64,32]{1,0:T(8,128)S(1)}, f32[64,32]{1,0:T(8,128)S(1)}, u32[]{:S(2)}, u32[]{:S(2)}) collective-permute-start(f32[64,32]{1,0:T(8,128)S(1)} %add.35.refs_0_), channel_id=1, source_target_pairs={{0,4},{4,0},{8,12},{12,8},{1,5},{5,1},{9,13},{13,9},{2,6},{6,2},{1... | collective-permute-start | bytes 24584 | tf_op jit(solution)/shard_map/ppermute | solution.py:17
  58.2 4.8 %collective-permute-start.16 = (f32[64,32]{1,0:T(8,128)S(1)}, f32[64,32]{1,0:T(8,128)S(1)}, u32[]{:S(2)}, u32[]{:S(2)}) collective-permute-start(f32[64,32]{1,0:T(8,128)S(1)} %add.35.refs_0_), channel_id=1, source_target_pairs={{0,8},{4,12},{8,0},{12,4},{1,9},{5,13},{9,1},{13,5},{2,10},{6,14},... | collective-permute-start | bytes 24584 | tf_op jit(solution)/shard_map/ppermute | solution.py:17
  64.9 10.5 %collective-permute-start.19 = (f32[4,8,8,128]{3,2,1,0:T(8,128)S(1)}, f32[4,8,8,128]{3,2,1,0:T(8,128)S(1)}, u32[]{:S(2)}, u32[]{:S(2)}) collective-permute-start(f32[4,8,8,128]{3,2,1,0:T(8,128)S(1)} %get-tuple-element.17), channel_id=1, source_target_pairs={{0,8},{4,12},{8,0},{12,4},{1,9},{5,13},{9,1},{13,5},{2,10},{6,14},... | collective-permute-start | bytes 393224 | tf_op jit(solution)/shard_map/ppermute | solution.py:17
  65.4 10.1 %collective-permute-start.20 = (f32[4,8,8,128]{3,2,1,0:T(8,128)S(1)}, f32[4,8,8,128]{3,2,1,0:T(8,128)S(1)}, u32[]{:S(2)}, u32[]{:S(2)}) collective-permute-start(f32[4,8,8,128]{3,2,1,0:T(8,128)S(1)} %get-tuple-element.18), channel_id=1, source_target_pairs={{0,4},{4,0},{8,12},{12,8},{1,5},{5,1},{9,13},{13,9},{2,6},{6,2},{1... | collective-permute-start | bytes 393224 | tf_op jit(solution)/shard_map/ppermute | solution.py:17
  67.2 8.3 %collective-permute-start.21 = (f32[4,8,8,128]{3,2,1,0:T(8,128)S(1)}, f32[4,8,8,128]{3,2,1,0:T(8,128)S(1)}, u32[]{:S(2)}, u32[]{:S(2)}) collective-permute-start(f32[4,8,8,128]{3,2,1,0:T(8,128)S(1)} %get-tuple-element.19), channel_id=1, source_target_pairs={{0,12},{4,8},{8,4},{12,0},{1,13},{5,9},{9,5},{13,1},{2,14},{6,10},... | collective-permute-start | bytes 393224 | tf_op jit(solution)/shard_map/ppermute | solution.py:17

commit v8 on v7

--- a/solution.py
+++ b/solution.py
@@ -32,7 +32,7 @@
 
 def sum_over_gy(part):
     count = lax.axis_size("gy")
-    got = [swap(part, "gy", s) for s in steps(count)]
+    got = [swap(part, "gy", s) for s in ((3, 1, 2) if count == 4 else steps(count))]
     for other in got:
         part = part + other
     return part
@@ -366,20 +366,21 @@
     share_z = rows_z // n_gy
     share_k = ranks_y // n_gy
     field_z = field_v.reshape(planes * rows_y, rows_z, cells_x)
-    tiled = share_z % 8 == 0 and share_k % 8 == 0
+    tiled = share_z % 8 == 0 and share_k % 8 == 0 and n_gy == 4 and n_quarter == 4
+    inverse_x = inverse_factor_x(scale, rank_x, quarter, pieces)
     order = steps(n_gy)
     chunks = [[] for _ in range(n_gy)]
     if tiled:
         after, ahead = [], []
         for s in order:
             if s & 2:
-                part = field_chunk(scale, s, here, field_z, pieces[:1], share_z, after)
+                part = field_chunk(scale, s, here, field_z, pieces[:2], share_z, after)
                 after = [part]
                 chunks[s].append(swap(part, "gy", s))
                 ahead.append(chunks[s][0])
-        for s in [2, 1, 3] + [0]:
-            wait = ahead if s == 3 else []
-            part = field_chunk(scale, s, here, field_z, pieces[len(chunks[s]):], share_z, after + wait)
+        for s in [2, 1, 0, 3]:
+            wait = ahead + [inverse_x] if s == 3 else []
+            part = field_chunk(scale, s, here, field_z, pieces[2 * len(chunks[s]):], share_z, after + wait)
             after = [part]
             chunks[s].append(swap(part, "gy", s) if s else part)
     else:
@@ -390,7 +391,6 @@
             chunk = lax.dynamic_slice_in_dim(raw, (gy ^ s) * share_z, share_z, 1)
             chunks[s] = swap(chunk, "gy", s) if s else chunk
 
-    inverse_x = inverse_factor_x(scale, rank_x, quarter, pieces)
     factor_x = make_factor_x(scale, inverse_x, pieces)
 
     if tiled:
@@ -416,7 +416,7 @@
         got = [swap(part_y, axis, s) for s in steps(count)]
         for other in got:
             part_y = part_y + other
-    parts = [part_y] + [swap(part_y, "gy", s) for s in steps(n_gy)]
+    parts = [part_y] + [swap(part_y, "gy", s) for s in range(1, n_gy)]
     factor_y = make_factor_y(rank_y, parts, float(all_planes * all_rows_z * ranks_x))
 
     if tiled:

time: 76.4 us -> 75.6 us (0.990)
  starting transfers between devices: 29.7 us -> 26.4 us
  waiting for transfers between devices: 24.8 us -> 27.2 us
    ppermute x22, starting transfers between devices: 29.7 us -> 26.4 us  [swap(): return lax.ppermute(value, axes, [(i, i ^ step) for i in range(count)])]
    ppermute x22, waiting for transfers between devices: 24.8 us -> 27.2 us  [swap(): return lax.ppermute(value, axes, [(i, i ^ step) for i in range(count)])]
  transfers between devices with their start and end apart: 22 -> 22, of which waited for: 13 -> 13; matrix products, arithmetic and copies ran while one was open for 1% -> 1% of each run, Pallas kernels for 14% -> 15%
where the time goes in v8:
time: 75.6 us; the launch traced here: 75.4 us
  waiting for transfers between devices  27.2 us (36%)
  starting transfers between devices  26.4 us (35%)
  Pallas kernels  18.8 us (25%)
  between operations  2.11 us (3%)
    ppermute x22, waiting for transfers between devices, swap(): return lax.ppermute(value, axes, [(i, i ^ step) for i in range(count)])  27.2 us
    ppermute x22, starting transfers between devices, swap(): return lax.ppermute(value, axes, [(i, i ^ step) for i in range(count)])  26.4 us
    pallas_call x15, Pallas kernels, kernel_call(): pl.pallas_call(body, in_specs=[SMEM] * len(scalars) + [VMEM] * len(values...  14.2 us
    pallas_call x1, Pallas kernels, sketch_parts(): pl.pallas_call(sketch_kernel, in_specs=[SMEM, SMEM, far, far], out_specs=...  3.85 us
  transfers between devices with their start and end apart: 22, of which 13 were waited for; matrix products, arithmetic and copies ran while one was open for 1% of the time, Pallas kernels for 15%

profile of v8, /device:TPU:0, one launch (start us, length us, event | category | flops | bytes accessed | tf_op | source)
XLA Modules:
  0.0 75.4 jit_solution(10191083339676298509)
XLA Ops:
  0.6 3.9 %sketch.1 = (f32[2048,512]{1,0:T(8,128)S(1)}, f32[32,512]{1,0:T(8,128)S(1)}, f32[32,512]{1,0:T(8,128)S(1)}, f32[32,512]{1,0:T(8,128)S(1)}, f32[32,512]{1,0:T(8,128)S(1)}) custom-call(s32[1]{0:T(128)} %bitcast.2.me_ref, s32[1]{0:T(128)} %bitcast.here_ref.me_ref, f32[2048,512]{1,0:T(8,128)} %bitcast.12, f32[512,128]{1,0:T(8,128)} %omega_hbm.1), custom_call_target="tpu_custom_call" | custom-call | tf_op jit(solution)/shard_map/sketch/pallas_call | solution.py:140
  4.5 0.5 collective-permute-start.1
  5.0 0.1 collective-permute-start
  5.1 0.8 %collective-permute-done.1 = f32[32,512]{1,0:T(8,128)S(1)} collective-permute-done((f32[32,512]{1,0:T(8,128)S(1)}, f32[32,512]{1,0:T(8,128)S(1)}, u32[]{:S(2)}, u32[]{:S(2)}) %collective-permute-start.1) | collective-permute-done | bytes 65568 | tf_op jit(solution)/shard_map/ppermute | solution.py:17
  5.9 2.9 %collective-permute-start.2 = (f32[32,512]{1,0:T(8,128)S(1)}, f32[32,512]{1,0:T(8,128)S(1)}, u32[]{:S(2)}, u32[]{:S(2)}) collective-permute-start(f32[32,512]{1,0:T(8,128)S(1)} %add.29), channel_id=1, source_target_pairs={{0,2},{2,0},{1,3},{3,1},{4,6},{6,4},{5,7},{7,5},{8,10},{10,8},{9,1... | collective-permute-start | bytes 196616 | tf_op jit(solution)/shard_map/ppermute | solution.py:17
  8.8 0.0 collective-permute-done
  8.8 2.4 %collective-permute-done.2 = f32[32,512]{1,0:T(8,128)S(1)} collective-permute-done((f32[32,512]{1,0:T(8,128)S(1)}, f32[32,512]{1,0:T(8,128)S(1)}, u32[]{:S(2)}, u32[]{:S(2)}) %collective-permute-start.2) | collective-permute-done | bytes 65568 | tf_op jit(solution)/shard_map/ppermute | solution.py:17
  11.3 3.0 %collective-permute-start.5 = (f32[32,512]{1,0:T(8,128)S(1)}, f32[32,512]{1,0:T(8,128)S(1)}, u32[]{:S(2)}, u32[]{:S(2)}) collective-permute-start(f32[32,512]{1,0:T(8,128)S(1)} %add_add_fusion.1), channel_id=1, source_target_pairs={{0,8},{4,12},{8,0},{12,4},{1,9},{5,13},{9,1},{13,5},{2,10},{6,14},... | collective-permute-start | bytes 196616 | tf_op jit(solution)/shard_map/ppermute | solution.py:17
  14.3 1.6 %collective-permute-start.4 = (f32[32,512]{1,0:T(8,128)S(1)}, f32[32,512]{1,0:T(8,128)S(1)}, u32[]{:S(2)}, u32[]{:S(2)}) collective-permute-start(f32[32,512]{1,0:T(8,128)S(1)} %add_add_fusion.1), channel_id=1, source_target_pairs={{0,4},{4,0},{8,12},{12,8},{1,5},{5,1},{9,13},{13,9},{2,6},{6,2},{1... | collective-permute-start | bytes 196616 | tf_op jit(solution)/shard_map/ppermute | solution.py:17
  15.9 0.0 collective-permute-start.3
  15.9 0.9 %collective-permute-done.5 = f32[32,512]{1,0:T(8,128)S(1)} collective-permute-done((f32[32,512]{1,0:T(8,128)S(1)}, f32[32,512]{1,0:T(8,128)S(1)}, u32[]{:S(2)}, u32[]{:S(2)}) %collective-permute-start.5) | collective-permute-done | bytes 65568 | tf_op jit(solution)/shard_map/ppermute | solution.py:17
  16.8 1.8 %collective-permute-done.4 = f32[32,512]{1,0:T(8,128)S(1)} collective-permute-done((f32[32,512]{1,0:T(8,128)S(1)}, f32[32,512]{1,0:T(8,128)S(1)}, u32[]{:S(2)}, u32[]{:S(2)}) %collective-permute-start.4) | collective-permute-done | bytes 65568 | tf_op jit(solution)/shard_map/ppermute | solution.py:17
  18.6 3.4 %collective-permute-done.3 = f32[32,512]{1,0:T(8,128)S(1)} collective-permute-done((f32[32,512]{1,0:T(8,128)S(1)}, f32[32,512]{1,0:T(8,128)S(1)}, u32[]{:S(2)}, u32[]{:S(2)}) %collective-permute-start.3) | collective-permute-done | bytes 65568 | tf_op jit(solution)/shard_map/ppermute | solution.py:17
  21.9 0.1 collective-permute-start.6
  22.0 1.6 %collective-permute-start.8 = (f32[32,512]{1,0:T(8,128)S(1)}, f32[32,512]{1,0:T(8,128)S(1)}, u32[]{:S(2)}, u32[]{:S(2)}) collective-permute-start(f32[32,512]{1,0:T(8,128)S(1)} %add_add_fusion.refs_0_), channel_id=1, source_target_pairs={{0,3},{1,2},{2,1},{3,0},{4,7},{5,6},{6,5},{7,4},{8,11},{9,10},{10,... | collective-permute-start | bytes 196616 | tf_op jit(solution)/shard_map/ppermute | solution.py:17
  23.6 0.5 collective-permute-start.7
  24.2 0.0 collective-permute-done.6.refs_1_
  24.2 0.5 chunk.6.refs_2_
  24.7 0.6 collective-permute-start.10
  25.2 0.5 chunk.7.refs_2_
  25.7 0.7 collective-permute-start.12
  26.4 0.0 collective-permute-done.8.refs_3_.refs_1_
  26.4 1.5 %collective-permute-done.7.refs_2_.refs_0_ = f32[32,512]{1,0:T(8,128)S(1)} collective-permute-done((f32[32,512]{1,0:T(8,128)S(1)}, f32[32,512]{1,0:T(8,128)S(1)}, u32[]{:S(2)}, u32[]{:S(2)}) %collective-permute-start.7) | collective-permute-done | bytes 65568 | tf_op jit(solution)/shard_map/ppermute | solution.py:17
  27.9 0.5 chunk.8.refs_4_
  28.4 0.5 chunk.9.refs_4_
  28.9 0.9 %collective-permute-start.9 = (f32[128,512]{1,0:T(8,128)S(1)}, f32[128,512]{1,0:T(8,128)S(1)}, u32[]{:S(2)}, u32[]{:S(2)}) collective-permute-start(f32[128,512]{1,0:T(8,128)S(1)} %chunk.9.refs_4_), channel_id=1, source_target_pairs={{0,4},{4,0},{8,12},{12,8},{1,5},{5,1},{9,13},{13,9},{2,6},{6,2},{1... | collective-permute-start | bytes 786440 | tf_op jit(solution)/shard_map/ppermute | solution.py:17
  30.4 1.5 %collective-permute-start.11 = (f32[64,512]{1,0:T(8,128)S(1)}, f32[64,512]{1,0:T(8,128)S(1)}, u32[]{:S(2)}, u32[]{:S(2)}) collective-permute-start(f32[64,512]{1,0:T(8,128)S(1)} %chunk.8.refs_4_), channel_id=1, source_target_pairs={{0,8},{4,12},{8,0},{12,4},{1,9},{5,13},{9,1},{13,5},{2,10},{6,14},... | collective-permute-start | bytes 393224 | tf_op jit(solution)/shard_map/ppermute | solution.py:17
  31.9 0.5 chunk.10.refs_0_.refs_2_
  32.4 0.0 copy-start
  32.4 6.1 %factor_x.1.inverse_ref.refs_5_ = f32[128,128]{1,0:T(8,128)S(1)} custom-call(s32[1]{0:T(128)S(6)} %copy.9.rank_ref, s32[1]{0:T(128)} %bitcast.2.me_ref, f32[32,512]{1,0:T(8,128)S(1)} %add_add_fusion.refs_0_, f32[32,512]{1,0:T(8,128)S(1)} %collective-permute-done.6.refs_1_, f32[32,512]{1,0:T(8,128)S(1)} %collective-permute-done.7.refs_2_.refs_0_, ...), custom_call_target="tpu_custom_call" | custom-call | tf_op jit(solution)/shard_map/factor_x/pallas_call | solution.py:89
  38.5 0.0 collective-permute-done.12.refs_4_.refs_0_
  38.5 0.0 collective-permute-done.10.refs_0_.refs_3_
  38.5 0.5 chunk.11
  39.0 2.2 %collective-permute-start.13 = (f32[64,512]{1,0:T(8,128)S(1)}, f32[64,512]{1,0:T(8,128)S(1)}, u32[]{:S(2)}, u32[]{:S(2)}) collective-permute-start(f32[64,512]{1,0:T(8,128)S(1)} %chunk.11), channel_id=1, source_target_pairs={{0,12},{4,8},{8,4},{12,0},{1,13},{5,9},{9,5},{13,1},{2,14},{6,10},... | collective-permute-start | bytes 393224 | tf_op jit(solution)/shard_map/ppermute | solution.py:17
  41.2 0.3 lift.4.refs_2_.refs_0_
  41.6 4.5 %collective-permute-done.11.refs_1_ = f32[64,512]{1,0:T(8,128)S(1)} collective-permute-done((f32[64,512]{1,0:T(8,128)S(1)}, f32[64,512]{1,0:T(8,128)S(1)}, u32[]{:S(2)}, u32[]{:S(2)}) %collective-permute-start.11) | collective-permute-done | bytes 131104 | tf_op jit(solution)/shard_map/ppermute | solution.py:17
  46.1 0.3 lift.5.refs_1_.refs_2_
  46.4 0.0 collective-permute-done.9.refs_0_
  46.4 0.3 lift.6.refs_2_.refs_1_
  46.7 0.0 collective-permute-done.13.refs_1_
  46.7 0.3 lift.7.refs_3_
  47.0 0.0 copy-done
  47.0 0.9 %gram.1 = f32[64,32]{1,0:T(8,128)S(1)} custom-call(s32[1]{0:T(128)} %bitcast.here_ref.me_ref, f32[32,64]{1,0:T(8,128)S(1)} %bitcast.11, f32[16,4096]{1,0:T(8,128)S(1)} %lift.4.refs_2_.refs_0_, f32[16,4096]{1,0:T(8,128)S(1)} %lift.6.refs_2_.refs_1_, f32[16,4096]{1,0:T(8,128)S(1)} %lift.5.refs_1_.refs_2_, f32[16,4096]{1,0:T(8,128)S(1)} %lift.7.refs_3_), custom_call_target="tpu_custom_call" | custom-call | tf_op jit(solution)/shard_map/gram/pallas_call | solution.py:89
  48.0 0.0 collective-permute-start.14
  48.0 1.2 %collective-permute-done.14 = f32[64,32]{1,0:T(8,128)S(1)} collective-permute-done((f32[64,32]{1,0:T(8,128)S(1)}, f32[64,32]{1,0:T(8,128)S(1)}, u32[]{:S(2)}, u32[]{:S(2)}) %collective-permute-start.14) | collective-permute-done | bytes 8224 | tf_op jit(solution)/shard_map/ppermute | solution.py:17
  49.2 1.5 %collective-permute-start.15 = (f32[64,32]{1,0:T(8,128)S(1)}, f32[64,32]{1,0:T(8,128)S(1)}, u32[]{:S(2)}, u32[]{:S(2)}) collective-permute-start(f32[64,32]{1,0:T(8,128)S(1)} %add.34), channel_id=1, source_target_pairs={{0,2},{2,0},{1,3},{3,1},{4,6},{6,4},{5,7},{7,5},{8,10},{10,8},{9,1... | collective-permute-start | bytes 24584 | tf_op jit(solution)/shard_map/ppermute | solution.py:17
  50.7 2.4 %collective-permute-done.15 = f32[64,32]{1,0:T(8,128)S(1)} collective-permute-done((f32[64,32]{1,0:T(8,128)S(1)}, f32[64,32]{1,0:T(8,128)S(1)}, u32[]{:S(2)}, u32[]{:S(2)}) %collective-permute-start.15) | collective-permute-done | bytes 8224 | tf_op jit(solution)/shard_map/ppermute | solution.py:17
  53.1 3.1 %collective-permute-start.18 = (f32[64,32]{1,0:T(8,128)S(1)}, f32[64,32]{1,0:T(8,128)S(1)}, u32[]{:S(2)}, u32[]{:S(2)}) collective-permute-start(f32[64,32]{1,0:T(8,128)S(1)} %add.35.refs_0_), channel_id=1, source_target_pairs={{0,12},{4,8},{8,4},{12,0},{1,13},{5,9},{9,5},{13,1},{2,14},{6,10},... | collective-permute-start | bytes 24584 | tf_op jit(solution)/shard_map/ppermute | solution.py:17
  56.3 0.9 %collective-permute-start.17 = (f32[64,32]{1,0:T(8,128)S(1)}, f32[64,32]{1,0:T(8,128)S(1)}, u32[]{:S(2)}, u32[]{:S(2)}) collective-permute-start(f32[64,32]{1,0:T(8,128)S(1)} %add.35.refs_0_), channel_id=1, source_target_pairs={{0,8},{4,12},{8,0},{12,4},{1,9},{5,13},{9,1},{13,5},{2,10},{6,14},... | collective-permute-start | bytes 24584 | tf_op jit(solution)/shard_map/ppermute | solution.py:17
  57.1 0.4 collective-permute-start.16
  58.2 0.8 %collective-permute-done.18.refs_3_ = f32[64,32]{1,0:T(8,128)S(1)} collective-permute-done((f32[64,32]{1,0:T(8,128)S(1)}, f32[64,32]{1,0:T(8,128)S(1)}, u32[]{:S(2)}, u32[]{:S(2)}) %collective-permute-start.18) | collective-permute-done | bytes 8224 | tf_op jit(solution)/shard_map/ppermute | solution.py:17
  59.0 2.2 %collective-permute-done.17.refs_2_ = f32[64,32]{1,0:T(8,128)S(1)} collective-permute-done((f32[64,32]{1,0:T(8,128)S(1)}, f32[64,32]{1,0:T(8,128)S(1)}, u32[]{:S(2)}, u32[]{:S(2)}) %collective-permute-start.17) | collective-permute-done | bytes 8224 | tf_op jit(solution)/shard_map/ppermute | solution.py:17
  61.2 0.2 collective-permute-done.16.refs_1_
  61.4 1.4 %factor_y.1.factor_ref = f32[64,32]{1,0:T(8,128)S(1)} custom-call(s32[1]{0:T(128)S(6)} %copy.10.rank_ref, f32[64,32]{1,0:T(8,128)S(1)} %add.35.refs_0_, f32[64,32]{1,0:T(8,128)S(1)} %collective-permute-done.16.refs_1_, f32[64,32]{1,0:T(8,128)S(1)} %collective-permute-done.17.refs_2_, f32[64,32]{1,0:T(8,128)S(1)} %collective-permute-done.18.refs_3_), custom_call_target="tpu_custom_call" | custom-call | tf_op jit(solution)/shard_map/factor_y/pallas_call | solution.py:89
  62.8 0.5 mix.1
  63.3 1.8 %collective-permute-start.19 = (f32[4,8,8,128]{3,2,1,0:T(8,128)S(1)}, f32[4,8,8,128]{3,2,1,0:T(8,128)S(1)}, u32[]{:S(2)}, u32[]{:S(2)}) collective-permute-start(f32[4,8,8,128]{3,2,1,0:T(8,128)S(1)} %get-tuple-element.17), channel_id=1, source_target_pairs={{0,8},{4,12},{8,0},{12,4},{1,9},{5,13},{9,1},{13,5},{2,10},{6,14},... | collective-permute-start | bytes 393224 | tf_op jit(solution)/shard_map/ppermute | solution.py:17
  65.1 1.1 %collective-permute-start.20 = (f32[4,8,8,128]{3,2,1,0:T(8,128)S(1)}, f32[4,8,8,128]{3,2,1,0:T(8,128)S(1)}, u32[]{:S(2)}, u32[]{:S(2)}) collective-permute-start(f32[4,8,8,128]{3,2,1,0:T(8,128)S(1)} %get-tuple-element.18), channel_id=1, source_target_pairs={{0,4},{4,0},{8,12},{12,8},{1,5},{5,1},{9,13},{13,9},{2,6},{6,2},{1... | collective-permute-start | bytes 393224 | tf_op jit(solution)/shard_map/ppermute | solution.py:17
  66.2 1.6 %collective-permute-start.21 = (f32[4,8,8,128]{3,2,1,0:T(8,128)S(1)}, f32[4,8,8,128]{3,2,1,0:T(8,128)S(1)}, u32[]{:S(2)}, u32[]{:S(2)}) collective-permute-start(f32[4,8,8,128]{3,2,1,0:T(8,128)S(1)} %get-tuple-element.19), channel_id=1, source_target_pairs={{0,12},{4,8},{8,4},{12,0},{1,13},{5,9},{9,5},{13,1},{2,14},{6,10},... | collective-permute-start | bytes 393224 | tf_op jit(solution)/shard_map/ppermute | solution.py:17
  67.8 1.1 %apply.1 = f32[512,128]{1,0:T(8,128)} custom-call(f32[128,128]{1,0:T(8,128)S(1)} %factor_x.1.inverse_ref.refs_5_, f32[32,512]{1,0:T(8,128)S(1)} %add_add_fusion.refs_0_, f32[32,512]{1,0:T(8,128)S(1)} %collective-permute-done.6.refs_1_, f32[32,512]{1,0:T(8,128)S(1)} %collective-permute-done.7.refs_2_.refs_0_, f32[32,512]{1,0:T(8,128)S(1)} %collective-permute-done.8.refs_3_.refs_1_), custom_call_target="tpu_custom_call" | custom-call | tf_op jit(solution)/shard_map/apply/pallas_call | solution.py:89
  68.9 0.7 copy.8
  69.6 5.0 %collective-permute-done.19.refs_0_ = f32[4,8,8,128]{3,2,1,0:T(8,128)S(1)} collective-permute-done((f32[4,8,8,128]{3,2,1,0:T(8,128)S(1)}, f32[4,8,8,128]{3,2,1,0:T(8,128)S(1)}, u32[]{:S(2)}, u32[]{:S(2)}) %collective-permute-start.19) | collective-permute-done | bytes 131104 | tf_op jit(solution)/shard_map/ppermute | solution.py:17
  74.6 0.0 collective-permute-done.20.refs_1_
  74.6 0.0 collective-permute-done.21.refs_2_
  74.6 0.8 %place.1 = f32[4,8,32,128]{3,2,1,0:T(8,128)} custom-call(s32[1]{0:T(128)} %bitcast.here_ref.me_ref, f32[4,8,8,128]{3,2,1,0:T(8,128)S(1)} %collective-permute-done.19.refs_0_, f32[4,8,8,128]{3,2,1,0:T(8,128)S(1)} %collective-permute-done.20.refs_1_, f32[4,8,8,128]{3,2,1,0:T(8,128)S(1)} %collective-permute-done.21.refs_2_, ...), custom_call_target="tpu_custom_call" | custom-call | tf_op jit(solution)/shard_map/place/pallas_call | solution.py:251
  (5 shorter events, 0.1 us)
Async XLA Ops:
  4.5 1.4 %collective-permute-start.1 = (f32[32,512]{1,0:T(8,128)S(1)}, f32[32,512]{1,0:T(8,128)S(1)}, u32[]{:S(2)}, u32[]{:S(2)}) collective-permute-start(f32[32,512]{1,0:T(8,128)S(1)} %get-tuple-element.15), channel_id=1, source_target_pairs={{0,1},{1,0},{2,3},{3,2},{4,5},{5,4},{6,7},{7,6},{8,9},{9,8},{10,11... | collective-permute-start | bytes 196616 | tf_op jit(solution)/shard_map/ppermute | solution.py:17
  5.0 3.8 %collective-permute-start = (f32[32,512]{1,0:T(8,128)S(1)}, f32[32,512]{1,0:T(8,128)S(1)}, u32[]{:S(2)}, u32[]{:S(2)}) collective-permute-start(f32[32,512]{1,0:T(8,128)S(1)} %get-tuple-element.13), channel_id=1, source_target_pairs={{0,1},{1,0},{2,3},{3,2},{4,5},{5,4},{6,7},{7,6},{8,9},{9,8},{10,11... | collective-permute-start | bytes 196616 | tf_op jit(solution)/shard_map/ppermute | solution.py:17
  5.9 5.3 %collective-permute-start.2 = (f32[32,512]{1,0:T(8,128)S(1)}, f32[32,512]{1,0:T(8,128)S(1)}, u32[]{:S(2)}, u32[]{:S(2)}) collective-permute-start(f32[32,512]{1,0:T(8,128)S(1)} %add.29), channel_id=1, source_target_pairs={{0,2},{2,0},{1,3},{3,1},{4,6},{6,4},{5,7},{7,5},{8,10},{10,8},{9,1... | collective-permute-start | bytes 196616 | tf_op jit(solution)/shard_map/ppermute | solution.py:17
  11.3 5.5 %collective-permute-start.5 = (f32[32,512]{1,0:T(8,128)S(1)}, f32[32,512]{1,0:T(8,128)S(1)}, u32[]{:S(2)}, u32[]{:S(2)}) collective-permute-start(f32[32,512]{1,0:T(8,128)S(1)} %add_add_fusion.1), channel_id=1, source_target_pairs={{0,8},{4,12},{8,0},{12,4},{1,9},{5,13},{9,1},{13,5},{2,10},{6,14},... | collective-permute-start | bytes 196616 | tf_op jit(solution)/shard_map/ppermute | solution.py:17
  14.3 4.3 %collective-permute-start.4 = (f32[32,512]{1,0:T(8,128)S(1)}, f32[32,512]{1,0:T(8,128)S(1)}, u32[]{:S(2)}, u32[]{:S(2)}) collective-permute-start(f32[32,512]{1,0:T(8,128)S(1)} %add_add_fusion.1), channel_id=1, source_target_pairs={{0,4},{4,0},{8,12},{12,8},{1,5},{5,1},{9,13},{13,9},{2,6},{6,2},{1... | collective-permute-start | bytes 196616 | tf_op jit(solution)/shard_map/ppermute | solution.py:17
  15.9 6.1 %collective-permute-start.3 = (f32[32,512]{1,0:T(8,128)S(1)}, f32[32,512]{1,0:T(8,128)S(1)}, u32[]{:S(2)}, u32[]{:S(2)}) collective-permute-start(f32[32,512]{1,0:T(8,128)S(1)} %add_add_fusion.1), channel_id=1, source_target_pairs={{0,12},{4,8},{8,4},{12,0},{1,13},{5,9},{9,5},{13,1},{2,14},{6,10},... | collective-permute-start | bytes 196616 | tf_op jit(solution)/shard_map/ppermute | solution.py:17
  21.9 2.2 %collective-permute-start.6 = (f32[32,512]{1,0:T(8,128)S(1)}, f32[32,512]{1,0:T(8,128)S(1)}, u32[]{:S(2)}, u32[]{:S(2)}) collective-permute-start(f32[32,512]{1,0:T(8,128)S(1)} %add_add_fusion.refs_0_), channel_id=1, source_target_pairs={{0,1},{1,0},{2,3},{3,2},{4,5},{5,4},{6,7},{7,6},{8,9},{9,8},{10,11... | collective-permute-start | bytes 196616 | tf_op jit(solution)/shard_map/ppermute | solution.py:17
  22.0 4.3 %collective-permute-start.8 = (f32[32,512]{1,0:T(8,128)S(1)}, f32[32,512]{1,0:T(8,128)S(1)}, u32[]{:S(2)}, u32[]{:S(2)}) collective-permute-start(f32[32,512]{1,0:T(8,128)S(1)} %add_add_fusion.refs_0_), channel_id=1, source_target_pairs={{0,3},{1,2},{2,1},{3,0},{4,7},{5,6},{6,5},{7,4},{8,11},{9,10},{10,... | collective-permute-start | bytes 196616 | tf_op jit(solution)/shard_map/ppermute | solution.py:17
  23.6 4.3 %collective-permute-start.7 = (f32[32,512]{1,0:T(8,128)S(1)}, f32[32,512]{1,0:T(8,128)S(1)}, u32[]{:S(2)}, u32[]{:S(2)}) collective-permute-start(f32[32,512]{1,0:T(8,128)S(1)} %add_add_fusion.refs_0_), channel_id=1, source_target_pairs={{0,2},{1,3},{2,0},{3,1},{4,6},{5,7},{6,4},{7,5},{8,10},{9,11},{10,... | collective-permute-start | bytes 196616 | tf_op jit(solution)/shard_map/ppermute | solution.py:17
  24.7 13.9 %collective-permute-start.10 = (f32[64,512]{1,0:T(8,128)S(1)}, f32[64,512]{1,0:T(8,128)S(1)}, u32[]{:S(2)}, u32[]{:S(2)}) collective-permute-start(f32[64,512]{1,0:T(8,128)S(1)} %chunk.6.refs_2_), channel_id=1, source_target_pairs={{0,8},{4,12},{8,0},{12,4},{1,9},{5,13},{9,1},{13,5},{2,10},{6,14},... | collective-permute-start | bytes 393224 | tf_op jit(solution)/shard_map/ppermute | solution.py:17
  25.7 12.8 %collective-permute-start.12 = (f32[64,512]{1,0:T(8,128)S(1)}, f32[64,512]{1,0:T(8,128)S(1)}, u32[]{:S(2)}, u32[]{:S(2)}) collective-permute-start(f32[64,512]{1,0:T(8,128)S(1)} %chunk.7.refs_2_), channel_id=1, source_target_pairs={{0,12},{4,8},{8,4},{12,0},{1,13},{5,9},{9,5},{13,1},{2,14},{6,10},... | collective-permute-start | bytes 393224 | tf_op jit(solution)/shard_map/ppermute | solution.py:17
  28.9 17.5 %collective-permute-start.9 = (f32[128,512]{1,0:T(8,128)S(1)}, f32[128,512]{1,0:T(8,128)S(1)}, u32[]{:S(2)}, u32[]{:S(2)}) collective-permute-start(f32[128,512]{1,0:T(8,128)S(1)} %chunk.9.refs_4_), channel_id=1, source_target_pairs={{0,4},{4,0},{8,12},{12,8},{1,5},{5,1},{9,13},{13,9},{2,6},{6,2},{1... | collective-permute-start | bytes 786440 | tf_op jit(solution)/shard_map/ppermute | solution.py:17
  30.4 15.6 %collective-permute-start.11 = (f32[64,512]{1,0:T(8,128)S(1)}, f32[64,512]{1,0:T(8,128)S(1)}, u32[]{:S(2)}, u32[]{:S(2)}) collective-permute-start(f32[64,512]{1,0:T(8,128)S(1)} %chunk.8.refs_4_), channel_id=1, source_target_pairs={{0,8},{4,12},{8,0},{12,4},{1,9},{5,13},{9,1},{13,5},{2,10},{6,14},... | collective-permute-start | bytes 393224 | tf_op jit(solution)/shard_map/ppermute | solution.py:17
  32.4 14.6 %copy-start = (f32[64,32]{0,1:T(8,128)S(1)}, f32[64,32]{0,1:T(8,128)}, u32[]{:S(2)}) copy-start(f32[64,32]{0,1:T(8,128)} %param.7) | copy-start | bytes 24580
  39.0 7.7 %collective-permute-start.13 = (f32[64,512]{1,0:T(8,128)S(1)}, f32[64,512]{1,0:T(8,128)S(1)}, u32[]{:S(2)}, u32[]{:S(2)}) collective-permute-start(f32[64,512]{1,0:T(8,128)S(1)} %chunk.11), channel_id=1, source_target_pairs={{0,12},{4,8},{8,4},{12,0},{1,13},{5,9},{9,5},{13,1},{2,14},{6,10},... | collective-permute-start | bytes 393224 | tf_op jit(solution)/shard_map/ppermute | solution.py:17
  48.0 1.2 %collective-permute-start.14 = (f32[64,32]{1,0:T(8,128)S(1)}, f32[64,32]{1,0:T(8,128)S(1)}, u32[]{:S(2)}, u32[]{:S(2)}) collective-permute-start(f32[64,32]{1,0:T(8,128)S(1)} %gram.1), channel_id=1, source_target_pairs={{0,1},{1,0},{2,3},{3,2},{4,5},{5,4},{6,7},{7,6},{8,9},{9,8},{10,11... | collective-permute-start | bytes 24584 | tf_op jit(solution)/shard_map/ppermute | solution.py:17
  49.2 3.9 %collective-permute-start.15 = (f32[64,32]{1,0:T(8,128)S(1)}, f32[64,32]{1,0:T(8,128)S(1)}, u32[]{:S(2)}, u32[]{:S(2)}) collective-permute-start(f32[64,32]{1,0:T(8,128)S(1)} %add.34), channel_id=1, source_target_pairs={{0,2},{2,0},{1,3},{3,1},{4,6},{6,4},{5,7},{7,5},{8,10},{10,8},{9,1... | collective-permute-start | bytes 24584 | tf_op jit(solution)/shard_map/ppermute | solution.py:17
  53.1 5.8 %collective-permute-start.18 = (f32[64,32]{1,0:T(8,128)S(1)}, f32[64,32]{1,0:T(8,128)S(1)}, u32[]{:S(2)}, u32[]{:S(2)}) collective-permute-start(f32[64,32]{1,0:T(8,128)S(1)} %add.35.refs_0_), channel_id=1, source_target_pairs={{0,12},{4,8},{8,4},{12,0},{1,13},{5,9},{9,5},{13,1},{2,14},{6,10},... | collective-permute-start | bytes 24584 | tf_op jit(solution)/shard_map/ppermute | solution.py:17
  56.3 4.9 %collective-permute-start.17 = (f32[64,32]{1,0:T(8,128)S(1)}, f32[64,32]{1,0:T(8,128)S(1)}, u32[]{:S(2)}, u32[]{:S(2)}) collective-permute-start(f32[64,32]{1,0:T(8,128)S(1)} %add.35.refs_0_), channel_id=1, source_target_pairs={{0,8},{4,12},{8,0},{12,4},{1,9},{5,13},{9,1},{13,5},{2,10},{6,14},... | collective-permute-start | bytes 24584 | tf_op jit(solution)/shard_map/ppermute | solution.py:17
  57.1 4.3 %collective-permute-start.16 = (f32[64,32]{1,0:T(8,128)S(1)}, f32[64,32]{1,0:T(8,128)S(1)}, u32[]{:S(2)}, u32[]{:S(2)}) collective-permute-start(f32[64,32]{1,0:T(8,128)S(1)} %add.35.refs_0_), channel_id=1, source_target_pairs={{0,4},{4,0},{8,12},{12,8},{1,5},{5,1},{9,13},{13,9},{2,6},{6,2},{1... | collective-permute-start | bytes 24584 | tf_op jit(solution)/shard_map/ppermute | solution.py:17
  63.3 11.3 %collective-permute-start.19 = (f32[4,8,8,128]{3,2,1,0:T(8,128)S(1)}, f32[4,8,8,128]{3,2,1,0:T(8,128)S(1)}, u32[]{:S(2)}, u32[]{:S(2)}) collective-permute-start(f32[4,8,8,128]{3,2,1,0:T(8,128)S(1)} %get-tuple-element.17), channel_id=1, source_target_pairs={{0,8},{4,12},{8,0},{12,4},{1,9},{5,13},{9,1},{13,5},{2,10},{6,14},... | collective-permute-start | bytes 393224 | tf_op jit(solution)/shard_map/ppermute | solution.py:17
  65.1 9.5 %collective-permute-start.20 = (f32[4,8,8,128]{3,2,1,0:T(8,128)S(1)}, f32[4,8,8,128]{3,2,1,0:T(8,128)S(1)}, u32[]{:S(2)}, u32[]{:S(2)}) collective-permute-start(f32[4,8,8,128]{3,2,1,0:T(8,128)S(1)} %get-tuple-element.18), channel_id=1, source_target_pairs={{0,4},{4,0},{8,12},{12,8},{1,5},{5,1},{9,13},{13,9},{2,6},{6,2},{1... | collective-permute-start | bytes 393224 | tf_op jit(solution)/shard_map/ppermute | solution.py:17
  66.2 8.4 %collective-permute-start.21 = (f32[4,8,8,128]{3,2,1,0:T(8,128)S(1)}, f32[4,8,8,128]{3,2,1,0:T(8,128)S(1)}, u32[]{:S(2)}, u32[]{:S(2)}) collective-permute-start(f32[4,8,8,128]{3,2,1,0:T(8,128)S(1)} %get-tuple-element.19), channel_id=1, source_target_pairs={{0,12},{4,8},{8,4},{12,0},{1,13},{5,9},{9,5},{13,1},{2,14},{6,10},... | collective-permute-start | bytes 393224 | tf_op jit(solution)/shard_map/ppermute | solution.py:17

commit v9 on v8

--- a/solution.py
+++ b/solution.py
@@ -7,7 +7,6 @@
 from jax.experimental.pallas import tpu as pltpu
 from jax.sharding import PartitionSpec as P
 
-HIGH = lax.Precision.HIGH
 HIGHEST = lax.Precision.HIGHEST
 
 
@@ -32,7 +31,7 @@
 
 def sum_over_gy(part):
     count = lax.axis_size("gy")
-    got = [swap(part, "gy", s) for s in ((3, 1, 2) if count == 4 else steps(count))]
+    got = [swap(part, "gy", s) for s in steps(count)]
     for other in got:
         part = part + other
     return part
@@ -385,7 +384,7 @@
             chunks[s].append(swap(part, "gy", s) if s else part)
     else:
         sketch = jnp.concatenate(pieces, axis=0) * scale
-        raw = lax.dot_general(flat, sketch, dims(1, 1), precision=HIGH)
+        raw = lax.dot_general(flat, sketch, dims(1, 1), precision=HIGHEST)
         raw = raw.reshape(planes * rows_y, rows_z, ranks_x)
         for s in order + [0]:
             chunk = lax.dynamic_slice_in_dim(raw, (gy ^ s) * share_z, share_z, 1)
@@ -404,9 +403,9 @@
         part_y = kernel_call(gram_kernel, "gram", shape, [here], [omega_y.T] + slabs, scratch)
     else:
         spread = jnp.stack(chunks).reshape(-1, ranks_x)
-        spread = lax.dot_general(spread, inverse_x, dims(1, 0), precision=HIGH)
+        spread = lax.dot_general(spread, inverse_x, dims(1, 0), precision=HIGHEST)
         spread = spread.reshape(n_gy, planes, rows_y, share_z, ranks_x)
-        local_gram_y = jnp.einsum("gvazr,hvbzr->gahb", spread, spread, precision=HIGH)
+        local_gram_y = jnp.einsum("gvazr,hvbzr->gahb", spread, spread, precision=HIGHEST)
         local_gram_y = local_gram_y.reshape(all_rows_y, all_rows_y)
         omega_p = by_step(omega_y.reshape(n_gy, rows_y, ranks_y), gy, n_gy).reshape(all_rows_y, ranks_y)
         part_y = jnp.dot(local_gram_y, omega_p, precision=HIGHEST)
@@ -434,7 +433,7 @@
     weights = by_step(factor_y.reshape(n_gy, rows_y, ranks_y), gy, n_gy)
     weights = weights.reshape(n_gy, rows_y, n_gy, share_k)
     weights = jnp.moveaxis(by_step(jnp.moveaxis(weights, 2, 0), gy, n_gy), 0, 2)
-    mixed = jnp.einsum("gvyzr,gyhk->hvkzr", spread, weights, precision=HIGH)
+    mixed = jnp.einsum("gvyzr,gyhk->hvkzr", spread, weights, precision=HIGHEST)
     pieces = [None] * n_gy
     for s in steps(n_gy):
         pieces[s] = swap(mixed[s], "gy", s)

time: 75.6 us -> 75 us (level)
  waiting for transfers between devices: 27.2 us -> 23.4 us
  starting transfers between devices: 26.4 us -> 29.7 us
    ppermute x22, waiting for transfers between devices: 27.2 us -> 23.4 us  [swap(): return lax.ppermute(value, axes, [(i, i ^ step) for i in range(count)])]
    ppermute x22, starting transfers between devices: 26.4 us -> 29.7 us  [swap(): return lax.ppermute(value, axes, [(i, i ^ step) for i in range(count)])]
  transfers between devices with their start and end apart: 22 -> 22, of which waited for: 13 -> 12; matrix products, arithmetic and copies ran while one was open for 1% -> 1% of each run, Pallas kernels for 15% -> 15%
where the time goes in v9:
time: 75 us; the launch traced here: 74.9 us
  starting transfers between devices  29.7 us (40%)
  waiting for transfers between devices  23.4 us (31%)
  Pallas kernels  18.9 us (25%)
  between operations  2.11 us (3%)
    ppermute x22, starting transfers between devices, swap(): return lax.ppermute(value, axes, [(i, i ^ step) for i in range(count)])  29.7 us
    ppermute x22, waiting for transfers between devices, swap(): return lax.ppermute(value, axes, [(i, i ^ step) for i in range(count)])  23.4 us
    pallas_call x15, Pallas kernels, kernel_call(): pl.pallas_call(body, in_specs=[SMEM] * len(scalars) + [VMEM] * len(values...  14.2 us
    pallas_call x1, Pallas kernels, sketch_parts(): pl.pallas_call(sketch_kernel, in_specs=[SMEM, SMEM, far, far], out_specs=...  3.85 us
  transfers between devices with their start and end apart: 22, of which 12 were waited for; matrix products, arithmetic and copies ran while one was open for 1% of the time, Pallas kernels for 15%

profile of v9, /device:TPU:0, one launch (start us, length us, event | category | flops | bytes accessed | tf_op | source)
XLA Modules:
  0.0 74.9 jit_solution(541375134501919944)
XLA Ops:
  0.6 3.9 %sketch.1 = (f32[2048,512]{1,0:T(8,128)S(1)}, f32[32,512]{1,0:T(8,128)S(1)}, f32[32,512]{1,0:T(8,128)S(1)}, f32[32,512]{1,0:T(8,128)S(1)}, f32[32,512]{1,0:T(8,128)S(1)}) custom-call(s32[1]{0:T(128)} %bitcast.2.me_ref, s32[1]{0:T(128)} %bitcast.here_ref.me_ref, f32[2048,512]{1,0:T(8,128)} %bitcast.12, f32[512,128]{1,0:T(8,128)} %omega_hbm.1), custom_call_target="tpu_custom_call" | custom-call | tf_op jit(solution)/shard_map/sketch/pallas_call | solution.py:139
  4.5 0.5 collective-permute-start.1
  5.0 0.1 collective-permute-start
  5.1 0.8 %collective-permute-done.1 = f32[32,512]{1,0:T(8,128)S(1)} collective-permute-done((f32[32,512]{1,0:T(8,128)S(1)}, f32[32,512]{1,0:T(8,128)S(1)}, u32[]{:S(2)}, u32[]{:S(2)}) %collective-permute-start.1) | collective-permute-done | bytes 65568 | tf_op jit(solution)/shard_map/ppermute | solution.py:16
  5.9 2.9 %collective-permute-start.2 = (f32[32,512]{1,0:T(8,128)S(1)}, f32[32,512]{1,0:T(8,128)S(1)}, u32[]{:S(2)}, u32[]{:S(2)}) collective-permute-start(f32[32,512]{1,0:T(8,128)S(1)} %add.29), channel_id=1, source_target_pairs={{0,2},{2,0},{1,3},{3,1},{4,6},{6,4},{5,7},{7,5},{8,10},{10,8},{9,1... | collective-permute-start | bytes 196616 | tf_op jit(solution)/shard_map/ppermute | solution.py:16
  8.8 0.0 collective-permute-done
  8.8 2.4 %collective-permute-done.2 = f32[32,512]{1,0:T(8,128)S(1)} collective-permute-done((f32[32,512]{1,0:T(8,128)S(1)}, f32[32,512]{1,0:T(8,128)S(1)}, u32[]{:S(2)}, u32[]{:S(2)}) %collective-permute-start.2) | collective-permute-done | bytes 65568 | tf_op jit(solution)/shard_map/ppermute | solution.py:16
  11.3 4.0 %collective-permute-start.5 = (f32[32,512]{1,0:T(8,128)S(1)}, f32[32,512]{1,0:T(8,128)S(1)}, u32[]{:S(2)}, u32[]{:S(2)}) collective-permute-start(f32[32,512]{1,0:T(8,128)S(1)} %add_add_fusion.1), channel_id=1, source_target_pairs={{0,12},{4,8},{8,4},{12,0},{1,13},{5,9},{9,5},{13,1},{2,14},{6,10},... | collective-permute-start | bytes 196616 | tf_op jit(solution)/shard_map/ppermute | solution.py:16
  15.3 0.0 collective-permute-start.4
  15.3 0.6 collective-permute-start.3
  15.9 1.8 %collective-permute-done.5 = f32[32,512]{1,0:T(8,128)S(1)} collective-permute-done((f32[32,512]{1,0:T(8,128)S(1)}, f32[32,512]{1,0:T(8,128)S(1)}, u32[]{:S(2)}, u32[]{:S(2)}) %collective-permute-start.5) | collective-permute-done | bytes 65568 | tf_op jit(solution)/shard_map/ppermute | solution.py:16
  17.7 1.9 %collective-permute-done.4 = f32[32,512]{1,0:T(8,128)S(1)} collective-permute-done((f32[32,512]{1,0:T(8,128)S(1)}, f32[32,512]{1,0:T(8,128)S(1)}, u32[]{:S(2)}, u32[]{:S(2)}) %collective-permute-start.4) | collective-permute-done | bytes 65568 | tf_op jit(solution)/shard_map/ppermute | solution.py:16
  19.6 0.9 %collective-permute-done.3 = f32[32,512]{1,0:T(8,128)S(1)} collective-permute-done((f32[32,512]{1,0:T(8,128)S(1)}, f32[32,512]{1,0:T(8,128)S(1)}, u32[]{:S(2)}, u32[]{:S(2)}) %collective-permute-start.3) | collective-permute-done | bytes 65568 | tf_op jit(solution)/shard_map/ppermute | solution.py:16
  20.5 0.1 collective-permute-start.6
  20.6 1.6 %collective-permute-start.8 = (f32[32,512]{1,0:T(8,128)S(1)}, f32[32,512]{1,0:T(8,128)S(1)}, u32[]{:S(2)}, u32[]{:S(2)}) collective-permute-start(f32[32,512]{1,0:T(8,128)S(1)} %add_add_fusion.refs_0_), channel_id=1, source_target_pairs={{0,3},{1,2},{2,1},{3,0},{4,7},{5,6},{6,5},{7,4},{8,11},{9,10},{10,... | collective-permute-start | bytes 196616 | tf_op jit(solution)/shard_map/ppermute | solution.py:16
  22.2 0.5 collective-permute-start.7
  22.7 0.0 collective-permute-done.6.refs_1_
  22.7 0.5 chunk.6.refs_2_
  23.2 1.8 %collective-permute-start.10 = (f32[64,512]{1,0:T(8,128)S(1)}, f32[64,512]{1,0:T(8,128)S(1)}, u32[]{:S(2)}, u32[]{:S(2)}) collective-permute-start(f32[64,512]{1,0:T(8,128)S(1)} %chunk.6.refs_2_), channel_id=1, source_target_pairs={{0,8},{4,12},{8,0},{12,4},{1,9},{5,13},{9,1},{13,5},{2,10},{6,14},... | collective-permute-start | bytes 393224 | tf_op jit(solution)/shard_map/ppermute | solution.py:16
  24.9 0.5 chunk.7.refs_2_
  25.4 2.8 %collective-permute-start.12 = (f32[64,512]{1,0:T(8,128)S(1)}, f32[64,512]{1,0:T(8,128)S(1)}, u32[]{:S(2)}, u32[]{:S(2)}) collective-permute-start(f32[64,512]{1,0:T(8,128)S(1)} %chunk.7.refs_2_), channel_id=1, source_target_pairs={{0,12},{4,8},{8,4},{12,0},{1,13},{5,9},{9,5},{13,1},{2,14},{6,10},... | collective-permute-start | bytes 393224 | tf_op jit(solution)/shard_map/ppermute | solution.py:16
  28.2 0.0 collective-permute-done.8.refs_3_.refs_1_
  28.2 0.0 collective-permute-done.7.refs_2_.refs_0_
  28.2 0.5 chunk.8.refs_4_
  28.7 0.5 chunk.9.refs_4_
  29.2 0.3 collective-permute-start.9
  30.2 1.8 %collective-permute-start.11 = (f32[64,512]{1,0:T(8,128)S(1)}, f32[64,512]{1,0:T(8,128)S(1)}, u32[]{:S(2)}, u32[]{:S(2)}) collective-permute-start(f32[64,512]{1,0:T(8,128)S(1)} %chunk.8.refs_4_), channel_id=1, source_target_pairs={{0,8},{4,12},{8,0},{12,4},{1,9},{5,13},{9,1},{13,5},{2,10},{6,14},... | collective-permute-start | bytes 393224 | tf_op jit(solution)/shard_map/ppermute | solution.py:16
  31.9 0.5 chunk.10.refs_0_.refs_2_
  32.4 0.0 copy-start
  32.4 6.1 %factor_x.1.inverse_ref.refs_5_ = f32[128,128]{1,0:T(8,128)S(1)} custom-call(s32[1]{0:T(128)S(6)} %copy.9.rank_ref, s32[1]{0:T(128)} %bitcast.2.me_ref, f32[32,512]{1,0:T(8,128)S(1)} %add_add_fusion.refs_0_, f32[32,512]{1,0:T(8,128)S(1)} %collective-permute-done.6.refs_1_, f32[32,512]{1,0:T(8,128)S(1)} %collective-permute-done.7.refs_2_.refs_0_, ...), custom_call_target="tpu_custom_call" | custom-call | tf_op jit(solution)/shard_map/factor_x/pallas_call | solution.py:88
  38.5 0.0 collective-permute-done.12.refs_4_.refs_0_
  38.6 0.0 collective-permute-done.10.refs_0_.refs_3_
  38.6 0.5 chunk.11
  39.0 2.5 %collective-permute-start.13 = (f32[64,512]{1,0:T(8,128)S(1)}, f32[64,512]{1,0:T(8,128)S(1)}, u32[]{:S(2)}, u32[]{:S(2)}) collective-permute-start(f32[64,512]{1,0:T(8,128)S(1)} %chunk.11), channel_id=1, source_target_pairs={{0,12},{4,8},{8,4},{12,0},{1,13},{5,9},{9,5},{13,1},{2,14},{6,10},... | collective-permute-start | bytes 393224 | tf_op jit(solution)/shard_map/ppermute | solution.py:16
  41.5 0.3 lift.4.refs_2_.refs_0_
  41.8 5.5 %collective-permute-done.11.refs_1_ = f32[64,512]{1,0:T(8,128)S(1)} collective-permute-done((f32[64,512]{1,0:T(8,128)S(1)}, f32[64,512]{1,0:T(8,128)S(1)}, u32[]{:S(2)}, u32[]{:S(2)}) %collective-permute-start.11) | collective-permute-done | bytes 131104 | tf_op jit(solution)/shard_map/ppermute | solution.py:16
  47.3 0.3 lift.5.refs_1_.refs_2_
  47.6 0.0 collective-permute-done.9.refs_0_
  47.7 0.3 lift.6.refs_2_.refs_1_
  48.0 0.0 collective-permute-done.13.refs_1_
  48.0 0.3 lift.7.refs_3_
  48.3 0.0 copy-done
  48.3 1.0 %gram.1 = f32[64,32]{1,0:T(8,128)S(1)} custom-call(s32[1]{0:T(128)} %bitcast.here_ref.me_ref, f32[32,64]{1,0:T(8,128)S(1)} %bitcast.11, f32[16,4096]{1,0:T(8,128)S(1)} %lift.4.refs_2_.refs_0_, f32[16,4096]{1,0:T(8,128)S(1)} %lift.6.refs_2_.refs_1_, f32[16,4096]{1,0:T(8,128)S(1)} %lift.5.refs_1_.refs_2_, f32[16,4096]{1,0:T(8,128)S(1)} %lift.7.refs_3_), custom_call_target="tpu_custom_call" | custom-call | tf_op jit(solution)/shard_map/gram/pallas_call | solution.py:88
  49.3 0.0 collective-permute-start.14
  49.3 1.2 %collective-permute-done.14 = f32[64,32]{1,0:T(8,128)S(1)} collective-permute-done((f32[64,32]{1,0:T(8,128)S(1)}, f32[64,32]{1,0:T(8,128)S(1)}, u32[]{:S(2)}, u32[]{:S(2)}) %collective-permute-start.14) | collective-permute-done | bytes 8224 | tf_op jit(solution)/shard_map/ppermute | solution.py:16
  50.5 1.4 %collective-permute-start.15 = (f32[64,32]{1,0:T(8,128)S(1)}, f32[64,32]{1,0:T(8,128)S(1)}, u32[]{:S(2)}, u32[]{:S(2)}) collective-permute-start(f32[64,32]{1,0:T(8,128)S(1)} %add.34), channel_id=1, source_target_pairs={{0,2},{2,0},{1,3},{3,1},{4,6},{6,4},{5,7},{7,5},{8,10},{10,8},{9,1... | collective-permute-start | bytes 24584 | tf_op jit(solution)/shard_map/ppermute | solution.py:16
  51.9 2.5 %collective-permute-done.15 = f32[64,32]{1,0:T(8,128)S(1)} collective-permute-done((f32[64,32]{1,0:T(8,128)S(1)}, f32[64,32]{1,0:T(8,128)S(1)}, u32[]{:S(2)}, u32[]{:S(2)}) %collective-permute-start.15) | collective-permute-done | bytes 8224 | tf_op jit(solution)/shard_map/ppermute | solution.py:16
  54.4 1.6 %collective-permute-start.18 = (f32[64,32]{1,0:T(8,128)S(1)}, f32[64,32]{1,0:T(8,128)S(1)}, u32[]{:S(2)}, u32[]{:S(2)}) collective-permute-start(f32[64,32]{1,0:T(8,128)S(1)} %add.35.refs_0_), channel_id=1, source_target_pairs={{0,12},{4,8},{8,4},{12,0},{1,13},{5,9},{9,5},{13,1},{2,14},{6,10},... | collective-permute-start | bytes 24584 | tf_op jit(solution)/shard_map/ppermute | solution.py:16
  56.0 1.5 %collective-permute-start.17 = (f32[64,32]{1,0:T(8,128)S(1)}, f32[64,32]{1,0:T(8,128)S(1)}, u32[]{:S(2)}, u32[]{:S(2)}) collective-permute-start(f32[64,32]{1,0:T(8,128)S(1)} %add.35.refs_0_), channel_id=1, source_target_pairs={{0,8},{4,12},{8,0},{12,4},{1,9},{5,13},{9,1},{13,5},{2,10},{6,14},... | collective-permute-start | bytes 24584 | tf_op jit(solution)/shard_map/ppermute | solution.py:16
  57.4 1.3 %collective-permute-start.16 = (f32[64,32]{1,0:T(8,128)S(1)}, f32[64,32]{1,0:T(8,128)S(1)}, u32[]{:S(2)}, u32[]{:S(2)}) collective-permute-start(f32[64,32]{1,0:T(8,128)S(1)} %add.35.refs_0_), channel_id=1, source_target_pairs={{0,4},{4,0},{8,12},{12,8},{1,5},{5,1},{9,13},{13,9},{2,6},{6,2},{1... | collective-permute-start | bytes 24584 | tf_op jit(solution)/shard_map/ppermute | solution.py:16
  59.4 0.9 %collective-permute-done.18.refs_3_ = f32[64,32]{1,0:T(8,128)S(1)} collective-permute-done((f32[64,32]{1,0:T(8,128)S(1)}, f32[64,32]{1,0:T(8,128)S(1)}, u32[]{:S(2)}, u32[]{:S(2)}) %collective-permute-start.18) | collective-permute-done | bytes 8224 | tf_op jit(solution)/shard_map/ppermute | solution.py:16
  60.4 0.4 collective-permute-done.17.refs_2_
  60.8 0.6 collective-permute-done.16.refs_1_
  61.4 1.4 %factor_y.1.factor_ref = f32[64,32]{1,0:T(8,128)S(1)} custom-call(s32[1]{0:T(128)S(6)} %copy.10.rank_ref, f32[64,32]{1,0:T(8,128)S(1)} %add.35.refs_0_, f32[64,32]{1,0:T(8,128)S(1)} %collective-permute-done.16.refs_1_, f32[64,32]{1,0:T(8,128)S(1)} %collective-permute-done.17.refs_2_, f32[64,32]{1,0:T(8,128)S(1)} %collective-permute-done.18.refs_3_), custom_call_target="tpu_custom_call" | custom-call | tf_op jit(solution)/shard_map/factor_y/pallas_call | solution.py:88
  62.7 0.5 mix.1
  63.3 1.6 %collective-permute-start.19 = (f32[4,8,8,128]{3,2,1,0:T(8,128)S(1)}, f32[4,8,8,128]{3,2,1,0:T(8,128)S(1)}, u32[]{:S(2)}, u32[]{:S(2)}) collective-permute-start(f32[4,8,8,128]{3,2,1,0:T(8,128)S(1)} %get-tuple-element.17), channel_id=1, source_target_pairs={{0,8},{4,12},{8,0},{12,4},{1,9},{5,13},{9,1},{13,5},{2,10},{6,14},... | collective-permute-start | bytes 393224 | tf_op jit(solution)/shard_map/ppermute | solution.py:16
  64.9 1.7 %collective-permute-start.20 = (f32[4,8,8,128]{3,2,1,0:T(8,128)S(1)}, f32[4,8,8,128]{3,2,1,0:T(8,128)S(1)}, u32[]{:S(2)}, u32[]{:S(2)}) collective-permute-start(f32[4,8,8,128]{3,2,1,0:T(8,128)S(1)} %get-tuple-element.18), channel_id=1, source_target_pairs={{0,4},{4,0},{8,12},{12,8},{1,5},{5,1},{9,13},{13,9},{2,6},{6,2},{1... | collective-permute-start | bytes 393224 | tf_op jit(solution)/shard_map/ppermute | solution.py:16
  66.5 1.2 %collective-permute-start.21 = (f32[4,8,8,128]{3,2,1,0:T(8,128)S(1)}, f32[4,8,8,128]{3,2,1,0:T(8,128)S(1)}, u32[]{:S(2)}, u32[]{:S(2)}) collective-permute-start(f32[4,8,8,128]{3,2,1,0:T(8,128)S(1)} %get-tuple-element.19), channel_id=1, source_target_pairs={{0,12},{4,8},{8,4},{12,0},{1,13},{5,9},{9,5},{13,1},{2,14},{6,10},... | collective-permute-start | bytes 393224 | tf_op jit(solution)/shard_map/ppermute | solution.py:16
  67.7 1.1 %apply.1 = f32[512,128]{1,0:T(8,128)} custom-call(f32[128,128]{1,0:T(8,128)S(1)} %factor_x.1.inverse_ref.refs_5_, f32[32,512]{1,0:T(8,128)S(1)} %add_add_fusion.refs_0_, f32[32,512]{1,0:T(8,128)S(1)} %collective-permute-done.6.refs_1_, f32[32,512]{1,0:T(8,128)S(1)} %collective-permute-done.7.refs_2_.refs_0_, f32[32,512]{1,0:T(8,128)S(1)} %collective-permute-done.8.refs_3_.refs_1_), custom_call_target="tpu_custom_call" | custom-call | tf_op jit(solution)/shard_map/apply/pallas_call | solution.py:88
  68.8 0.7 copy.8
  69.5 4.5 %collective-permute-done.19.refs_0_ = f32[4,8,8,128]{3,2,1,0:T(8,128)S(1)} collective-permute-done((f32[4,8,8,128]{3,2,1,0:T(8,128)S(1)}, f32[4,8,8,128]{3,2,1,0:T(8,128)S(1)}, u32[]{:S(2)}, u32[]{:S(2)}) %collective-permute-start.19) | collective-permute-done | bytes 131104 | tf_op jit(solution)/shard_map/ppermute | solution.py:16
  74.0 0.0 collective-permute-done.20.refs_1_
  74.0 0.0 collective-permute-done.21.refs_2_
  74.0 0.8 %place.1 = f32[4,8,32,128]{3,2,1,0:T(8,128)} custom-call(s32[1]{0:T(128)} %bitcast.here_ref.me_ref, f32[4,8,8,128]{3,2,1,0:T(8,128)S(1)} %collective-permute-done.19.refs_0_, f32[4,8,8,128]{3,2,1,0:T(8,128)S(1)} %collective-permute-done.20.refs_1_, f32[4,8,8,128]{3,2,1,0:T(8,128)S(1)} %collective-permute-done.21.refs_2_, ...), custom_call_target="tpu_custom_call" | custom-call | tf_op jit(solution)/shard_map/place/pallas_call | solution.py:250
  (5 shorter events, 0.1 us)
Async XLA Ops:
  4.5 1.4 %collective-permute-start.1 = (f32[32,512]{1,0:T(8,128)S(1)}, f32[32,512]{1,0:T(8,128)S(1)}, u32[]{:S(2)}, u32[]{:S(2)}) collective-permute-start(f32[32,512]{1,0:T(8,128)S(1)} %get-tuple-element.15), channel_id=1, source_target_pairs={{0,1},{1,0},{2,3},{3,2},{4,5},{5,4},{6,7},{7,6},{8,9},{9,8},{10,11... | collective-permute-start | bytes 196616 | tf_op jit(solution)/shard_map/ppermute | solution.py:16
  5.0 3.8 %collective-permute-start = (f32[32,512]{1,0:T(8,128)S(1)}, f32[32,512]{1,0:T(8,128)S(1)}, u32[]{:S(2)}, u32[]{:S(2)}) collective-permute-start(f32[32,512]{1,0:T(8,128)S(1)} %get-tuple-element.13), channel_id=1, source_target_pairs={{0,1},{1,0},{2,3},{3,2},{4,5},{5,4},{6,7},{7,6},{8,9},{9,8},{10,11... | collective-permute-start | bytes 196616 | tf_op jit(solution)/shard_map/ppermute | solution.py:16
  5.9 5.3 %collective-permute-start.2 = (f32[32,512]{1,0:T(8,128)S(1)}, f32[32,512]{1,0:T(8,128)S(1)}, u32[]{:S(2)}, u32[]{:S(2)}) collective-permute-start(f32[32,512]{1,0:T(8,128)S(1)} %add.29), channel_id=1, source_target_pairs={{0,2},{2,0},{1,3},{3,1},{4,6},{6,4},{5,7},{7,5},{8,10},{10,8},{9,1... | collective-permute-start | bytes 196616 | tf_op jit(solution)/shard_map/ppermute | solution.py:16
  11.3 6.4 %collective-permute-start.5 = (f32[32,512]{1,0:T(8,128)S(1)}, f32[32,512]{1,0:T(8,128)S(1)}, u32[]{:S(2)}, u32[]{:S(2)}) collective-permute-start(f32[32,512]{1,0:T(8,128)S(1)} %add_add_fusion.1), channel_id=1, source_target_pairs={{0,12},{4,8},{8,4},{12,0},{1,13},{5,9},{9,5},{13,1},{2,14},{6,10},... | collective-permute-start | bytes 196616 | tf_op jit(solution)/shard_map/ppermute | solution.py:16
  15.3 4.3 %collective-permute-start.4 = (f32[32,512]{1,0:T(8,128)S(1)}, f32[32,512]{1,0:T(8,128)S(1)}, u32[]{:S(2)}, u32[]{:S(2)}) collective-permute-start(f32[32,512]{1,0:T(8,128)S(1)} %add_add_fusion.1), channel_id=1, source_target_pairs={{0,4},{4,0},{8,12},{12,8},{1,5},{5,1},{9,13},{13,9},{2,6},{6,2},{1... | collective-permute-start | bytes 196616 | tf_op jit(solution)/shard_map/ppermute | solution.py:16
  15.3 5.2 %collective-permute-start.3 = (f32[32,512]{1,0:T(8,128)S(1)}, f32[32,512]{1,0:T(8,128)S(1)}, u32[]{:S(2)}, u32[]{:S(2)}) collective-permute-start(f32[32,512]{1,0:T(8,128)S(1)} %add_add_fusion.1), channel_id=1, source_target_pairs={{0,8},{4,12},{8,0},{12,4},{1,9},{5,13},{9,1},{13,5},{2,10},{6,14},... | collective-permute-start | bytes 196616 | tf_op jit(solution)/shard_map/ppermute | solution.py:16
  20.5 2.2 %collective-permute-start.6 = (f32[32,512]{1,0:T(8,128)S(1)}, f32[32,512]{1,0:T(8,128)S(1)}, u32[]{:S(2)}, u32[]{:S(2)}) collective-permute-start(f32[32,512]{1,0:T(8,128)S(1)} %add_add_fusion.refs_0_), channel_id=1, source_target_pairs={{0,1},{1,0},{2,3},{3,2},{4,5},{5,4},{6,7},{7,6},{8,9},{9,8},{10,11... | collective-permute-start | bytes 196616 | tf_op jit(solution)/shard_map/ppermute | solution.py:16
  20.6 7.6 %collective-permute-start.8 = (f32[32,512]{1,0:T(8,128)S(1)}, f32[32,512]{1,0:T(8,128)S(1)}, u32[]{:S(2)}, u32[]{:S(2)}) collective-permute-start(f32[32,512]{1,0:T(8,128)S(1)} %add_add_fusion.refs_0_), channel_id=1, source_target_pairs={{0,3},{1,2},{2,1},{3,0},{4,7},{5,6},{6,5},{7,4},{8,11},{9,10},{10,... | collective-permute-start | bytes 196616 | tf_op jit(solution)/shard_map/ppermute | solution.py:16
  22.2 6.0 %collective-permute-start.7 = (f32[32,512]{1,0:T(8,128)S(1)}, f32[32,512]{1,0:T(8,128)S(1)}, u32[]{:S(2)}, u32[]{:S(2)}) collective-permute-start(f32[32,512]{1,0:T(8,128)S(1)} %add_add_fusion.refs_0_), channel_id=1, source_target_pairs={{0,2},{1,3},{2,0},{3,1},{4,6},{5,7},{6,4},{7,5},{8,10},{9,11},{10,... | collective-permute-start | bytes 196616 | tf_op jit(solution)/shard_map/ppermute | solution.py:16
  23.2 15.4 %collective-permute-start.10 = (f32[64,512]{1,0:T(8,128)S(1)}, f32[64,512]{1,0:T(8,128)S(1)}, u32[]{:S(2)}, u32[]{:S(2)}) collective-permute-start(f32[64,512]{1,0:T(8,128)S(1)} %chunk.6.refs_2_), channel_id=1, source_target_pairs={{0,8},{4,12},{8,0},{12,4},{1,9},{5,13},{9,1},{13,5},{2,10},{6,14},... | collective-permute-start | bytes 393224 | tf_op jit(solution)/shard_map/ppermute | solution.py:16
  25.4 13.1 %collective-permute-start.12 = (f32[64,512]{1,0:T(8,128)S(1)}, f32[64,512]{1,0:T(8,128)S(1)}, u32[]{:S(2)}, u32[]{:S(2)}) collective-permute-start(f32[64,512]{1,0:T(8,128)S(1)} %chunk.7.refs_2_), channel_id=1, source_target_pairs={{0,12},{4,8},{8,4},{12,0},{1,13},{5,9},{9,5},{13,1},{2,14},{6,10},... | collective-permute-start | bytes 393224 | tf_op jit(solution)/shard_map/ppermute | solution.py:16
  29.2 18.5 %collective-permute-start.9 = (f32[128,512]{1,0:T(8,128)S(1)}, f32[128,512]{1,0:T(8,128)S(1)}, u32[]{:S(2)}, u32[]{:S(2)}) collective-permute-start(f32[128,512]{1,0:T(8,128)S(1)} %chunk.9.refs_4_), channel_id=1, source_target_pairs={{0,4},{4,0},{8,12},{12,8},{1,5},{5,1},{9,13},{13,9},{2,6},{6,2},{1... | collective-permute-start | bytes 786440 | tf_op jit(solution)/shard_map/ppermute | solution.py:16
  30.2 17.2 %collective-permute-start.11 = (f32[64,512]{1,0:T(8,128)S(1)}, f32[64,512]{1,0:T(8,128)S(1)}, u32[]{:S(2)}, u32[]{:S(2)}) collective-permute-start(f32[64,512]{1,0:T(8,128)S(1)} %chunk.8.refs_4_), channel_id=1, source_target_pairs={{0,8},{4,12},{8,0},{12,4},{1,9},{5,13},{9,1},{13,5},{2,10},{6,14},... | collective-permute-start | bytes 393224 | tf_op jit(solution)/shard_map/ppermute | solution.py:16
  32.4 15.9 %copy-start = (f32[64,32]{0,1:T(8,128)S(1)}, f32[64,32]{0,1:T(8,128)}, u32[]{:S(2)}) copy-start(f32[64,32]{0,1:T(8,128)} %param.7) | copy-start | bytes 24580
  39.0 8.9 %collective-permute-start.13 = (f32[64,512]{1,0:T(8,128)S(1)}, f32[64,512]{1,0:T(8,128)S(1)}, u32[]{:S(2)}, u32[]{:S(2)}) collective-permute-start(f32[64,512]{1,0:T(8,128)S(1)} %chunk.11), channel_id=1, source_target_pairs={{0,12},{4,8},{8,4},{12,0},{1,13},{5,9},{9,5},{13,1},{2,14},{6,10},... | collective-permute-start | bytes 393224 | tf_op jit(solution)/shard_map/ppermute | solution.py:16
  49.3 1.2 %collective-permute-start.14 = (f32[64,32]{1,0:T(8,128)S(1)}, f32[64,32]{1,0:T(8,128)S(1)}, u32[]{:S(2)}, u32[]{:S(2)}) collective-permute-start(f32[64,32]{1,0:T(8,128)S(1)} %gram.1), channel_id=1, source_target_pairs={{0,1},{1,0},{2,3},{3,2},{4,5},{5,4},{6,7},{7,6},{8,9},{9,8},{10,11... | collective-permute-start | bytes 24584 | tf_op jit(solution)/shard_map/ppermute | solution.py:16
  50.5 3.9 %collective-permute-start.15 = (f32[64,32]{1,0:T(8,128)S(1)}, f32[64,32]{1,0:T(8,128)S(1)}, u32[]{:S(2)}, u32[]{:S(2)}) collective-permute-start(f32[64,32]{1,0:T(8,128)S(1)} %add.34), channel_id=1, source_target_pairs={{0,2},{2,0},{1,3},{3,1},{4,6},{6,4},{5,7},{7,5},{8,10},{10,8},{9,1... | collective-permute-start | bytes 24584 | tf_op jit(solution)/shard_map/ppermute | solution.py:16
  54.4 6.0 %collective-permute-start.18 = (f32[64,32]{1,0:T(8,128)S(1)}, f32[64,32]{1,0:T(8,128)S(1)}, u32[]{:S(2)}, u32[]{:S(2)}) collective-permute-start(f32[64,32]{1,0:T(8,128)S(1)} %add.35.refs_0_), channel_id=1, source_target_pairs={{0,12},{4,8},{8,4},{12,0},{1,13},{5,9},{9,5},{13,1},{2,14},{6,10},... | collective-permute-start | bytes 24584 | tf_op jit(solution)/shard_map/ppermute | solution.py:16
  56.0 4.8 %collective-permute-start.17 = (f32[64,32]{1,0:T(8,128)S(1)}, f32[64,32]{1,0:T(8,128)S(1)}, u32[]{:S(2)}, u32[]{:S(2)}) collective-permute-start(f32[64,32]{1,0:T(8,128)S(1)} %add.35.refs_0_), channel_id=1, source_target_pairs={{0,8},{4,12},{8,0},{12,4},{1,9},{5,13},{9,1},{13,5},{2,10},{6,14},... | collective-permute-start | bytes 24584 | tf_op jit(solution)/shard_map/ppermute | solution.py:16
  57.4 3.9 %collective-permute-start.16 = (f32[64,32]{1,0:T(8,128)S(1)}, f32[64,32]{1,0:T(8,128)S(1)}, u32[]{:S(2)}, u32[]{:S(2)}) collective-permute-start(f32[64,32]{1,0:T(8,128)S(1)} %add.35.refs_0_), channel_id=1, source_target_pairs={{0,4},{4,0},{8,12},{12,8},{1,5},{5,1},{9,13},{13,9},{2,6},{6,2},{1... | collective-permute-start | bytes 24584 | tf_op jit(solution)/shard_map/ppermute | solution.py:16
  63.3 10.8 %collective-permute-start.19 = (f32[4,8,8,128]{3,2,1,0:T(8,128)S(1)}, f32[4,8,8,128]{3,2,1,0:T(8,128)S(1)}, u32[]{:S(2)}, u32[]{:S(2)}) collective-permute-start(f32[4,8,8,128]{3,2,1,0:T(8,128)S(1)} %get-tuple-element.17), channel_id=1, source_target_pairs={{0,8},{4,12},{8,0},{12,4},{1,9},{5,13},{9,1},{13,5},{2,10},{6,14},... | collective-permute-start | bytes 393224 | tf_op jit(solution)/shard_map/ppermute | solution.py:16
  64.9 9.2 %collective-permute-start.20 = (f32[4,8,8,128]{3,2,1,0:T(8,128)S(1)}, f32[4,8,8,128]{3,2,1,0:T(8,128)S(1)}, u32[]{:S(2)}, u32[]{:S(2)}) collective-permute-start(f32[4,8,8,128]{3,2,1,0:T(8,128)S(1)} %get-tuple-element.18), channel_id=1, source_target_pairs={{0,4},{4,0},{8,12},{12,8},{1,5},{5,1},{9,13},{13,9},{2,6},{6,2},{1... | collective-permute-start | bytes 393224 | tf_op jit(solution)/shard_map/ppermute | solution.py:16
  66.5 7.5 %collective-permute-start.21 = (f32[4,8,8,128]{3,2,1,0:T(8,128)S(1)}, f32[4,8,8,128]{3,2,1,0:T(8,128)S(1)}, u32[]{:S(2)}, u32[]{:S(2)}) collective-permute-start(f32[4,8,8,128]{3,2,1,0:T(8,128)S(1)} %get-tuple-element.19), channel_id=1, source_target_pairs={{0,12},{4,8},{8,4},{12,0},{1,13},{5,9},{9,5},{13,1},{2,14},{6,10},... | collective-permute-start | bytes 393224 | tf_op jit(solution)/shard_map/ppermute | solution.py:16

commit v10 on v9

--- a/solution.py
+++ b/solution.py
@@ -201,8 +201,13 @@
     return kernel_call(kernel, "lift", shape, [], [inverse] + chunk + after)
 
 
-def gram_kernel(me_ref, omega_ref, *refs):
-    *slab_refs, part_ref, rows_ref, cols_ref = refs
+def gram_kernel(planes, share_z, order, count, me_ref, omega_ref, inverse_ref, *refs):
+    chunk_refs, early = refs[:count], refs[count:-4]
+    part_ref, last_ref, rows_ref, cols_ref = refs[-4:]
+    lift_kernel(planes, share_z, count, inverse_ref, *chunk_refs, last_ref)
+    slab_refs = [None] * (len(order))
+    for k, ref in zip(order, [*early, last_ref]):
+        slab_refs[k] = ref
     share = slab_refs[0].shape[0]
     high, low = halves(jnp.concatenate([ref[...] for ref in slab_refs], axis=0))
     rows_ref[...] = mxu(high, high, dims(1, 1)) + (mxu(high, low, dims(1, 1)) + mxu(low, high, dims(1, 1)))
@@ -230,6 +235,13 @@
             at = lambda z: (v * share_z + z) * width
             rows = jnp.stack([block[:, at(z):at(z) + width] for z in range(share_z)], axis=0)
             ref[v] = jnp.swapaxes(rows, 0, 1)
+
+
+def last_kernel(divisor, which, count, rank_ref, me_ref, *refs):
+    parts, slabs, blocks = refs[:count], refs[count:2 * count], refs[2 * count + 1:-2]
+    factor_ref, inverse, mixed = refs[2 * count], refs[-2], refs[-1]
+    factor_y_kernel(divisor, rank_ref, *parts, factor_ref, inverse)
+    mix_kernel(which, me_ref, factor_ref, *slabs, *blocks, mixed)
 
 
 def place_kernel(order, me_ref, *refs):
@@ -395,12 +407,15 @@
     if tiled:
         slabs = [None] * n_gy
         after = []
-        for s in [0] + order:
+        for s in ([0] + order)[:-1]:
             slabs[s] = lift(planes, share_z, inverse_x, chunks[s], after)
             after = [slabs[s]]
         scratch = [pltpu.VMEM((all_rows_y, all_rows_y), jnp.float32)] * 2
-        shape = (all_rows_y, ranks_y)
-        part_y = kernel_call(gram_kernel, "gram", shape, [here], [omega_y.T] + slabs, scratch)
+        last = order[-1]
+        kernel = functools.partial(gram_kernel, planes, share_z, [0] + order, len(chunks[last]))
+        values = [omega_y.T, inverse_x] + chunks[last] + [slabs[s] for s in [0] + order[:-1]]
+        shapes = [(all_rows_y, ranks_y), slabs[0].shape]
+        part_y, slabs[last] = kernel_call(kernel, "gram", shapes, [here], values, scratch)
     else:
         spread = jnp.stack(chunks).reshape(-1, ranks_x)
         spread = lax.dot_general(spread, inverse_x, dims(1, 0), precision=HIGHEST)
@@ -416,20 +431,23 @@
         for other in got:
             part_y = part_y + other
     parts = [part_y] + [swap(part_y, "gy", s) for s in range(1, n_gy)]
-    factor_y = make_factor_y(rank_y, parts, float(all_planes * all_rows_z * ranks_x))
-
+    divisor = float(all_planes * all_rows_z * ranks_x)
     if tiled:
         shape = (planes, share_k, share_z, ranks_x)
-        scratch = [pltpu.VMEM((ranks_y, planes * share_z * ranks_x), jnp.float32)]
-
         which = steps(n_gy) + [0]
-        kernel = functools.partial(mix_kernel, which)
-        blocks = kernel_call(kernel, "mix", [shape] * n_gy, [here], [factor_y] + slabs, scratch)
+        kernel = functools.partial(last_kernel, divisor, which, n_gy)
+        shapes = [(all_rows_y, ranks_y)] + [shape] * n_gy
+        scratch = [
+            pltpu.VMEM((ranks_y, ranks_y), jnp.float32),
+            pltpu.VMEM((ranks_y, planes * share_z * ranks_x), jnp.float32),
+        ]
+        factor_y, *blocks = kernel_call(kernel, "last", shapes, [rank_y, here], parts + slabs, scratch)
         pieces = [None] * n_gy
         for s, block in zip(which, blocks):
             pieces[s] = swap(block, "gy", s) if s else block
         core = place(here, pieces, (planes, share_k, rows_z, ranks_x))
         return (core, factor_x, factor_y)
+    factor_y = make_factor_y(rank_y, parts, divisor)
     weights = by_step(factor_y.reshape(n_gy, rows_y, ranks_y), gy, n_gy)
     weights = weights.reshape(n_gy, rows_y, n_gy, share_k)
     weights = jnp.moveaxis(by_step(jnp.moveaxis(weights, 2, 0), gy, n_gy), 0, 2)

time: 75 us -> 75.1 us (level)
    pallas_call x15 -> x13, Pallas kernels: 14.2 us -> 14.3 us  [kernel_call(): pl.pallas_call(body, in_specs=[SMEM] * len(scalars) + [VMEM] * len(values...]
where the time goes in v10:
time: 75.1 us; the launch traced here: 74.9 us
  starting transfers between devices  29.7 us (40%)
  waiting for transfers between devices  23.4 us (31%)
  Pallas kernels  18.9 us (25%)
  between operations  2.1 us (3%)
    ppermute x22, starting transfers between devices, swap(): return lax.ppermute(value, axes, [(i, i ^ step) for i in range(count)])  29.7 us
    ppermute x22, waiting for transfers between devices, swap(): return lax.ppermute(value, axes, [(i, i ^ step) for i in range(count)])  23.4 us
    pallas_call x13, Pallas kernels, kernel_call(): pl.pallas_call(body, in_specs=[SMEM] * len(scalars) + [VMEM] * len(values...  14.3 us
    pallas_call x1, Pallas kernels, sketch_parts(): pl.pallas_call(sketch_kernel, in_specs=[SMEM, SMEM, far, far], out_specs=...  3.85 us
  transfers between devices with their start and end apart: 22, of which 12 were waited for; matrix products, arithmetic and copies ran while one was open for 1% of the time, Pallas kernels for 15%

profile of v10, /device:TPU:0, one launch (start us, length us, event | category | flops | bytes accessed | tf_op | source)
XLA Modules:
  0.0 74.9 jit_solution(18424490231996710787)
XLA Ops:
  0.6 3.9 %sketch.1 = (f32[2048,512]{1,0:T(8,128)S(1)}, f32[32,512]{1,0:T(8,128)S(1)}, f32[32,512]{1,0:T(8,128)S(1)}, f32[32,512]{1,0:T(8,128)S(1)}, f32[32,512]{1,0:T(8,128)S(1)}) custom-call(s32[1]{0:T(128)} %bitcast.2.me_ref, s32[1]{0:T(128)} %bitcast.here_ref.me_ref, f32[2048,512]{1,0:T(8,128)} %bitcast.12, f32[512,128]{1,0:T(8,128)} %omega_hbm.1), custom_call_target="tpu_custom_call" | custom-call | tf_op jit(solution)/shard_map/sketch/pallas_call | solution.py:139
  4.5 0.5 collective-permute-start.1
  5.0 0.1 collective-permute-start
  5.1 0.8 %collective-permute-done.1 = f32[32,512]{1,0:T(8,128)S(1)} collective-permute-done((f32[32,512]{1,0:T(8,128)S(1)}, f32[32,512]{1,0:T(8,128)S(1)}, u32[]{:S(2)}, u32[]{:S(2)}) %collective-permute-start.1) | collective-permute-done | bytes 65568 | tf_op jit(solution)/shard_map/ppermute | solution.py:16
  5.9 2.9 %collective-permute-start.2 = (f32[32,512]{1,0:T(8,128)S(1)}, f32[32,512]{1,0:T(8,128)S(1)}, u32[]{:S(2)}, u32[]{:S(2)}) collective-permute-start(f32[32,512]{1,0:T(8,128)S(1)} %add.29), channel_id=1, source_target_pairs={{0,2},{2,0},{1,3},{3,1},{4,6},{6,4},{5,7},{7,5},{8,10},{10,8},{9,1... | collective-permute-start | bytes 196616 | tf_op jit(solution)/shard_map/ppermute | solution.py:16
  8.8 0.0 collective-permute-done
  8.8 2.4 %collective-permute-done.2 = f32[32,512]{1,0:T(8,128)S(1)} collective-permute-done((f32[32,512]{1,0:T(8,128)S(1)}, f32[32,512]{1,0:T(8,128)S(1)}, u32[]{:S(2)}, u32[]{:S(2)}) %collective-permute-start.2) | collective-permute-done | bytes 65568 | tf_op jit(solution)/shard_map/ppermute | solution.py:16
  11.3 4.0 %collective-permute-start.5 = (f32[32,512]{1,0:T(8,128)S(1)}, f32[32,512]{1,0:T(8,128)S(1)}, u32[]{:S(2)}, u32[]{:S(2)}) collective-permute-start(f32[32,512]{1,0:T(8,128)S(1)} %add_add_fusion.1), channel_id=1, source_target_pairs={{0,12},{4,8},{8,4},{12,0},{1,13},{5,9},{9,5},{13,1},{2,14},{6,10},... | collective-permute-start | bytes 196616 | tf_op jit(solution)/shard_map/ppermute | solution.py:16
  15.3 0.0 collective-permute-start.4
  15.3 0.6 collective-permute-start.3
  15.9 1.8 %collective-permute-done.5 = f32[32,512]{1,0:T(8,128)S(1)} collective-permute-done((f32[32,512]{1,0:T(8,128)S(1)}, f32[32,512]{1,0:T(8,128)S(1)}, u32[]{:S(2)}, u32[]{:S(2)}) %collective-permute-start.5) | collective-permute-done | bytes 65568 | tf_op jit(solution)/shard_map/ppermute | solution.py:16
  17.7 1.9 %collective-permute-done.4 = f32[32,512]{1,0:T(8,128)S(1)} collective-permute-done((f32[32,512]{1,0:T(8,128)S(1)}, f32[32,512]{1,0:T(8,128)S(1)}, u32[]{:S(2)}, u32[]{:S(2)}) %collective-permute-start.4) | collective-permute-done | bytes 65568 | tf_op jit(solution)/shard_map/ppermute | solution.py:16
  19.6 0.9 %collective-permute-done.3 = f32[32,512]{1,0:T(8,128)S(1)} collective-permute-done((f32[32,512]{1,0:T(8,128)S(1)}, f32[32,512]{1,0:T(8,128)S(1)}, u32[]{:S(2)}, u32[]{:S(2)}) %collective-permute-start.3) | collective-permute-done | bytes 65568 | tf_op jit(solution)/shard_map/ppermute | solution.py:16
  20.5 0.1 collective-permute-start.6
  20.6 1.6 %collective-permute-start.8 = (f32[32,512]{1,0:T(8,128)S(1)}, f32[32,512]{1,0:T(8,128)S(1)}, u32[]{:S(2)}, u32[]{:S(2)}) collective-permute-start(f32[32,512]{1,0:T(8,128)S(1)} %add_add_fusion.refs_0_), channel_id=1, source_target_pairs={{0,3},{1,2},{2,1},{3,0},{4,7},{5,6},{6,5},{7,4},{8,11},{9,10},{10,... | collective-permute-start | bytes 196616 | tf_op jit(solution)/shard_map/ppermute | solution.py:16
  22.2 0.5 collective-permute-start.7
  22.7 0.0 collective-permute-done.6.refs_1_
  22.7 0.5 chunk.6.refs_2_
  23.2 1.8 %collective-permute-start.10 = (f32[64,512]{1,0:T(8,128)S(1)}, f32[64,512]{1,0:T(8,128)S(1)}, u32[]{:S(2)}, u32[]{:S(2)}) collective-permute-start(f32[64,512]{1,0:T(8,128)S(1)} %chunk.6.refs_2_), channel_id=1, source_target_pairs={{0,8},{4,12},{8,0},{12,4},{1,9},{5,13},{9,1},{13,5},{2,10},{6,14},... | collective-permute-start | bytes 393224 | tf_op jit(solution)/shard_map/ppermute | solution.py:16
  24.9 0.5 chunk.7.refs_2_
  25.4 2.8 %collective-permute-start.9 = (f32[64,512]{1,0:T(8,128)S(1)}, f32[64,512]{1,0:T(8,128)S(1)}, u32[]{:S(2)}, u32[]{:S(2)}) collective-permute-start(f32[64,512]{1,0:T(8,128)S(1)} %chunk.7.refs_2_), channel_id=1, source_target_pairs={{0,12},{4,8},{8,4},{12,0},{1,13},{5,9},{9,5},{13,1},{2,14},{6,10},... | collective-permute-start | bytes 393224 | tf_op jit(solution)/shard_map/ppermute | solution.py:16
  28.2 0.0 collective-permute-done.8.refs_3_.refs_1_
  28.2 0.0 collective-permute-done.7.refs_2_.refs_0_
  28.2 0.5 chunk.8.refs_4_
  28.7 0.5 chunk.9.refs_4_
  29.2 0.3 collective-permute-start.13
  30.2 1.8 %collective-permute-start.12 = (f32[64,512]{1,0:T(8,128)S(1)}, f32[64,512]{1,0:T(8,128)S(1)}, u32[]{:S(2)}, u32[]{:S(2)}) collective-permute-start(f32[64,512]{1,0:T(8,128)S(1)} %chunk.8.refs_4_), channel_id=1, source_target_pairs={{0,8},{4,12},{8,0},{12,4},{1,9},{5,13},{9,1},{13,5},{2,10},{6,14},... | collective-permute-start | bytes 393224 | tf_op jit(solution)/shard_map/ppermute | solution.py:16
  31.9 0.5 chunk.10.refs_2_.refs_0_
  32.4 0.0 copy-start
  32.4 6.1 %factor_x.1.refs_5_.inverse_ref = f32[128,128]{1,0:T(8,128)S(1)} custom-call(s32[1]{0:T(128)S(6)} %copy.9.rank_ref, s32[1]{0:T(128)} %bitcast.2.me_ref, f32[32,512]{1,0:T(8,128)S(1)} %add_add_fusion.refs_0_, f32[32,512]{1,0:T(8,128)S(1)} %collective-permute-done.6.refs_1_, f32[32,512]{1,0:T(8,128)S(1)} %collective-permute-done.7.refs_2_.refs_0_, ...), custom_call_target="tpu_custom_call" | custom-call | tf_op jit(solution)/shard_map/factor_x/pallas_call | solution.py:88
  38.5 0.0 collective-permute-done.9.refs_4_.refs_0_
  38.6 0.0 collective-permute-done.10.refs_3_.refs_0_
  38.6 0.5 chunk.11
  39.0 2.5 %collective-permute-start.11 = (f32[64,512]{1,0:T(8,128)S(1)}, f32[64,512]{1,0:T(8,128)S(1)}, u32[]{:S(2)}, u32[]{:S(2)}) collective-permute-start(f32[64,512]{1,0:T(8,128)S(1)} %chunk.11), channel_id=1, source_target_pairs={{0,12},{4,8},{8,4},{12,0},{1,13},{5,9},{9,5},{13,1},{2,14},{6,10},... | collective-permute-start | bytes 393224 | tf_op jit(solution)/shard_map/ppermute | solution.py:16
  41.5 0.3 lift.3.refs_2_.refs_4_
  41.8 5.5 %collective-permute-done.12.refs_1_ = f32[64,512]{1,0:T(8,128)S(1)} collective-permute-done((f32[64,512]{1,0:T(8,128)S(1)}, f32[64,512]{1,0:T(8,128)S(1)}, u32[]{:S(2)}, u32[]{:S(2)}) %collective-permute-start.12) | collective-permute-done | bytes 131104 | tf_op jit(solution)/shard_map/ppermute | solution.py:16
  47.3 0.3 lift.4.refs_1_.refs_3_.refs_6_
  47.6 0.0 collective-permute-done.13.refs_0_
  47.7 0.3 lift.5.refs_4_.refs_5_
  48.0 0.0 collective-permute-done.11.refs_1_
  48.0 0.0 copy-done
  48.0 1.3 %gram.1 = (f32[64,32]{1,0:T(8,128)S(1)}, f32[16,4096]{1,0:T(8,128)S(1)}) custom-call(s32[1]{0:T(128)} %bitcast.here_ref.me_ref, f32[32,64]{1,0:T(8,128)S(1)} %bitcast.11, f32[128,128]{1,0:T(8,128)S(1)} %factor_x.1.refs_5_.inverse_ref, f32[64,512]{1,0:T(8,128)S(1)} %collective-permute-done.9.refs_4_.refs_0_, f32[64,512]{1,0:T(8,128)S(1)} %collective-permute-done.11.refs_1_, ...), custom_call_target="tpu_custom_call" | custom-call | tf_op jit(solution)/shard_map/gram/pallas_call | solution.py:88
  49.3 0.0 collective-permute-start.14
  49.3 1.2 %collective-permute-done.14 = f32[64,32]{1,0:T(8,128)S(1)} collective-permute-done((f32[64,32]{1,0:T(8,128)S(1)}, f32[64,32]{1,0:T(8,128)S(1)}, u32[]{:S(2)}, u32[]{:S(2)}) %collective-permute-start.14) | collective-permute-done | bytes 8224 | tf_op jit(solution)/shard_map/ppermute | solution.py:16
  50.6 1.4 %collective-permute-start.15 = (f32[64,32]{1,0:T(8,128)S(1)}, f32[64,32]{1,0:T(8,128)S(1)}, u32[]{:S(2)}, u32[]{:S(2)}) collective-permute-start(f32[64,32]{1,0:T(8,128)S(1)} %add.34), channel_id=1, source_target_pairs={{0,2},{2,0},{1,3},{3,1},{4,6},{6,4},{5,7},{7,5},{8,10},{10,8},{9,1... | collective-permute-start | bytes 24584 | tf_op jit(solution)/shard_map/ppermute | solution.py:16
  52.0 2.5 %collective-permute-done.15 = f32[64,32]{1,0:T(8,128)S(1)} collective-permute-done((f32[64,32]{1,0:T(8,128)S(1)}, f32[64,32]{1,0:T(8,128)S(1)}, u32[]{:S(2)}, u32[]{:S(2)}) %collective-permute-start.15) | collective-permute-done | bytes 8224 | tf_op jit(solution)/shard_map/ppermute | solution.py:16
  54.5 1.6 %collective-permute-start.18 = (f32[64,32]{1,0:T(8,128)S(1)}, f32[64,32]{1,0:T(8,128)S(1)}, u32[]{:S(2)}, u32[]{:S(2)}) collective-permute-start(f32[64,32]{1,0:T(8,128)S(1)} %add.35.refs_0_), channel_id=1, source_target_pairs={{0,12},{4,8},{8,4},{12,0},{1,13},{5,9},{9,5},{13,1},{2,14},{6,10},... | collective-permute-start | bytes 24584 | tf_op jit(solution)/shard_map/ppermute | solution.py:16
  56.1 1.5 %collective-permute-start.17 = (f32[64,32]{1,0:T(8,128)S(1)}, f32[64,32]{1,0:T(8,128)S(1)}, u32[]{:S(2)}, u32[]{:S(2)}) collective-permute-start(f32[64,32]{1,0:T(8,128)S(1)} %add.35.refs_0_), channel_id=1, source_target_pairs={{0,8},{4,12},{8,0},{12,4},{1,9},{5,13},{9,1},{13,5},{2,10},{6,14},... | collective-permute-start | bytes 24584 | tf_op jit(solution)/shard_map/ppermute | solution.py:16
  57.5 1.3 %collective-permute-start.16 = (f32[64,32]{1,0:T(8,128)S(1)}, f32[64,32]{1,0:T(8,128)S(1)}, u32[]{:S(2)}, u32[]{:S(2)}) collective-permute-start(f32[64,32]{1,0:T(8,128)S(1)} %add.35.refs_0_), channel_id=1, source_target_pairs={{0,4},{4,0},{8,12},{12,8},{1,5},{5,1},{9,13},{13,9},{2,6},{6,2},{1... | collective-permute-start | bytes 24584 | tf_op jit(solution)/shard_map/ppermute | solution.py:16
  59.5 0.9 %collective-permute-done.18.refs_3_ = f32[64,32]{1,0:T(8,128)S(1)} collective-permute-done((f32[64,32]{1,0:T(8,128)S(1)}, f32[64,32]{1,0:T(8,128)S(1)}, u32[]{:S(2)}, u32[]{:S(2)}) %collective-permute-start.18) | collective-permute-done | bytes 8224 | tf_op jit(solution)/shard_map/ppermute | solution.py:16
  60.5 0.4 collective-permute-done.17.refs_2_
  60.9 0.6 collective-permute-done.16.refs_1_
  61.4 1.9 %last.1 = (f32[64,32]{1,0:T(8,128)S(1)}, f32[4,8,8,128]{3,2,1,0:T(8,128)S(1)}, f32[4,8,8,128]{3,2,1,0:T(8,128)S(1)}, f32[4,8,8,128]{3,2,1,0:T(8,128)S(1)}, f32[4,8,8,128]{3,2,1,0:T(8,128)S(1)}) custom-call(s32[1]{0:T(128)S(6)} %copy.10.rank_ref, s32[1]{0:T(128)} %bitcast.here_ref.me_ref, f32[64,32]{1,0:T(8,128)S(1)} %add.35.refs_0_, ...), custom_call_target="tpu_custom_call" | custom-call | tf_op jit(solution)/shard_map/last/pallas_call | solution.py:88
  63.3 1.6 %collective-permute-start.19 = (f32[4,8,8,128]{3,2,1,0:T(8,128)S(1)}, f32[4,8,8,128]{3,2,1,0:T(8,128)S(1)}, u32[]{:S(2)}, u32[]{:S(2)}) collective-permute-start(f32[4,8,8,128]{3,2,1,0:T(8,128)S(1)} %get-tuple-element.22), channel_id=1, source_target_pairs={{0,8},{4,12},{8,0},{12,4},{1,9},{5,13},{9,1},{13,5},{2,10},{6,14},... | collective-permute-start | bytes 393224 | tf_op jit(solution)/shard_map/ppermute | solution.py:16
  64.9 1.7 %collective-permute-start.20 = (f32[4,8,8,128]{3,2,1,0:T(8,128)S(1)}, f32[4,8,8,128]{3,2,1,0:T(8,128)S(1)}, u32[]{:S(2)}, u32[]{:S(2)}) collective-permute-start(f32[4,8,8,128]{3,2,1,0:T(8,128)S(1)} %get-tuple-element.23), channel_id=1, source_target_pairs={{0,4},{4,0},{8,12},{12,8},{1,5},{5,1},{9,13},{13,9},{2,6},{6,2},{1... | collective-permute-start | bytes 393224 | tf_op jit(solution)/shard_map/ppermute | solution.py:16
  66.6 1.2 %collective-permute-start.21 = (f32[4,8,8,128]{3,2,1,0:T(8,128)S(1)}, f32[4,8,8,128]{3,2,1,0:T(8,128)S(1)}, u32[]{:S(2)}, u32[]{:S(2)}) collective-permute-start(f32[4,8,8,128]{3,2,1,0:T(8,128)S(1)} %get-tuple-element.24), channel_id=1, source_target_pairs={{0,12},{4,8},{8,4},{12,0},{1,13},{5,9},{9,5},{13,1},{2,14},{6,10},... | collective-permute-start | bytes 393224 | tf_op jit(solution)/shard_map/ppermute | solution.py:16
  67.8 1.1 %apply.1 = f32[512,128]{1,0:T(8,128)} custom-call(f32[128,128]{1,0:T(8,128)S(1)} %factor_x.1.refs_5_.inverse_ref, f32[32,512]{1,0:T(8,128)S(1)} %add_add_fusion.refs_0_, f32[32,512]{1,0:T(8,128)S(1)} %collective-permute-done.6.refs_1_, f32[32,512]{1,0:T(8,128)S(1)} %collective-permute-done.7.refs_2_.refs_0_, f32[32,512]{1,0:T(8,128)S(1)} %collective-permute-done.8.refs_3_.refs_1_), custom_call_target="tpu_custom_call" | custom-call | tf_op jit(solution)/shard_map/apply/pallas_call | solution.py:88
  68.9 0.7 copy.8
  69.6 4.5 %collective-permute-done.19.refs_0_ = f32[4,8,8,128]{3,2,1,0:T(8,128)S(1)} collective-permute-done((f32[4,8,8,128]{3,2,1,0:T(8,128)S(1)}, f32[4,8,8,128]{3,2,1,0:T(8,128)S(1)}, u32[]{:S(2)}, u32[]{:S(2)}) %collective-permute-start.19) | collective-permute-done | bytes 131104 | tf_op jit(solution)/shard_map/ppermute | solution.py:16
  74.1 0.0 collective-permute-done.20.refs_1_
  74.1 0.0 collective-permute-done.21.refs_2_
  74.1 0.8 %place.1 = f32[4,8,32,128]{3,2,1,0:T(8,128)} custom-call(s32[1]{0:T(128)} %bitcast.here_ref.me_ref, f32[4,8,8,128]{3,2,1,0:T(8,128)S(1)} %collective-permute-done.19.refs_0_, f32[4,8,8,128]{3,2,1,0:T(8,128)S(1)} %collective-permute-done.20.refs_1_, f32[4,8,8,128]{3,2,1,0:T(8,128)S(1)} %collective-permute-done.21.refs_2_, ...), custom_call_target="tpu_custom_call" | custom-call | tf_op jit(solution)/shard_map/place/pallas_call | solution.py:262
  (5 shorter events, 0.1 us)
Async XLA Ops:
  4.5 1.4 %collective-permute-start.1 = (f32[32,512]{1,0:T(8,128)S(1)}, f32[32,512]{1,0:T(8,128)S(1)}, u32[]{:S(2)}, u32[]{:S(2)}) collective-permute-start(f32[32,512]{1,0:T(8,128)S(1)} %get-tuple-element.18), channel_id=1, source_target_pairs={{0,1},{1,0},{2,3},{3,2},{4,5},{5,4},{6,7},{7,6},{8,9},{9,8},{10,11... | collective-permute-start | bytes 196616 | tf_op jit(solution)/shard_map/ppermute | solution.py:16
  5.0 3.8 %collective-permute-start = (f32[32,512]{1,0:T(8,128)S(1)}, f32[32,512]{1,0:T(8,128)S(1)}, u32[]{:S(2)}, u32[]{:S(2)}) collective-permute-start(f32[32,512]{1,0:T(8,128)S(1)} %get-tuple-element.16), channel_id=1, source_target_pairs={{0,1},{1,0},{2,3},{3,2},{4,5},{5,4},{6,7},{7,6},{8,9},{9,8},{10,11... | collective-permute-start | bytes 196616 | tf_op jit(solution)/shard_map/ppermute | solution.py:16
  5.9 5.3 %collective-permute-start.2 = (f32[32,512]{1,0:T(8,128)S(1)}, f32[32,512]{1,0:T(8,128)S(1)}, u32[]{:S(2)}, u32[]{:S(2)}) collective-permute-start(f32[32,512]{1,0:T(8,128)S(1)} %add.29), channel_id=1, source_target_pairs={{0,2},{2,0},{1,3},{3,1},{4,6},{6,4},{5,7},{7,5},{8,10},{10,8},{9,1... | collective-permute-start | bytes 196616 | tf_op jit(solution)/shard_map/ppermute | solution.py:16
  11.3 6.4 %collective-permute-start.5 = (f32[32,512]{1,0:T(8,128)S(1)}, f32[32,512]{1,0:T(8,128)S(1)}, u32[]{:S(2)}, u32[]{:S(2)}) collective-permute-start(f32[32,512]{1,0:T(8,128)S(1)} %add_add_fusion.1), channel_id=1, source_target_pairs={{0,12},{4,8},{8,4},{12,0},{1,13},{5,9},{9,5},{13,1},{2,14},{6,10},... | collective-permute-start | bytes 196616 | tf_op jit(solution)/shard_map/ppermute | solution.py:16
  15.3 4.3 %collective-permute-start.4 = (f32[32,512]{1,0:T(8,128)S(1)}, f32[32,512]{1,0:T(8,128)S(1)}, u32[]{:S(2)}, u32[]{:S(2)}) collective-permute-start(f32[32,512]{1,0:T(8,128)S(1)} %add_add_fusion.1), channel_id=1, source_target_pairs={{0,4},{4,0},{8,12},{12,8},{1,5},{5,1},{9,13},{13,9},{2,6},{6,2},{1... | collective-permute-start | bytes 196616 | tf_op jit(solution)/shard_map/ppermute | solution.py:16
  15.3 5.2 %collective-permute-start.3 = (f32[32,512]{1,0:T(8,128)S(1)}, f32[32,512]{1,0:T(8,128)S(1)}, u32[]{:S(2)}, u32[]{:S(2)}) collective-permute-start(f32[32,512]{1,0:T(8,128)S(1)} %add_add_fusion.1), channel_id=1, source_target_pairs={{0,8},{4,12},{8,0},{12,4},{1,9},{5,13},{9,1},{13,5},{2,10},{6,14},... | collective-permute-start | bytes 196616 | tf_op jit(solution)/shard_map/ppermute | solution.py:16
  20.5 2.2 %collective-permute-start.6 = (f32[32,512]{1,0:T(8,128)S(1)}, f32[32,512]{1,0:T(8,128)S(1)}, u32[]{:S(2)}, u32[]{:S(2)}) collective-permute-start(f32[32,512]{1,0:T(8,128)S(1)} %add_add_fusion.refs_0_), channel_id=1, source_target_pairs={{0,1},{1,0},{2,3},{3,2},{4,5},{5,4},{6,7},{7,6},{8,9},{9,8},{10,11... | collective-permute-start | bytes 196616 | tf_op jit(solution)/shard_map/ppermute | solution.py:16
  20.6 7.6 %collective-permute-start.8 = (f32[32,512]{1,0:T(8,128)S(1)}, f32[32,512]{1,0:T(8,128)S(1)}, u32[]{:S(2)}, u32[]{:S(2)}) collective-permute-start(f32[32,512]{1,0:T(8,128)S(1)} %add_add_fusion.refs_0_), channel_id=1, source_target_pairs={{0,3},{1,2},{2,1},{3,0},{4,7},{5,6},{6,5},{7,4},{8,11},{9,10},{10,... | collective-permute-start | bytes 196616 | tf_op jit(solution)/shard_map/ppermute | solution.py:16
  22.2 6.0 %collective-permute-start.7 = (f32[32,512]{1,0:T(8,128)S(1)}, f32[32,512]{1,0:T(8,128)S(1)}, u32[]{:S(2)}, u32[]{:S(2)}) collective-permute-start(f32[32,512]{1,0:T(8,128)S(1)} %add_add_fusion.refs_0_), channel_id=1, source_target_pairs={{0,2},{1,3},{2,0},{3,1},{4,6},{5,7},{6,4},{7,5},{8,10},{9,11},{10,... | collective-permute-start | bytes 196616 | tf_op jit(solution)/shard_map/ppermute | solution.py:16
  23.2 15.4 %collective-permute-start.10 = (f32[64,512]{1,0:T(8,128)S(1)}, f32[64,512]{1,0:T(8,128)S(1)}, u32[]{:S(2)}, u32[]{:S(2)}) collective-permute-start(f32[64,512]{1,0:T(8,128)S(1)} %chunk.6.refs_2_), channel_id=1, source_target_pairs={{0,8},{4,12},{8,0},{12,4},{1,9},{5,13},{9,1},{13,5},{2,10},{6,14},... | collective-permute-start | bytes 393224 | tf_op jit(solution)/shard_map/ppermute | solution.py:16
  25.4 13.1 %collective-permute-start.9 = (f32[64,512]{1,0:T(8,128)S(1)}, f32[64,512]{1,0:T(8,128)S(1)}, u32[]{:S(2)}, u32[]{:S(2)}) collective-permute-start(f32[64,512]{1,0:T(8,128)S(1)} %chunk.7.refs_2_), channel_id=1, source_target_pairs={{0,12},{4,8},{8,4},{12,0},{1,13},{5,9},{9,5},{13,1},{2,14},{6,10},... | collective-permute-start | bytes 393224 | tf_op jit(solution)/shard_map/ppermute | solution.py:16
  29.2 18.5 %collective-permute-start.13 = (f32[128,512]{1,0:T(8,128)S(1)}, f32[128,512]{1,0:T(8,128)S(1)}, u32[]{:S(2)}, u32[]{:S(2)}) collective-permute-start(f32[128,512]{1,0:T(8,128)S(1)} %chunk.9.refs_4_), channel_id=1, source_target_pairs={{0,4},{4,0},{8,12},{12,8},{1,5},{5,1},{9,13},{13,9},{2,6},{6,2},{1... | collective-permute-start | bytes 786440 | tf_op jit(solution)/shard_map/ppermute | solution.py:16
  30.2 17.2 %collective-permute-start.12 = (f32[64,512]{1,0:T(8,128)S(1)}, f32[64,512]{1,0:T(8,128)S(1)}, u32[]{:S(2)}, u32[]{:S(2)}) collective-permute-start(f32[64,512]{1,0:T(8,128)S(1)} %chunk.8.refs_4_), channel_id=1, source_target_pairs={{0,8},{4,12},{8,0},{12,4},{1,9},{5,13},{9,1},{13,5},{2,10},{6,14},... | collective-permute-start | bytes 393224 | tf_op jit(solution)/shard_map/ppermute | solution.py:16
  32.4 15.6 %copy-start = (f32[64,32]{0,1:T(8,128)S(1)}, f32[64,32]{0,1:T(8,128)}, u32[]{:S(2)}) copy-start(f32[64,32]{0,1:T(8,128)} %param.7) | copy-start | bytes 24580
  39.0 8.9 %collective-permute-start.11 = (f32[64,512]{1,0:T(8,128)S(1)}, f32[64,512]{1,0:T(8,128)S(1)}, u32[]{:S(2)}, u32[]{:S(2)}) collective-permute-start(f32[64,512]{1,0:T(8,128)S(1)} %chunk.11), channel_id=1, source_target_pairs={{0,12},{4,8},{8,4},{12,0},{1,13},{5,9},{9,5},{13,1},{2,14},{6,10},... | collective-permute-start | bytes 393224 | tf_op jit(solution)/shard_map/ppermute | solution.py:16
  49.3 1.2 %collective-permute-start.14 = (f32[64,32]{1,0:T(8,128)S(1)}, f32[64,32]{1,0:T(8,128)S(1)}, u32[]{:S(2)}, u32[]{:S(2)}) collective-permute-start(f32[64,32]{1,0:T(8,128)S(1)} %get-tuple-element.20), channel_id=1, source_target_pairs={{0,1},{1,0},{2,3},{3,2},{4,5},{5,4},{6,7},{7,6},{8,9},{9,8},{10,11... | collective-permute-start | bytes 24584 | tf_op jit(solution)/shard_map/ppermute | solution.py:16
  50.6 3.9 %collective-permute-start.15 = (f32[64,32]{1,0:T(8,128)S(1)}, f32[64,32]{1,0:T(8,128)S(1)}, u32[]{:S(2)}, u32[]{:S(2)}) collective-permute-start(f32[64,32]{1,0:T(8,128)S(1)} %add.34), channel_id=1, source_target_pairs={{0,2},{2,0},{1,3},{3,1},{4,6},{6,4},{5,7},{7,5},{8,10},{10,8},{9,1... | collective-permute-start | bytes 24584 | tf_op jit(solution)/shard_map/ppermute | solution.py:16
  54.5 6.0 %collective-permute-start.18 = (f32[64,32]{1,0:T(8,128)S(1)}, f32[64,32]{1,0:T(8,128)S(1)}, u32[]{:S(2)}, u32[]{:S(2)}) collective-permute-start(f32[64,32]{1,0:T(8,128)S(1)} %add.35.refs_0_), channel_id=1, source_target_pairs={{0,12},{4,8},{8,4},{12,0},{1,13},{5,9},{9,5},{13,1},{2,14},{6,10},... | collective-permute-start | bytes 24584 | tf_op jit(solution)/shard_map/ppermute | solution.py:16
  56.1 4.8 %collective-permute-start.17 = (f32[64,32]{1,0:T(8,128)S(1)}, f32[64,32]{1,0:T(8,128)S(1)}, u32[]{:S(2)}, u32[]{:S(2)}) collective-permute-start(f32[64,32]{1,0:T(8,128)S(1)} %add.35.refs_0_), channel_id=1, source_target_pairs={{0,8},{4,12},{8,0},{12,4},{1,9},{5,13},{9,1},{13,5},{2,10},{6,14},... | collective-permute-start | bytes 24584 | tf_op jit(solution)/shard_map/ppermute | solution.py:16
  57.5 3.9 %collective-permute-start.16 = (f32[64,32]{1,0:T(8,128)S(1)}, f32[64,32]{1,0:T(8,128)S(1)}, u32[]{:S(2)}, u32[]{:S(2)}) collective-permute-start(f32[64,32]{1,0:T(8,128)S(1)} %add.35.refs_0_), channel_id=1, source_target_pairs={{0,4},{4,0},{8,12},{12,8},{1,5},{5,1},{9,13},{13,9},{2,6},{6,2},{1... | collective-permute-start | bytes 24584 | tf_op jit(solution)/shard_map/ppermute | solution.py:16
  63.3 10.8 %collective-permute-start.19 = (f32[4,8,8,128]{3,2,1,0:T(8,128)S(1)}, f32[4,8,8,128]{3,2,1,0:T(8,128)S(1)}, u32[]{:S(2)}, u32[]{:S(2)}) collective-permute-start(f32[4,8,8,128]{3,2,1,0:T(8,128)S(1)} %get-tuple-element.22), channel_id=1, source_target_pairs={{0,8},{4,12},{8,0},{12,4},{1,9},{5,13},{9,1},{13,5},{2,10},{6,14},... | collective-permute-start | bytes 393224 | tf_op jit(solution)/shard_map/ppermute | solution.py:16
  64.9 9.2 %collective-permute-start.20 = (f32[4,8,8,128]{3,2,1,0:T(8,128)S(1)}, f32[4,8,8,128]{3,2,1,0:T(8,128)S(1)}, u32[]{:S(2)}, u32[]{:S(2)}) collective-permute-start(f32[4,8,8,128]{3,2,1,0:T(8,128)S(1)} %get-tuple-element.23), channel_id=1, source_target_pairs={{0,4},{4,0},{8,12},{12,8},{1,5},{5,1},{9,13},{13,9},{2,6},{6,2},{1... | collective-permute-start | bytes 393224 | tf_op jit(solution)/shard_map/ppermute | solution.py:16
  66.6 7.5 %collective-permute-start.21 = (f32[4,8,8,128]{3,2,1,0:T(8,128)S(1)}, f32[4,8,8,128]{3,2,1,0:T(8,128)S(1)}, u32[]{:S(2)}, u32[]{:S(2)}) collective-permute-start(f32[4,8,8,128]{3,2,1,0:T(8,128)S(1)} %get-tuple-element.24), channel_id=1, source_target_pairs={{0,12},{4,8},{8,4},{12,0},{1,13},{5,9},{9,5},{13,1},{2,14},{6,10},... | collective-permute-start | bytes 393224 | tf_op jit(solution)/shard_map/ppermute | solution.py:16
